TPU v7x, 32 devices: a whole 2x2x4 slice. The times are simulated.
32 devices in a mesh: lag: 4 (over z), elem: 8 (over y, x, core).
Axes of the slice: x: 2, y: 2, z: 4, core: 2. Of those that a mesh axis runs over, the one named last changes fastest.
Arguments:
- kernel_tiles: bfloat16 [4, 8192, 1536], P('lag', 'elem'), may hold values from -0.078125 to 0.078125
- shell_index: int32 [4, 8, 3], P('lag', 'elem'), may hold values from 0 to 5
- cone_blocks: int32 [4], P('lag'), may hold values from 1 to 3
- history: bfloat16 [4, 8192, 256], P('lag', 'elem'), may hold values from -6 to 6
- prestress: float32 [8, 4, 256, 256], P('elem', 'lag'), may hold values from -6 to 6
- log_state: float32 [8, 4, 256, 256], P('elem', 'lag'), may hold values from -0.7 to 0.7
- fric_a: float32 [8, 4, 256], P('elem', 'lag'), may hold values from 0.3 to 1
- fric_b: float32 [8, 4, 256], P('elem', 'lag'), may hold values from 0.3 to 1
- normal_stress: float32 [8, 4, 256], P('elem', 'lag'), may hold values from 1 to 4
Outputs:
- final_rates: bfloat16 [8, 4, 256, 256], P('elem', 'lag')
- final_state: float32 [8, 4, 256, 256], P('elem', 'lag')
Inputs may be any that keep to these rules, and one draw needn't show every extreme that they name: `shell_index`: 0 and 1 name the two blocks of the element block below the receiver block, 2 and 3 its own, 4 and 5 those of the block above.
All inputs are finite; a program needn't handle non-finite values.
Results may differ from a plain program's by a relative error of at most 0.0034.
Values may be sent and summed in bfloat16 or wider, within the bound.
No kernel may reach another device: no remote copies, remote signals or barrier semaphores. Data moves between devices by JAX's collectives and lax.ppermute only.
A program may use at most 64 MiB of HBM per device.

v0:
```python
import jax
import jax.numpy as jnp
from jax import lax
from jax.sharding import PartitionSpec as P

BLOCK = 512
SHELL = 3
STEPS = 4
NEWTON = 3


damping = 0.5
time_step = 0.25
creep_square = 0.01


def padded(value, sides, width):
    for axis, dim in sides:
        count, length = (lax.axis_size(axis), value.shape[dim])
        up = [(i, (i + 1) % count) for i in range(count - 1)]
        down = [(j, i) for i, j in up]
        last = lax.slice_in_dim(value, length - width, length, axis=dim)
        leading = lax.slice_in_dim(value, 0, width, axis=dim)
        before = lax.ppermute(last, axis, up)
        after = lax.ppermute(leading, axis, down)
        value = jnp.concatenate([before, value, after], axis=dim)
    return value


def passed_along(block, axis, distance):
    devices = range(lax.axis_size(axis))
    route = [(i - distance, i) for i in devices if i - distance in devices]
    return lax.ppermute(block, axis, route)


def inverse_sinh(value):
    magnitude = jnp.abs(value)
    positive = jnp.log(magnitude + jnp.sqrt(magnitude * magnitude + 1.0))
    return jnp.where(value < 0.0, -positive, positive)


def pick_sources(window, shell_pick, live_count):
    pieces = []
    for shell_slot in range(SHELL):
        row_start = shell_pick[shell_slot] * BLOCK
        source_block = lax.dynamic_slice_in_dim(window, row_start, BLOCK, 0)
        pieces.append(jnp.where(shell_slot < live_count, source_block, jnp.zeros((), jnp.bfloat16)))
    return jnp.concatenate(pieces, 0)


def settle_friction(shear_load, state_now, coef_a, coef_b, sigma):
    scale = 0.5 * jnp.exp(coef_b / coef_a * state_now)
    strength = sigma * coef_a
    velocity = shear_load / (strength * scale + damping)
    for iteration in range(NEWTON):
        scaled = scale * velocity
        residual = strength * inverse_sinh(scaled) + damping * velocity - shear_load
        derivative = strength * scale / jnp.sqrt(1.0 + scaled * scaled) + damping
        velocity = velocity - residual / derivative
    speed = jnp.sqrt(velocity * velocity + creep_square)
    new_state = state_now + time_step * (jnp.exp(-state_now) - speed)
    return (velocity.astype(jnp.bfloat16), new_state)


def shards(
    kernel_tiles,
    shell_index,
    cone_blocks,
    history,
    prestress,
    log_state,
    fric_a,
    fric_b,
    normal_stress,
):
    kernel_tile = kernel_tiles[0]
    lag_rates = history[0]
    shell_pick = shell_index[0, 0]
    live_count = cone_blocks[0]
    first_lag = lax.axis_index("lag") == 0
    own_rows = prestress.shape[2]
    scenarios = prestress.shape[3]
    stress_rows = prestress[0, 0]
    state_rows = log_state[0, 0]
    coef_a = fric_a[0, 0][:, None]
    coef_b = fric_b[0, 0][:, None]
    sigma = normal_stress[0, 0][:, None]
    new_rates = lag_rates
    for step_index in range(STEPS):
        window = padded(lag_rates, (("elem", 0),), lag_rates.shape[0])
        sources = pick_sources(window, shell_pick, live_count)
        traction = lax.psum_scatter(
            jnp.dot(kernel_tile, sources, preferred_element_type=jnp.float32),
            "lag",
            scatter_dimension=0,
            tiled=True,
        )
        new_rates, state_rows = settle_friction(
            stress_rows + traction, state_rows, coef_a, coef_b, sigma
        )
        if step_index + 1 < STEPS:
            arrived = lax.all_gather(new_rates, "lag", axis=0, tiled=True)
        if step_index + 1 < STEPS:
            older = passed_along(lag_rates, "lag", 1)
            lag_rates = jnp.where(first_lag, arrived, older)
    return (
        new_rates.reshape(1, 1, own_rows, scenarios),
        state_rows.reshape(1, 1, own_rows, scenarios),
    )


def solution(mesh):
    in_specs = (
        P("lag", "elem", None),
        P("lag", "elem", None),
        P("lag"),
        P("lag", "elem", None),
        P("elem", "lag", None, None),
        P("elem", "lag", None, None),
        P("elem", "lag", None),
        P("elem", "lag", None),
        P("elem", "lag", None),
    )
    out_specs = (P("elem", "lag", None, None), P("elem", "lag", None, None))
    return jax.shard_map(shards, mesh=mesh, in_specs=in_specs, out_specs=out_specs, check_vma=False)
```

profile of v0, /device:TPU:2, one launch (start us, length us, event | category | flops | bytes accessed | tf_op | source)
XLA Modules:
  0.0 282.6 jit_solution(7725415806515662641)
XLA Ops:
  7.2 0.0 copy-start
  7.2 0.0 reduce-scatter.5.cloned.1.call-start
  7.2 2.2 copy.12
  9.4 1.9 collective-permute-start.1
  11.3 2.4 collective-permute-start
  13.7 1.4 fusion.116
  17.8 2.4 collective-permute-done.1
  20.2 1.9 collective-permute-done
  22.1 1.5 pad_maximum_fusion
  23.6 0.2 dynamic-slice_select_fusion.11
  23.8 0.0 copy-start.4
  23.8 0.0 copy-start.5
  23.8 0.0 copy-start.6
  23.8 0.0 copy-start.3
  23.9 2.1 fusion.8
  25.9 0.0 reduce-scatter.5.cloned.1.call-update
  25.9 0.0 reduce-scatter.7.cloned.1.call-start
  26.0 4.3 %collective-permute-start.2 = (bf16[1024,256]{0,1:T(8,128)(2,1)}, bf16[1024,256]{0,1:T(8,128)(2,1)}, u32[]{:S(2)}, u32[]{:S(2)}) collective-permute-start(bf16[1024,256]{0,1:T(8,128)(2,1)} %bitcast.77), channel_id=1, source_target_pairs={{0,8},{8,16},{16,24},{1,9},{9,17},{17,25},{2,10},{10,18},{18,26},{... | collective-permute-start | bytes 1572872 | tf_op jit(solution)/shard_map/ppermute | solution.py:33
  30.3 0.8 copy.13
  31.1 1.1 copy.11
  32.2 28.5 %reduce-scatter.5.cloned.1.call-done = f32[256,256]{0,1:T(8,128)} async-done(((f32[1024,256]{0,1:T(8,128)}), f32[256,256]{0,1:T(8,128)}) %reduce-scatter.5.cloned.1.call-update) | async-done | bytes 262160 | tf_op jit(solution)/shard_map/reduce_scatter | solution.py:92
  60.7 2.6 fusion.113
  63.3 16.1 %all_gather.9 = bf16[1024,256]{0,1:T(8,128)(2,1)S(1)} all-gather(bf16[256,256]{0,1:T(8,128)(2,1)S(1)} %get-tuple-element.11), channel_id=1, replica_groups=mesh['lag'=4,'elem'=8] {'lag'}, dimensions={0}, use_global_device_ids=true | all-gather | bytes 655360 | tf_op jit(solution)/shard_map/all_gather | solution.py:102
  79.3 0.1 broadcast_select_fusion.2
  79.4 1.9 collective-permute-start.4
  81.3 2.4 collective-permute-start.3
  83.7 5.4 %collective-permute-done.4 = bf16[1024,256]{0,1:T(8,128)(2,1)S(1)} collective-permute-done((bf16[1024,256]{0,1:T(8,128)(2,1)S(1)}, bf16[1024,256]{0,1:T(8,128)(2,1)S(1)}, u32[]{:S(2)}, u32[]{:S(2)}) %collective-permute-start.4) | collective-permute-done | bytes 524320 | tf_op jit(solution)/shard_map/ppermute | solution.py:25
  89.2 2.7 collective-permute-done.3
  91.8 0.1 pad_maximum_fusion.1
  91.9 0.2 dynamic-slice_select_fusion.8
  92.1 2.0 fusion.11
  94.2 0.0 reduce-scatter.7.cloned.1.call-update
  94.2 0.0 reduce-scatter.9.cloned.1.call-start
  94.2 5.7 %collective-permute-start.5 = (bf16[1024,256]{0,1:T(8,128)(2,1)}, bf16[1024,256]{0,1:T(8,128)(2,1)}, u32[]{:S(2)}, u32[]{:S(2)}) collective-permute-start(bf16[1024,256]{0,1:T(8,128)(2,1)} %copy-done.1), channel_id=1, source_target_pairs={{0,8},{8,16},{16,24},{1,9},{9,17},{17,25},{2,10},{10,18},{18,26},{... | collective-permute-start | bytes 1572872 | tf_op jit(solution)/shard_map/ppermute | solution.py:33
  100.0 30.5 %reduce-scatter.7.cloned.1.call-done = f32[256,256]{0,1:T(8,128)} async-done(((f32[1024,256]{0,1:T(8,128)}), f32[256,256]{0,1:T(8,128)}) %reduce-scatter.7.cloned.1.call-update) | async-done | bytes 262160 | tf_op jit(solution)/shard_map/reduce_scatter | solution.py:92
  130.4 2.7 fusion.111
  133.2 16.0 %all_gather.10 = bf16[1024,256]{0,1:T(8,128)(2,1)S(1)} all-gather(bf16[256,256]{0,1:T(8,128)(2,1)S(1)} %get-tuple-element.8), channel_id=1, replica_groups=mesh['lag'=4,'elem'=8] {'lag'}, dimensions={0}, use_global_device_ids=true | all-gather | bytes 655360 | tf_op jit(solution)/shard_map/all_gather | solution.py:102
  149.2 0.1 broadcast_select_fusion.1
  149.2 1.9 collective-permute-start.7
  151.2 2.4 collective-permute-start.6
  153.6 4.3 %collective-permute-done.7 = bf16[1024,256]{0,1:T(8,128)(2,1)S(1)} collective-permute-done((bf16[1024,256]{0,1:T(8,128)(2,1)S(1)}, bf16[1024,256]{0,1:T(8,128)(2,1)S(1)}, u32[]{:S(2)}, u32[]{:S(2)}) %collective-permute-start.7) | collective-permute-done | bytes 524320 | tf_op jit(solution)/shard_map/ppermute | solution.py:25
  157.8 3.8 %collective-permute-done.6 = bf16[1024,256]{0,1:T(8,128)(2,1)S(1)} collective-permute-done((bf16[1024,256]{0,1:T(8,128)(2,1)S(1)}, bf16[1024,256]{0,1:T(8,128)(2,1)S(1)}, u32[]{:S(2)}, u32[]{:S(2)}) %collective-permute-start.6) | collective-permute-done | bytes 524320 | tf_op jit(solution)/shard_map/ppermute | solution.py:24
  161.7 0.1 pad_maximum_fusion.2
  161.8 0.2 dynamic-slice_select_fusion.5
  162.0 2.0 fusion.14
  164.0 0.0 reduce-scatter.9.cloned.1.call-update
  164.0 0.0 reduce-scatter.11.cloned.1.call-start
  164.1 5.7 %collective-permute-start.8 = (bf16[1024,256]{0,1:T(8,128)(2,1)}, bf16[1024,256]{0,1:T(8,128)(2,1)}, u32[]{:S(2)}, u32[]{:S(2)}) collective-permute-start(bf16[1024,256]{0,1:T(8,128)(2,1)} %copy-done.2), channel_id=1, source_target_pairs={{0,8},{8,16},{16,24},{1,9},{9,17},{17,25},{2,10},{10,18},{18,26},{... | collective-permute-start | bytes 1572872 | tf_op jit(solution)/shard_map/ppermute | solution.py:33
  169.8 30.5 %reduce-scatter.9.cloned.1.call-done = f32[256,256]{0,1:T(8,128)} async-done(((f32[1024,256]{0,1:T(8,128)}), f32[256,256]{0,1:T(8,128)}) %reduce-scatter.9.cloned.1.call-update) | async-done | bytes 262160 | tf_op jit(solution)/shard_map/reduce_scatter | solution.py:92
  200.3 2.8 fusion.109
  203.0 15.8 %all_gather.11 = bf16[1024,256]{0,1:T(8,128)(2,1)S(1)} all-gather(bf16[256,256]{0,1:T(8,128)(2,1)S(1)} %get-tuple-element.6), channel_id=1, replica_groups=mesh['lag'=4,'elem'=8] {'lag'}, dimensions={0}, use_global_device_ids=true | all-gather | bytes 655360 | tf_op jit(solution)/shard_map/all_gather | solution.py:102
  218.8 0.1 broadcast_select_fusion
  218.9 1.9 collective-permute-start.10
  220.8 2.4 collective-permute-start.9
  223.2 4.3 %collective-permute-done.10 = bf16[1024,256]{0,1:T(8,128)(2,1)S(1)} collective-permute-done((bf16[1024,256]{0,1:T(8,128)(2,1)S(1)}, bf16[1024,256]{0,1:T(8,128)(2,1)S(1)}, u32[]{:S(2)}, u32[]{:S(2)}) %collective-permute-start.10) | collective-permute-done | bytes 524320 | tf_op jit(solution)/shard_map/ppermute | solution.py:25
  227.5 3.8 %collective-permute-done.9 = bf16[1024,256]{0,1:T(8,128)(2,1)S(1)} collective-permute-done((bf16[1024,256]{0,1:T(8,128)(2,1)S(1)}, bf16[1024,256]{0,1:T(8,128)(2,1)S(1)}, u32[]{:S(2)}, u32[]{:S(2)}) %collective-permute-start.9) | collective-permute-done | bytes 524320 | tf_op jit(solution)/shard_map/ppermute | solution.py:24
  231.3 0.1 pad_maximum_fusion.3
  231.4 0.2 dynamic-slice_select_fusion.2
  231.6 2.0 fusion.17
  233.6 0.0 reduce-scatter.11.cloned.1.call-update
  233.7 36.7 %reduce-scatter.11.cloned.1.call-done = f32[256,256]{0,1:T(8,128)} async-done(((f32[1024,256]{0,1:T(8,128)}), f32[256,256]{0,1:T(8,128)}) %reduce-scatter.11.cloned.1.call-update) | async-done | bytes 262160 | tf_op jit(solution)/shard_map/reduce_scatter | solution.py:92
  270.4 3.1 %add_bitcast_fusion = (f32[1,1,256,256]{2,3,1,0:T(8,128)}, bf16[256,256]{0,1:T(8,128)(2,1)S(1)}) fusion(f32[256,256]{0,1:T(8,128)} %get-tuple-element.7, f32[256,256]{0,1:T(8,128)} %get-tuple-element.10, f32[256,256]{0,1:T(8,128)} %get-tuple-element.9, f32[256]{0:T(256)S(1)} %bitcast.83, f32[256]{0:T(256)S(1)} %broadcast_multiply_fusion, ...), kind=kLoop, calls=%fused_computation.122 | loop fusion | flops 4784128 | bytes 1707008 | tf_op jit(solution)/shard_map/reshape | solution.py:108
  273.5 0.8 copy.14
  274.2 1.8 copy.15
  (14 shorter events, 0.0 us)
Async XLA Ops:
  7.2 16.6 %copy-start = (bf16[1,1024,1536]{2,1,0:T(8,128)(2,1)S(1)}, bf16[1,1024,1536]{2,1,0:T(8,128)(2,1)}, u32[]{:S(2)}) copy-start(bf16[1,1024,1536]{2,1,0:T(8,128)(2,1)} %param.9) | copy-start | bytes 9437188
  7.2 53.5 %reduce-scatter.5.cloned.1.call-start = ((), (), s32[]{:S(2)}) async-start(), calls=%async_computation.4 | async-start | bytes 1310720 | tf_op jit(solution)/shard_map/reduce_scatter | solution.py:92
  9.4 10.8 %collective-permute-start.1 = (bf16[1024,256]{0,1:T(8,128)(2,1)}, bf16[1024,256]{0,1:T(8,128)(2,1)}, u32[]{:S(2)}, u32[]{:S(2)}) collective-permute-start(bf16[1024,256]{0,1:T(8,128)(2,1)} %bitcast.74), channel_id=1, source_target_pairs={{1,0},{2,1},{3,2},{4,3},{5,4},{6,5},{7,6},{9,8},{10,9},{11,10},{12... | collective-permute-start | bytes 1572872 | tf_op jit(solution)/shard_map/ppermute | solution.py:25
  11.3 10.8 %collective-permute-start = (bf16[1024,256]{0,1:T(8,128)(2,1)}, bf16[1024,256]{0,1:T(8,128)(2,1)}, u32[]{:S(2)}, u32[]{:S(2)}) collective-permute-start(bf16[1024,256]{0,1:T(8,128)(2,1)} %bitcast.75), channel_id=1, source_target_pairs={{0,1},{1,2},{2,3},{3,4},{4,5},{5,6},{6,7},{8,9},{9,10},{10,11},{11... | collective-permute-start | bytes 1572872 | tf_op jit(solution)/shard_map/ppermute | solution.py:24
  23.8 6.5 %copy-start.4 = (f32[1,1,256]{2,1,0:T(1,128)S(1)}, f32[1,1,256]{2,1,0:T(1,128)}, u32[]{:S(2)}) copy-start(f32[1,1,256]{2,1,0:T(1,128)} %param.16) | copy-start | bytes 3076
  23.8 6.4 %copy-start.5 = (f32[1,1,256]{2,1,0:T(1,128)S(1)}, f32[1,1,256]{2,1,0:T(1,128)}, u32[]{:S(2)}) copy-start(f32[1,1,256]{2,1,0:T(1,128)} %param.15) | copy-start | bytes 3076
  23.8 6.4 %copy-start.6 = (f32[1,1,256]{2,1,0:T(1,128)S(1)}, f32[1,1,256]{2,1,0:T(1,128)}, u32[]{:S(2)}) copy-start(f32[1,1,256]{2,1,0:T(1,128)} %param.17) | copy-start | bytes 3076
  23.8 6.5 %copy-start.3 = (f32[1,1,256,256]{3,2,1,0:T(8,128)S(1)}, f32[1,1,256,256]{3,2,1,0:T(8,128)}, u32[]{:S(2)}) copy-start(f32[1,1,256,256]{3,2,1,0:T(8,128)} %param.14) | copy-start | bytes 786436
  25.9 104.5 %reduce-scatter.7.cloned.1.call-start = ((), (), s32[]{:S(2)}) async-start(), calls=%async_computation.5 | async-start | bytes 1310720 | tf_op jit(solution)/shard_map/reduce_scatter | solution.py:92
  26.0 53.3 %collective-permute-start.2 = (bf16[1024,256]{0,1:T(8,128)(2,1)}, bf16[1024,256]{0,1:T(8,128)(2,1)}, u32[]{:S(2)}, u32[]{:S(2)}) collective-permute-start(bf16[1024,256]{0,1:T(8,128)(2,1)} %bitcast.77), channel_id=1, source_target_pairs={{0,8},{8,16},{16,24},{1,9},{9,17},{17,25},{2,10},{10,18},{18,26},{... | collective-permute-start | bytes 1572872 | tf_op jit(solution)/shard_map/ppermute | solution.py:33
  79.4 12.5 %copy-start.1 = (bf16[1024,256]{0,1:T(8,128)(2,1)}, bf16[1024,256]{0,1:T(8,128)(2,1)S(1)}, u32[]{:S(2)}) copy-start(bf16[1024,256]{0,1:T(8,128)(2,1)S(1)} %broadcast_select_fusion.2) | copy-start | bytes 1572868
  79.4 9.8 %collective-permute-start.4 = (bf16[1024,256]{0,1:T(8,128)(2,1)S(1)}, bf16[1024,256]{0,1:T(8,128)(2,1)S(1)}, u32[]{:S(2)}, u32[]{:S(2)}) collective-permute-start(bf16[1024,256]{0,1:T(8,128)(2,1)S(1)} %broadcast_select_fusion.2), channel_id=1, source_target_pairs={{1,0},{2,1},{3,2},{4,3},{5,4},{6,5},{7,6},{9,8},{10,9},{11,10},{12... | collective-permute-start | bytes 1572872 | tf_op jit(solution)/shard_map/ppermute | solution.py:25
  81.3 10.5 %collective-permute-start.3 = (bf16[1024,256]{0,1:T(8,128)(2,1)S(1)}, bf16[1024,256]{0,1:T(8,128)(2,1)S(1)}, u32[]{:S(2)}, u32[]{:S(2)}) collective-permute-start(bf16[1024,256]{0,1:T(8,128)(2,1)S(1)} %broadcast_select_fusion.2), channel_id=1, source_target_pairs={{0,1},{1,2},{2,3},{3,4},{4,5},{5,6},{6,7},{8,9},{9,10},{10,11},{11... | collective-permute-start | bytes 1572872 | tf_op jit(solution)/shard_map/ppermute | solution.py:24
  94.2 106.1 %reduce-scatter.9.cloned.1.call-start = ((), (), s32[]{:S(2)}) async-start(), calls=%async_computation.6 | async-start | bytes 1310720 | tf_op jit(solution)/shard_map/reduce_scatter | solution.py:92
  94.2 54.9 %collective-permute-start.5 = (bf16[1024,256]{0,1:T(8,128)(2,1)}, bf16[1024,256]{0,1:T(8,128)(2,1)}, u32[]{:S(2)}, u32[]{:S(2)}) collective-permute-start(bf16[1024,256]{0,1:T(8,128)(2,1)} %copy-done.1), channel_id=1, source_target_pairs={{0,8},{8,16},{16,24},{1,9},{9,17},{17,25},{2,10},{10,18},{18,26},{... | collective-permute-start | bytes 1572872 | tf_op jit(solution)/shard_map/ppermute | solution.py:33
  149.2 12.5 %copy-start.2 = (bf16[1024,256]{0,1:T(8,128)(2,1)}, bf16[1024,256]{0,1:T(8,128)(2,1)S(1)}, u32[]{:S(2)}) copy-start(bf16[1024,256]{0,1:T(8,128)(2,1)S(1)} %broadcast_select_fusion.1) | copy-start | bytes 1572868
  149.2 8.6 %collective-permute-start.7 = (bf16[1024,256]{0,1:T(8,128)(2,1)S(1)}, bf16[1024,256]{0,1:T(8,128)(2,1)S(1)}, u32[]{:S(2)}, u32[]{:S(2)}) collective-permute-start(bf16[1024,256]{0,1:T(8,128)(2,1)S(1)} %broadcast_select_fusion.1), channel_id=1, source_target_pairs={{1,0},{2,1},{3,2},{4,3},{5,4},{6,5},{7,6},{9,8},{10,9},{11,10},{12... | collective-permute-start | bytes 1572872 | tf_op jit(solution)/shard_map/ppermute | solution.py:25
  151.2 10.5 %collective-permute-start.6 = (bf16[1024,256]{0,1:T(8,128)(2,1)S(1)}, bf16[1024,256]{0,1:T(8,128)(2,1)S(1)}, u32[]{:S(2)}, u32[]{:S(2)}) collective-permute-start(bf16[1024,256]{0,1:T(8,128)(2,1)S(1)} %broadcast_select_fusion.1), channel_id=1, source_target_pairs={{0,1},{1,2},{2,3},{3,4},{4,5},{5,6},{6,7},{8,9},{9,10},{10,11},{11... | collective-permute-start | bytes 1572872 | tf_op jit(solution)/shard_map/ppermute | solution.py:24
  164.0 106.3 %reduce-scatter.11.cloned.1.call-start = ((), (), s32[]{:S(2)}) async-start(), calls=%async_computation.7 | async-start | bytes 1310720 | tf_op jit(solution)/shard_map/reduce_scatter | solution.py:92
  164.1 54.7 %collective-permute-start.8 = (bf16[1024,256]{0,1:T(8,128)(2,1)}, bf16[1024,256]{0,1:T(8,128)(2,1)}, u32[]{:S(2)}, u32[]{:S(2)}) collective-permute-start(bf16[1024,256]{0,1:T(8,128)(2,1)} %copy-done.2), channel_id=1, source_target_pairs={{0,8},{8,16},{16,24},{1,9},{9,17},{17,25},{2,10},{10,18},{18,26},{... | collective-permute-start | bytes 1572872 | tf_op jit(solution)/shard_map/ppermute | solution.py:33
  218.9 8.6 %collective-permute-start.10 = (bf16[1024,256]{0,1:T(8,128)(2,1)S(1)}, bf16[1024,256]{0,1:T(8,128)(2,1)S(1)}, u32[]{:S(2)}, u32[]{:S(2)}) collective-permute-start(bf16[1024,256]{0,1:T(8,128)(2,1)S(1)} %broadcast_select_fusion), channel_id=1, source_target_pairs={{1,0},{2,1},{3,2},{4,3},{5,4},{6,5},{7,6},{9,8},{10,9},{11,10},{12... | collective-permute-start | bytes 1572872 | tf_op jit(solution)/shard_map/ppermute | solution.py:25
  220.8 10.5 %collective-permute-start.9 = (bf16[1024,256]{0,1:T(8,128)(2,1)S(1)}, bf16[1024,256]{0,1:T(8,128)(2,1)S(1)}, u32[]{:S(2)}, u32[]{:S(2)}) collective-permute-start(bf16[1024,256]{0,1:T(8,128)(2,1)S(1)} %broadcast_select_fusion), channel_id=1, source_target_pairs={{0,1},{1,2},{2,3},{3,4},{4,5},{5,6},{6,7},{8,9},{9,10},{10,11},{11... | collective-permute-start | bytes 1572872 | tf_op jit(solution)/shard_map/ppermute | solution.py:24
Sparse Core Ops, SparseCore 0:
  26.1 34.6 reduce-scatter.4
  94.3 36.0 reduce-scatter.6
  164.1 36.0 reduce-scatter.8
  233.8 36.5 reduce-scatter.10
where the time goes:
time: 285 us; the launch traced here: 283 us
  waiting for transfers between devices  155 us (54%)
  blocking collectives  47.9 us (17%)
  starting transfers between devices  33.2 us (12%)
  between operations  16.7 us (6%)
  other arithmetic  13.9 us (5%)
  local copies, waits for them, and re-layouts  8.12 us (3%)
  matrix products  8.12 us (3%)
    reduce_scatter x4, waiting for transfers between devices, shards(): lax.psum_scatter(jnp.dot(kernel_tile, sources, preferred_element_type=jnp...  126 us
    all_gather x3, blocking collectives, shards(): arrived = lax.all_gather(new_rates, 'lag', axis=0, tiled=True)  47.9 us
    ppermute x4, waiting for transfers between devices, padded(): after = lax.ppermute(leading, axis, down)  16.4 us
    ppermute x3, starting transfers between devices, passed_along(): return lax.ppermute(block, axis, route)  15.7 us
    ppermute x4, waiting for transfers between devices, padded(): before = lax.ppermute(last, axis, up)  12.2 us
    ppermute x4, starting transfers between devices, padded(): before = lax.ppermute(last, axis, up)  9.63 us
    dot_general x4, matrix products, shards(): jnp.dot(kernel_tile, sources, preferred_element_type=jnp.float32)  8.12 us
    convert_element_type x3, other arithmetic, settle_friction(): return (velocity.astype(jnp.bfloat16), new_state)  8.05 us
  transfers between devices with their start and end apart: 15, of which 12 were waited for; matrix products, arithmetic and copies ran while one was open for 4% of the time, Pallas kernels for 0%

commit v1 on v0

v1 whole, which is shorter than its diff:
```python
import functools

import jax
import jax.numpy as jnp
from jax import lax
from jax.experimental import pallas as pl
from jax.experimental.pallas import tpu as pltpu
from jax.sharding import PartitionSpec as P

STEPS = 4
NEWTON = 3

damping = 0.5
time_step = 0.25
creep_square = 0.01


def exchange(value):
    count = lax.axis_size("elem")
    up = [(i, i + 1) for i in range(count - 1)]
    down = [(j, i) for i, j in up]
    return lax.ppermute(value, "elem", up), lax.ppermute(value, "elem", down)


def product_kernel(lags, rows, meta, tile, below, own, above, *refs):
    outs, sources, sems = refs[:lags], refs[lags], refs[lags + 1]
    slots = sems.shape[0]
    block = sources.shape[0] // slots
    per = own.shape[0] // block
    live, me = meta[slots], meta[slots + 1]

    for k in range(slots):
        spot = sources.at[pl.ds(k * block, block)]
        pick = meta[k]
        start = pl.multiple_of(lax.rem(pick, per) * block, block)
        for which, ref in enumerate((below, own, above)):

            @pl.when((k < live) & (lax.div(pick, per) == which))
            def _():
                pltpu.make_async_copy(ref.at[pl.ds(start, block)], spot, sems.at[k]).start()

        @pl.when(k >= live)
        def _():
            spot[...] = jnp.zeros(spot.shape, spot.dtype)

    for k in range(slots):
        spot = sources.at[pl.ds(k * block, block)]

        @pl.when(k < live)
        def _():
            pltpu.make_async_copy(own.at[pl.ds(0, block)], spot, sems.at[k]).wait()

    for d in range(lags):
        first = pl.multiple_of(lax.rem(me + d, lags) * rows, rows)
        part = jnp.dot(tile[pl.ds(first, rows), :], sources[...], preferred_element_type=jnp.float32)
        outs[d][...] = part.astype(outs[d].dtype)


def product(meta, tile, below, own, above, lags):
    rows, cols = own.shape[0] // lags, own.shape[1]
    slots = meta.shape[0] - 2
    kernel = functools.partial(product_kernel, lags, rows)
    kinds = [jnp.float32] + [jnp.bfloat16] * (lags - 1)
    return pl.pallas_call(
        kernel,
        grid_spec=pltpu.PrefetchScalarGridSpec(
            num_scalar_prefetch=1,
            grid=(1,),
            in_specs=[pl.BlockSpec(memory_space=pltpu.VMEM)] + [pl.BlockSpec(memory_space=pl.ANY)] * 3,
            out_specs=[pl.BlockSpec(memory_space=pltpu.VMEM)] * lags,
            scratch_shapes=[
                pltpu.VMEM((tile.shape[1], cols), jnp.bfloat16),
                pltpu.SemaphoreType.DMA((slots,)),
            ],
        ),
        out_shape=[jax.ShapeDtypeStruct((rows, cols), kind) for kind in kinds],
        compiler_params=pltpu.CompilerParams(vmem_limit_bytes=24 * 1024 * 1024),
        cost_estimate=pl.CostEstimate(
            flops=2 * tile.size * cols, bytes_accessed=2 * (tile.size + 4 * own.size), transcendentals=0
        ),
        name="product",
    )(meta, tile, below, own, above)


def scatter_sum(parts):
    lags = len(parts)
    total = parts[0]
    for d in range(1, lags):
        route = [(i, (i + d) % lags) for i in range(lags)]
        total = total + lax.ppermute(parts[d], "lag", route).astype(jnp.float32)
    return total


def settle_friction(shear_load, state_now, coef_a, coef_b, sigma):
    scale = 0.5 * jnp.exp(coef_b / coef_a * state_now)
    strength = sigma * coef_a
    velocity = shear_load / (strength * scale + damping)
    for _ in range(NEWTON):
        scaled = scale * velocity
        magnitude = jnp.abs(scaled)
        root = jnp.sqrt(magnitude * magnitude + 1.0)
        positive = jnp.log(magnitude + root)
        arc = jnp.where(scaled < 0.0, -positive, positive)
        residual = strength * arc + damping * velocity - shear_load
        derivative = strength * scale / root + damping
        velocity = velocity - residual / derivative
    speed = jnp.sqrt(velocity * velocity + creep_square)
    new_state = state_now + time_step * (jnp.exp(-state_now) - speed)
    return velocity.astype(jnp.bfloat16), new_state


def shards(kernel_tiles, shell_index, cone_blocks, history, prestress, log_state, fric_a, fric_b, normal_stress):
    lags = lax.axis_size("lag")
    me = lax.axis_index("lag")
    tile, field = kernel_tiles[0], history[0]
    meta = jnp.concatenate([shell_index[0, 0], cone_blocks, me[None].astype(jnp.int32)])
    stress, state = prestress[0, 0], log_state[0, 0]
    coef_a, coef_b = fric_a[0, 0][:, None], fric_b[0, 0][:, None]
    sigma = normal_stress[0, 0][:, None]
    for step in range(STEPS):
        below, above = exchange(field)
        traction = scatter_sum(product(meta, tile, below, field, above, lags))
        rates, state = settle_friction(stress + traction, state, coef_a, coef_b, sigma)
        if step + 1 < STEPS:
            older = lax.ppermute(field, "lag", [(i, i + 1) for i in range(lags - 1)])
            newest = lax.all_gather(rates, "lag", axis=0, tiled=True)
            field = jnp.where(me == 0, newest, older)
    return rates[None, None], state[None, None]


def solution(mesh):
    in_specs = (
        P("lag", "elem", None),
        P("lag", "elem", None),
        P("lag"),
        P("lag", "elem", None),
        P("elem", "lag", None, None),
        P("elem", "lag", None, None),
        P("elem", "lag", None),
        P("elem", "lag", None),
        P("elem", "lag", None),
    )
    out_specs = (P("elem", "lag", None, None), P("elem", "lag", None, None))
    return jax.shard_map(shards, mesh=mesh, in_specs=in_specs, out_specs=out_specs, check_vma=False)
```

time: 285 us -> 186 us (0.65)
  waiting for transfers between devices: 155 us -> 60 us
  between operations: 16.7 us -> 1.46 us
  blocking collectives: 47.9 us -> 62.4 us
  starting transfers between devices: 33.2 us -> 45 us
  matrix products: 8.12 us -> 0 us
  other arithmetic: 13.9 us -> 6.93 us
  Pallas kernels: 0 us -> 6.69 us
  local copies, waits for them, and re-layouts: 8.12 us -> 2.94 us
    reduce_scatter x4 -> x0, waiting for transfers between devices: 126 us -> none  [shards(): lax.psum_scatter(jnp.dot(kernel_tile, sources, preferred_element_type=jnp...]
    ppermute x11 -> x23, waiting for transfers between devices: 28.6 us -> 60 us  [the longest x12 34.9 us: scatter_sum(): total = total + lax.ppermute(parts[d], 'lag', route).astype(jnp.float32)]
    all_gather x3, blocking collectives: 47.9 us -> 62.4 us  [shards(): newest = lax.all_gather(rates, 'lag', axis=0, tiled=True)]
    ppermute x11 -> x23, starting transfers between devices: 33 us -> 45 us  [the longest x8 22.3 us: exchange(): return (lax.ppermute(value, 'elem', up), lax.ppermute(value, 'elem', down))]
    dot_general x4 -> x0, matrix products: 8.12 us -> none  [shards(): jnp.dot(kernel_tile, sources, preferred_element_type=jnp.float32)]
    pallas_call x0 -> x4, Pallas kernels: none -> 6.69 us  [product(): pl.pallas_call(kernel, grid_spec=pltpu.PrefetchScalarGridSpec(num_scalar_...]
    convert_element_type x3, other arithmetic: 8.05 us -> 3.17 us  [settle_friction(): return (velocity.astype(jnp.bfloat16), new_state)]
    unnamed x19 -> x8, local copies, waits for them, and re-layouts: 6.69 us -> 2.94 us
  transfers between devices with their start and end apart: 15 -> 23, of which waited for: 12 -> 14; matrix products, arithmetic and copies ran while one was open for 4% -> 2% of each run, Pallas kernels for 0% -> 1%
where the time goes in v1:
time: 186 us; the launch traced here: 185 us
  blocking collectives  62.4 us (34%)
  waiting for transfers between devices  60 us (32%)
  starting transfers between devices  45 us (24%)
  other arithmetic  6.93 us (4%)
  Pallas kernels  6.69 us (4%)
  local copies, waits for them, and re-layouts  2.94 us (2%)
    all_gather x3, blocking collectives, shards(): newest = lax.all_gather(rates, 'lag', axis=0, tiled=True)  62.4 us
    ppermute x12, waiting for transfers between devices, scatter_sum(): total = total + lax.ppermute(parts[d], 'lag', route).astype(jnp.float32)  34.9 us
    ppermute x8, waiting for transfers between devices, exchange(): return (lax.ppermute(value, 'elem', up), lax.ppermute(value, 'elem', down))  25.2 us
    ppermute x8, starting transfers between devices, exchange(): return (lax.ppermute(value, 'elem', up), lax.ppermute(value, 'elem', down))  22.3 us
    ppermute x12, starting transfers between devices, scatter_sum(): total = total + lax.ppermute(parts[d], 'lag', route).astype(jnp.float32)  13.1 us
    ppermute x3, starting transfers between devices, shards(): older = lax.ppermute(field, 'lag', [(i, i + 1) for i in range(lags - 1)])  9.61 us
    pallas_call x4, Pallas kernels, product(): pl.pallas_call(kernel, grid_spec=pltpu.PrefetchScalarGridSpec(num_scalar_...  6.69 us
  transfers between devices with their start and end apart: 23, of which 14 were waited for; matrix products, arithmetic and copies ran while one was open for 2% of the time, Pallas kernels for 1%

profile of v1, /device:TPU:2, one launch (start us, length us, event | category | flops | bytes accessed | tf_op | source)
XLA Modules:
  0.0 185.5 jit_solution(7589861668314959376)
XLA Ops:
  0.6 1.9 %collective-permute-start = (bf16[1024,256]{1,0:T(8,128)(2,1)}, bf16[1024,256]{1,0:T(8,128)(2,1)S(1)}, u32[]{:S(2)}, u32[]{:S(2)}) collective-permute-start(bf16[1024,256]{1,0:T(8,128)(2,1)} %bitcast.50), channel_id=1, source_target_pairs={{0,1},{1,2},{2,3},{3,4},{4,5},{5,6},{6,7},{8,9},{9,10},{10,11},{11... | collective-permute-start | bytes 1572872 | tf_op jit(solution)/shard_map/ppermute | solution.py:22
  2.6 3.6 %collective-permute-start.1 = (bf16[1024,256]{1,0:T(8,128)(2,1)}, bf16[1024,256]{1,0:T(8,128)(2,1)S(1)}, u32[]{:S(2)}, u32[]{:S(2)}) collective-permute-start(bf16[1024,256]{1,0:T(8,128)(2,1)} %bitcast.51), channel_id=1, source_target_pairs={{1,0},{2,1},{3,2},{4,3},{5,4},{6,5},{7,6},{9,8},{10,9},{11,10},{12... | collective-permute-start | bytes 1572872 | tf_op jit(solution)/shard_map/ppermute | solution.py:22
  6.2 3.5 %collective-permute-start.5 = (bf16[1024,256]{1,0:T(8,128)(2,1)}, bf16[1024,256]{1,0:T(8,128)(2,1)S(1)}, u32[]{:S(2)}, u32[]{:S(2)}) collective-permute-start(bf16[1024,256]{1,0:T(8,128)(2,1)} %bitcast.52), channel_id=1, source_target_pairs={{0,8},{8,16},{16,24},{1,9},{9,17},{17,25},{2,10},{10,18},{18,26},{... | collective-permute-start | bytes 1572872 | tf_op jit(solution)/shard_map/ppermute | solution.py:125
  10.4 0.7 pad_add_fusion.meta
  11.1 0.7 fusion.71
  11.8 0.0 collective-permute-done.below
  11.8 4.2 %collective-permute-done.1.above = bf16[1024,256]{1,0:T(8,128)(2,1)S(1)} collective-permute-done((bf16[1024,256]{1,0:T(8,128)(2,1)}, bf16[1024,256]{1,0:T(8,128)(2,1)S(1)}, u32[]{:S(2)}, u32[]{:S(2)}) %collective-permute-start.1) | collective-permute-done | bytes 524320 | tf_op jit(solution)/shard_map/ppermute | solution.py:22
  16.1 1.9 %copy-done = bf16[1,1024,1536]{2,1,0:T(8,128)(2,1)S(1)} copy-done((bf16[1,1024,1536]{2,1,0:T(8,128)(2,1)S(1)}, bf16[1,1024,1536]{2,1,0:T(8,128)(2,1)}, u32[]{:S(2)}) %copy-start) | copy-done | bytes 3145752
  18.0 1.0 copy-done.1
  19.0 1.7 product.4
  20.7 3.7 %collective-permute-start.4 = (bf16[256,256]{1,0:T(8,128)(2,1)S(1)}, bf16[256,256]{1,0:T(8,128)(2,1)S(1)}, u32[]{:S(2)}, u32[]{:S(2)}) collective-permute-start(bf16[256,256]{1,0:T(8,128)(2,1)S(1)} %get-tuple-element.21), channel_id=1, source_target_pairs={{0,24},{8,0},{16,8},{24,16},{1,25},{9,1},{17,9},{25,17},{2,26},{10... | collective-permute-start | bytes 393224 | tf_op jit(solution)/shard_map/ppermute | solution.py:90
  24.4 0.0 collective-permute-start.3
  24.4 1.0 collective-permute-start.2
  25.4 2.2 %collective-permute-done.4 = bf16[256,256]{1,0:T(8,128)(2,1)S(1)} collective-permute-done((bf16[256,256]{1,0:T(8,128)(2,1)S(1)}, bf16[256,256]{1,0:T(8,128)(2,1)S(1)}, u32[]{:S(2)}, u32[]{:S(2)}) %collective-permute-start.4) | collective-permute-done | bytes 131104 | tf_op jit(solution)/shard_map/ppermute | solution.py:90
  27.6 9.3 %collective-permute-done.3 = bf16[256,256]{1,0:T(8,128)(2,1)S(1)} collective-permute-done((bf16[256,256]{1,0:T(8,128)(2,1)S(1)}, bf16[256,256]{1,0:T(8,128)(2,1)S(1)}, u32[]{:S(2)}, u32[]{:S(2)}) %collective-permute-start.3) | collective-permute-done | bytes 131104 | tf_op jit(solution)/shard_map/ppermute | solution.py:90
  36.9 0.0 collective-permute-done.2
  36.9 1.0 fusion.69
  37.9 16.2 %all_gather.9 = bf16[1024,256]{1,0:T(8,128)(2,1)S(1)} all-gather(bf16[256,256]{1,0:T(8,128)(2,1)S(1)} %get-tuple-element.41), channel_id=1, replica_groups=mesh['lag'=4,'elem'=8] {'lag'}, dimensions={0}, use_global_device_ids=true | all-gather | bytes 655360 | tf_op jit(solution)/shard_map/all_gather | solution.py:126
  54.1 0.0 collective-permute-done.5
  54.1 0.1 broadcast_select_fusion.2.own
  54.1 1.9 %collective-permute-start.6 = (bf16[1024,256]{1,0:T(8,128)(2,1)S(1)}, bf16[1024,256]{1,0:T(8,128)(2,1)S(1)}, u32[]{:S(2)}, u32[]{:S(2)}) collective-permute-start(bf16[1024,256]{1,0:T(8,128)(2,1)S(1)} %broadcast_select_fusion.2.own), channel_id=1, source_target_pairs={{0,1},{1,2},{2,3},{3,4},{4,5},{5,6},{6,7},{8,9},{9,10},{10,11},{11... | collective-permute-start | bytes 1572872 | tf_op jit(solution)/shard_map/ppermute | solution.py:22
  56.1 3.6 %collective-permute-start.7 = (bf16[1024,256]{1,0:T(8,128)(2,1)S(1)}, bf16[1024,256]{1,0:T(8,128)(2,1)S(1)}, u32[]{:S(2)}, u32[]{:S(2)}) collective-permute-start(bf16[1024,256]{1,0:T(8,128)(2,1)S(1)} %broadcast_select_fusion.2.own), channel_id=1, source_target_pairs={{1,0},{2,1},{3,2},{4,3},{5,4},{6,5},{7,6},{9,8},{10,9},{11,10},{12... | collective-permute-start | bytes 1572872 | tf_op jit(solution)/shard_map/ppermute | solution.py:22
  59.7 4.9 %collective-permute-done.6.below = bf16[1024,256]{1,0:T(8,128)(2,1)S(1)} collective-permute-done((bf16[1024,256]{1,0:T(8,128)(2,1)S(1)}, bf16[1024,256]{1,0:T(8,128)(2,1)S(1)}, u32[]{:S(2)}, u32[]{:S(2)}) %collective-permute-start.6) | collective-permute-done | bytes 524320 | tf_op jit(solution)/shard_map/ppermute | solution.py:22
  64.6 2.6 %collective-permute-done.7.above = bf16[1024,256]{1,0:T(8,128)(2,1)S(1)} collective-permute-done((bf16[1024,256]{1,0:T(8,128)(2,1)S(1)}, bf16[1024,256]{1,0:T(8,128)(2,1)S(1)}, u32[]{:S(2)}, u32[]{:S(2)}) %collective-permute-start.7) | collective-permute-done | bytes 524320 | tf_op jit(solution)/shard_map/ppermute | solution.py:22
  67.3 1.7 product.5
  68.9 0.8 collective-permute-start.10
  69.7 0.1 collective-permute-start.9
  69.8 1.9 %collective-permute-start.8 = (bf16[256,256]{1,0:T(8,128)(2,1)S(1)}, bf16[256,256]{1,0:T(8,128)(2,1)S(1)}, u32[]{:S(2)}, u32[]{:S(2)}) collective-permute-start(bf16[256,256]{1,0:T(8,128)(2,1)S(1)} %get-tuple-element.23), channel_id=1, source_target_pairs={{0,8},{8,16},{16,24},{24,0},{1,9},{9,17},{17,25},{25,1},{2,10},{10... | collective-permute-start | bytes 393224 | tf_op jit(solution)/shard_map/ppermute | solution.py:90
  71.8 3.4 %collective-permute-start.11 = (bf16[1024,256]{1,0:T(8,128)(2,1)S(1)}, bf16[1024,256]{1,0:T(8,128)(2,1)S(1)}, u32[]{:S(2)}, u32[]{:S(2)}) collective-permute-start(bf16[1024,256]{1,0:T(8,128)(2,1)S(1)} %broadcast_select_fusion.2.own), channel_id=1, source_target_pairs={{0,8},{8,16},{16,24},{1,9},{9,17},{17,25},{2,10},{10,18},{18,26},{... | collective-permute-start | bytes 1572872 | tf_op jit(solution)/shard_map/ppermute | solution.py:125
  75.1 0.0 collective-permute-done.10
  75.2 6.7 %collective-permute-done.9 = bf16[256,256]{1,0:T(8,128)(2,1)S(1)} collective-permute-done((bf16[256,256]{1,0:T(8,128)(2,1)S(1)}, bf16[256,256]{1,0:T(8,128)(2,1)S(1)}, u32[]{:S(2)}, u32[]{:S(2)}) %collective-permute-start.9) | collective-permute-done | bytes 131104 | tf_op jit(solution)/shard_map/ppermute | solution.py:90
  81.9 0.0 collective-permute-done.8
  81.9 1.1 fusion.67
  83.0 23.6 %all_gather.10 = bf16[1024,256]{1,0:T(8,128)(2,1)S(1)} all-gather(bf16[256,256]{1,0:T(8,128)(2,1)S(1)} %get-tuple-element.38), channel_id=1, replica_groups=mesh['lag'=4,'elem'=8] {'lag'}, dimensions={0}, use_global_device_ids=true | all-gather | bytes 655360 | tf_op jit(solution)/shard_map/all_gather | solution.py:126
  106.5 0.0 collective-permute-done.11
  106.5 0.1 broadcast_select_fusion.1.own
  106.6 1.9 %collective-permute-start.12 = (bf16[1024,256]{1,0:T(8,128)(2,1)S(1)}, bf16[1024,256]{1,0:T(8,128)(2,1)S(1)}, u32[]{:S(2)}, u32[]{:S(2)}) collective-permute-start(bf16[1024,256]{1,0:T(8,128)(2,1)S(1)} %broadcast_select_fusion.1.own), channel_id=1, source_target_pairs={{0,1},{1,2},{2,3},{3,4},{4,5},{5,6},{6,7},{8,9},{9,10},{10,11},{11... | collective-permute-start | bytes 1572872 | tf_op jit(solution)/shard_map/ppermute | solution.py:22
  108.5 3.6 %collective-permute-start.13 = (bf16[1024,256]{1,0:T(8,128)(2,1)S(1)}, bf16[1024,256]{1,0:T(8,128)(2,1)S(1)}, u32[]{:S(2)}, u32[]{:S(2)}) collective-permute-start(bf16[1024,256]{1,0:T(8,128)(2,1)S(1)} %broadcast_select_fusion.1.own), channel_id=1, source_target_pairs={{1,0},{2,1},{3,2},{4,3},{5,4},{6,5},{7,6},{9,8},{10,9},{11,10},{12... | collective-permute-start | bytes 1572872 | tf_op jit(solution)/shard_map/ppermute | solution.py:22
  112.2 4.9 %collective-permute-done.12.below = bf16[1024,256]{1,0:T(8,128)(2,1)S(1)} collective-permute-done((bf16[1024,256]{1,0:T(8,128)(2,1)S(1)}, bf16[1024,256]{1,0:T(8,128)(2,1)S(1)}, u32[]{:S(2)}, u32[]{:S(2)}) %collective-permute-start.12) | collective-permute-done | bytes 524320 | tf_op jit(solution)/shard_map/ppermute | solution.py:22
  117.1 1.8 collective-permute-done.13.above
  118.9 1.7 product.6
  120.5 0.1 collective-permute-start.16
  120.6 0.8 collective-permute-start.15
  121.4 1.9 %collective-permute-start.14 = (bf16[256,256]{1,0:T(8,128)(2,1)S(1)}, bf16[256,256]{1,0:T(8,128)(2,1)S(1)}, u32[]{:S(2)}, u32[]{:S(2)}) collective-permute-start(bf16[256,256]{1,0:T(8,128)(2,1)S(1)} %get-tuple-element.27), channel_id=1, source_target_pairs={{0,8},{8,16},{16,24},{24,0},{1,9},{9,17},{17,25},{25,1},{2,10},{10... | collective-permute-start | bytes 393224 | tf_op jit(solution)/shard_map/ppermute | solution.py:90
  123.4 2.7 %collective-permute-start.17 = (bf16[1024,256]{1,0:T(8,128)(2,1)S(1)}, bf16[1024,256]{1,0:T(8,128)(2,1)S(1)}, u32[]{:S(2)}, u32[]{:S(2)}) collective-permute-start(bf16[1024,256]{1,0:T(8,128)(2,1)S(1)} %broadcast_select_fusion.1.own), channel_id=1, source_target_pairs={{0,8},{8,16},{16,24},{1,9},{9,17},{17,25},{2,10},{10,18},{18,26},{... | collective-permute-start | bytes 1572872 | tf_op jit(solution)/shard_map/ppermute | solution.py:125
  126.1 0.6 collective-permute-done.16
  126.7 6.2 %collective-permute-done.15 = bf16[256,256]{1,0:T(8,128)(2,1)S(1)} collective-permute-done((bf16[256,256]{1,0:T(8,128)(2,1)S(1)}, bf16[256,256]{1,0:T(8,128)(2,1)S(1)}, u32[]{:S(2)}, u32[]{:S(2)}) %collective-permute-start.15) | collective-permute-done | bytes 131104 | tf_op jit(solution)/shard_map/ppermute | solution.py:90
  132.9 0.0 collective-permute-done.14
  132.9 1.1 fusion.65
  134.0 22.7 %all_gather.11 = bf16[1024,256]{1,0:T(8,128)(2,1)S(1)} all-gather(bf16[256,256]{1,0:T(8,128)(2,1)S(1)} %get-tuple-element.36), channel_id=1, replica_groups=mesh['lag'=4,'elem'=8] {'lag'}, dimensions={0}, use_global_device_ids=true | all-gather | bytes 655360 | tf_op jit(solution)/shard_map/all_gather | solution.py:126
  156.6 0.0 collective-permute-done.17
  156.7 0.1 broadcast_select_fusion.own
  156.7 1.9 %collective-permute-start.18 = (bf16[1024,256]{1,0:T(8,128)(2,1)S(1)}, bf16[1024,256]{1,0:T(8,128)(2,1)S(1)}, u32[]{:S(2)}, u32[]{:S(2)}) collective-permute-start(bf16[1024,256]{1,0:T(8,128)(2,1)S(1)} %broadcast_select_fusion.own), channel_id=1, source_target_pairs={{0,1},{1,2},{2,3},{3,4},{4,5},{5,6},{6,7},{8,9},{9,10},{10,11},{11... | collective-permute-start | bytes 1572872 | tf_op jit(solution)/shard_map/ppermute | solution.py:22
  158.6 3.6 %collective-permute-start.19 = (bf16[1024,256]{1,0:T(8,128)(2,1)S(1)}, bf16[1024,256]{1,0:T(8,128)(2,1)S(1)}, u32[]{:S(2)}, u32[]{:S(2)}) collective-permute-start(bf16[1024,256]{1,0:T(8,128)(2,1)S(1)} %broadcast_select_fusion.own), channel_id=1, source_target_pairs={{1,0},{2,1},{3,2},{4,3},{5,4},{6,5},{7,6},{9,8},{10,9},{11,10},{12... | collective-permute-start | bytes 1572872 | tf_op jit(solution)/shard_map/ppermute | solution.py:22
  162.3 4.9 %collective-permute-done.18.below = bf16[1024,256]{1,0:T(8,128)(2,1)S(1)} collective-permute-done((bf16[1024,256]{1,0:T(8,128)(2,1)S(1)}, bf16[1024,256]{1,0:T(8,128)(2,1)S(1)}, u32[]{:S(2)}, u32[]{:S(2)}) %collective-permute-start.18) | collective-permute-done | bytes 524320 | tf_op jit(solution)/shard_map/ppermute | solution.py:22
  167.2 1.8 collective-permute-done.19.above
  169.0 1.7 product.7
  170.7 0.5 collective-permute-start.22
  171.2 0.5 collective-permute-start.21
  171.7 1.8 collective-permute-start.20
  173.5 3.2 %collective-permute-done.22 = bf16[256,256]{1,0:T(8,128)(2,1)S(1)} collective-permute-done((bf16[256,256]{1,0:T(8,128)(2,1)S(1)}, bf16[256,256]{1,0:T(8,128)(2,1)S(1)}, u32[]{:S(2)}, u32[]{:S(2)}) %collective-permute-start.22) | collective-permute-done | bytes 131104 | tf_op jit(solution)/shard_map/ppermute | solution.py:90
  176.6 6.7 %collective-permute-done.21 = bf16[256,256]{1,0:T(8,128)(2,1)S(1)} collective-permute-done((bf16[256,256]{1,0:T(8,128)(2,1)S(1)}, bf16[256,256]{1,0:T(8,128)(2,1)S(1)}, u32[]{:S(2)}, u32[]{:S(2)}) %collective-permute-start.21) | collective-permute-done | bytes 131104 | tf_op jit(solution)/shard_map/ppermute | solution.py:90
  183.3 0.0 collective-permute-done.20
  183.3 2.1 %add_bitcast_fusion = (f32[1,1,256,256]{3,2,1,0:T(8,128)}, bf16[256,256]{1,0:T(8,128)(2,1)}) fusion(f32[256,256]{1,0:T(8,128)S(1)} %get-tuple-element.37, f32[256,256]{1,0:T(8,128)S(1)} %get-tuple-element.40, f32[256,256]{1,0:T(8,128)S(1)} %get-tuple-element.39, f32[256]{0:T(256)S(1)} %bitcast.59, f32[256]{0:T(256)S(1)} %broadcast_multiply_fusion, ...), kind=kLoop, calls=%fused_computation.86 | loop fusion | flops 5177344 | bytes 2100224 | tf_op jit(solution)/shard_map/broadcast_in_dim | solution.py:128
  (7 shorter events, 0.0 us)
Async XLA Ops:
  0.6 11.2 %collective-permute-start = (bf16[1024,256]{1,0:T(8,128)(2,1)}, bf16[1024,256]{1,0:T(8,128)(2,1)S(1)}, u32[]{:S(2)}, u32[]{:S(2)}) collective-permute-start(bf16[1024,256]{1,0:T(8,128)(2,1)} %bitcast.50), channel_id=1, source_target_pairs={{0,1},{1,2},{2,3},{3,4},{4,5},{5,6},{6,7},{8,9},{9,10},{10,11},{11... | collective-permute-start | bytes 1572872 | tf_op jit(solution)/shard_map/ppermute | solution.py:22
  2.6 13.5 %collective-permute-start.1 = (bf16[1024,256]{1,0:T(8,128)(2,1)}, bf16[1024,256]{1,0:T(8,128)(2,1)S(1)}, u32[]{:S(2)}, u32[]{:S(2)}) collective-permute-start(bf16[1024,256]{1,0:T(8,128)(2,1)} %bitcast.51), channel_id=1, source_target_pairs={{1,0},{2,1},{3,2},{4,3},{5,4},{6,5},{7,6},{9,8},{10,9},{11,10},{12... | collective-permute-start | bytes 1572872 | tf_op jit(solution)/shard_map/ppermute | solution.py:22
  6.2 47.8 %collective-permute-start.5 = (bf16[1024,256]{1,0:T(8,128)(2,1)}, bf16[1024,256]{1,0:T(8,128)(2,1)S(1)}, u32[]{:S(2)}, u32[]{:S(2)}) collective-permute-start(bf16[1024,256]{1,0:T(8,128)(2,1)} %bitcast.52), channel_id=1, source_target_pairs={{0,8},{8,16},{16,24},{1,9},{9,17},{17,25},{2,10},{10,18},{18,26},{... | collective-permute-start | bytes 1572872 | tf_op jit(solution)/shard_map/ppermute | solution.py:125
  16.1 1.9 %copy-start = (bf16[1,1024,1536]{2,1,0:T(8,128)(2,1)S(1)}, bf16[1,1024,1536]{2,1,0:T(8,128)(2,1)}, u32[]{:S(2)}) copy-start(bf16[1,1024,1536]{2,1,0:T(8,128)(2,1)} %param.9) | copy-start | bytes 9437188
  18.0 1.0 copy-start.1
  19.0 17.9 %copy-start.2 = (f32[1,1,256,256]{3,2,1,0:T(8,128)S(1)}, f32[1,1,256,256]{3,2,1,0:T(8,128)}, u32[]{:S(2)}) copy-start(f32[1,1,256,256]{3,2,1,0:T(8,128)} %param.13) | copy-start | bytes 786436
  19.0 17.9 %copy-start.3 = (f32[1,1,256,256]{3,2,1,0:T(8,128)S(1)}, f32[1,1,256,256]{3,2,1,0:T(8,128)}, u32[]{:S(2)}) copy-start(f32[1,1,256,256]{3,2,1,0:T(8,128)} %param.14) | copy-start | bytes 786436
  20.7 6.9 %collective-permute-start.4 = (bf16[256,256]{1,0:T(8,128)(2,1)S(1)}, bf16[256,256]{1,0:T(8,128)(2,1)S(1)}, u32[]{:S(2)}, u32[]{:S(2)}) collective-permute-start(bf16[256,256]{1,0:T(8,128)(2,1)S(1)} %get-tuple-element.21), channel_id=1, source_target_pairs={{0,24},{8,0},{16,8},{24,16},{1,25},{9,1},{17,9},{25,17},{2,26},{10... | collective-permute-start | bytes 393224 | tf_op jit(solution)/shard_map/ppermute | solution.py:90
  24.4 12.5 %collective-permute-start.3 = (bf16[256,256]{1,0:T(8,128)(2,1)S(1)}, bf16[256,256]{1,0:T(8,128)(2,1)S(1)}, u32[]{:S(2)}, u32[]{:S(2)}) collective-permute-start(bf16[256,256]{1,0:T(8,128)(2,1)S(1)} %get-tuple-element.20), channel_id=1, source_target_pairs={{0,16},{8,24},{16,0},{24,8},{1,17},{9,25},{17,1},{25,9},{2,18},{10... | collective-permute-start | bytes 393224 | tf_op jit(solution)/shard_map/ppermute | solution.py:90
  24.4 12.5 %collective-permute-start.2 = (bf16[256,256]{1,0:T(8,128)(2,1)S(1)}, bf16[256,256]{1,0:T(8,128)(2,1)S(1)}, u32[]{:S(2)}, u32[]{:S(2)}) collective-permute-start(bf16[256,256]{1,0:T(8,128)(2,1)S(1)} %get-tuple-element.19), channel_id=1, source_target_pairs={{0,8},{8,16},{16,24},{24,0},{1,9},{9,17},{17,25},{25,1},{2,10},{10... | collective-permute-start | bytes 393224 | tf_op jit(solution)/shard_map/ppermute | solution.py:90
  54.1 10.5 %collective-permute-start.6 = (bf16[1024,256]{1,0:T(8,128)(2,1)S(1)}, bf16[1024,256]{1,0:T(8,128)(2,1)S(1)}, u32[]{:S(2)}, u32[]{:S(2)}) collective-permute-start(bf16[1024,256]{1,0:T(8,128)(2,1)S(1)} %broadcast_select_fusion.2.own), channel_id=1, source_target_pairs={{0,1},{1,2},{2,3},{3,4},{4,5},{5,6},{6,7},{8,9},{9,10},{10,11},{11... | collective-permute-start | bytes 1572872 | tf_op jit(solution)/shard_map/ppermute | solution.py:22
  56.1 11.2 %collective-permute-start.7 = (bf16[1024,256]{1,0:T(8,128)(2,1)S(1)}, bf16[1024,256]{1,0:T(8,128)(2,1)S(1)}, u32[]{:S(2)}, u32[]{:S(2)}) collective-permute-start(bf16[1024,256]{1,0:T(8,128)(2,1)S(1)} %broadcast_select_fusion.2.own), channel_id=1, source_target_pairs={{1,0},{2,1},{3,2},{4,3},{5,4},{6,5},{7,6},{9,8},{10,9},{11,10},{12... | collective-permute-start | bytes 1572872 | tf_op jit(solution)/shard_map/ppermute | solution.py:22
  68.9 6.2 %collective-permute-start.10 = (bf16[256,256]{1,0:T(8,128)(2,1)S(1)}, bf16[256,256]{1,0:T(8,128)(2,1)S(1)}, u32[]{:S(2)}, u32[]{:S(2)}) collective-permute-start(bf16[256,256]{1,0:T(8,128)(2,1)S(1)} %get-tuple-element.25), channel_id=1, source_target_pairs={{0,24},{8,0},{16,8},{24,16},{1,25},{9,1},{17,9},{25,17},{2,26},{10... | collective-permute-start | bytes 393224 | tf_op jit(solution)/shard_map/ppermute | solution.py:90
  69.7 12.2 %collective-permute-start.9 = (bf16[256,256]{1,0:T(8,128)(2,1)S(1)}, bf16[256,256]{1,0:T(8,128)(2,1)S(1)}, u32[]{:S(2)}, u32[]{:S(2)}) collective-permute-start(bf16[256,256]{1,0:T(8,128)(2,1)S(1)} %get-tuple-element.24), channel_id=1, source_target_pairs={{0,16},{8,24},{16,0},{24,8},{1,17},{9,25},{17,1},{25,9},{2,18},{10... | collective-permute-start | bytes 393224 | tf_op jit(solution)/shard_map/ppermute | solution.py:90
  69.8 12.1 %collective-permute-start.8 = (bf16[256,256]{1,0:T(8,128)(2,1)S(1)}, bf16[256,256]{1,0:T(8,128)(2,1)S(1)}, u32[]{:S(2)}, u32[]{:S(2)}) collective-permute-start(bf16[256,256]{1,0:T(8,128)(2,1)S(1)} %get-tuple-element.23), channel_id=1, source_target_pairs={{0,8},{8,16},{16,24},{24,0},{1,9},{9,17},{17,25},{25,1},{2,10},{10... | collective-permute-start | bytes 393224 | tf_op jit(solution)/shard_map/ppermute | solution.py:90
  71.8 34.8 %collective-permute-start.11 = (bf16[1024,256]{1,0:T(8,128)(2,1)S(1)}, bf16[1024,256]{1,0:T(8,128)(2,1)S(1)}, u32[]{:S(2)}, u32[]{:S(2)}) collective-permute-start(bf16[1024,256]{1,0:T(8,128)(2,1)S(1)} %broadcast_select_fusion.2.own), channel_id=1, source_target_pairs={{0,8},{8,16},{16,24},{1,9},{9,17},{17,25},{2,10},{10,18},{18,26},{... | collective-permute-start | bytes 1572872 | tf_op jit(solution)/shard_map/ppermute | solution.py:125
  106.6 10.5 %collective-permute-start.12 = (bf16[1024,256]{1,0:T(8,128)(2,1)S(1)}, bf16[1024,256]{1,0:T(8,128)(2,1)S(1)}, u32[]{:S(2)}, u32[]{:S(2)}) collective-permute-start(bf16[1024,256]{1,0:T(8,128)(2,1)S(1)} %broadcast_select_fusion.1.own), channel_id=1, source_target_pairs={{0,1},{1,2},{2,3},{3,4},{4,5},{5,6},{6,7},{8,9},{9,10},{10,11},{11... | collective-permute-start | bytes 1572872 | tf_op jit(solution)/shard_map/ppermute | solution.py:22
  108.5 10.3 %collective-permute-start.13 = (bf16[1024,256]{1,0:T(8,128)(2,1)S(1)}, bf16[1024,256]{1,0:T(8,128)(2,1)S(1)}, u32[]{:S(2)}, u32[]{:S(2)}) collective-permute-start(bf16[1024,256]{1,0:T(8,128)(2,1)S(1)} %broadcast_select_fusion.1.own), channel_id=1, source_target_pairs={{1,0},{2,1},{3,2},{4,3},{5,4},{6,5},{7,6},{9,8},{10,9},{11,10},{12... | collective-permute-start | bytes 1572872 | tf_op jit(solution)/shard_map/ppermute | solution.py:22
  120.5 6.2 %collective-permute-start.16 = (bf16[256,256]{1,0:T(8,128)(2,1)S(1)}, bf16[256,256]{1,0:T(8,128)(2,1)S(1)}, u32[]{:S(2)}, u32[]{:S(2)}) collective-permute-start(bf16[256,256]{1,0:T(8,128)(2,1)S(1)} %get-tuple-element.29), channel_id=1, source_target_pairs={{0,24},{8,0},{16,8},{24,16},{1,25},{9,1},{17,9},{25,17},{2,26},{10... | collective-permute-start | bytes 393224 | tf_op jit(solution)/shard_map/ppermute | solution.py:90
  120.6 12.3 %collective-permute-start.15 = (bf16[256,256]{1,0:T(8,128)(2,1)S(1)}, bf16[256,256]{1,0:T(8,128)(2,1)S(1)}, u32[]{:S(2)}, u32[]{:S(2)}) collective-permute-start(bf16[256,256]{1,0:T(8,128)(2,1)S(1)} %get-tuple-element.28), channel_id=1, source_target_pairs={{0,16},{8,24},{16,0},{24,8},{1,17},{9,25},{17,1},{25,9},{2,18},{10... | collective-permute-start | bytes 393224 | tf_op jit(solution)/shard_map/ppermute | solution.py:90
  121.4 11.5 %collective-permute-start.14 = (bf16[256,256]{1,0:T(8,128)(2,1)S(1)}, bf16[256,256]{1,0:T(8,128)(2,1)S(1)}, u32[]{:S(2)}, u32[]{:S(2)}) collective-permute-start(bf16[256,256]{1,0:T(8,128)(2,1)S(1)} %get-tuple-element.27), channel_id=1, source_target_pairs={{0,8},{8,16},{16,24},{24,0},{1,9},{9,17},{17,25},{25,1},{2,10},{10... | collective-permute-start | bytes 393224 | tf_op jit(solution)/shard_map/ppermute | solution.py:90
  123.4 33.3 %collective-permute-start.17 = (bf16[1024,256]{1,0:T(8,128)(2,1)S(1)}, bf16[1024,256]{1,0:T(8,128)(2,1)S(1)}, u32[]{:S(2)}, u32[]{:S(2)}) collective-permute-start(bf16[1024,256]{1,0:T(8,128)(2,1)S(1)} %broadcast_select_fusion.1.own), channel_id=1, source_target_pairs={{0,8},{8,16},{16,24},{1,9},{9,17},{17,25},{2,10},{10,18},{18,26},{... | collective-permute-start | bytes 1572872 | tf_op jit(solution)/shard_map/ppermute | solution.py:125
  156.7 10.5 %collective-permute-start.18 = (bf16[1024,256]{1,0:T(8,128)(2,1)S(1)}, bf16[1024,256]{1,0:T(8,128)(2,1)S(1)}, u32[]{:S(2)}, u32[]{:S(2)}) collective-permute-start(bf16[1024,256]{1,0:T(8,128)(2,1)S(1)} %broadcast_select_fusion.own), channel_id=1, source_target_pairs={{0,1},{1,2},{2,3},{3,4},{4,5},{5,6},{6,7},{8,9},{9,10},{10,11},{11... | collective-permute-start | bytes 1572872 | tf_op jit(solution)/shard_map/ppermute | solution.py:22
  158.6 10.3 %collective-permute-start.19 = (bf16[1024,256]{1,0:T(8,128)(2,1)S(1)}, bf16[1024,256]{1,0:T(8,128)(2,1)S(1)}, u32[]{:S(2)}, u32[]{:S(2)}) collective-permute-start(bf16[1024,256]{1,0:T(8,128)(2,1)S(1)} %broadcast_select_fusion.own), channel_id=1, source_target_pairs={{1,0},{2,1},{3,2},{4,3},{5,4},{6,5},{7,6},{9,8},{10,9},{11,10},{12... | collective-permute-start | bytes 1572872 | tf_op jit(solution)/shard_map/ppermute | solution.py:22
  170.7 6.0 %collective-permute-start.22 = (bf16[256,256]{1,0:T(8,128)(2,1)S(1)}, bf16[256,256]{1,0:T(8,128)(2,1)S(1)}, u32[]{:S(2)}, u32[]{:S(2)}) collective-permute-start(bf16[256,256]{1,0:T(8,128)(2,1)S(1)} %get-tuple-element.33), channel_id=1, source_target_pairs={{0,24},{8,0},{16,8},{24,16},{1,25},{9,1},{17,9},{25,17},{2,26},{10... | collective-permute-start | bytes 393224 | tf_op jit(solution)/shard_map/ppermute | solution.py:90
  171.2 12.1 %collective-permute-start.21 = (bf16[256,256]{1,0:T(8,128)(2,1)S(1)}, bf16[256,256]{1,0:T(8,128)(2,1)S(1)}, u32[]{:S(2)}, u32[]{:S(2)}) collective-permute-start(bf16[256,256]{1,0:T(8,128)(2,1)S(1)} %get-tuple-element.32), channel_id=1, source_target_pairs={{0,16},{8,24},{16,0},{24,8},{1,17},{9,25},{17,1},{25,9},{2,18},{10... | collective-permute-start | bytes 393224 | tf_op jit(solution)/shard_map/ppermute | solution.py:90
  171.7 11.6 %collective-permute-start.20 = (bf16[256,256]{1,0:T(8,128)(2,1)S(1)}, bf16[256,256]{1,0:T(8,128)(2,1)S(1)}, u32[]{:S(2)}, u32[]{:S(2)}) collective-permute-start(bf16[256,256]{1,0:T(8,128)(2,1)S(1)} %get-tuple-element.31), channel_id=1, source_target_pairs={{0,8},{8,16},{16,24},{24,0},{1,9},{9,17},{17,25},{25,1},{2,10},{10... | collective-permute-start | bytes 393224 | tf_op jit(solution)/shard_map/ppermute | solution.py:90

commit v2 on v1

--- a/solution.py
+++ b/solution.py
@@ -15,19 +15,19 @@
 creep_square = 0.01
 
 
-def exchange(value):
+def exchange(value, planes):
     count = lax.axis_size("elem")
-    up = [(i, i + 1) for i in range(count - 1)]
+    up = [(i * count + j, i * count + j + 1) for i in planes for j in range(count - 1)]
     down = [(j, i) for i, j in up]
-    return lax.ppermute(value, "elem", up), lax.ppermute(value, "elem", down)
-
-
-def product_kernel(lags, rows, meta, tile, below, own, above, *refs):
-    outs, sources, sems = refs[:lags], refs[lags], refs[lags + 1]
+    axes = ("lag", "elem")
+    return lax.ppermute(value, axes, up), lax.ppermute(value, axes, down)
+
+
+def fetch(meta, below, own, above, sources, sems):
     slots = sems.shape[0]
     block = sources.shape[0] // slots
     per = own.shape[0] // block
-    live, me = meta[slots], meta[slots + 1]
+    live = meta[slots]
 
     for k in range(slots):
         spot = sources.at[pl.ds(k * block, block)]
@@ -50,6 +50,11 @@
         def _():
             pltpu.make_async_copy(own.at[pl.ds(0, block)], spot, sems.at[k]).wait()
 
+
+def product_kernel(lags, rows, meta, tile, below, own, above, *refs):
+    outs, sources, sems = refs[:lags], refs[lags], refs[lags + 1]
+    me = meta[sems.shape[0] + 1]
+    fetch(meta, below, own, above, sources, sems)
     for d in range(lags):
         first = pl.multiple_of(lax.rem(me + d, lags) * rows, rows)
         part = jnp.dot(tile[pl.ds(first, rows), :], sources[...], preferred_element_type=jnp.float32)
@@ -109,22 +114,111 @@
     return velocity.astype(jnp.bfloat16), new_state
 
 
+def full_product_kernel(meta, tile, below, own, above, out, sources, sems):
+    slots = sems.shape[0]
+    active = meta[slots + 1] > 0
+
+    @pl.when(active)
+    def _():
+        fetch(meta, below, own, above, sources, sems)
+        rows = out.shape[0] // 4
+        for d in range(4):
+            spot = pl.ds(d * rows, rows)
+            out[spot, :] = jnp.dot(tile[spot, :], sources[...], preferred_element_type=jnp.float32)
+
+    @pl.when(jnp.logical_not(active))
+    def _():
+        out[...] = jnp.zeros(out.shape, out.dtype)
+
+
+def full_product(meta, active, tile, below, own, above):
+    slots = meta.shape[0] - 2
+    meta = jnp.concatenate([meta[: slots + 1], active.astype(jnp.int32)[None]])
+    return pl.pallas_call(
+        full_product_kernel,
+        grid_spec=pltpu.PrefetchScalarGridSpec(
+            num_scalar_prefetch=1,
+            grid=(1,),
+            in_specs=[pl.BlockSpec(memory_space=pltpu.VMEM)] + [pl.BlockSpec(memory_space=pl.ANY)] * 3,
+            out_specs=pl.BlockSpec(memory_space=pltpu.VMEM),
+            scratch_shapes=[
+                pltpu.VMEM((tile.shape[1], own.shape[1]), jnp.bfloat16),
+                pltpu.SemaphoreType.DMA((slots,)),
+            ],
+        ),
+        out_shape=jax.ShapeDtypeStruct(own.shape, jnp.float32),
+        compiler_params=pltpu.CompilerParams(vmem_limit_bytes=24 * 1024 * 1024),
+        cost_estimate=pl.CostEstimate(
+            flops=2 * tile.size * own.shape[1], bytes_accessed=2 * (tile.size + 5 * own.size), transcendentals=0
+        ),
+        name="full_product",
+    )(meta, tile, below, own, above)
+
+
+def tree_to_first(value, lags, least):
+    stride = 1
+    while stride < lags:
+        route = [(i + stride, i) for i in range(0, lags - stride, 2 * stride) if i + stride >= least]
+        value = value + lax.ppermute(value.astype(jnp.bfloat16), "lag", route).astype(jnp.float32)
+        stride *= 2
+    return value
+
+
 def shards(kernel_tiles, shell_index, cone_blocks, history, prestress, log_state, fric_a, fric_b, normal_stress):
     lags = lax.axis_size("lag")
     me = lax.axis_index("lag")
+    every = range(lags)
     tile, field = kernel_tiles[0], history[0]
+    rows = prestress.shape[2]
     meta = jnp.concatenate([shell_index[0, 0], cone_blocks, me[None].astype(jnp.int32)])
     stress, state = prestress[0, 0], log_state[0, 0]
-    coef_a, coef_b = fric_a[0, 0][:, None], fric_b[0, 0][:, None]
-    sigma = normal_stress[0, 0][:, None]
-    for step in range(STEPS):
-        below, above = exchange(field)
-        traction = scatter_sum(product(meta, tile, below, field, above, lags))
-        rates, state = settle_friction(stress + traction, state, coef_a, coef_b, sigma)
-        if step + 1 < STEPS:
-            older = lax.ppermute(field, "lag", [(i, i + 1) for i in range(lags - 1)])
-            newest = lax.all_gather(rates, "lag", axis=0, tiled=True)
-            field = jnp.where(me == 0, newest, older)
+    coefs = [fric_a[0, 0], fric_b[0, 0], normal_stress[0, 0]]
+    columns = [c[:, None] for c in coefs]
+
+    below, above = exchange(field, every)
+    shifted = lax.ppermute(field, "lag", [(i, i + 1) for i in range(lags - 1)])
+    packed = jnp.concatenate([state, jnp.pad(jnp.stack(coefs), ((0, 5), (0, state.shape[1] - rows)))], 0)
+    gathered = [packed] + [lax.ppermute(packed, "lag", [(d, 0)]) for d in range(1, lags)]
+    parts = product(meta, tile, below, field, above, lags)
+    traction = scatter_sum(parts)
+    rates, state = settle_friction(stress + traction, state, *columns)
+
+    placed = lax.dynamic_update_slice_in_dim(jnp.zeros(field.shape, jnp.float32), stress, me * rows, 0)
+    later = [i for i in every if i >= 1]
+    below_1, above_1 = exchange(shifted, later)
+    base_1 = tree_to_first(full_product(meta, me >= 1, tile, below_1, shifted, above_1) + placed, lags, 1)
+    twice = lax.ppermute(shifted, "lag", [(i, i + 1) for i in range(1, lags - 1)])
+    below_2, above_2 = exchange(twice, [i for i in every if i >= 2])
+    base_2 = tree_to_first(full_product(meta, me >= 2, tile, below_2, twice, above_2) + placed, lags, 2)
+
+    block_state = jnp.concatenate([g[:rows] for g in gathered], 0)
+    block_columns = [jnp.concatenate([g[rows + k, :rows] for g in gathered])[:, None] for k in range(3)]
+    first = lax.all_gather(rates, "lag", axis=0, tiled=True)
+    speed = jnp.sqrt(jnp.square(first.astype(jnp.float32)) + creep_square)
+    block_state = block_state + time_step * (jnp.exp(-block_state) - speed)
+    before = block_state
+
+    below_v, above_v = exchange(first, [0, 1])
+    part = full_product(meta, me <= 1, tile, below_v, first, above_v)
+    from_next = lax.ppermute((part + placed).astype(jnp.bfloat16), "lag", [(1, 0)])
+    second, block_state = settle_friction(base_1 + part, block_state, *block_columns)
+    below_v, above_v = exchange(second, [0])
+    part = full_product(meta, me == 0, tile, below_v, second, above_v)
+    sent = jnp.where(me == 0, second, twice)
+    moved = lax.ppermute(sent, "lag", [(0, 1)] + [(i, i + 1) for i in range(2, lags - 1)])
+    load = base_2 + from_next.astype(jnp.float32) + part
+    third, block_state = settle_friction(load, block_state, *block_columns)
+
+    last = jnp.where(me == 0, third, jnp.where(me == 2, first, moved))
+    below_v, above_v = exchange(last, every)
+    change = block_state - before
+    mine = change[:rows]
+    for d in range(1, lags):
+        piece = lax.ppermute(change[d * rows : (d + 1) * rows], "lag", [(0, d)])
+        mine = jnp.where(me == d, piece, mine)
+    state = state + mine
+    traction = scatter_sum(product(meta, tile, below_v, last, above_v, lags))
+    rates, state = settle_friction(stress + traction, state, *columns)
     return rates[None, None], state[None, None]
 
 

time: 186 us -> 221 us (1.19)
  blocking collectives: 62.4 us -> 15.6 us
  waiting for transfers between devices: 60 us -> 96.3 us
  starting transfers between devices: 45 us -> 63.6 us
  other arithmetic: 6.93 us -> 23.5 us
  local copies, waits for them, and re-layouts: 2.94 us -> 8.37 us
  Pallas kernels: 6.69 us -> 10.5 us
    ppermute x11 -> x26, waiting for transfers between devices: 25.2 us -> 81.3 us  [the longest x3 28 us: shards(): lax.ppermute(packed, 'lag', [(d, 0)])]
    all_gather x3 -> x1, blocking collectives: 62.4 us -> 15.6 us  [shards(): first = lax.all_gather(rates, 'lag', axis=0, tiled=True)]
    ppermute x12 -> x6, waiting for transfers between devices: 34.9 us -> 15 us  [scatter_sum(): total = total + lax.ppermute(parts[d], 'lag', route).astype(jnp.float32)]
    ppermute x11 -> x26, starting transfers between devices: 31.9 us -> 49.3 us  [the longest x12 26.7 us: exchange(): return (lax.ppermute(value, axes, up), lax.ppermute(value, axes, down))]
    sub x0 -> x1, other arithmetic: none -> 7.89 us  [shards(): change = block_state - before]
    select_n x3 -> x2, other arithmetic: 0.17 us -> 6.55 us  [the longest x1 6.42 us: shards(): sent = jnp.where(me == 0, second, twice)]
    pallas_call x0 -> x4, Pallas kernels: none -> 5.84 us  [full_product(): pl.pallas_call(full_product_kernel, grid_spec=pltpu.PrefetchScalarGridSpe...]
    unnamed x8 -> x57, local copies, waits for them, and re-layouts: 2.94 us -> 7.45 us
  transfers between devices with their start and end apart: 23 -> 32, of which waited for: 14 -> 19; matrix products, arithmetic and copies ran while one was open for 2% -> 9% of each run, Pallas kernels for 1% -> 4%
where the time goes in v2:
time: 221 us; the launch traced here: 220 us
  waiting for transfers between devices  96.3 us (44%)
  starting transfers between devices  63.6 us (29%)
  other arithmetic  23.5 us (11%)
  blocking collectives  15.6 us (7%)
  Pallas kernels  10.5 us (5%)
  local copies, waits for them, and re-layouts  8.37 us (4%)
    ppermute x3, waiting for transfers between devices, shards(): lax.ppermute(packed, 'lag', [(d, 0)])  28 us
    ppermute x12, starting transfers between devices, exchange(): return (lax.ppermute(value, axes, up), lax.ppermute(value, axes, down))  26.7 us
    ppermute x4, waiting for transfers between devices, tree_to_first(): lax.ppermute(value.astype(jnp.bfloat16), 'lag', route).astype(jnp.float32)  19.1 us
    ppermute x12, waiting for transfers between devices, exchange(): return (lax.ppermute(value, axes, up), lax.ppermute(value, axes, down))  17.3 us
    all_gather x1, blocking collectives, shards(): first = lax.all_gather(rates, 'lag', axis=0, tiled=True)  15.6 us
    ppermute x6, waiting for transfers between devices, scatter_sum(): total = total + lax.ppermute(parts[d], 'lag', route).astype(jnp.float32)  15 us
    ppermute x6, starting transfers between devices, scatter_sum(): total = total + lax.ppermute(parts[d], 'lag', route).astype(jnp.float32)  14.3 us
    ppermute x1, waiting for transfers between devices, shards(): shifted = lax.ppermute(field, 'lag', [(i, i + 1) for i in range(lags - 1)])  10.7 us
  transfers between devices with their start and end apart: 32, of which 19 were waited for; matrix products, arithmetic and copies ran while one was open for 9% of the time, Pallas kernels for 4%

profile of v2, /device:TPU:2, one launch (start us, length us, event | category | flops | bytes accessed | tf_op | source)
XLA Modules:
  0.0 219.8 jit_solution(17729444587976196486)
XLA Ops:
  0.7 4.4 %collective-permute-start = (bf16[1024,256]{1,0:T(8,128)(2,1)}, bf16[1024,256]{1,0:T(8,128)(2,1)}, u32[]{:S(2)}, u32[]{:S(2)}) collective-permute-start(bf16[1024,256]{1,0:T(8,128)(2,1)} %bitcast.58), channel_id=1, source_target_pairs={{0,8},{8,16},{16,24},{1,9},{9,17},{17,25},{2,10},{10,18},{18,26},{... | collective-permute-start | bytes 1572872 | tf_op jit(solution)/shard_map/ppermute | solution.py:179
  5.1 10.7 %collective-permute-done.own = bf16[1024,256]{1,0:T(8,128)(2,1)} collective-permute-done((bf16[1024,256]{1,0:T(8,128)(2,1)}, bf16[1024,256]{1,0:T(8,128)(2,1)}, u32[]{:S(2)}, u32[]{:S(2)}) %collective-permute-start) | collective-permute-done | bytes 524320 | tf_op jit(solution)/shard_map/ppermute | solution.py:179
  15.8 1.5 collective-permute-start.1
  17.2 1.9 collective-permute-start.6
  19.1 3.6 %collective-permute-start.7 = (bf16[1024,256]{1,0:T(8,128)(2,1)}, bf16[1024,256]{1,0:T(8,128)(2,1)S(1)}, u32[]{:S(2)}, u32[]{:S(2)}) collective-permute-start(bf16[1024,256]{1,0:T(8,128)(2,1)} %bitcast.60), channel_id=1, source_target_pairs={{1,0},{2,1},{3,2},{4,3},{5,4},{6,5},{7,6},{9,8},{10,9},{11,10},{12... | collective-permute-start | bytes 1572872 | tf_op jit(solution)/shard_map/ppermute | solution.py:23
  23.5 0.7 pad_add_fusion.2
  24.2 1.5 collective-permute-start.2
  25.7 1.5 collective-permute-start.3
  27.2 0.7 collective-permute-done.6.below
  27.9 0.8 copy-done.7
  28.7 3.9 %collective-permute-done.7.above = bf16[1024,256]{1,0:T(8,128)(2,1)S(1)} collective-permute-done((bf16[1024,256]{1,0:T(8,128)(2,1)}, bf16[1024,256]{1,0:T(8,128)(2,1)S(1)}, u32[]{:S(2)}, u32[]{:S(2)}) %collective-permute-start.7) | collective-permute-done | bytes 524320 | tf_op jit(solution)/shard_map/ppermute | solution.py:23
  32.7 0.8 copy-done.9
  33.5 1.9 copy-done
  35.3 1.0 copy-done.6
  36.4 1.0 copy-done.8
  37.4 1.0 copy-done.10
  38.5 2.4 %product.2 = (f32[256,256]{1,0:T(8,128)S(1)}, bf16[256,256]{1,0:T(8,128)(2,1)}, bf16[256,256]{1,0:T(8,128)(2,1)}, bf16[256,256]{1,0:T(8,128)(2,1)}) custom-call(s32[5]{0:T(128)S(1)} %get-tuple-element.53.meta, bf16[1024,1536]{1,0:T(8,128)(2,1)S(1)} %bitcast.52, bf16[1024,256]{1,0:T(8,128)(2,1)S(1)} %copy-done.8, bf16[1024,256]{1,0:T(8,128)(2,1)S(1)} %bitcast.61, ...), custom_call_target="tpu_custom_call" | custom-call | flops 805306368 | bytes 5242880 | tf_op jit(solution)/shard_map/product/pallas_call | solution.py:69
  40.8 9.1 %collective-permute-start.10 = (bf16[256,256]{1,0:T(8,128)(2,1)}, bf16[256,256]{1,0:T(8,128)(2,1)}, u32[]{:S(2)}, u32[]{:S(2)}) collective-permute-start(bf16[256,256]{1,0:T(8,128)(2,1)} %get-tuple-element.13), channel_id=1, source_target_pairs={{0,24},{8,0},{16,8},{24,16},{1,25},{9,1},{17,9},{25,17},{2,26},{10... | collective-permute-start | bytes 393224 | tf_op jit(solution)/shard_map/ppermute | solution.py:95
  50.0 1.0 collective-permute-start.9
  51.0 0.8 collective-permute-start.14
  53.3 0.9 collective-permute-done.10
  54.2 4.3 %collective-permute-done.8 = bf16[256,256]{1,0:T(8,128)(2,1)} collective-permute-done((bf16[256,256]{1,0:T(8,128)(2,1)}, bf16[256,256]{1,0:T(8,128)(2,1)}, u32[]{:S(2)}, u32[]{:S(2)}) %collective-permute-start.8) | collective-permute-done | bytes 131104 | tf_op jit(solution)/shard_map/ppermute | solution.py:95
  58.5 3.3 %collective-permute-done.9 = bf16[256,256]{1,0:T(8,128)(2,1)} collective-permute-done((bf16[256,256]{1,0:T(8,128)(2,1)}, bf16[256,256]{1,0:T(8,128)(2,1)}, u32[]{:S(2)}, u32[]{:S(2)}) %collective-permute-start.9) | collective-permute-done | bytes 131104 | tf_op jit(solution)/shard_map/ppermute | solution.py:95
  61.8 2.8 %fusion.71 = (bf16[256,256]{1,0:T(8,128)(2,1)S(1)}, f32[256,256]{1,0:T(8,128)}, f32[1024,256]{1,0:T(8,128)S(1)}) fusion(f32[256]{0:T(256)S(1)} %get-tuple-element.32, f32[256]{0:T(256)S(1)} %get-tuple-element.31, f32[1,1,256,256]{3,2,1,0:T(8,128)S(1)} %copy-done.11, f32[256]{0:T(256)S(1)} %get-tuple-element.49, ...), kind=kLoop, calls=%fused_computation.121 | loop fusion | flops 4063232 | bytes 2100228 | tf_op jit(solution)/shard_map/convert_element_type | solution.py:114
  64.6 15.6 %all_gather.3.own = bf16[1024,256]{1,0:T(8,128)(2,1)S(1)} all-gather(bf16[256,256]{1,0:T(8,128)(2,1)S(1)} %get-tuple-element.29), channel_id=1, replica_groups=mesh['lag'=4,'elem'=8] {'lag'}, dimensions={0}, use_global_device_ids=true | all-gather | bytes 655360 | tf_op jit(solution)/shard_map/all_gather | solution.py:196
  80.2 1.9 collective-permute-start.11
  82.1 3.6 %collective-permute-start.12 = (bf16[1024,256]{1,0:T(8,128)(2,1)S(1)}, bf16[1024,256]{1,0:T(8,128)(2,1)S(1)}, u32[]{:S(2)}, u32[]{:S(2)}) collective-permute-start(bf16[1024,256]{1,0:T(8,128)(2,1)S(1)} %all_gather.3.own), channel_id=1, source_target_pairs={{1,0},{2,1},{3,2},{4,3},{5,4},{6,5},{7,6},{9,8},{10,9},{11,10},{12... | collective-permute-start | bytes 1572872 | tf_op jit(solution)/shard_map/ppermute | solution.py:23
  86.4 4.2 %collective-permute-done.11.below = bf16[1024,256]{1,0:T(8,128)(2,1)S(1)} collective-permute-done((bf16[1024,256]{1,0:T(8,128)(2,1)S(1)}, bf16[1024,256]{1,0:T(8,128)(2,1)S(1)}, u32[]{:S(2)}, u32[]{:S(2)}) %collective-permute-start.11) | collective-permute-done | bytes 524320 | tf_op jit(solution)/shard_map/ppermute | solution.py:23
  90.7 4.0 %collective-permute-done.12.above = bf16[1024,256]{1,0:T(8,128)(2,1)S(1)} collective-permute-done((bf16[1024,256]{1,0:T(8,128)(2,1)S(1)}, bf16[1024,256]{1,0:T(8,128)(2,1)S(1)}, u32[]{:S(2)}, u32[]{:S(2)}) %collective-permute-start.12) | collective-permute-done | bytes 524320 | tf_op jit(solution)/shard_map/ppermute | solution.py:23
  94.6 1.7 full_product.5
  96.6 1.3 collective-permute-start.16
  97.9 1.3 collective-permute-start.18
  99.2 1.3 collective-permute-start.19
  100.5 1.3 collective-permute-start.20
  101.8 28.0 %collective-permute-done.18 = f32[264,256]{1,0:T(8,128)S(1)} collective-permute-done((f32[264,256]{1,0:T(8,128)S(1)}, f32[264,256]{1,0:T(8,128)S(1)}, u32[]{:S(2)}, u32[]{:S(2)}) %collective-permute-start.18) | collective-permute-done | bytes 270368 | tf_op jit(solution)/shard_map/ppermute | solution.py:181
  130.1 1.3 collective-permute-start.17
  131.5 0.7 collective-permute-start.4
  132.2 0.9 convert_element_type.77
  133.1 1.3 collective-permute-start.13
  134.3 13.1 %collective-permute-done.17 = bf16[1024,256]{1,0:T(8,128)(2,1)S(1)} collective-permute-done((bf16[1024,256]{1,0:T(8,128)(2,1)S(1)}, bf16[1024,256]{1,0:T(8,128)(2,1)S(1)}, u32[]{:S(2)}, u32[]{:S(2)}) %collective-permute-start.17) | collective-permute-done | bytes 524320 | tf_op jit(solution)/shard_map/ppermute | solution.py:162
  147.4 6.4 %broadcast_select_fusion = (bf16[1024,256]{1,0:T(8,128)(2,1)}, bf16[1024,256]{1,0:T(8,128)(2,1)}, f32[1024,256]{1,0:T(8,128)}) fusion(bf16[1024,256]{1,0:T(8,128)(2,1)} %collective-permute-done.1.own, pred[]{:T(512)S(6)} %eq.15, f32[1024]{0:T(1024)S(1)} %get-tuple-element.28, f32[1024]{0:T(1024)S(1)} %get-tuple-element.27, ...), kind=kLoop, calls=%fused_computation.51 | loop fusion | flops 18350080 | bytes 7352321 | tf_op jit(solution)/shard_map/jit(_where)/select_n | solution.py:207
  153.9 1.9 collective-permute-start.21
  155.8 3.6 %collective-permute-start.22 = (bf16[1024,256]{1,0:T(8,128)(2,1)}, bf16[1024,256]{1,0:T(8,128)(2,1)}, u32[]{:S(2)}, u32[]{:S(2)}) collective-permute-start(bf16[1024,256]{1,0:T(8,128)(2,1)} %get-tuple-element.25.own), channel_id=1, source_target_pairs={{1,0},{2,1},{3,2},{4,3},{5,4},{6,5},{7,6}} | collective-permute-start | bytes 1572872 | tf_op jit(solution)/shard_map/ppermute | solution.py:23
  159.5 1.0 fusion.30
  160.5 1.4 collective-permute-start.5
  162.0 1.6 collective-permute-start.23
  163.6 1.1 collective-permute-done.21.below
  164.7 2.8 %collective-permute-done.22.above = bf16[1024,256]{1,0:T(8,128)(2,1)} collective-permute-done((bf16[1024,256]{1,0:T(8,128)(2,1)}, bf16[1024,256]{1,0:T(8,128)(2,1)}, u32[]{:S(2)}, u32[]{:S(2)}) %collective-permute-start.22) | collective-permute-done | bytes 524320 | tf_op jit(solution)/shard_map/ppermute | solution.py:23
  167.5 2.9 %full_product.7 = f32[1024,256]{1,0:T(8,128)S(1)} custom-call(s32[5]{0:T(128)S(1)} %get-tuple-element.50.meta, bf16[1024,1536]{1,0:T(8,128)(2,1)S(1)} %bitcast.56, bf16[1024,256]{1,0:T(8,128)(2,1)} %collective-permute-done.21.below, bf16[1024,256]{1,0:T(8,128)(2,1)} %get-tuple-element.25.own, bf16[1024,256]{1,0:T(8,128)(2,1)} %collective-permute-done.22.above), custom_call_target="tpu_custom_call" | custom-call | flops 805306368 | bytes 5767168 | tf_op jit(solution)/shard_map/full_product/pallas_call | solution.py:137
  170.4 6.0 %collective-permute-done.5 = bf16[1024,256]{1,0:T(8,128)(2,1)} collective-permute-done((bf16[1024,256]{1,0:T(8,128)(2,1)}, bf16[1024,256]{1,0:T(8,128)(2,1)}, u32[]{:S(2)}, u32[]{:S(2)}) %collective-permute-start.5) | collective-permute-done | bytes 524320 | tf_op jit(solution)/shard_map/ppermute | solution.py:162
  176.4 7.9 %add_subtract_fusion = (f32[1024,256]{1,0:T(8,128)S(1)}, bf16[1024,256]{1,0:T(8,128)(2,1)S(1)}) fusion(f32[1024,256]{1,0:T(8,128)S(1)} %copy-done.14, bf16[1024,256]{1,0:T(8,128)(2,1)S(1)} %copy-done.5, f32[256,256]{1,0:T(8,128)S(1)} %copy-done.21, f32[256,256]{1,0:T(8,128)S(1)} %copy-done.19, f32[256,256]{1,0:T(8,128)S(1)} %copy-done.17, ...), kind=kLoop, calls=%fused_computation.37 | loop fusion | flops 22020096 | bytes 7876608 | tf_op jit(solution)/shard_map/sub | solution.py:214
  184.5 1.9 collective-permute-start.24
  186.4 3.6 %collective-permute-start.25 = (bf16[1024,256]{1,0:T(8,128)(2,1)S(1)}, bf16[1024,256]{1,0:T(8,128)(2,1)S(1)}, u32[]{:S(2)}, u32[]{:S(2)}) collective-permute-start(bf16[1024,256]{1,0:T(8,128)(2,1)S(1)} %select_select_fusion.own), channel_id=1, source_target_pairs={{1,0},{2,1},{3,2},{4,3},{5,4},{6,5},{7,6},{9,8},{10,9},{11,10},{12... | collective-permute-start | bytes 1572872 | tf_op jit(solution)/shard_map/ppermute | solution.py:23
  190.0 0.8 fusion.73
  190.9 1.3 collective-permute-start.29
  192.2 2.0 collective-permute-start.30
  194.2 2.0 collective-permute-start.31
  196.7 2.3 %product.3 = (f32[256,256]{1,0:T(8,128)S(1)}, bf16[256,256]{1,0:T(8,128)(2,1)}, bf16[256,256]{1,0:T(8,128)(2,1)}, bf16[256,256]{1,0:T(8,128)(2,1)S(1)}) custom-call(s32[5]{0:T(128)S(1)} %get-tuple-element.53.meta, bf16[1024,1536]{1,0:T(8,128)(2,1)S(1)} %bitcast.57, bf16[1024,256]{1,0:T(8,128)(2,1)S(1)} %collective-permute-done.24.below, ...), custom_call_target="tpu_custom_call" | custom-call | flops 805306368 | bytes 5242880 | tf_op jit(solution)/shard_map/product/pallas_call | solution.py:69
  199.9 4.0 %collective-permute-start.28 = (bf16[256,256]{1,0:T(8,128)(2,1)S(1)}, bf16[256,256]{1,0:T(8,128)(2,1)S(1)}, u32[]{:S(2)}, u32[]{:S(2)}) collective-permute-start(bf16[256,256]{1,0:T(8,128)(2,1)S(1)} %get-tuple-element.17), channel_id=1, source_target_pairs={{0,24},{8,0},{16,8},{24,16},{1,25},{9,1},{17,9},{25,17},{2,26},{10... | collective-permute-start | bytes 393224 | tf_op jit(solution)/shard_map/ppermute | solution.py:95
  204.6 5.6 %collective-permute-done.31 = f32[256,256]{1,0:T(8,128)} collective-permute-done((f32[256,256]{1,0:T(8,128)}, f32[256,256]{1,0:T(8,128)}, u32[]{:S(2)}, u32[]{:S(2)}) %collective-permute-start.31) | collective-permute-done | bytes 262176 | tf_op jit(solution)/shard_map/ppermute | solution.py:217
  210.2 2.8 %collective-permute-done.26 = bf16[256,256]{1,0:T(8,128)(2,1)S(1)} collective-permute-done((bf16[256,256]{1,0:T(8,128)(2,1)}, bf16[256,256]{1,0:T(8,128)(2,1)S(1)}, u32[]{:S(2)}, u32[]{:S(2)}) %collective-permute-start.26) | collective-permute-done | bytes 131104 | tf_op jit(solution)/shard_map/ppermute | solution.py:95
  213.0 2.3 %collective-permute-done.27 = bf16[256,256]{1,0:T(8,128)(2,1)S(1)} collective-permute-done((bf16[256,256]{1,0:T(8,128)(2,1)}, bf16[256,256]{1,0:T(8,128)(2,1)S(1)}, u32[]{:S(2)}, u32[]{:S(2)}) %collective-permute-start.27) | collective-permute-done | bytes 131104 | tf_op jit(solution)/shard_map/ppermute | solution.py:95
  215.3 1.3 collective-permute-done.28
  216.6 3.2 %add_bitcast_fusion = (f32[1,1,256,256]{3,2,1,0:T(8,128)}, bf16[256,256]{1,0:T(8,128)(2,1)}) fusion(f32[256]{0:T(256)S(1)} %get-tuple-element.32, f32[256]{0:T(256)S(1)} %get-tuple-element.31, f32[256]{0:T(256)S(1)} %get-tuple-element.49, bf16[256,256]{1,0:T(8,128)(2,1)S(1)} %collective-permute-done.28, bf16[256,256]{1,0:T(8,128)(2,1)S(1)} %collective-permute-done.27, ...), kind=kLoop, calls=%fused_computation.101 | loop fusion | flops 5046272 | bytes 2886659 | tf_op jit(solution)/shard_map/broadcast_in_dim | solution.py:222
  (88 shorter events, 4.9 us)
Async XLA Ops:
  0.6 50.4 %copy-start.25 = (f32[1,1,256]{2,1,0:T(1,128)S(1)}, f32[1,1,256]{2,1,0:T(1,128)}, u32[]{:S(2)}) copy-start(f32[1,1,256]{2,1,0:T(1,128)} %param.17) | copy-start | bytes 3076
  0.6 50.4 %copy-start.27 = (f32[1,1,256]{2,1,0:T(1,128)S(1)}, f32[1,1,256]{2,1,0:T(1,128)}, u32[]{:S(2)}) copy-start(f32[1,1,256]{2,1,0:T(1,128)} %param.16) | copy-start | bytes 3076
  0.7 50.3 %copy-start.26 = (f32[1,1,256]{2,1,0:T(1,128)S(1)}, f32[1,1,256]{2,1,0:T(1,128)}, u32[]{:S(2)}) copy-start(f32[1,1,256]{2,1,0:T(1,128)} %param.15) | copy-start | bytes 3076
  0.7 15.1 %collective-permute-start = (bf16[1024,256]{1,0:T(8,128)(2,1)}, bf16[1024,256]{1,0:T(8,128)(2,1)}, u32[]{:S(2)}, u32[]{:S(2)}) collective-permute-start(bf16[1024,256]{1,0:T(8,128)(2,1)} %bitcast.58), channel_id=1, source_target_pairs={{0,8},{8,16},{16,24},{1,9},{9,17},{17,25},{2,10},{10,18},{18,26},{... | collective-permute-start | bytes 1572872 | tf_op jit(solution)/shard_map/ppermute | solution.py:179
  15.8 8.4 %collective-permute-start.1 = (bf16[1024,256]{1,0:T(8,128)(2,1)}, bf16[1024,256]{1,0:T(8,128)(2,1)}, u32[]{:S(2)}, u32[]{:S(2)}) collective-permute-start(bf16[1024,256]{1,0:T(8,128)(2,1)} %collective-permute-done.own), channel_id=1, source_target_pairs={{8,16},{16,24},{9,17},{17,25},{10,18},{18,26},{11,19},{19,27},{12,... | collective-permute-start | bytes 1572872 | tf_op jit(solution)/shard_map/ppermute | solution.py:190
  17.2 10.7 %collective-permute-start.6 = (bf16[1024,256]{1,0:T(8,128)(2,1)}, bf16[1024,256]{1,0:T(8,128)(2,1)S(1)}, u32[]{:S(2)}, u32[]{:S(2)}) collective-permute-start(bf16[1024,256]{1,0:T(8,128)(2,1)} %bitcast.59), channel_id=1, source_target_pairs={{0,1},{1,2},{2,3},{3,4},{4,5},{5,6},{6,7},{8,9},{9,10},{10,11},{11... | collective-permute-start | bytes 1572872 | tf_op jit(solution)/shard_map/ppermute | solution.py:23
  19.1 13.5 %collective-permute-start.7 = (bf16[1024,256]{1,0:T(8,128)(2,1)}, bf16[1024,256]{1,0:T(8,128)(2,1)S(1)}, u32[]{:S(2)}, u32[]{:S(2)}) collective-permute-start(bf16[1024,256]{1,0:T(8,128)(2,1)} %bitcast.60), channel_id=1, source_target_pairs={{1,0},{2,1},{3,2},{4,3},{5,4},{6,5},{7,6},{9,8},{10,9},{11,10},{12... | collective-permute-start | bytes 1572872 | tf_op jit(solution)/shard_map/ppermute | solution.py:23
  24.2 26.8 %collective-permute-start.2 = (bf16[1024,256]{1,0:T(8,128)(2,1)}, bf16[1024,256]{1,0:T(8,128)(2,1)}, u32[]{:S(2)}, u32[]{:S(2)}) collective-permute-start(bf16[1024,256]{1,0:T(8,128)(2,1)} %collective-permute-done.1.own), channel_id=1, source_target_pairs={{16,17},{17,18},{18,19},{19,20},{20,21},{21,22},{22,23},{24,25},{2... | collective-permute-start | bytes 1572872 | tf_op jit(solution)/shard_map/ppermute | solution.py:23
  25.7 26.2 %collective-permute-start.3 = (bf16[1024,256]{1,0:T(8,128)(2,1)}, bf16[1024,256]{1,0:T(8,128)(2,1)}, u32[]{:S(2)}, u32[]{:S(2)}) collective-permute-start(bf16[1024,256]{1,0:T(8,128)(2,1)} %collective-permute-done.1.own), channel_id=1, source_target_pairs={{17,16},{18,17},{19,18},{20,19},{21,20},{22,21},{23,22},{25,24},{2... | collective-permute-start | bytes 1572872 | tf_op jit(solution)/shard_map/ppermute | solution.py:23
  27.9 0.8 copy-start.7
  32.7 0.8 copy-start.9
  33.5 1.9 copy-start
  35.3 1.0 copy-start.6
  36.4 1.0 copy-start.8
  37.4 1.0 copy-start.10
  38.5 14.1 %copy-start.1 = (bf16[1,1024,1536]{2,1,0:T(8,128)(2,1)S(1)}, bf16[1,1024,1536]{2,1,0:T(8,128)(2,1)}, u32[]{:S(2)}) copy-start(bf16[1,1024,1536]{2,1,0:T(8,128)(2,1)} %param.9) | copy-start | bytes 9437188
  40.8 13.3 %collective-permute-start.10 = (bf16[256,256]{1,0:T(8,128)(2,1)}, bf16[256,256]{1,0:T(8,128)(2,1)}, u32[]{:S(2)}, u32[]{:S(2)}) collective-permute-start(bf16[256,256]{1,0:T(8,128)(2,1)} %get-tuple-element.13), channel_id=1, source_target_pairs={{0,24},{8,0},{16,8},{24,16},{1,25},{9,1},{17,9},{25,17},{2,26},{10... | collective-permute-start | bytes 393224 | tf_op jit(solution)/shard_map/ppermute | solution.py:95
  50.0 8.5 %collective-permute-start.8 = (bf16[256,256]{1,0:T(8,128)(2,1)}, bf16[256,256]{1,0:T(8,128)(2,1)}, u32[]{:S(2)}, u32[]{:S(2)}) collective-permute-start(bf16[256,256]{1,0:T(8,128)(2,1)} %get-tuple-element.11), channel_id=1, source_target_pairs={{0,8},{8,16},{16,24},{24,0},{1,9},{9,17},{17,25},{25,1},{2,10},{10... | collective-permute-start | bytes 393224 | tf_op jit(solution)/shard_map/ppermute | solution.py:95
  50.0 11.8 %collective-permute-start.9 = (bf16[256,256]{1,0:T(8,128)(2,1)}, bf16[256,256]{1,0:T(8,128)(2,1)}, u32[]{:S(2)}, u32[]{:S(2)}) collective-permute-start(bf16[256,256]{1,0:T(8,128)(2,1)} %get-tuple-element.12), channel_id=1, source_target_pairs={{0,16},{8,24},{16,0},{24,8},{1,17},{9,25},{17,1},{25,9},{2,18},{10... | collective-permute-start | bytes 393224 | tf_op jit(solution)/shard_map/ppermute | solution.py:95
  51.0 10.8 %copy-start.11 = (f32[1,1,256,256]{3,2,1,0:T(8,128)S(1)}, f32[1,1,256,256]{3,2,1,0:T(8,128)}, u32[]{:S(2)}) copy-start(f32[1,1,256,256]{3,2,1,0:T(8,128)} %param.14) | copy-start | bytes 786436
  51.0 10.8 %copy-start.15 = (f32[1,1,256,256]{3,2,1,0:T(8,128)S(1)}, f32[1,1,256,256]{3,2,1,0:T(8,128)}, u32[]{:S(2)}) copy-start(f32[1,1,256,256]{3,2,1,0:T(8,128)} %param.13) | copy-start | bytes 786436
  51.0 34.7 %collective-permute-start.14 = (bf16[1024,256]{1,0:T(8,128)(2,1)}, bf16[1024,256]{1,0:T(8,128)(2,1)S(1)}, u32[]{:S(2)}, u32[]{:S(2)}) collective-permute-start(bf16[1024,256]{1,0:T(8,128)(2,1)} %collective-permute-done.own), channel_id=1, source_target_pairs={{8,9},{9,10},{10,11},{11,12},{12,13},{13,14},{14,15},{16,17},{17,1... | collective-permute-start | bytes 1572872 | tf_op jit(solution)/shard_map/ppermute | solution.py:23
  51.9 33.9 %collective-permute-start.15 = (bf16[1024,256]{1,0:T(8,128)(2,1)}, bf16[1024,256]{1,0:T(8,128)(2,1)S(1)}, u32[]{:S(2)}, u32[]{:S(2)}) collective-permute-start(bf16[1024,256]{1,0:T(8,128)(2,1)} %collective-permute-done.own), channel_id=1, source_target_pairs={{9,8},{10,9},{11,10},{12,11},{13,12},{14,13},{15,14},{17,16},{18,1... | collective-permute-start | bytes 1572872 | tf_op jit(solution)/shard_map/ppermute | solution.py:23
  64.6 94.9 %copy-start.2 = (f32[1024,256]{1,0:T(8,128)}, f32[1024,256]{1,0:T(8,128)S(1)}, u32[]{:S(2)}) copy-start(f32[1024,256]{1,0:T(8,128)S(1)} %get-tuple-element.45) | copy-start | bytes 3145732
  80.2 67.3 %copy-start.4 = (bf16[1024,256]{1,0:T(8,128)(2,1)}, bf16[1024,256]{1,0:T(8,128)(2,1)S(1)}, u32[]{:S(2)}) copy-start(bf16[1024,256]{1,0:T(8,128)(2,1)S(1)} %all_gather.3.own) | copy-start | bytes 1572868
  80.2 10.5 %collective-permute-start.11 = (bf16[1024,256]{1,0:T(8,128)(2,1)S(1)}, bf16[1024,256]{1,0:T(8,128)(2,1)S(1)}, u32[]{:S(2)}, u32[]{:S(2)}) collective-permute-start(bf16[1024,256]{1,0:T(8,128)(2,1)S(1)} %all_gather.3.own), channel_id=1, source_target_pairs={{0,1},{1,2},{2,3},{3,4},{4,5},{5,6},{6,7},{8,9},{9,10},{10,11},{11... | collective-permute-start | bytes 1572872 | tf_op jit(solution)/shard_map/ppermute | solution.py:23
  82.1 12.6 %collective-permute-start.12 = (bf16[1024,256]{1,0:T(8,128)(2,1)S(1)}, bf16[1024,256]{1,0:T(8,128)(2,1)S(1)}, u32[]{:S(2)}, u32[]{:S(2)}) collective-permute-start(bf16[1024,256]{1,0:T(8,128)(2,1)S(1)} %all_gather.3.own), channel_id=1, source_target_pairs={{1,0},{2,1},{3,2},{4,3},{5,4},{6,5},{7,6},{9,8},{10,9},{11,10},{12... | collective-permute-start | bytes 1572872 | tf_op jit(solution)/shard_map/ppermute | solution.py:23
  96.6 33.4 %collective-permute-start.16 = (bf16[1024,256]{1,0:T(8,128)(2,1)S(1)}, bf16[1024,256]{1,0:T(8,128)(2,1)S(1)}, u32[]{:S(2)}, u32[]{:S(2)}) collective-permute-start(bf16[1024,256]{1,0:T(8,128)(2,1)S(1)} %convert_element_type.79), channel_id=1, source_target_pairs={{8,0},{24,16},{9,1},{25,17},{10,2},{26,18},{11,3},{27,19},{12,4},{... | collective-permute-start | bytes 1572872 | tf_op jit(solution)/shard_map/ppermute | solution.py:162
  97.9 31.9 %collective-permute-start.18 = (f32[264,256]{1,0:T(8,128)S(1)}, f32[264,256]{1,0:T(8,128)S(1)}, u32[]{:S(2)}, u32[]{:S(2)}) collective-permute-start(f32[264,256]{1,0:T(8,128)S(1)} %pad_maximum_fusion.1), channel_id=1, source_target_pairs={{8,0},{9,1},{10,2},{11,3},{12,4},{13,5},{14,6},{15,7}} | collective-permute-start | bytes 811016 | tf_op jit(solution)/shard_map/ppermute | solution.py:181
  99.2 30.6 %collective-permute-start.19 = (f32[264,256]{1,0:T(8,128)S(1)}, f32[264,256]{1,0:T(8,128)S(1)}, u32[]{:S(2)}, u32[]{:S(2)}) collective-permute-start(f32[264,256]{1,0:T(8,128)S(1)} %pad_maximum_fusion.1), channel_id=1, source_target_pairs={{16,0},{17,1},{18,2},{19,3},{20,4},{21,5},{22,6},{23,7}} | collective-permute-start | bytes 811016 | tf_op jit(solution)/shard_map/ppermute | solution.py:181
  100.5 29.4 %collective-permute-start.20 = (f32[264,256]{1,0:T(8,128)S(1)}, f32[264,256]{1,0:T(8,128)S(1)}, u32[]{:S(2)}, u32[]{:S(2)}) collective-permute-start(f32[264,256]{1,0:T(8,128)S(1)} %pad_maximum_fusion.1), channel_id=1, source_target_pairs={{24,0},{25,1},{26,2},{27,3},{28,4},{29,5},{30,6},{31,7}} | collective-permute-start | bytes 811016 | tf_op jit(solution)/shard_map/ppermute | solution.py:181
  129.8 17.6 %copy-start.16 = (f32[256,256]{1,0:T(8,128)}, f32[256,256]{1,0:T(8,128)S(1)}, u32[]{:S(2)}) copy-start(f32[256,256]{1,0:T(8,128)S(1)} %slice.81) | copy-start | bytes 786436
  129.8 24.0 %copy-start.18 = (f32[256,256]{1,0:T(8,128)}, f32[256,256]{1,0:T(8,128)S(1)}, u32[]{:S(2)}) copy-start(f32[256,256]{1,0:T(8,128)S(1)} %slice.82) | copy-start | bytes 786436
  129.9 24.0 %copy-start.20 = (f32[256,256]{1,0:T(8,128)}, f32[256,256]{1,0:T(8,128)S(1)}, u32[]{:S(2)}) copy-start(f32[256,256]{1,0:T(8,128)S(1)} %slice.83) | copy-start | bytes 786436
  130.1 17.4 %collective-permute-start.17 = (bf16[1024,256]{1,0:T(8,128)(2,1)S(1)}, bf16[1024,256]{1,0:T(8,128)(2,1)S(1)}, u32[]{:S(2)}, u32[]{:S(2)}) collective-permute-start(bf16[1024,256]{1,0:T(8,128)(2,1)S(1)} %fusion.31), channel_id=1, source_target_pairs={{16,0},{17,1},{18,2},{19,3},{20,4},{21,5},{22,6},{23,7}} | collective-permute-start | bytes 1572872 | tf_op jit(solution)/shard_map/ppermute | solution.py:162
  131.5 28.0 %collective-permute-start.4 = (bf16[1024,256]{1,0:T(8,128)(2,1)S(1)}, bf16[1024,256]{1,0:T(8,128)(2,1)S(1)}, u32[]{:S(2)}, u32[]{:S(2)}) collective-permute-start(bf16[1024,256]{1,0:T(8,128)(2,1)S(1)} %convert_element_type.69), channel_id=1, source_target_pairs={{24,16},{25,17},{26,18},{27,19},{28,20},{29,21},{30,22},{31,23}} | collective-permute-start | bytes 1572872 | tf_op jit(solution)/shard_map/ppermute | solution.py:162
  133.1 37.3 %collective-permute-start.13 = (bf16[1024,256]{1,0:T(8,128)(2,1)}, bf16[1024,256]{1,0:T(8,128)(2,1)}, u32[]{:S(2)}, u32[]{:S(2)}) collective-permute-start(bf16[1024,256]{1,0:T(8,128)(2,1)} %convert_element_type.77), channel_id=1, source_target_pairs={{8,0},{9,1},{10,2},{11,3},{12,4},{13,5},{14,6},{15,7}} | collective-permute-start | bytes 1572872 | tf_op jit(solution)/shard_map/ppermute | solution.py:203
  153.9 10.8 %collective-permute-start.21 = (bf16[1024,256]{1,0:T(8,128)(2,1)}, bf16[1024,256]{1,0:T(8,128)(2,1)}, u32[]{:S(2)}, u32[]{:S(2)}) collective-permute-start(bf16[1024,256]{1,0:T(8,128)(2,1)} %get-tuple-element.25.own), channel_id=1, source_target_pairs={{0,1},{1,2},{2,3},{3,4},{4,5},{5,6},{6,7}} | collective-permute-start | bytes 1572872 | tf_op jit(solution)/shard_map/ppermute | solution.py:23
  155.8 11.7 %collective-permute-start.22 = (bf16[1024,256]{1,0:T(8,128)(2,1)}, bf16[1024,256]{1,0:T(8,128)(2,1)}, u32[]{:S(2)}, u32[]{:S(2)}) collective-permute-start(bf16[1024,256]{1,0:T(8,128)(2,1)} %get-tuple-element.25.own), channel_id=1, source_target_pairs={{1,0},{2,1},{3,2},{4,3},{5,4},{6,5},{7,6}} | collective-permute-start | bytes 1572872 | tf_op jit(solution)/shard_map/ppermute | solution.py:23
  159.5 1.0 copy-start.22
  160.5 15.8 %copy-start.12 = (f32[1,1,256,256]{3,2,1,0:T(8,128)S(1)}, f32[1,1,256,256]{3,2,1,0:T(8,128)}, u32[]{:S(2)}) copy-start(f32[1,1,256,256]{3,2,1,0:T(8,128)} %param.14) | copy-start | bytes 786436
  160.5 15.8 %collective-permute-start.5 = (bf16[1024,256]{1,0:T(8,128)(2,1)}, bf16[1024,256]{1,0:T(8,128)(2,1)}, u32[]{:S(2)}, u32[]{:S(2)}) collective-permute-start(bf16[1024,256]{1,0:T(8,128)(2,1)} %fusion.30), channel_id=1, source_target_pairs={{16,0},{17,1},{18,2},{19,3},{20,4},{21,5},{22,6},{23,7}} | collective-permute-start | bytes 1572872 | tf_op jit(solution)/shard_map/ppermute | solution.py:162
  161.9 14.4 %copy-start.3 = (f32[1024,256]{1,0:T(8,128)S(1)}, f32[1024,256]{1,0:T(8,128)}, u32[]{:S(2)}) copy-start(f32[1024,256]{1,0:T(8,128)} %copy-done.2) | copy-start | bytes 3145732
  161.9 14.4 %copy-start.5 = (bf16[1024,256]{1,0:T(8,128)(2,1)S(1)}, bf16[1024,256]{1,0:T(8,128)(2,1)}, u32[]{:S(2)}) copy-start(bf16[1024,256]{1,0:T(8,128)(2,1)} %copy-done.4) | copy-start | bytes 1572868
  161.9 14.4 %copy-start.14 = (f32[1024,256]{1,0:T(8,128)S(1)}, f32[1024,256]{1,0:T(8,128)}, u32[]{:S(2)}) copy-start(f32[1024,256]{1,0:T(8,128)} %get-tuple-element.26) | copy-start | bytes 3145732
  162.0 14.4 %copy-start.17 = (f32[256,256]{1,0:T(8,128)S(1)}, f32[256,256]{1,0:T(8,128)}, u32[]{:S(2)}) copy-start(f32[256,256]{1,0:T(8,128)} %copy-done.16) | copy-start | bytes 786436
  162.0 14.4 %copy-start.19 = (f32[256,256]{1,0:T(8,128)S(1)}, f32[256,256]{1,0:T(8,128)}, u32[]{:S(2)}) copy-start(f32[256,256]{1,0:T(8,128)} %copy-done.18) | copy-start | bytes 786436
  162.0 14.4 %copy-start.21 = (f32[256,256]{1,0:T(8,128)S(1)}, f32[256,256]{1,0:T(8,128)}, u32[]{:S(2)}) copy-start(f32[256,256]{1,0:T(8,128)} %copy-done.20) | copy-start | bytes 786436
  162.0 14.4 %copy-start.23 = (bf16[1024,256]{1,0:T(8,128)(2,1)S(1)}, bf16[1024,256]{1,0:T(8,128)(2,1)}, u32[]{:S(2)}) copy-start(bf16[1024,256]{1,0:T(8,128)(2,1)} %copy-done.22) | copy-start | bytes 1572868
  162.0 22.3 %collective-permute-start.23 = (bf16[1024,256]{1,0:T(8,128)(2,1)}, bf16[1024,256]{1,0:T(8,128)(2,1)S(1)}, u32[]{:S(2)}, u32[]{:S(2)}) collective-permute-start(bf16[1024,256]{1,0:T(8,128)(2,1)} %get-tuple-element.24), channel_id=1, source_target_pairs={{0,8},{16,24},{1,9},{17,25},{2,10},{18,26},{3,11},{19,27},{4,12},{... | collective-permute-start | bytes 1572872 | tf_op jit(solution)/shard_map/ppermute | solution.py:208
  184.3 14.9 %copy-start.13 = (f32[1024,256]{1,0:T(8,128)}, f32[1024,256]{1,0:T(8,128)S(1)}, u32[]{:S(2)}) copy-start(f32[1024,256]{1,0:T(8,128)S(1)} %get-tuple-element.20) | copy-start | bytes 3145732
  184.5 11.7 %collective-permute-start.24 = (bf16[1024,256]{1,0:T(8,128)(2,1)S(1)}, bf16[1024,256]{1,0:T(8,128)(2,1)S(1)}, u32[]{:S(2)}, u32[]{:S(2)}) collective-permute-start(bf16[1024,256]{1,0:T(8,128)(2,1)S(1)} %select_select_fusion.own), channel_id=1, source_target_pairs={{0,1},{1,2},{2,3},{3,4},{4,5},{5,6},{6,7},{8,9},{9,10},{10,11},{11... | collective-permute-start | bytes 1572872 | tf_op jit(solution)/shard_map/ppermute | solution.py:23
  186.4 10.3 %collective-permute-start.25 = (bf16[1024,256]{1,0:T(8,128)(2,1)S(1)}, bf16[1024,256]{1,0:T(8,128)(2,1)S(1)}, u32[]{:S(2)}, u32[]{:S(2)}) collective-permute-start(bf16[1024,256]{1,0:T(8,128)(2,1)S(1)} %select_select_fusion.own), channel_id=1, source_target_pairs={{1,0},{2,1},{3,2},{4,3},{5,4},{6,5},{7,6},{9,8},{10,9},{11,10},{12... | collective-permute-start | bytes 1572872 | tf_op jit(solution)/shard_map/ppermute | solution.py:23
  190.9 8.3 %collective-permute-start.29 = (f32[256,256]{1,0:T(8,128)S(1)}, f32[256,256]{1,0:T(8,128)S(1)}, u32[]{:S(2)}, u32[]{:S(2)}) collective-permute-start(f32[256,256]{1,0:T(8,128)S(1)} %get-tuple-element.35), channel_id=1, source_target_pairs={{0,24},{1,25},{2,26},{3,27},{4,28},{5,29},{6,30},{7,31}} | collective-permute-start | bytes 786440 | tf_op jit(solution)/shard_map/ppermute | solution.py:217
  192.2 12.4 %collective-permute-start.30 = (f32[256,256]{1,0:T(8,128)}, f32[256,256]{1,0:T(8,128)}, u32[]{:S(2)}, u32[]{:S(2)}) collective-permute-start(f32[256,256]{1,0:T(8,128)} %get-tuple-element.34), channel_id=1, source_target_pairs={{0,16},{1,17},{2,18},{3,19},{4,20},{5,21},{6,22},{7,23}} | collective-permute-start | bytes 786440 | tf_op jit(solution)/shard_map/ppermute | solution.py:217
  194.2 16.0 %collective-permute-start.31 = (f32[256,256]{1,0:T(8,128)}, f32[256,256]{1,0:T(8,128)}, u32[]{:S(2)}, u32[]{:S(2)}) collective-permute-start(f32[256,256]{1,0:T(8,128)} %get-tuple-element.33), channel_id=1, source_target_pairs={{0,8},{1,9},{2,10},{3,11},{4,12},{5,13},{6,14},{7,15}} | collective-permute-start | bytes 786440 | tf_op jit(solution)/shard_map/ppermute | solution.py:217
  199.0 14.0 %collective-permute-start.26 = (bf16[256,256]{1,0:T(8,128)(2,1)}, bf16[256,256]{1,0:T(8,128)(2,1)S(1)}, u32[]{:S(2)}, u32[]{:S(2)}) collective-permute-start(bf16[256,256]{1,0:T(8,128)(2,1)} %get-tuple-element.15), channel_id=1, source_target_pairs={{0,8},{8,16},{16,24},{24,0},{1,9},{9,17},{17,25},{25,1},{2,10},{10... | collective-permute-start | bytes 393224 | tf_op jit(solution)/shard_map/ppermute | solution.py:95
  199.1 16.2 %collective-permute-start.27 = (bf16[256,256]{1,0:T(8,128)(2,1)}, bf16[256,256]{1,0:T(8,128)(2,1)S(1)}, u32[]{:S(2)}, u32[]{:S(2)}) collective-permute-start(bf16[256,256]{1,0:T(8,128)(2,1)} %get-tuple-element.16), channel_id=1, source_target_pairs={{0,16},{8,24},{16,0},{24,8},{1,17},{9,25},{17,1},{25,9},{2,18},{10... | collective-permute-start | bytes 393224 | tf_op jit(solution)/shard_map/ppermute | solution.py:95
  199.2 0.7 copy-start.24
  199.9 16.7 %collective-permute-start.28 = (bf16[256,256]{1,0:T(8,128)(2,1)S(1)}, bf16[256,256]{1,0:T(8,128)(2,1)S(1)}, u32[]{:S(2)}, u32[]{:S(2)}) collective-permute-start(bf16[256,256]{1,0:T(8,128)(2,1)S(1)} %get-tuple-element.17), channel_id=1, source_target_pairs={{0,24},{8,0},{16,8},{24,16},{1,25},{9,1},{17,9},{25,17},{2,26},{10... | collective-permute-start | bytes 393224 | tf_op jit(solution)/shard_map/ppermute | solution.py:95

commit v3 on v2

--- a/solution.py
+++ b/solution.py
@@ -7,8 +7,9 @@
 from jax.experimental.pallas import tpu as pltpu
 from jax.sharding import PartitionSpec as P
 
-STEPS = 4
+
 NEWTON = 3
+
 
 damping = 0.5
 time_step = 0.25
@@ -114,53 +115,63 @@
     return velocity.astype(jnp.bfloat16), new_state
 
 
-def full_product_kernel(meta, tile, below, own, above, out, sources, sems):
+def full_product_kernel(chunks, meta, tile, below, own, above, stress, *refs):
+    outs, sources, sems = refs[:-2], refs[-2], refs[-1]
     slots = sems.shape[0]
-    active = meta[slots + 1] > 0
+    me, active = meta[slots + 1], meta[slots + 2] > 0
+    rows = outs[0].shape[0] // chunks
+    mine = pl.ds(pl.multiple_of(me * stress.shape[0], stress.shape[0]), stress.shape[0])
 
     @pl.when(active)
     def _():
         fetch(meta, below, own, above, sources, sems)
-        rows = out.shape[0] // 4
-        for d in range(4):
+        for d in range(chunks):
             spot = pl.ds(d * rows, rows)
-            out[spot, :] = jnp.dot(tile[spot, :], sources[...], preferred_element_type=jnp.float32)
+            part = jnp.dot(tile[spot, :], sources[...], preferred_element_type=jnp.float32)
+            for out in outs:
+                out[spot, :] = part.astype(out.dtype)
+        part = jnp.dot(tile[mine, :], sources[...], preferred_element_type=jnp.float32)
+        outs[0][mine, :] = (part + stress[...]).astype(outs[0].dtype)
 
     @pl.when(jnp.logical_not(active))
     def _():
-        out[...] = jnp.zeros(out.shape, out.dtype)
-
-
-def full_product(meta, active, tile, below, own, above):
+        outs[0][...] = jnp.zeros(outs[0].shape, outs[0].dtype)
+        outs[0][mine, :] = stress[...].astype(outs[0].dtype)
+
+
+def full_product(meta, active, tile, below, own, above, stress, kinds):
     slots = meta.shape[0] - 2
-    meta = jnp.concatenate([meta[: slots + 1], active.astype(jnp.int32)[None]])
+    meta = jnp.concatenate([meta, active.astype(jnp.int32)[None]])
+    chunks = tile.shape[0] // min(tile.shape[0], 256)
     return pl.pallas_call(
-        full_product_kernel,
+        functools.partial(full_product_kernel, chunks),
         grid_spec=pltpu.PrefetchScalarGridSpec(
             num_scalar_prefetch=1,
             grid=(1,),
-            in_specs=[pl.BlockSpec(memory_space=pltpu.VMEM)] + [pl.BlockSpec(memory_space=pl.ANY)] * 3,
-            out_specs=pl.BlockSpec(memory_space=pltpu.VMEM),
-            scratch_shapes=[
-                pltpu.VMEM((tile.shape[1], own.shape[1]), jnp.bfloat16),
-                pltpu.SemaphoreType.DMA((slots,)),
-            ],
-        ),
-        out_shape=jax.ShapeDtypeStruct(own.shape, jnp.float32),
+            in_specs=[pl.BlockSpec(memory_space=pltpu.VMEM)]
+            + [pl.BlockSpec(memory_space=pl.ANY)] * 3
+            + [pl.BlockSpec(memory_space=pltpu.VMEM)],
+            out_specs=[pl.BlockSpec(memory_space=pltpu.VMEM)] * len(kinds),
+            scratch_shapes=[pltpu.VMEM((tile.shape[1], own.shape[1]), jnp.bfloat16), pltpu.SemaphoreType.DMA((slots,))],
+        ),
+        out_shape=[jax.ShapeDtypeStruct(own.shape, kind) for kind in kinds],
         compiler_params=pltpu.CompilerParams(vmem_limit_bytes=24 * 1024 * 1024),
         cost_estimate=pl.CostEstimate(
             flops=2 * tile.size * own.shape[1], bytes_accessed=2 * (tile.size + 5 * own.size), transcendentals=0
         ),
         name="full_product",
-    )(meta, tile, below, own, above)
+    )(meta, tile, below, own, above, stress)
 
 
 def tree_to_first(value, lags, least):
     stride = 1
     while stride < lags:
         route = [(i + stride, i) for i in range(0, lags - stride, 2 * stride) if i + stride >= least]
-        value = value + lax.ppermute(value.astype(jnp.bfloat16), "lag", route).astype(jnp.float32)
+        added = lax.ppermute(value, "lag", route)
+        value = lax.optimization_barrier(value.astype(jnp.float32) + added.astype(jnp.float32))
         stride *= 2
+        if stride < lags:
+            value = value.astype(jnp.bfloat16)
     return value
 
 
@@ -183,13 +194,13 @@
     traction = scatter_sum(parts)
     rates, state = settle_friction(stress + traction, state, *columns)
 
-    placed = lax.dynamic_update_slice_in_dim(jnp.zeros(field.shape, jnp.float32), stress, me * rows, 0)
-    later = [i for i in every if i >= 1]
-    below_1, above_1 = exchange(shifted, later)
-    base_1 = tree_to_first(full_product(meta, me >= 1, tile, below_1, shifted, above_1) + placed, lags, 1)
+    below_1, above_1 = exchange(shifted, [i for i in every if i >= 1])
+    (part,) = full_product(meta, me >= 1, tile, below_1, shifted, above_1, stress, [jnp.bfloat16])
+    base_1 = tree_to_first(part, lags, 1)
     twice = lax.ppermute(shifted, "lag", [(i, i + 1) for i in range(1, lags - 1)])
     below_2, above_2 = exchange(twice, [i for i in every if i >= 2])
-    base_2 = tree_to_first(full_product(meta, me >= 2, tile, below_2, twice, above_2) + placed, lags, 2)
+    (part,) = full_product(meta, me >= 2, tile, below_2, twice, above_2, stress, [jnp.bfloat16])
+    base_2 = tree_to_first(part, lags, 2)
 
     block_state = jnp.concatenate([g[:rows] for g in gathered], 0)
     block_columns = [jnp.concatenate([g[rows + k, :rows] for g in gathered])[:, None] for k in range(3)]
@@ -199,11 +210,13 @@
     before = block_state
 
     below_v, above_v = exchange(first, [0, 1])
-    part = full_product(meta, me <= 1, tile, below_v, first, above_v)
-    from_next = lax.ppermute((part + placed).astype(jnp.bfloat16), "lag", [(1, 0)])
+    kinds = [jnp.bfloat16, jnp.float32]
+    sent, part = full_product(meta, me <= 1, tile, below_v, first, above_v, stress, kinds)
+    from_next = lax.ppermute(sent, "lag", [(1, 0)])
     second, block_state = settle_friction(base_1 + part, block_state, *block_columns)
     below_v, above_v = exchange(second, [0])
-    part = full_product(meta, me == 0, tile, below_v, second, above_v)
+    kinds = [jnp.bfloat16, jnp.float32]
+    _, part = full_product(meta, me == 0, tile, below_v, second, above_v, stress, kinds)
     sent = jnp.where(me == 0, second, twice)
     moved = lax.ppermute(sent, "lag", [(0, 1)] + [(i, i + 1) for i in range(2, lags - 1)])
     load = base_2 + from_next.astype(jnp.float32) + part
@@ -217,7 +230,8 @@
         piece = lax.ppermute(change[d * rows : (d + 1) * rows], "lag", [(0, d)])
         mine = jnp.where(me == d, piece, mine)
     state = state + mine
-    traction = scatter_sum(product(meta, tile, below_v, last, above_v, lags))
+    parts = product(meta, tile, below_v, last, above_v, lags)
+    traction = scatter_sum(parts)
     rates, state = settle_friction(stress + traction, state, *columns)
     return rates[None, None], state[None, None]
 

time: 221 us -> 183 us (0.83)
  waiting for transfers between devices: 96.3 us -> 33.5 us
  blocking collectives: 15.6 us -> 31.5 us
  other arithmetic: 23.5 us -> 26.2 us
  local copies, waits for them, and re-layouts: 8.37 us -> 10.8 us
    ppermute x3, waiting for transfers between devices: 28 us -> 0.01 us  [shards(): lax.ppermute(packed, 'lag', [(d, 0)])]
    all_gather x1, blocking collectives: 15.6 us -> 31.5 us  [shards(): first = lax.all_gather(rates, 'lag', axis=0, tiled=True)]
    ppermute x5, waiting for transfers between devices: 19.1 us -> 6.91 us  [the longest x4 4.63 us: tree_to_first(): added = lax.ppermute(value, 'lag', route)]
    ppermute x1, waiting for transfers between devices: 10.7 us -> 0.01 us  [shards(): shifted = lax.ppermute(field, 'lag', [(i, i + 1) for i in range(lags - 1)])]
    ppermute x12, waiting for transfers between devices: 17.3 us -> 7.55 us  [exchange(): return (lax.ppermute(value, axes, up), lax.ppermute(value, axes, down))]
    ppermute x1, starting transfers between devices: 1.59 us -> 5.45 us  [shards(): lax.ppermute(sent, 'lag', [(0, 1)] + [(i, i + 1) for i in range(2, lags -...]
    add x1 -> x4, other arithmetic: 0.1 us -> 2.48 us  [tree_to_first(): value.astype(jnp.float32) + added.astype(jnp.float32)]
    unnamed x57 -> x54, local copies, waits for them, and re-layouts: 7.45 us -> 8.09 us
  transfers between devices with their start and end apart: 32 -> 32, of which waited for: 19 -> 13; matrix products, arithmetic and copies ran while one was open for 9% -> 14% of each run, Pallas kernels for 4% -> 6%
where the time goes in v3:
time: 183 us; the launch traced here: 181 us
  starting transfers between devices  65.1 us (36%)
  waiting for transfers between devices  33.5 us (18%)
  blocking collectives  31.5 us (17%)
  other arithmetic  26.2 us (14%)
  Pallas kernels  11.8 us (6%)
  local copies, waits for them, and re-layouts  10.8 us (6%)
  between operations  1.98 us (1%)
    all_gather x1, blocking collectives, shards(): first = lax.all_gather(rates, 'lag', axis=0, tiled=True)  31.5 us
    ppermute x12, starting transfers between devices, exchange(): return (lax.ppermute(value, axes, up), lax.ppermute(value, axes, down))  25 us
    ppermute x6, starting transfers between devices, scatter_sum(): total = total + lax.ppermute(parts[d], 'lag', route).astype(jnp.float32)  14.6 us
    ppermute x6, waiting for transfers between devices, scatter_sum(): total = total + lax.ppermute(parts[d], 'lag', route).astype(jnp.float32)  13.2 us
    unnamed x54, local copies, waits for them, and re-layouts  8.09 us
    sub x1, other arithmetic, shards(): change = block_state - before  7.77 us
    pallas_call x4, Pallas kernels, full_product(): pl.pallas_call(functools.partial(full_product_kernel, chunks), grid_spec=...  7.72 us
    ppermute x12, waiting for transfers between devices, exchange(): return (lax.ppermute(value, axes, up), lax.ppermute(value, axes, down))  7.55 us
  transfers between devices with their start and end apart: 32, of which 13 were waited for; matrix products, arithmetic and copies ran while one was open for 14% of the time, Pallas kernels for 6%

profile of v3, /device:TPU:2, one launch (start us, length us, event | category | flops | bytes accessed | tf_op | source)
XLA Modules:
  0.0 181.0 jit_solution(3469607577306739589)
XLA Ops:
  0.6 4.5 %collective-permute-start = (bf16[1024,256]{1,0:T(8,128)(2,1)}, bf16[1024,256]{1,0:T(8,128)(2,1)}, u32[]{:S(2)}, u32[]{:S(2)}) collective-permute-start(bf16[1024,256]{1,0:T(8,128)(2,1)} %bitcast.49), channel_id=1, source_target_pairs={{0,8},{8,16},{16,24},{1,9},{9,17},{17,25},{2,10},{10,18},{18,26},{... | collective-permute-start | bytes 1572872 | tf_op jit(solution)/shard_map/ppermute | solution.py:190
  5.1 1.9 %collective-permute-start.6 = (bf16[1024,256]{1,0:T(8,128)(2,1)}, bf16[1024,256]{1,0:T(8,128)(2,1)S(1)}, u32[]{:S(2)}, u32[]{:S(2)}) collective-permute-start(bf16[1024,256]{1,0:T(8,128)(2,1)} %bitcast.50), channel_id=1, source_target_pairs={{0,1},{1,2},{2,3},{3,4},{4,5},{5,6},{6,7},{8,9},{9,10},{10,11},{11... | collective-permute-start | bytes 1572872 | tf_op jit(solution)/shard_map/ppermute | solution.py:24
  7.0 3.6 %collective-permute-start.7 = (bf16[1024,256]{1,0:T(8,128)(2,1)}, bf16[1024,256]{1,0:T(8,128)(2,1)S(1)}, u32[]{:S(2)}, u32[]{:S(2)}) collective-permute-start(bf16[1024,256]{1,0:T(8,128)(2,1)} %bitcast.51), channel_id=1, source_target_pairs={{1,0},{2,1},{3,2},{4,3},{5,4},{6,5},{7,6},{9,8},{10,9},{11,10},{12... | collective-permute-start | bytes 1572872 | tf_op jit(solution)/shard_map/ppermute | solution.py:24
  10.7 0.7 select_maximum_fusion
  11.4 1.7 pad_maximum_fusion.1
  13.1 1.3 collective-permute-start.20
  14.4 0.7 broadcast_multiply_fusion.1
  15.8 0.7 collective-permute-start.14
  16.5 0.7 pad_add_fusion.1
  17.9 0.8 copy-done.6
  19.5 0.7 pad_add_fusion.meta
  20.5 0.8 copy-done.8
  21.3 1.9 %copy-done = bf16[1,1024,1536]{2,1,0:T(8,128)(2,1)S(1)} copy-done((bf16[1,1024,1536]{2,1,0:T(8,128)(2,1)S(1)}, bf16[1,1024,1536]{2,1,0:T(8,128)(2,1)}, u32[]{:S(2)}) %copy-start) | copy-done | bytes 3145752
  23.2 1.0 copy-done.5
  24.3 1.0 copy-done.7
  25.3 1.0 copy-done.9
  26.4 1.7 product.2
  28.1 9.6 %collective-permute-start.10 = (bf16[256,256]{1,0:T(8,128)(2,1)S(1)}, bf16[256,256]{1,0:T(8,128)(2,1)S(1)}, u32[]{:S(2)}, u32[]{:S(2)}) collective-permute-start(bf16[256,256]{1,0:T(8,128)(2,1)S(1)} %get-tuple-element.16), channel_id=1, source_target_pairs={{0,24},{8,0},{16,8},{24,16},{1,25},{9,1},{17,9},{25,17},{2,26},{10... | collective-permute-start | bytes 393224 | tf_op jit(solution)/shard_map/ppermute | solution.py:96
  37.7 1.0 collective-permute-start.9
  38.7 1.9 %collective-permute-start.8 = (bf16[256,256]{1,0:T(8,128)(2,1)S(1)}, bf16[256,256]{1,0:T(8,128)(2,1)S(1)}, u32[]{:S(2)}, u32[]{:S(2)}) collective-permute-start(bf16[256,256]{1,0:T(8,128)(2,1)S(1)} %get-tuple-element.14), channel_id=1, source_target_pairs={{0,8},{8,16},{16,24},{24,0},{1,9},{9,17},{17,25},{25,1},{2,10},{10... | collective-permute-start | bytes 393224 | tf_op jit(solution)/shard_map/ppermute | solution.py:96
  40.6 0.8 fusion.71
  41.4 1.3 collective-permute-start.19
  43.4 1.3 collective-permute-start.18
  44.7 6.7 %collective-permute-done.9 = bf16[256,256]{1,0:T(8,128)(2,1)S(1)} collective-permute-done((bf16[256,256]{1,0:T(8,128)(2,1)S(1)}, bf16[256,256]{1,0:T(8,128)(2,1)S(1)}, u32[]{:S(2)}, u32[]{:S(2)}) %collective-permute-start.9) | collective-permute-done | bytes 131104 | tf_op jit(solution)/shard_map/ppermute | solution.py:96
  51.4 1.3 collective-permute-start.16
  52.7 0.7 collective-permute-start.2
  53.4 1.7 fusion.66
  55.8 31.5 %all_gather.3.own = bf16[1024,256]{1,0:T(8,128)(2,1)S(1)} all-gather(bf16[256,256]{1,0:T(8,128)(2,1)S(1)} %get-tuple-element.35), channel_id=1, replica_groups=mesh['lag'=4,'elem'=8] {'lag'}, dimensions={0}, use_global_device_ids=true | all-gather | bytes 655360 | tf_op jit(solution)/shard_map/all_gather | solution.py:207
  87.3 1.9 %collective-permute-start.11 = (bf16[1024,256]{1,0:T(8,128)(2,1)S(1)}, bf16[1024,256]{1,0:T(8,128)(2,1)S(1)}, u32[]{:S(2)}, u32[]{:S(2)}) collective-permute-start(bf16[1024,256]{1,0:T(8,128)(2,1)S(1)} %all_gather.3.own), channel_id=1, source_target_pairs={{0,1},{1,2},{2,3},{3,4},{4,5},{5,6},{6,7},{8,9},{9,10},{10,11},{11... | collective-permute-start | bytes 1572872 | tf_op jit(solution)/shard_map/ppermute | solution.py:24
  89.4 3.6 %collective-permute-start.12 = (bf16[1024,256]{1,0:T(8,128)(2,1)S(1)}, bf16[1024,256]{1,0:T(8,128)(2,1)S(1)}, u32[]{:S(2)}, u32[]{:S(2)}) collective-permute-start(bf16[1024,256]{1,0:T(8,128)(2,1)S(1)} %all_gather.3.own), channel_id=1, source_target_pairs={{1,0},{2,1},{3,2},{4,3},{5,4},{6,5},{7,6},{9,8},{10,9},{11,10},{12... | collective-permute-start | bytes 1572872 | tf_op jit(solution)/shard_map/ppermute | solution.py:24
  93.1 1.3 collective-permute-start.17
  95.0 0.7 collective-permute-start.4
  95.8 1.0 slice.78
  96.9 0.9 collective-permute-done.11.below
  97.8 3.3 %collective-permute-done.12.above = bf16[1024,256]{1,0:T(8,128)(2,1)S(1)} collective-permute-done((bf16[1024,256]{1,0:T(8,128)(2,1)S(1)}, bf16[1024,256]{1,0:T(8,128)(2,1)S(1)}, u32[]{:S(2)}, u32[]{:S(2)}) %collective-permute-start.12) | collective-permute-done | bytes 524320 | tf_op jit(solution)/shard_map/ppermute | solution.py:24
  101.1 2.7 %full_product.5 = (bf16[1024,256]{1,0:T(8,128)(2,1)}, f32[1024,256]{1,0:T(8,128)S(1)}) custom-call(s32[6]{0:T(128)S(1)} %get-tuple-element.54.meta, bf16[1024,1536]{1,0:T(8,128)(2,1)S(1)} %bitcast.42, bf16[1024,256]{1,0:T(8,128)(2,1)S(1)} %collective-permute-done.11.below, bf16[1024,256]{1,0:T(8,128)(2,1)S(1)} %all_gather.3.own, ...), custom_call_target="tpu_custom_call" | custom-call | flops 805306368 | bytes 5767168 | tf_op jit(solution)/shard_map/full_product/pallas_call | solution.py:146
  103.8 4.6 %collective-permute-done.17 = bf16[1024,256]{1,0:T(8,128)(2,1)S(1)} collective-permute-done((bf16[1024,256]{1,0:T(8,128)(2,1)S(1)}, bf16[1024,256]{1,0:T(8,128)(2,1)S(1)}, u32[]{:S(2)}, u32[]{:S(2)}) %collective-permute-start.17) | collective-permute-done | bytes 524320 | tf_op jit(solution)/shard_map/ppermute | solution.py:170
  108.6 0.9 convert_add_fusion.3
  109.5 1.3 collective-permute-start.5
  110.8 6.3 %broadcast_select_fusion = (bf16[1024,256]{1,0:T(8,128)(2,1)}, bf16[1024,256]{1,0:T(8,128)(2,1)}, f32[1024,256]{1,0:T(8,128)}) fusion(bf16[1024,256]{1,0:T(8,128)(2,1)S(1)} %collective-permute-done.1.own, pred[]{:T(512)S(6)} %eq.15, f32[1024]{0:T(1024)S(1)} %get-tuple-element.34, f32[1024]{0:T(1024)S(1)} %get-tuple-element.33, ...), kind=kLoop, calls=%fused_computation.50 | loop fusion | flops 17301504 | bytes 6303745 | tf_op jit(solution)/shard_map/jit(_where)/select_n | solution.py:220
  117.1 1.9 %collective-permute-start.21 = (bf16[1024,256]{1,0:T(8,128)(2,1)}, bf16[1024,256]{1,0:T(8,128)(2,1)}, u32[]{:S(2)}, u32[]{:S(2)}) collective-permute-start(bf16[1024,256]{1,0:T(8,128)(2,1)} %get-tuple-element.31.own), channel_id=1, source_target_pairs={{0,1},{1,2},{2,3},{3,4},{4,5},{5,6},{6,7}} | collective-permute-start | bytes 1572872 | tf_op jit(solution)/shard_map/ppermute | solution.py:24
  119.0 3.6 %collective-permute-start.22 = (bf16[1024,256]{1,0:T(8,128)(2,1)}, bf16[1024,256]{1,0:T(8,128)(2,1)}, u32[]{:S(2)}, u32[]{:S(2)}) collective-permute-start(bf16[1024,256]{1,0:T(8,128)(2,1)} %get-tuple-element.31.own), channel_id=1, source_target_pairs={{1,0},{2,1},{3,2},{4,3},{5,4},{6,5},{7,6}} | collective-permute-start | bytes 1572872 | tf_op jit(solution)/shard_map/ppermute | solution.py:24
  122.7 1.3 collective-permute-start.13
  124.1 5.5 %collective-permute-start.23 = (bf16[1024,256]{1,0:T(8,128)(2,1)}, bf16[1024,256]{1,0:T(8,128)(2,1)S(1)}, u32[]{:S(2)}, u32[]{:S(2)}) collective-permute-start(bf16[1024,256]{1,0:T(8,128)(2,1)} %get-tuple-element.30), channel_id=1, source_target_pairs={{0,8},{16,24},{1,9},{17,25},{2,10},{18,26},{3,11},{19,27},{4,12},{... | collective-permute-start | bytes 1572872 | tf_op jit(solution)/shard_map/ppermute | solution.py:221
  129.5 1.3 convert_add_fusion.2
  131.5 3.8 %full_product.7 = (bf16[1024,256]{1,0:T(8,128)(2,1)}, f32[1024,256]{1,0:T(8,128)S(1)}) custom-call(s32[6]{0:T(128)S(1)} %get-tuple-element.53.meta, bf16[1024,1536]{1,0:T(8,128)(2,1)S(1)} %bitcast.43, bf16[1024,256]{1,0:T(8,128)(2,1)} %collective-permute-done.21.below, bf16[1024,256]{1,0:T(8,128)(2,1)} %get-tuple-element.31.own, ...), custom_call_target="tpu_custom_call" | custom-call | flops 805306368 | bytes 5767168 | tf_op jit(solution)/shard_map/full_product/pallas_call | solution.py:146
  135.3 2.3 %collective-permute-done.13 = bf16[1024,256]{1,0:T(8,128)(2,1)} collective-permute-done((bf16[1024,256]{1,0:T(8,128)(2,1)}, bf16[1024,256]{1,0:T(8,128)(2,1)}, u32[]{:S(2)}, u32[]{:S(2)}) %collective-permute-start.13) | collective-permute-done | bytes 524320 | tf_op jit(solution)/shard_map/ppermute | solution.py:215
  137.6 7.8 %add_subtract_fusion = (f32[1024,256]{1,0:T(8,128)S(1)}, bf16[1024,256]{1,0:T(8,128)(2,1)S(1)}) fusion(f32[1024,256]{1,0:T(8,128)S(1)} %copy-done.14, bf16[1024,256]{1,0:T(8,128)(2,1)S(1)} %copy-done.3, f32[256,256]{1,0:T(8,128)S(1)} %copy-done.16, f32[256,256]{1,0:T(8,128)S(1)} %copy-done.18, f32[256,256]{1,0:T(8,128)S(1)} %copy-done.20, ...), kind=kLoop, calls=%fused_computation.37 | loop fusion | flops 20971520 | bytes 6828032 | tf_op jit(solution)/shard_map/sub | solution.py:227
  145.5 1.9 %collective-permute-start.24 = (bf16[1024,256]{1,0:T(8,128)(2,1)S(1)}, bf16[1024,256]{1,0:T(8,128)(2,1)S(1)}, u32[]{:S(2)}, u32[]{:S(2)}) collective-permute-start(bf16[1024,256]{1,0:T(8,128)(2,1)S(1)} %select_select_fusion.own), channel_id=1, source_target_pairs={{0,1},{1,2},{2,3},{3,4},{4,5},{5,6},{6,7},{8,9},{9,10},{10,11},{11... | collective-permute-start | bytes 1572872 | tf_op jit(solution)/shard_map/ppermute | solution.py:24
  147.5 3.6 %collective-permute-start.25 = (bf16[1024,256]{1,0:T(8,128)(2,1)S(1)}, bf16[1024,256]{1,0:T(8,128)(2,1)S(1)}, u32[]{:S(2)}, u32[]{:S(2)}) collective-permute-start(bf16[1024,256]{1,0:T(8,128)(2,1)S(1)} %select_select_fusion.own), channel_id=1, source_target_pairs={{1,0},{2,1},{3,2},{4,3},{5,4},{6,5},{7,6},{9,8},{10,9},{11,10},{12... | collective-permute-start | bytes 1572872 | tf_op jit(solution)/shard_map/ppermute | solution.py:24
  151.1 0.9 fusion.68
  152.0 1.3 collective-permute-start.29
  153.3 2.0 %collective-permute-start.30 = (f32[256,256]{1,0:T(8,128)}, f32[256,256]{1,0:T(8,128)}, u32[]{:S(2)}, u32[]{:S(2)}) collective-permute-start(f32[256,256]{1,0:T(8,128)} %get-tuple-element.40), channel_id=1, source_target_pairs={{0,16},{1,17},{2,18},{3,19},{4,20},{5,21},{6,22},{7,23}} | collective-permute-start | bytes 786440 | tf_op jit(solution)/shard_map/ppermute | solution.py:230
  155.3 2.0 %collective-permute-start.31 = (f32[256,256]{1,0:T(8,128)}, f32[256,256]{1,0:T(8,128)}, u32[]{:S(2)}, u32[]{:S(2)}) collective-permute-start(f32[256,256]{1,0:T(8,128)} %get-tuple-element.39), channel_id=1, source_target_pairs={{0,8},{1,9},{2,10},{3,11},{4,12},{5,13},{6,14},{7,15}} | collective-permute-start | bytes 786440 | tf_op jit(solution)/shard_map/ppermute | solution.py:230
  157.3 2.3 %collective-permute-done.25.above = bf16[1024,256]{1,0:T(8,128)(2,1)S(1)} collective-permute-done((bf16[1024,256]{1,0:T(8,128)(2,1)S(1)}, bf16[1024,256]{1,0:T(8,128)(2,1)S(1)}, u32[]{:S(2)}, u32[]{:S(2)}) %collective-permute-start.25) | collective-permute-done | bytes 524320 | tf_op jit(solution)/shard_map/ppermute | solution.py:24
  159.6 2.4 %product.3 = (f32[256,256]{1,0:T(8,128)S(1)}, bf16[256,256]{1,0:T(8,128)(2,1)S(1)}, bf16[256,256]{1,0:T(8,128)(2,1)}, bf16[256,256]{1,0:T(8,128)(2,1)}) custom-call(s32[5]{0:T(128)S(1)} %pad_add_fusion.meta, bf16[1024,1536]{1,0:T(8,128)(2,1)S(1)} %bitcast.44, bf16[1024,256]{1,0:T(8,128)(2,1)S(1)} %collective-permute-done.24.below, ...), custom_call_target="tpu_custom_call" | custom-call | flops 805306368 | bytes 5242880 | tf_op jit(solution)/shard_map/product/pallas_call | solution.py:70
  162.7 1.0 collective-permute-start.27
  163.7 0.7 copy-done.21
  164.4 1.0 collective-permute-start.26
  165.7 5.6 %collective-permute-done.31 = f32[256,256]{1,0:T(8,128)} collective-permute-done((f32[256,256]{1,0:T(8,128)}, f32[256,256]{1,0:T(8,128)}, u32[]{:S(2)}, u32[]{:S(2)}) %collective-permute-start.31) | collective-permute-done | bytes 262176 | tf_op jit(solution)/shard_map/ppermute | solution.py:230
  171.3 2.9 %collective-permute-done.28 = bf16[256,256]{1,0:T(8,128)(2,1)S(1)} collective-permute-done((bf16[256,256]{1,0:T(8,128)(2,1)}, bf16[256,256]{1,0:T(8,128)(2,1)S(1)}, u32[]{:S(2)}, u32[]{:S(2)}) %collective-permute-start.28) | collective-permute-done | bytes 131104 | tf_op jit(solution)/shard_map/ppermute | solution.py:96
  174.2 2.3 %collective-permute-done.27 = bf16[256,256]{1,0:T(8,128)(2,1)S(1)} collective-permute-done((bf16[256,256]{1,0:T(8,128)(2,1)}, bf16[256,256]{1,0:T(8,128)(2,1)S(1)}, u32[]{:S(2)}, u32[]{:S(2)}) %collective-permute-start.27) | collective-permute-done | bytes 131104 | tf_op jit(solution)/shard_map/ppermute | solution.py:96
  176.5 1.3 collective-permute-done.26
  177.8 3.2 %add_bitcast_fusion = (f32[1,1,256,256]{3,2,1,0:T(8,128)}, bf16[256,256]{1,0:T(8,128)(2,1)}) fusion(f32[256]{0:T(256)S(1)} %get-tuple-element.38, f32[256]{0:T(256)S(1)} %get-tuple-element.37, f32[256]{0:T(256)S(1)} %copy-done.26, bf16[256,256]{1,0:T(8,128)(2,1)S(1)} %collective-permute-done.28, bf16[256,256]{1,0:T(8,128)(2,1)S(1)} %collective-permute-done.27, ...), kind=kLoop, calls=%fused_computation.92 | loop fusion | flops 5046272 | bytes 2886659 | tf_op jit(solution)/shard_map/broadcast_in_dim | solution.py:236
  (84 shorter events, 5.9 us)
Async XLA Ops:
  0.6 42.1 %copy-start.4 = (f32[1,1,256,256]{3,2,1,0:T(8,128)S(1)}, f32[1,1,256,256]{3,2,1,0:T(8,128)}, u32[]{:S(2)}) copy-start(f32[1,1,256,256]{3,2,1,0:T(8,128)} %param.13) | copy-start | bytes 786436
  0.6 15.1 %collective-permute-start = (bf16[1024,256]{1,0:T(8,128)(2,1)}, bf16[1024,256]{1,0:T(8,128)(2,1)}, u32[]{:S(2)}, u32[]{:S(2)}) collective-permute-start(bf16[1024,256]{1,0:T(8,128)(2,1)} %bitcast.49), channel_id=1, source_target_pairs={{0,8},{8,16},{16,24},{1,9},{9,17},{17,25},{2,10},{10,18},{18,26},{... | collective-permute-start | bytes 1572872 | tf_op jit(solution)/shard_map/ppermute | solution.py:190
  5.1 12.8 %collective-permute-start.6 = (bf16[1024,256]{1,0:T(8,128)(2,1)}, bf16[1024,256]{1,0:T(8,128)(2,1)S(1)}, u32[]{:S(2)}, u32[]{:S(2)}) collective-permute-start(bf16[1024,256]{1,0:T(8,128)(2,1)} %bitcast.50), channel_id=1, source_target_pairs={{0,1},{1,2},{2,3},{3,4},{4,5},{5,6},{6,7},{8,9},{9,10},{10,11},{11... | collective-permute-start | bytes 1572872 | tf_op jit(solution)/shard_map/ppermute | solution.py:24
  7.0 13.5 %collective-permute-start.7 = (bf16[1024,256]{1,0:T(8,128)(2,1)}, bf16[1024,256]{1,0:T(8,128)(2,1)S(1)}, u32[]{:S(2)}, u32[]{:S(2)}) collective-permute-start(bf16[1024,256]{1,0:T(8,128)(2,1)} %bitcast.51), channel_id=1, source_target_pairs={{1,0},{2,1},{3,2},{4,3},{5,4},{6,5},{7,6},{9,8},{10,9},{11,10},{12... | collective-permute-start | bytes 1572872 | tf_op jit(solution)/shard_map/ppermute | solution.py:24
  13.1 24.6 %collective-permute-start.20 = (f32[264,256]{1,0:T(8,128)}, f32[264,256]{1,0:T(8,128)}, u32[]{:S(2)}, u32[]{:S(2)}) collective-permute-start(f32[264,256]{1,0:T(8,128)} %pad_maximum_fusion.1), channel_id=1, source_target_pairs={{24,0},{25,1},{26,2},{27,3},{28,4},{29,5},{30,6},{31,7}} | collective-permute-start | bytes 811016 | tf_op jit(solution)/shard_map/ppermute | solution.py:192
  15.1 38.3 %copy-start.25 = (f32[256]{0:T(256)}, f32[256]{0:T(256)S(1)}, u32[]{:S(2)}) copy-start(f32[256]{0:T(256)S(1)} %get-tuple-element.52) | copy-start | bytes 3076
  15.8 22.9 %collective-permute-start.14 = (bf16[1024,256]{1,0:T(8,128)(2,1)}, bf16[1024,256]{1,0:T(8,128)(2,1)S(1)}, u32[]{:S(2)}, u32[]{:S(2)}) collective-permute-start(bf16[1024,256]{1,0:T(8,128)(2,1)} %collective-permute-done.own), channel_id=1, source_target_pairs={{8,9},{9,10},{10,11},{11,12},{12,13},{13,14},{14,15},{16,17},{17,1... | collective-permute-start | bytes 1572872 | tf_op jit(solution)/shard_map/ppermute | solution.py:24
  17.2 35.5 %collective-permute-start.1 = (bf16[1024,256]{1,0:T(8,128)(2,1)}, bf16[1024,256]{1,0:T(8,128)(2,1)S(1)}, u32[]{:S(2)}, u32[]{:S(2)}) collective-permute-start(bf16[1024,256]{1,0:T(8,128)(2,1)} %collective-permute-done.own), channel_id=1, source_target_pairs={{8,16},{16,24},{9,17},{17,25},{10,18},{18,26},{11,19},{19,27},{12,... | collective-permute-start | bytes 1572872 | tf_op jit(solution)/shard_map/ppermute | solution.py:200
  17.9 0.8 copy-start.6
  18.7 22.7 %collective-permute-start.15 = (bf16[1024,256]{1,0:T(8,128)(2,1)}, bf16[1024,256]{1,0:T(8,128)(2,1)S(1)}, u32[]{:S(2)}, u32[]{:S(2)}) collective-permute-start(bf16[1024,256]{1,0:T(8,128)(2,1)} %collective-permute-done.own), channel_id=1, source_target_pairs={{9,8},{10,9},{11,10},{12,11},{13,12},{14,13},{15,14},{17,16},{18,1... | collective-permute-start | bytes 1572872 | tf_op jit(solution)/shard_map/ppermute | solution.py:24
  20.5 0.8 copy-start.8
  21.3 1.9 %copy-start = (bf16[1,1024,1536]{2,1,0:T(8,128)(2,1)S(1)}, bf16[1,1024,1536]{2,1,0:T(8,128)(2,1)}, u32[]{:S(2)}) copy-start(bf16[1,1024,1536]{2,1,0:T(8,128)(2,1)} %param.9) | copy-start | bytes 9437188
  23.2 1.0 copy-start.5
  24.3 1.0 copy-start.7
  25.3 1.0 copy-start.9
  26.4 16.4 %copy-start.1 = (bf16[1,1024,1536]{2,1,0:T(8,128)(2,1)S(1)}, bf16[1,1024,1536]{2,1,0:T(8,128)(2,1)}, u32[]{:S(2)}) copy-start(bf16[1,1024,1536]{2,1,0:T(8,128)(2,1)} %param.9) | copy-start | bytes 9437188
  28.0 25.4 %copy-start.11 = (f32[1,1,256,256]{3,2,1,0:T(8,128)S(1)}, f32[1,1,256,256]{3,2,1,0:T(8,128)}, u32[]{:S(2)}) copy-start(f32[1,1,256,256]{3,2,1,0:T(8,128)} %param.14) | copy-start | bytes 786436
  28.1 15.3 %collective-permute-start.10 = (bf16[256,256]{1,0:T(8,128)(2,1)S(1)}, bf16[256,256]{1,0:T(8,128)(2,1)S(1)}, u32[]{:S(2)}, u32[]{:S(2)}) collective-permute-start(bf16[256,256]{1,0:T(8,128)(2,1)S(1)} %get-tuple-element.16), channel_id=1, source_target_pairs={{0,24},{8,0},{16,8},{24,16},{1,25},{9,1},{17,9},{25,17},{2,26},{10... | collective-permute-start | bytes 393224 | tf_op jit(solution)/shard_map/ppermute | solution.py:96
  37.7 13.7 %collective-permute-start.9 = (bf16[256,256]{1,0:T(8,128)(2,1)S(1)}, bf16[256,256]{1,0:T(8,128)(2,1)S(1)}, u32[]{:S(2)}, u32[]{:S(2)}) collective-permute-start(bf16[256,256]{1,0:T(8,128)(2,1)S(1)} %get-tuple-element.15), channel_id=1, source_target_pairs={{0,16},{8,24},{16,0},{24,8},{1,17},{9,25},{17,1},{25,9},{2,18},{10... | collective-permute-start | bytes 393224 | tf_op jit(solution)/shard_map/ppermute | solution.py:96
  38.7 14.7 %collective-permute-start.8 = (bf16[256,256]{1,0:T(8,128)(2,1)S(1)}, bf16[256,256]{1,0:T(8,128)(2,1)S(1)}, u32[]{:S(2)}, u32[]{:S(2)}) collective-permute-start(bf16[256,256]{1,0:T(8,128)(2,1)S(1)} %get-tuple-element.14), channel_id=1, source_target_pairs={{0,8},{8,16},{16,24},{24,0},{1,9},{9,17},{17,25},{25,1},{2,10},{10... | collective-permute-start | bytes 393224 | tf_op jit(solution)/shard_map/ppermute | solution.py:96
  41.4 48.0 %collective-permute-start.19 = (f32[264,256]{1,0:T(8,128)}, f32[264,256]{1,0:T(8,128)S(1)}, u32[]{:S(2)}, u32[]{:S(2)}) collective-permute-start(f32[264,256]{1,0:T(8,128)} %pad_maximum_fusion.1), channel_id=1, source_target_pairs={{16,0},{17,1},{18,2},{19,3},{20,4},{21,5},{22,6},{23,7}} | collective-permute-start | bytes 811016 | tf_op jit(solution)/shard_map/ppermute | solution.py:192
  43.4 52.4 %collective-permute-start.18 = (f32[264,256]{1,0:T(8,128)}, f32[264,256]{1,0:T(8,128)S(1)}, u32[]{:S(2)}, u32[]{:S(2)}) collective-permute-start(f32[264,256]{1,0:T(8,128)} %pad_maximum_fusion.1), channel_id=1, source_target_pairs={{8,0},{9,1},{10,2},{11,3},{12,4},{13,5},{14,6},{15,7}} | collective-permute-start | bytes 811016 | tf_op jit(solution)/shard_map/ppermute | solution.py:192
  51.4 35.9 %collective-permute-start.16 = (bf16[1024,256]{1,0:T(8,128)(2,1)S(1)}, bf16[1024,256]{1,0:T(8,128)(2,1)S(1)}, u32[]{:S(2)}, u32[]{:S(2)}) collective-permute-start(bf16[1024,256]{1,0:T(8,128)(2,1)S(1)} %full_product.6), channel_id=1, source_target_pairs={{8,0},{24,16},{9,1},{25,17},{10,2},{26,18},{11,3},{27,19},{12,4},{... | collective-permute-start | bytes 1572872 | tf_op jit(solution)/shard_map/ppermute | solution.py:170
  52.7 40.4 %collective-permute-start.2 = (bf16[1024,256]{1,0:T(8,128)(2,1)S(1)}, bf16[1024,256]{1,0:T(8,128)(2,1)S(1)}, u32[]{:S(2)}, u32[]{:S(2)}) collective-permute-start(bf16[1024,256]{1,0:T(8,128)(2,1)S(1)} %collective-permute-done.1.own), channel_id=1, source_target_pairs={{16,17},{17,18},{18,19},{19,20},{20,21},{21,22},{22,23},{24,25},{2... | collective-permute-start | bytes 1572872 | tf_op jit(solution)/shard_map/ppermute | solution.py:24
  55.1 39.3 %collective-permute-start.3 = (bf16[1024,256]{1,0:T(8,128)(2,1)S(1)}, bf16[1024,256]{1,0:T(8,128)(2,1)S(1)}, u32[]{:S(2)}, u32[]{:S(2)}) collective-permute-start(bf16[1024,256]{1,0:T(8,128)(2,1)S(1)} %collective-permute-done.1.own), channel_id=1, source_target_pairs={{17,16},{18,17},{19,18},{20,19},{21,20},{22,21},{23,22},{25,24},{2... | collective-permute-start | bytes 1572872 | tf_op jit(solution)/shard_map/ppermute | solution.py:24
  87.3 23.5 %copy-start.2 = (bf16[1024,256]{1,0:T(8,128)(2,1)}, bf16[1024,256]{1,0:T(8,128)(2,1)S(1)}, u32[]{:S(2)}) copy-start(bf16[1024,256]{1,0:T(8,128)(2,1)S(1)} %all_gather.3.own) | copy-start | bytes 1572868
  87.3 10.5 %collective-permute-start.11 = (bf16[1024,256]{1,0:T(8,128)(2,1)S(1)}, bf16[1024,256]{1,0:T(8,128)(2,1)S(1)}, u32[]{:S(2)}, u32[]{:S(2)}) collective-permute-start(bf16[1024,256]{1,0:T(8,128)(2,1)S(1)} %all_gather.3.own), channel_id=1, source_target_pairs={{0,1},{1,2},{2,3},{3,4},{4,5},{5,6},{6,7},{8,9},{9,10},{10,11},{11... | collective-permute-start | bytes 1572872 | tf_op jit(solution)/shard_map/ppermute | solution.py:24
  89.4 11.7 %collective-permute-start.12 = (bf16[1024,256]{1,0:T(8,128)(2,1)S(1)}, bf16[1024,256]{1,0:T(8,128)(2,1)S(1)}, u32[]{:S(2)}, u32[]{:S(2)}) collective-permute-start(bf16[1024,256]{1,0:T(8,128)(2,1)S(1)} %all_gather.3.own), channel_id=1, source_target_pairs={{1,0},{2,1},{3,2},{4,3},{5,4},{6,5},{7,6},{9,8},{10,9},{11,10},{12... | collective-permute-start | bytes 1572872 | tf_op jit(solution)/shard_map/ppermute | solution.py:24
  93.1 15.4 %collective-permute-start.17 = (bf16[1024,256]{1,0:T(8,128)(2,1)S(1)}, bf16[1024,256]{1,0:T(8,128)(2,1)S(1)}, u32[]{:S(2)}, u32[]{:S(2)}) collective-permute-start(bf16[1024,256]{1,0:T(8,128)(2,1)S(1)} %convert_add_fusion.1), channel_id=1, source_target_pairs={{16,0},{17,1},{18,2},{19,3},{20,4},{21,5},{22,6},{23,7}} | collective-permute-start | bytes 1572872 | tf_op jit(solution)/shard_map/ppermute | solution.py:170
  94.4 2.4 %copy-start.22 = (f32[1,1,256]{2,1,0:T(1,128)S(1)}, f32[1,1,256]{2,1,0:T(1,128)}, u32[]{:S(2)}) copy-start(f32[1,1,256]{2,1,0:T(1,128)} %param.17) | copy-start | bytes 3076
  94.4 2.4 %copy-start.23 = (f32[1,1,256]{2,1,0:T(1,128)S(1)}, f32[1,1,256]{2,1,0:T(1,128)}, u32[]{:S(2)}) copy-start(f32[1,1,256]{2,1,0:T(1,128)} %param.15) | copy-start | bytes 3076
  94.4 2.4 %copy-start.24 = (f32[1,1,256]{2,1,0:T(1,128)S(1)}, f32[1,1,256]{2,1,0:T(1,128)}, u32[]{:S(2)}) copy-start(f32[1,1,256]{2,1,0:T(1,128)} %param.16) | copy-start | bytes 3076
  95.0 13.5 %collective-permute-start.4 = (bf16[1024,256]{1,0:T(8,128)(2,1)S(1)}, bf16[1024,256]{1,0:T(8,128)(2,1)S(1)}, u32[]{:S(2)}, u32[]{:S(2)}) collective-permute-start(bf16[1024,256]{1,0:T(8,128)(2,1)S(1)} %full_product.4), channel_id=1, source_target_pairs={{24,16},{25,17},{26,18},{27,19},{28,20},{29,21},{30,22},{31,23}} | collective-permute-start | bytes 1572872 | tf_op jit(solution)/shard_map/ppermute | solution.py:170
  96.7 20.4 %copy-start.15 = (f32[256,256]{1,0:T(8,128)}, f32[256,256]{1,0:T(8,128)S(1)}, u32[]{:S(2)}) copy-start(f32[256,256]{1,0:T(8,128)S(1)} %slice.78) | copy-start | bytes 786436
  96.8 14.0 %copy-start.17 = (f32[256,256]{1,0:T(8,128)}, f32[256,256]{1,0:T(8,128)S(1)}, u32[]{:S(2)}) copy-start(f32[256,256]{1,0:T(8,128)S(1)} %slice.77) | copy-start | bytes 786436
  96.8 14.0 %copy-start.19 = (f32[256,256]{1,0:T(8,128)}, f32[256,256]{1,0:T(8,128)S(1)}, u32[]{:S(2)}) copy-start(f32[256,256]{1,0:T(8,128)S(1)} %slice.76) | copy-start | bytes 786436
  109.5 20.0 %collective-permute-start.5 = (bf16[1024,256]{1,0:T(8,128)(2,1)}, bf16[1024,256]{1,0:T(8,128)(2,1)}, u32[]{:S(2)}, u32[]{:S(2)}) collective-permute-start(bf16[1024,256]{1,0:T(8,128)(2,1)} %convert_add_fusion.3), channel_id=1, source_target_pairs={{16,0},{17,1},{18,2},{19,3},{20,4},{21,5},{22,6},{23,7}} | collective-permute-start | bytes 1572872 | tf_op jit(solution)/shard_map/ppermute | solution.py:170
  117.1 13.7 %collective-permute-start.21 = (bf16[1024,256]{1,0:T(8,128)(2,1)}, bf16[1024,256]{1,0:T(8,128)(2,1)}, u32[]{:S(2)}, u32[]{:S(2)}) collective-permute-start(bf16[1024,256]{1,0:T(8,128)(2,1)} %get-tuple-element.31.own), channel_id=1, source_target_pairs={{0,1},{1,2},{2,3},{3,4},{4,5},{5,6},{6,7}} | collective-permute-start | bytes 1572872 | tf_op jit(solution)/shard_map/ppermute | solution.py:24
  119.0 12.5 %collective-permute-start.22 = (bf16[1024,256]{1,0:T(8,128)(2,1)}, bf16[1024,256]{1,0:T(8,128)(2,1)}, u32[]{:S(2)}, u32[]{:S(2)}) collective-permute-start(bf16[1024,256]{1,0:T(8,128)(2,1)} %get-tuple-element.31.own), channel_id=1, source_target_pairs={{1,0},{2,1},{3,2},{4,3},{5,4},{6,5},{7,6}} | collective-permute-start | bytes 1572872 | tf_op jit(solution)/shard_map/ppermute | solution.py:24
  122.7 14.9 %collective-permute-start.13 = (bf16[1024,256]{1,0:T(8,128)(2,1)}, bf16[1024,256]{1,0:T(8,128)(2,1)}, u32[]{:S(2)}, u32[]{:S(2)}) collective-permute-start(bf16[1024,256]{1,0:T(8,128)(2,1)} %get-tuple-element.17), channel_id=1, source_target_pairs={{8,0},{9,1},{10,2},{11,3},{12,4},{13,5},{14,6},{15,7}} | collective-permute-start | bytes 1572872 | tf_op jit(solution)/shard_map/ppermute | solution.py:215
  124.0 13.6 %copy-start.3 = (bf16[1024,256]{1,0:T(8,128)(2,1)S(1)}, bf16[1024,256]{1,0:T(8,128)(2,1)}, u32[]{:S(2)}) copy-start(bf16[1024,256]{1,0:T(8,128)(2,1)} %copy-done.2) | copy-start | bytes 1572868
  124.0 13.6 %copy-start.12 = (f32[1,1,256,256]{3,2,1,0:T(8,128)S(1)}, f32[1,1,256,256]{3,2,1,0:T(8,128)}, u32[]{:S(2)}) copy-start(f32[1,1,256,256]{3,2,1,0:T(8,128)} %param.14) | copy-start | bytes 786436
  124.0 13.6 %copy-start.14 = (f32[1024,256]{1,0:T(8,128)S(1)}, f32[1024,256]{1,0:T(8,128)}, u32[]{:S(2)}) copy-start(f32[1024,256]{1,0:T(8,128)} %get-tuple-element.32) | copy-start | bytes 3145732
  124.0 13.6 %copy-start.16 = (f32[256,256]{1,0:T(8,128)S(1)}, f32[256,256]{1,0:T(8,128)}, u32[]{:S(2)}) copy-start(f32[256,256]{1,0:T(8,128)} %copy-done.15) | copy-start | bytes 786436
  124.0 13.6 %copy-start.18 = (f32[256,256]{1,0:T(8,128)S(1)}, f32[256,256]{1,0:T(8,128)}, u32[]{:S(2)}) copy-start(f32[256,256]{1,0:T(8,128)} %copy-done.17) | copy-start | bytes 786436
  124.0 13.6 %copy-start.20 = (f32[256,256]{1,0:T(8,128)S(1)}, f32[256,256]{1,0:T(8,128)}, u32[]{:S(2)}) copy-start(f32[256,256]{1,0:T(8,128)} %copy-done.19) | copy-start | bytes 786436
  124.1 21.3 %collective-permute-start.23 = (bf16[1024,256]{1,0:T(8,128)(2,1)}, bf16[1024,256]{1,0:T(8,128)(2,1)S(1)}, u32[]{:S(2)}, u32[]{:S(2)}) collective-permute-start(bf16[1024,256]{1,0:T(8,128)(2,1)} %get-tuple-element.30), channel_id=1, source_target_pairs={{0,8},{16,24},{1,9},{17,25},{2,10},{18,26},{3,11},{19,27},{4,12},{... | collective-permute-start | bytes 1572872 | tf_op jit(solution)/shard_map/ppermute | solution.py:221
  145.4 11.9 %copy-start.13 = (f32[1024,256]{1,0:T(8,128)}, f32[1024,256]{1,0:T(8,128)S(1)}, u32[]{:S(2)}) copy-start(f32[1024,256]{1,0:T(8,128)S(1)} %get-tuple-element.26) | copy-start | bytes 3145732
  145.5 11.7 %collective-permute-start.24 = (bf16[1024,256]{1,0:T(8,128)(2,1)S(1)}, bf16[1024,256]{1,0:T(8,128)(2,1)S(1)}, u32[]{:S(2)}, u32[]{:S(2)}) collective-permute-start(bf16[1024,256]{1,0:T(8,128)(2,1)S(1)} %select_select_fusion.own), channel_id=1, source_target_pairs={{0,1},{1,2},{2,3},{3,4},{4,5},{5,6},{6,7},{8,9},{9,10},{10,11},{11... | collective-permute-start | bytes 1572872 | tf_op jit(solution)/shard_map/ppermute | solution.py:24
  147.5 12.1 %collective-permute-start.25 = (bf16[1024,256]{1,0:T(8,128)(2,1)S(1)}, bf16[1024,256]{1,0:T(8,128)(2,1)S(1)}, u32[]{:S(2)}, u32[]{:S(2)}) collective-permute-start(bf16[1024,256]{1,0:T(8,128)(2,1)S(1)} %select_select_fusion.own), channel_id=1, source_target_pairs={{1,0},{2,1},{3,2},{4,3},{5,4},{6,5},{7,6},{9,8},{10,9},{11,10},{12... | collective-permute-start | bytes 1572872 | tf_op jit(solution)/shard_map/ppermute | solution.py:24
  151.1 26.7 %copy-start.26 = (f32[256]{0:T(256)S(1)}, f32[256]{0:T(256)}, u32[]{:S(2)}) copy-start(f32[256]{0:T(256)} %copy-done.25) | copy-start | bytes 3076
  152.0 11.7 %collective-permute-start.29 = (f32[256,256]{1,0:T(8,128)S(1)}, f32[256,256]{1,0:T(8,128)S(1)}, u32[]{:S(2)}, u32[]{:S(2)}) collective-permute-start(f32[256,256]{1,0:T(8,128)S(1)} %get-tuple-element.41), channel_id=1, source_target_pairs={{0,24},{1,25},{2,26},{3,27},{4,28},{5,29},{6,30},{7,31}} | collective-permute-start | bytes 786440 | tf_op jit(solution)/shard_map/ppermute | solution.py:230
  153.3 12.4 %collective-permute-start.30 = (f32[256,256]{1,0:T(8,128)}, f32[256,256]{1,0:T(8,128)}, u32[]{:S(2)}, u32[]{:S(2)}) collective-permute-start(f32[256,256]{1,0:T(8,128)} %get-tuple-element.40), channel_id=1, source_target_pairs={{0,16},{1,17},{2,18},{3,19},{4,20},{5,21},{6,22},{7,23}} | collective-permute-start | bytes 786440 | tf_op jit(solution)/shard_map/ppermute | solution.py:230
  155.3 16.0 %collective-permute-start.31 = (f32[256,256]{1,0:T(8,128)}, f32[256,256]{1,0:T(8,128)}, u32[]{:S(2)}, u32[]{:S(2)}) collective-permute-start(f32[256,256]{1,0:T(8,128)} %get-tuple-element.39), channel_id=1, source_target_pairs={{0,8},{1,9},{2,10},{3,11},{4,12},{5,13},{6,14},{7,15}} | collective-permute-start | bytes 786440 | tf_op jit(solution)/shard_map/ppermute | solution.py:230
  162.0 0.7 copy-start.10
  162.7 11.5 %collective-permute-start.28 = (bf16[256,256]{1,0:T(8,128)(2,1)}, bf16[256,256]{1,0:T(8,128)(2,1)S(1)}, u32[]{:S(2)}, u32[]{:S(2)}) collective-permute-start(bf16[256,256]{1,0:T(8,128)(2,1)} %get-tuple-element.23), channel_id=1, source_target_pairs={{0,24},{8,0},{16,8},{24,16},{1,25},{9,1},{17,9},{25,17},{2,26},{10... | collective-permute-start | bytes 393224 | tf_op jit(solution)/shard_map/ppermute | solution.py:96
  162.7 13.8 %collective-permute-start.27 = (bf16[256,256]{1,0:T(8,128)(2,1)}, bf16[256,256]{1,0:T(8,128)(2,1)S(1)}, u32[]{:S(2)}, u32[]{:S(2)}) collective-permute-start(bf16[256,256]{1,0:T(8,128)(2,1)} %get-tuple-element.22), channel_id=1, source_target_pairs={{0,16},{8,24},{16,0},{24,8},{1,17},{9,25},{17,1},{25,9},{2,18},{10... | collective-permute-start | bytes 393224 | tf_op jit(solution)/shard_map/ppermute | solution.py:96
  163.7 0.7 copy-start.21
  164.4 13.4 %collective-permute-start.26 = (bf16[256,256]{1,0:T(8,128)(2,1)S(1)}, bf16[256,256]{1,0:T(8,128)(2,1)S(1)}, u32[]{:S(2)}, u32[]{:S(2)}) collective-permute-start(bf16[256,256]{1,0:T(8,128)(2,1)S(1)} %get-tuple-element.21), channel_id=1, source_target_pairs={{0,8},{8,16},{16,24},{24,0},{1,9},{9,17},{17,25},{25,1},{2,10},{10... | collective-permute-start | bytes 393224 | tf_op jit(solution)/shard_map/ppermute | solution.py:96

commit v4 on v1

v4 whole, which is shorter than its diff:
```python
import functools

import jax
import jax.numpy as jnp
from jax import lax
from jax.experimental import pallas as pl
from jax.experimental.pallas import tpu as pltpu
from jax.sharding import PartitionSpec as P


NEWTON = 3

damping = 0.5
time_step = 0.25
creep_square = 0.01

HBM = pl.BlockSpec(memory_space=pltpu.HBM)
VMEM = pl.BlockSpec(memory_space=pltpu.VMEM)
PARAMS = pltpu.CompilerParams(vmem_limit_bytes=32 * 1024 * 1024)


def exchange(value, planes):
    count = lax.axis_size("elem")
    up = [(i * count + j, i * count + j + 1) for i in planes for j in range(count - 1)]
    down = [(j, i) for i, j in up]
    axes = ("lag", "elem")
    return lax.ppermute(value, axes, up), lax.ppermute(value, axes, down)


class Operands:
    def __init__(self, picks, live, tile, below, own, above, starts, rows, tile_buf, sources, tile_sems, sems):
        slots = sems.shape[0]
        block = sources.shape[0] // slots
        per = own.shape[0] // block
        self.sources, self.tile_buf, self.rows = sources, tile_buf, rows
        alive = live[0]
        for k in range(slots):
            spot = sources.at[pl.ds(k * block, block)]
            pick = picks[0, 0, k]
            start = pl.multiple_of(lax.rem(pick, per) * block, block)
            for which, ref in enumerate((below, own, above)):

                @pl.when((k < alive) & (lax.div(pick, per) == which))
                def _():
                    pltpu.make_async_copy(ref.at[pl.ds(start, block)], spot, sems.at[k]).start()

        self.copies = []
        for d, start in enumerate(starts):
            spot = pl.ds(d * rows, rows)
            copy = pltpu.make_async_copy(tile.at[0, pl.ds(start, rows)], tile_buf.at[spot], tile_sems.at[d])
            copy.start()
            self.copies.append(copy)
        for k in range(slots):
            spot = sources.at[pl.ds(k * block, block)]

            @pl.when(k >= alive)
            def _():
                spot[...] = jnp.zeros(spot.shape, spot.dtype)

            @pl.when(k < alive)
            def _():
                pltpu.make_async_copy(own.at[pl.ds(0, block)], spot, sems.at[k]).wait()

    def chunk(self, d):
        self.copies[d].wait()
        spot = pl.ds(d * self.rows, self.rows)
        return jnp.dot(self.tile_buf[spot, :], self.sources[...], preferred_element_type=jnp.float32)


def scratch(tile, own, chunks, slots):
    return [
        pltpu.VMEM(tile.shape[1:], tile.dtype),
        pltpu.VMEM((tile.shape[2], own.shape[1]), own.dtype),
        pltpu.SemaphoreType.DMA((chunks,)),
        pltpu.SemaphoreType.DMA((slots,)),
    ]


def cost(tile, own, parts=0):
    return pl.CostEstimate(
        flops=2 * tile.size * own.shape[1],
        bytes_accessed=2 * (tile.size + 4 * own.size),
        transcendentals=parts * own.size,
    )


def rows_kernel(lags, rows, picks, live, tile, below, own, above, *refs):
    outs, bufs = refs[:lags], refs[lags:]
    me = lax.axis_index("lag")
    starts = [pl.multiple_of(lax.rem(me + d, lags) * rows, rows) for d in range(lags)]
    operands = Operands(picks, live, tile, below, own, above, starts, rows, *bufs)
    for d in range(lags):
        outs[d][...] = operands.chunk(d).astype(outs[d].dtype)


def product_by_rows(picks, live, tile, below, own, above, lags):
    rows = own.shape[0] // lags
    kinds = [jnp.float32] + [jnp.bfloat16] * (lags - 1)
    return pl.pallas_call(
        functools.partial(rows_kernel, lags, rows),
        grid_spec=pltpu.PrefetchScalarGridSpec(
            num_scalar_prefetch=2,
            grid=(1,),
            in_specs=[HBM] * 4,
            out_specs=[VMEM] * lags,
            scratch_shapes=scratch(tile, own, lags, picks.shape[2]),
        ),
        out_shape=[jax.ShapeDtypeStruct((rows, own.shape[1]), kind) for kind in kinds],
        compiler_params=PARAMS,
        cost_estimate=cost(tile, own),
        name="product_by_rows",
    )(picks, live, tile, below, own, above)


def later_kernel(chunks, picks, live, tile, below, own, above, stress, out, *bufs):
    me = lax.axis_index("lag")
    rows = out.shape[0] // chunks

    @pl.when(me > 0)
    def _():
        operands = Operands(
            picks, live, tile, below, own, above, [d * rows for d in range(chunks)], rows, *bufs
        )
        for d in range(chunks):
            out[pl.ds(d * rows, rows), :] = operands.chunk(d).astype(out.dtype)
        height = stress.shape[2]
        mine = pl.ds(pl.multiple_of(me * height, height), height)
        part = jnp.dot(bufs[0][mine, :], bufs[1][...], preferred_element_type=jnp.float32)
        out[mine, :] = (part + stress[0, 0]).astype(out.dtype)


def later_product(picks, live, tile, below, own, above, stress):
    chunks = max(1, tile.shape[1] // 256)
    return pl.pallas_call(
        functools.partial(later_kernel, chunks),
        grid_spec=pltpu.PrefetchScalarGridSpec(
            num_scalar_prefetch=2,
            grid=(1,),
            in_specs=[HBM] * 4 + [VMEM],
            out_specs=VMEM,
            scratch_shapes=scratch(tile, own, chunks, picks.shape[2]),
        ),
        out_shape=jax.ShapeDtypeStruct(own.shape, jnp.bfloat16),
        compiler_params=PARAMS,
        cost_estimate=cost(tile, own),
        name="later_product",
    )(picks, live, tile, below, own, above, stress)


def pack_kernel(state, coef_a, coef_b, sigma, out):
    rows = state.shape[2]
    out[pl.ds(0, rows), :] = state[0, 0]
    out[pl.ds(rows, 8), :] = jnp.zeros((8, out.shape[1]), out.dtype)
    out[pl.ds(rows, 1), pl.ds(0, rows)] = coef_b[0] / coef_a[0]
    out[pl.ds(rows + 1, 1), pl.ds(0, rows)] = sigma[0] * coef_a[0]


def pack(state, coef_a, coef_b, sigma):
    return pl.pallas_call(
        pack_kernel,
        in_specs=[VMEM] * 4,
        out_specs=VMEM,
        out_shape=jax.ShapeDtypeStruct((state.shape[2] + 8, state.shape[3]), jnp.float32),
        compiler_params=PARAMS,
        name="pack",
    )(state, coef_a, coef_b, sigma)


def newton(load, state, ratio, strength):
    scale = 0.5 * jnp.exp(ratio * state)
    product = strength * scale
    velocity = load / (product + damping)
    for _ in range(NEWTON):
        scaled = scale * velocity
        magnitude = jnp.abs(scaled)
        root = jnp.sqrt(magnitude * magnitude + 1.0)
        positive = jnp.log(magnitude + root)
        arc = jnp.where(scaled < 0.0, -positive, positive)
        residual = strength * arc + damping * velocity - load
        velocity = velocity - residual / (product / root + damping)
    return velocity


def evolved(state, speed_of):
    return state + time_step * (jnp.exp(-state) - jnp.sqrt(speed_of * speed_of + creep_square))


def step_kernel(lags, count, fresh, picks, live, tile, below, own, above, stress, *refs):
    received, refs = refs[:count], refs[count:]
    packed, refs = refs[:lags], refs[lags:]
    before, refs = refs[0], refs[1:]
    rates, after, loads, columns = refs[:4]
    bufs = refs[4:]
    rows = rates.shape[0] // lags
    group = min(32, rows)

    @pl.when(lax.axis_index("lag") == 0)
    def _():
        operands = Operands(picks, live, tile, below, own, above, [d * rows for d in range(lags)], rows, *bufs)
        for d in range(lags):
            params = packed[d][pl.ds(rows, 8), :] if fresh else packed[d][...]
            columns[...] = jnp.transpose(params)
            loads[...] = operands.chunk(d)
            if d == 0:
                loads[...] += stress[0, 0]

            @pl.loop(0, rows // group)
            def _(i):
                part = pl.ds(pl.multiple_of(i * group, group), group)
                whole = pl.ds(pl.multiple_of(d * rows + i * group, group), group)
                load = loads[part, :]
                for ref in received:
                    load = load + ref[whole, :].astype(jnp.float32)
                if fresh:
                    state = evolved(packed[d][part, :], before[whole, :].astype(jnp.float32))
                else:
                    state = before[whole, :]
                both = columns[part, :]
                velocity = newton(load, state, both[:, 0:1], both[:, 1:2])
                rates[whole, :] = velocity.astype(rates.dtype)
                after[whole, :] = evolved(state, velocity)


def plane_step(picks, live, tile, below, own, above, stress, received, packed, before):
    lags, fresh = len(packed), before is None
    rows, cols = own.shape[0] // lags, own.shape[1]
    kernel = functools.partial(step_kernel, lags, len(received), fresh)
    param = VMEM if fresh else pl.BlockSpec((8, cols), lambda i, *_: (rows // 8, 0))
    more = [own] if fresh else [before]
    return pl.pallas_call(
        kernel,
        grid_spec=pltpu.PrefetchScalarGridSpec(
            num_scalar_prefetch=2,
            grid=(1,),
            in_specs=[HBM] * 4 + [VMEM] * (1 + len(received)) + [param] * lags + [VMEM],
            out_specs=[VMEM] * 2,
            scratch_shapes=[pltpu.VMEM((rows, cols), jnp.float32), pltpu.VMEM((cols, 8), jnp.float32)]
            + scratch(tile, own, lags, picks.shape[2]),
        ),
        out_shape=[jax.ShapeDtypeStruct(own.shape, jnp.bfloat16), jax.ShapeDtypeStruct(own.shape, jnp.float32)],
        compiler_params=PARAMS,
        cost_estimate=cost(tile, own, 10),
        name="plane_step",
    )(picks, live, tile, below, own, above, stress, *received, *packed, *more)


def scatter_sum(parts):
    lags = len(parts)
    total = parts[0]
    for d in range(1, lags):
        route = [(i, (i + d) % lags) for i in range(lags)]
        total = total + lax.ppermute(parts[d], "lag", route).astype(jnp.float32)
    return total


def tree_to_first(value, lags):
    received, stride = [], 1
    while stride < lags:
        route = [(i + stride, i) for i in range(0, lags - stride, 2 * stride)]
        received.append(lax.ppermute(value, "lag", route))
        stride *= 2
        if stride < lags:
            total = value.astype(jnp.float32) + received[-1].astype(jnp.float32)
            value = lax.optimization_barrier(total.astype(jnp.bfloat16))
    return received


def settle_friction(shear_load, state, coef_a, coef_b, sigma):
    velocity = newton(shear_load, state, coef_b / coef_a, sigma * coef_a)
    return velocity.astype(jnp.bfloat16), evolved(state, velocity)


def shards(kernel_tiles, shell_index, cone_blocks, history, prestress, log_state, fric_a, fric_b, normal_stress):
    lags = lax.axis_size("lag")
    me = lax.axis_index("lag")
    every = range(lags)
    local = (shell_index, cone_blocks, kernel_tiles)
    field = history[0]
    rows = prestress.shape[2]
    columns = [c[0, 0][:, None] for c in (fric_a, fric_b, normal_stress)]

    below, above = exchange(field, every)
    shifted = lax.ppermute(field, "lag", [(i, i + 1) for i in range(lags - 1)])
    packed = pack(log_state, fric_a, fric_b, normal_stress)
    packed = [packed] + [lax.ppermute(packed, "lag", [(d, 0)]) for d in range(1, lags)]
    traction = scatter_sum(product_by_rows(*local, below, field, above, lags))
    rates, _ = settle_friction(prestress[0, 0] + traction, log_state[0, 0], *columns)

    below, above = exchange(shifted, [i for i in every if i >= 1])
    base_1 = tree_to_first(later_product(*local, below, shifted, above, prestress), lags)
    twice = lax.ppermute(shifted, "lag", [(i, i + 1) for i in range(1, lags - 1)])

    first = lax.all_gather(rates, "lag", axis=0, tiled=True)
    source = jnp.where(me <= 1, first, twice)
    below, above = exchange(source, every)
    base_2 = tree_to_first(later_product(*local, below, source, above, prestress), lags)
    second, state = plane_step(*local, below, source, above, prestress, base_1, packed, None)
    below, above = exchange(second, [0])
    moved = jnp.where(me == 0, second, twice)
    moved = lax.ppermute(moved, "lag", [(0, 1)] + [(i, i + 1) for i in range(2, lags - 1)])
    third, state = plane_step(*local, below, second, above, prestress, base_2, packed, state)

    last = jnp.where(me == 0, third, jnp.where(me == 2, first, moved))
    below, above = exchange(last, every)
    mine = state[:rows]
    for d in range(1, lags):
        piece = lax.ppermute(state[d * rows : (d + 1) * rows], "lag", [(0, d)])
        mine = jnp.where(me == d, piece, mine)
    traction = scatter_sum(product_by_rows(*local, below, last, above, lags))
    rates, state = settle_friction(prestress[0, 0] + traction, mine, *columns)
    return rates[None, None], state[None, None]


def solution(mesh):
    in_specs = (
        P("lag", "elem", None),
        P("lag", "elem", None),
        P("lag"),
        P("lag", "elem", None),
        P("elem", "lag", None, None),
        P("elem", "lag", None, None),
        P("elem", "lag", None),
        P("elem", "lag", None),
        P("elem", "lag", None),
    )
    out_specs = (P("elem", "lag", None, None), P("elem", "lag", None, None))
    return jax.shard_map(shards, mesh=mesh, in_specs=in_specs, out_specs=out_specs, check_vma=False)
```

time: 186 us -> 221 us (1.19)
  the two profiles are of different devices: /device:TPU:2 before, /device:TPU:28 now
where the time goes in v4:
time: 221 us; the launch traced here: 220 us
  waiting for transfers between devices  86.5 us (39%)
  starting transfers between devices  67.8 us (31%)
  blocking collectives  22.6 us (10%)
  Pallas kernels  18.7 us (8%)
  local copies, waits for them, and re-layouts  13.1 us (6%)
  other arithmetic  9.86 us (4%)
    ppermute x1, waiting for transfers between devices, shards(): lax.ppermute(moved, 'lag', [(0, 1)] + [(i, i + 1) for i in range(2, lags...  41.7 us
    ppermute x10, starting transfers between devices, exchange(): return (lax.ppermute(value, axes, up), lax.ppermute(value, axes, down))  28 us
    all_gather x1, blocking collectives, shards(): first = lax.all_gather(rates, 'lag', axis=0, tiled=True)  22.6 us
    ppermute x10, waiting for transfers between devices, exchange(): return (lax.ppermute(value, axes, up), lax.ppermute(value, axes, down))  21.9 us
    ppermute x6, starting transfers between devices, scatter_sum(): total = total + lax.ppermute(parts[d], 'lag', route).astype(jnp.float32)  17 us
    ppermute x6, waiting for transfers between devices, scatter_sum(): total = total + lax.ppermute(parts[d], 'lag', route).astype(jnp.float32)  16.1 us
    unnamed x54, local copies, waits for them, and re-layouts  12.3 us
    ppermute x4, starting transfers between devices, tree_to_first(): received.append(lax.ppermute(value, 'lag', route))  10.3 us
  transfers between devices with their start and end apart: 29, of which 12 were waited for; matrix products, arithmetic and copies ran while one was open for 3% of the time, Pallas kernels for 8%

profile of v4, /device:TPU:28, one launch (start us, length us, event | category | flops | bytes accessed | tf_op | source)
XLA Modules:
  0.0 220.3 jit_solution(8455889455377388685)
XLA Ops:
  0.6 1.9 collective-permute-start
  2.6 4.5 %collective-permute-start.1 = (bf16[1024,256]{1,0:T(8,128)(2,1)}, bf16[1024,256]{1,0:T(8,128)(2,1)S(1)}, u32[]{:S(2)}, u32[]{:S(2)}) collective-permute-start(bf16[1024,256]{1,0:T(8,128)(2,1)} %bitcast.27), channel_id=1, source_target_pairs={{1,0},{2,1},{3,2},{4,3},{5,4},{6,5},{7,6},{9,8},{10,9},{11,10},{12... | collective-permute-start | bytes 1572872 | tf_op jit(solution)/shard_map/ppermute | solution.py:27
  7.1 1.3 collective-permute-start.5
  9.1 0.7 fusion.34
  9.8 5.3 %collective-permute-done.below = bf16[1024,256]{1,0:T(8,128)(2,1)S(1)} collective-permute-done((bf16[1024,256]{1,0:T(8,128)(2,1)}, bf16[1024,256]{1,0:T(8,128)(2,1)S(1)}, u32[]{:S(2)}, u32[]{:S(2)}) %collective-permute-start) | collective-permute-done | bytes 524320 | tf_op jit(solution)/shard_map/ppermute | solution.py:27
  15.1 1.0 collective-permute-done.1.above
  16.1 1.9 copy-done
  18.0 1.0 copy-done.15
  19.7 3.2 %product_by_rows.2 = (f32[256,256]{1,0:T(8,128)S(1)}, bf16[256,256]{1,0:T(8,128)(2,1)S(1)}, bf16[256,256]{1,0:T(8,128)(2,1)S(1)}, bf16[256,256]{1,0:T(8,128)(2,1)S(1)}) custom-call(s32[1,1,3]{2,1,0:T(1,128)S(1)} %copy-done.17, s32[1]{0:T(128)S(6)} %copy.11.live, bf16[1,1024,1536]{2,1,0:T(8,128)(2,1)S(1)} %copy-done, ...), custom_call_target="tpu_custom_call" | custom-call | flops 805306368 | bytes 5242880 | tf_op jit(solution)/shard_map/product_by_rows/pallas_call | solution.py:99
  23.1 1.7 collective-permute-start.3
  25.3 3.8 %collective-permute-start.10 = (bf16[1024,256]{1,0:T(8,128)(2,1)S(1)}, bf16[1024,256]{1,0:T(8,128)(2,1)S(1)}, u32[]{:S(2)}, u32[]{:S(2)}) collective-permute-start(bf16[1024,256]{1,0:T(8,128)(2,1)S(1)} %collective-permute-done.5.own), channel_id=1, source_target_pairs={{9,8},{10,9},{11,10},{12,11},{13,12},{14,13},{15,14},{17,16},{18,1... | collective-permute-start | bytes 1572872 | tf_op jit(solution)/shard_map/ppermute | solution.py:27
  29.0 1.9 collective-permute-start.9
  31.0 1.3 collective-permute-start.6
  32.3 4.2 %collective-permute-done.3 = bf16[256,256]{1,0:T(8,128)(2,1)S(1)} collective-permute-done((bf16[256,256]{1,0:T(8,128)(2,1)S(1)}, bf16[256,256]{1,0:T(8,128)(2,1)S(1)}, u32[]{:S(2)}, u32[]{:S(2)}) %collective-permute-start.3) | collective-permute-done | bytes 131104 | tf_op jit(solution)/shard_map/ppermute | solution.py:252
  36.5 1.0 fusion.31
  37.5 3.7 %collective-permute-done.10.above = bf16[1024,256]{1,0:T(8,128)(2,1)S(1)} collective-permute-done((bf16[1024,256]{1,0:T(8,128)(2,1)S(1)}, bf16[1024,256]{1,0:T(8,128)(2,1)S(1)}, u32[]{:S(2)}, u32[]{:S(2)}) %collective-permute-start.10) | collective-permute-done | bytes 524320 | tf_op jit(solution)/shard_map/ppermute | solution.py:27
  41.2 1.4 collective-permute-done.9.below
  42.6 3.0 %later_product.2 = bf16[1024,256]{1,0:T(8,128)(2,1)S(1)} custom-call(s32[1,1,3]{2,1,0:T(1,128)S(1)} %copy-done.17, s32[1]{0:T(128)S(6)} %copy.11.live, bf16[1,1024,1536]{2,1,0:T(8,128)(2,1)S(1)} %copy-done, bf16[1024,256]{1,0:T(8,128)(2,1)S(1)} %collective-permute-done.9.below, bf16[1024,256]{1,0:T(8,128)(2,1)S(1)} %collective-permute-done.5.own, ...), custom_call_target="tpu_custom_call" | custom-call | flops 805306368 | bytes 5242880 | tf_op jit(solution)/shard_map/later_product/pallas_call | solution.py:134
  45.6 3.4 %collective-permute-start.11 = (bf16[1024,256]{1,0:T(8,128)(2,1)S(1)}, bf16[1024,256]{1,0:T(8,128)(2,1)S(1)}, u32[]{:S(2)}, u32[]{:S(2)}) collective-permute-start(bf16[1024,256]{1,0:T(8,128)(2,1)S(1)} %later_product.2), channel_id=1, source_target_pairs={{8,0},{24,16},{9,1},{25,17},{10,2},{26,18},{11,3},{27,19},{12,4},{... | collective-permute-start | bytes 1572872 | tf_op jit(solution)/shard_map/ppermute | solution.py:260
  49.1 22.6 %all_gather.3 = bf16[1024,256]{1,0:T(8,128)(2,1)S(1)} all-gather(bf16[256,256]{1,0:T(8,128)(2,1)S(1)} %fusion.31), channel_id=1, replica_groups=mesh['lag'=4,'elem'=8] {'lag'}, dimensions={0}, use_global_device_ids=true | all-gather | bytes 655360 | tf_op jit(solution)/shard_map/all_gather | solution.py:293
  71.7 0.8 copy-done.22
  72.6 1.9 collective-permute-start.7
  74.5 4.5 %collective-permute-start.8 = (bf16[1024,256]{1,0:T(8,128)(2,1)S(1)}, bf16[1024,256]{1,0:T(8,128)(2,1)S(1)}, u32[]{:S(2)}, u32[]{:S(2)}) collective-permute-start(bf16[1024,256]{1,0:T(8,128)(2,1)S(1)} %broadcast_select_fusion.own.refs_6_), channel_id=1, source_target_pairs={{1,0},{2,1},{3,2},{4,3},{5,4},{6,5},{7,6},{9,8},{10,9},{11,10},{12... | collective-permute-start | bytes 1572872 | tf_op jit(solution)/shard_map/ppermute | solution.py:27
  79.1 1.0 add_convert_fusion.1
  80.1 1.6 collective-permute-start.12
  81.7 6.5 %collective-permute-done.7.below = bf16[1024,256]{1,0:T(8,128)(2,1)S(1)} collective-permute-done((bf16[1024,256]{1,0:T(8,128)(2,1)S(1)}, bf16[1024,256]{1,0:T(8,128)(2,1)S(1)}, u32[]{:S(2)}, u32[]{:S(2)}) %collective-permute-start.7) | collective-permute-done | bytes 524320 | tf_op jit(solution)/shard_map/ppermute | solution.py:27
  88.2 3.8 %later_product.3 = bf16[1024,256]{1,0:T(8,128)(2,1)} custom-call(s32[1,1,3]{2,1,0:T(1,128)S(1)} %copy-done.17, s32[1]{0:T(128)S(6)} %copy.11.live, bf16[1,1024,1536]{2,1,0:T(8,128)(2,1)S(1)} %copy-done, bf16[1024,256]{1,0:T(8,128)(2,1)S(1)} %collective-permute-done.7.below, bf16[1024,256]{1,0:T(8,128)(2,1)S(1)} %broadcast_select_fusion.own.refs_6_, ...), custom_call_target="tpu_custom_call" | custom-call | flops 805306368 | bytes 5242880 | tf_op jit(solution)/shard_map/later_product/pallas_call | solution.py:134
  92.1 3.8 %collective-permute-start.18 = (bf16[1024,256]{1,0:T(8,128)(2,1)}, bf16[1024,256]{1,0:T(8,128)(2,1)}, u32[]{:S(2)}, u32[]{:S(2)}) collective-permute-start(bf16[1024,256]{1,0:T(8,128)(2,1)} %later_product.3), channel_id=1, source_target_pairs={{8,0},{24,16},{9,1},{25,17},{10,2},{26,18},{11,3},{27,19},{12,4},{... | collective-permute-start | bytes 1572872 | tf_op jit(solution)/shard_map/ppermute | solution.py:260
  95.9 0.7 pack.1.refs_2_
  96.6 1.4 collective-permute-start.13
  98.0 1.4 collective-permute-start.14
  99.4 2.0 collective-permute-start.15
  101.4 6.6 %collective-permute-done.15.refs_5_ = f32[264,256]{1,0:T(8,128)} collective-permute-done((f32[264,256]{1,0:T(8,128)}, f32[264,256]{1,0:T(8,128)}, u32[]{:S(2)}, u32[]{:S(2)}) %collective-permute-start.15) | collective-permute-done | bytes 270368 | tf_op jit(solution)/shard_map/ppermute | solution.py:285
  108.0 1.0 copy-done.4
  109.1 1.0 copy-done.6
  110.1 1.0 copy-done.8
  111.1 1.0 copy-done.10
  112.2 2.8 %plane_step.2 = (bf16[1024,256]{1,0:T(8,128)(2,1)}, f32[1024,256]{1,0:T(8,128)S(1)}) custom-call(s32[1,1,3]{2,1,0:T(1,128)S(1)} %copy-done.18, s32[1]{0:T(128)S(6)} %copy.11.live, bf16[1,1024,1536]{2,1,0:T(8,128)(2,1)S(1)} %copy-done.1, bf16[1024,256]{1,0:T(8,128)(2,1)S(1)} %copy-done.8, bf16[1024,256]{1,0:T(8,128)(2,1)S(1)} %copy-done.4, ...), custom_call_target="tpu_custom_call" | custom-call | flops 805306368 | bytes 5242880 | tf_op jit(solution)/shard_map/plane_step/pallas_call | solution.py:230
  115.0 1.0 copy-done.11
  116.0 1.5 collective-permute-start.16
  117.5 1.5 collective-permute-start.17
  118.9 2.2 add_convert_fusion
  121.1 1.5 collective-permute-start.19
  122.6 0.9 broadcast_select_fusion.1
  123.4 1.3 collective-permute-start.20
  124.8 1.2 copy-done.12
  126.0 1.8 plane_step.3
  127.8 41.7 %collective-permute-done.20 = bf16[1024,256]{1,0:T(8,128)(2,1)} collective-permute-done((bf16[1024,256]{1,0:T(8,128)(2,1)}, bf16[1024,256]{1,0:T(8,128)(2,1)}, u32[]{:S(2)}, u32[]{:S(2)}) %collective-permute-start.20) | collective-permute-done | bytes 524320 | tf_op jit(solution)/shard_map/ppermute | solution.py:300
  169.6 1.1 select_select_fusion.own
  170.7 1.9 collective-permute-start.21
  172.6 4.5 %collective-permute-start.22 = (bf16[1024,256]{1,0:T(8,128)(2,1)S(1)}, bf16[1024,256]{1,0:T(8,128)(2,1)S(1)}, u32[]{:S(2)}, u32[]{:S(2)}) collective-permute-start(bf16[1024,256]{1,0:T(8,128)(2,1)S(1)} %select_select_fusion.own), channel_id=1, source_target_pairs={{1,0},{2,1},{3,2},{4,3},{5,4},{6,5},{7,6},{9,8},{10,9},{11,10},{12... | collective-permute-start | bytes 1572872 | tf_op jit(solution)/shard_map/ppermute | solution.py:27
  177.1 0.9 fusion.33
  178.0 1.3 collective-permute-start.26
  179.3 1.4 collective-permute-start.27
  180.7 1.4 collective-permute-start.28
  182.0 4.0 %collective-permute-done.21.below = bf16[1024,256]{1,0:T(8,128)(2,1)S(1)} collective-permute-done((bf16[1024,256]{1,0:T(8,128)(2,1)S(1)}, bf16[1024,256]{1,0:T(8,128)(2,1)S(1)}, u32[]{:S(2)}, u32[]{:S(2)}) %collective-permute-start.21) | collective-permute-done | bytes 524320 | tf_op jit(solution)/shard_map/ppermute | solution.py:27
  186.1 3.3 %product_by_rows.3 = (f32[256,256]{1,0:T(8,128)S(1)}, bf16[256,256]{1,0:T(8,128)(2,1)}, bf16[256,256]{1,0:T(8,128)(2,1)}, bf16[256,256]{1,0:T(8,128)(2,1)S(1)}) custom-call(s32[1,1,3]{2,1,0:T(1,128)S(1)} %copy-done.18, s32[1]{0:T(128)S(6)} %copy.11.live, bf16[1,1024,1536]{2,1,0:T(8,128)(2,1)S(1)} %copy-done.1, ...), custom_call_target="tpu_custom_call" | custom-call | flops 805306368 | bytes 5242880 | tf_op jit(solution)/shard_map/product_by_rows/pallas_call | solution.py:99
  189.4 0.7 copy-done.16
  190.1 14.0 %collective-permute-start.23 = (bf16[256,256]{1,0:T(8,128)(2,1)}, bf16[256,256]{1,0:T(8,128)(2,1)S(1)}, u32[]{:S(2)}, u32[]{:S(2)}) collective-permute-start(bf16[256,256]{1,0:T(8,128)(2,1)} %get-tuple-element.22), channel_id=1, source_target_pairs={{0,8},{8,16},{16,24},{24,0},{1,9},{9,17},{17,25},{25,1},{2,10},{10... | collective-permute-start | bytes 393224 | tf_op jit(solution)/shard_map/ppermute | solution.py:252
  204.1 0.7 copy-done.26
  205.4 1.6 collective-permute-done.23
  207.0 4.5 %collective-permute-done.24 = bf16[256,256]{1,0:T(8,128)(2,1)S(1)} collective-permute-done((bf16[256,256]{1,0:T(8,128)(2,1)}, bf16[256,256]{1,0:T(8,128)(2,1)S(1)}, u32[]{:S(2)}, u32[]{:S(2)}) %collective-permute-start.24) | collective-permute-done | bytes 131104 | tf_op jit(solution)/shard_map/ppermute | solution.py:252
  211.4 5.8 %collective-permute-done.25 = bf16[256,256]{1,0:T(8,128)(2,1)S(1)} collective-permute-done((bf16[256,256]{1,0:T(8,128)(2,1)S(1)}, bf16[256,256]{1,0:T(8,128)(2,1)S(1)}, u32[]{:S(2)}, u32[]{:S(2)}) %collective-permute-start.25) | collective-permute-done | bytes 131104 | tf_op jit(solution)/shard_map/ppermute | solution.py:252
  217.3 3.0 %add_bitcast_fusion = (f32[1,1,256,256]{3,2,1,0:T(8,128)}, bf16[256,256]{1,0:T(8,128)(2,1)}) fusion(f32[256]{0:T(256)S(1)} %bitcast.33, f32[256]{0:T(256)S(1)} %broadcast_multiply_fusion, f32[256]{0:T(256)S(1)} %bitcast.35, bf16[256,256]{1,0:T(8,128)(2,1)S(1)} %collective-permute-done.25, bf16[256,256]{1,0:T(8,128)(2,1)S(1)} %collective-permute-done.24, ...), kind=kLoop, calls=%fused_computation.45 | loop fusion | flops 4587520 | bytes 2362371 | tf_op jit(solution)/shard_map/broadcast_in_dim | solution.py:311
  (66 shorter events, 2.1 us)
Async XLA Ops:
  0.6 14.5 %collective-permute-start = (bf16[1024,256]{1,0:T(8,128)(2,1)}, bf16[1024,256]{1,0:T(8,128)(2,1)S(1)}, u32[]{:S(2)}, u32[]{:S(2)}) collective-permute-start(bf16[1024,256]{1,0:T(8,128)(2,1)} %bitcast.26), channel_id=1, source_target_pairs={{0,1},{1,2},{2,3},{3,4},{4,5},{5,6},{6,7},{8,9},{9,10},{10,11},{11... | collective-permute-start | bytes 1572872 | tf_op jit(solution)/shard_map/ppermute | solution.py:27
  2.6 13.5 %collective-permute-start.1 = (bf16[1024,256]{1,0:T(8,128)(2,1)}, bf16[1024,256]{1,0:T(8,128)(2,1)S(1)}, u32[]{:S(2)}, u32[]{:S(2)}) collective-permute-start(bf16[1024,256]{1,0:T(8,128)(2,1)} %bitcast.27), channel_id=1, source_target_pairs={{1,0},{2,1},{3,2},{4,3},{5,4},{6,5},{7,6},{9,8},{10,9},{11,10},{12... | collective-permute-start | bytes 1572872 | tf_op jit(solution)/shard_map/ppermute | solution.py:27
  7.1 18.2 %collective-permute-start.5 = (bf16[1024,256]{1,0:T(8,128)(2,1)}, bf16[1024,256]{1,0:T(8,128)(2,1)S(1)}, u32[]{:S(2)}, u32[]{:S(2)}) collective-permute-start(bf16[1024,256]{1,0:T(8,128)(2,1)} %bitcast.28), channel_id=1, source_target_pairs={{0,8},{8,16},{16,24},{1,9},{9,17},{17,25},{2,10},{10,18},{18,26},{... | collective-permute-start | bytes 1572872 | tf_op jit(solution)/shard_map/ppermute | solution.py:283
  16.1 1.9 copy-start
  18.0 1.0 copy-start.15
  19.0 0.7 copy-start.17
  19.7 16.8 %copy-start.2 = (f32[1,1,256,256]{3,2,1,0:T(8,128)S(1)}, f32[1,1,256,256]{3,2,1,0:T(8,128)}, u32[]{:S(2)}) copy-start(f32[1,1,256,256]{3,2,1,0:T(8,128)} %stress.7) | copy-start | bytes 786436
  19.7 16.8 %copy-start.14 = (f32[1,1,256,256]{3,2,1,0:T(8,128)S(1)}, f32[1,1,256,256]{3,2,1,0:T(8,128)}, u32[]{:S(2)}) copy-start(f32[1,1,256,256]{3,2,1,0:T(8,128)} %state.1) | copy-start | bytes 786436
  22.9 8.1 %collective-permute-start.2 = (bf16[256,256]{1,0:T(8,128)(2,1)S(1)}, bf16[256,256]{1,0:T(8,128)(2,1)S(1)}, u32[]{:S(2)}, u32[]{:S(2)}) collective-permute-start(bf16[256,256]{1,0:T(8,128)(2,1)S(1)} %get-tuple-element.15), channel_id=1, source_target_pairs={{0,8},{8,16},{16,24},{24,0},{1,9},{9,17},{17,25},{25,1},{2,10},{10... | collective-permute-start | bytes 393224 | tf_op jit(solution)/shard_map/ppermute | solution.py:252
  23.1 13.4 %collective-permute-start.3 = (bf16[256,256]{1,0:T(8,128)(2,1)S(1)}, bf16[256,256]{1,0:T(8,128)(2,1)S(1)}, u32[]{:S(2)}, u32[]{:S(2)}) collective-permute-start(bf16[256,256]{1,0:T(8,128)(2,1)S(1)} %get-tuple-element.16), channel_id=1, source_target_pairs={{0,16},{8,24},{16,0},{24,8},{1,17},{9,25},{17,1},{25,9},{2,18},{10... | collective-permute-start | bytes 393224 | tf_op jit(solution)/shard_map/ppermute | solution.py:252
  24.8 11.7 %collective-permute-start.4 = (bf16[256,256]{1,0:T(8,128)(2,1)S(1)}, bf16[256,256]{1,0:T(8,128)(2,1)S(1)}, u32[]{:S(2)}, u32[]{:S(2)}) collective-permute-start(bf16[256,256]{1,0:T(8,128)(2,1)S(1)} %get-tuple-element.17), channel_id=1, source_target_pairs={{0,24},{8,0},{16,8},{24,16},{1,25},{9,1},{17,9},{25,17},{2,26},{10... | collective-permute-start | bytes 393224 | tf_op jit(solution)/shard_map/ppermute | solution.py:252
  25.3 15.9 %collective-permute-start.10 = (bf16[1024,256]{1,0:T(8,128)(2,1)S(1)}, bf16[1024,256]{1,0:T(8,128)(2,1)S(1)}, u32[]{:S(2)}, u32[]{:S(2)}) collective-permute-start(bf16[1024,256]{1,0:T(8,128)(2,1)S(1)} %collective-permute-done.5.own), channel_id=1, source_target_pairs={{9,8},{10,9},{11,10},{12,11},{13,12},{14,13},{15,14},{17,16},{18,1... | collective-permute-start | bytes 1572872 | tf_op jit(solution)/shard_map/ppermute | solution.py:27
  29.0 13.6 %collective-permute-start.9 = (bf16[1024,256]{1,0:T(8,128)(2,1)S(1)}, bf16[1024,256]{1,0:T(8,128)(2,1)S(1)}, u32[]{:S(2)}, u32[]{:S(2)}) collective-permute-start(bf16[1024,256]{1,0:T(8,128)(2,1)S(1)} %collective-permute-done.5.own), channel_id=1, source_target_pairs={{8,9},{9,10},{10,11},{11,12},{12,13},{13,14},{14,15},{16,17},{17,1... | collective-permute-start | bytes 1572872 | tf_op jit(solution)/shard_map/ppermute | solution.py:27
  31.0 40.7 %collective-permute-start.6 = (bf16[1024,256]{1,0:T(8,128)(2,1)S(1)}, bf16[1024,256]{1,0:T(8,128)(2,1)S(1)}, u32[]{:S(2)}, u32[]{:S(2)}) collective-permute-start(bf16[1024,256]{1,0:T(8,128)(2,1)S(1)} %collective-permute-done.5.own), channel_id=1, source_target_pairs={{8,16},{16,24},{9,17},{17,25},{10,18},{18,26},{11,19},{19,27},{12,... | collective-permute-start | bytes 1572872 | tf_op jit(solution)/shard_map/ppermute | solution.py:291
  45.6 33.4 %collective-permute-start.11 = (bf16[1024,256]{1,0:T(8,128)(2,1)S(1)}, bf16[1024,256]{1,0:T(8,128)(2,1)S(1)}, u32[]{:S(2)}, u32[]{:S(2)}) collective-permute-start(bf16[1024,256]{1,0:T(8,128)(2,1)S(1)} %later_product.2), channel_id=1, source_target_pairs={{8,0},{24,16},{9,1},{25,17},{10,2},{26,18},{11,3},{27,19},{12,4},{... | collective-permute-start | bytes 1572872 | tf_op jit(solution)/shard_map/ppermute | solution.py:260
  71.7 0.8 copy-start.22
  72.5 19.6 %copy-start.24 = (bf16[1024,256]{1,0:T(8,128)(2,1)}, bf16[1024,256]{1,0:T(8,128)(2,1)S(1)}, u32[]{:S(2)}) copy-start(bf16[1024,256]{1,0:T(8,128)(2,1)S(1)} %collective-permute-done.6) | copy-start | bytes 1572868
  72.6 19.5 %copy-start.3 = (bf16[1024,256]{1,0:T(8,128)(2,1)}, bf16[1024,256]{1,0:T(8,128)(2,1)S(1)}, u32[]{:S(2)}) copy-start(bf16[1024,256]{1,0:T(8,128)(2,1)S(1)} %broadcast_select_fusion.own.refs_6_) | copy-start | bytes 1572868
  72.6 15.6 %collective-permute-start.7 = (bf16[1024,256]{1,0:T(8,128)(2,1)S(1)}, bf16[1024,256]{1,0:T(8,128)(2,1)S(1)}, u32[]{:S(2)}, u32[]{:S(2)}) collective-permute-start(bf16[1024,256]{1,0:T(8,128)(2,1)S(1)} %broadcast_select_fusion.own.refs_6_), channel_id=1, source_target_pairs={{0,1},{1,2},{2,3},{3,4},{4,5},{5,6},{6,7},{8,9},{9,10},{10,11},{11... | collective-permute-start | bytes 1572872 | tf_op jit(solution)/shard_map/ppermute | solution.py:27
  74.5 13.7 %collective-permute-start.8 = (bf16[1024,256]{1,0:T(8,128)(2,1)S(1)}, bf16[1024,256]{1,0:T(8,128)(2,1)S(1)}, u32[]{:S(2)}, u32[]{:S(2)}) collective-permute-start(bf16[1024,256]{1,0:T(8,128)(2,1)S(1)} %broadcast_select_fusion.own.refs_6_), channel_id=1, source_target_pairs={{1,0},{2,1},{3,2},{4,3},{5,4},{6,5},{7,6},{9,8},{10,9},{11,10},{12... | collective-permute-start | bytes 1572872 | tf_op jit(solution)/shard_map/ppermute | solution.py:27
  79.1 9.1 %copy-start.5 = (bf16[1024,256]{1,0:T(8,128)(2,1)}, bf16[1024,256]{1,0:T(8,128)(2,1)S(1)}, u32[]{:S(2)}) copy-start(bf16[1024,256]{1,0:T(8,128)(2,1)S(1)} %collective-permute-done.11.refs_0_) | copy-start | bytes 1572868
  80.0 15.8 %copy-start.19 = (f32[1,1,256]{2,1,0:T(1,128)S(1)}, f32[1,1,256]{2,1,0:T(1,128)}, u32[]{:S(2)}) copy-start(f32[1,1,256]{2,1,0:T(1,128)} %coef_b.1) | copy-start | bytes 3076
  80.0 15.8 %copy-start.20 = (f32[1,1,256]{2,1,0:T(1,128)S(1)}, f32[1,1,256]{2,1,0:T(1,128)}, u32[]{:S(2)}) copy-start(f32[1,1,256]{2,1,0:T(1,128)} %coef_a.1) | copy-start | bytes 3076
  80.0 15.8 %copy-start.21 = (f32[1,1,256]{2,1,0:T(1,128)S(1)}, f32[1,1,256]{2,1,0:T(1,128)}, u32[]{:S(2)}) copy-start(f32[1,1,256]{2,1,0:T(1,128)} %sigma.1) | copy-start | bytes 3076
  80.0 28.0 %copy-start.1 = (bf16[1,1024,1536]{2,1,0:T(8,128)(2,1)S(1)}, bf16[1,1024,1536]{2,1,0:T(8,128)(2,1)}, u32[]{:S(2)}) copy-start(bf16[1,1024,1536]{2,1,0:T(8,128)(2,1)} %tile.11) | copy-start | bytes 9437188
  80.0 28.0 %copy-start.18 = (s32[1,1,3]{2,1,0:T(1,128)S(1)}, s32[1,1,3]{2,1,0:T(1,128)}, u32[]{:S(2)}) copy-start(s32[1,1,3]{2,1,0:T(1,128)} %picks.11) | copy-start | bytes 40
  80.1 27.9 %collective-permute-start.12 = (bf16[1024,256]{1,0:T(8,128)(2,1)}, bf16[1024,256]{1,0:T(8,128)(2,1)}, u32[]{:S(2)}, u32[]{:S(2)}) collective-permute-start(bf16[1024,256]{1,0:T(8,128)(2,1)} %add_convert_fusion.1), channel_id=1, source_target_pairs={{16,0},{17,1},{18,2},{19,3},{20,4},{21,5},{22,6},{23,7}} | collective-permute-start | bytes 1572872 | tf_op jit(solution)/shard_map/ppermute | solution.py:260
  88.2 7.7 %copy-start.7 = (bf16[1024,256]{1,0:T(8,128)(2,1)}, bf16[1024,256]{1,0:T(8,128)(2,1)S(1)}, u32[]{:S(2)}) copy-start(bf16[1024,256]{1,0:T(8,128)(2,1)S(1)} %collective-permute-done.7.below) | copy-start | bytes 1572868
  88.2 8.4 %copy-start.9 = (bf16[1024,256]{1,0:T(8,128)(2,1)}, bf16[1024,256]{1,0:T(8,128)(2,1)S(1)}, u32[]{:S(2)}) copy-start(bf16[1024,256]{1,0:T(8,128)(2,1)S(1)} %collective-permute-done.8.above) | copy-start | bytes 1572868
  92.1 26.9 %collective-permute-start.18 = (bf16[1024,256]{1,0:T(8,128)(2,1)}, bf16[1024,256]{1,0:T(8,128)(2,1)}, u32[]{:S(2)}, u32[]{:S(2)}) collective-permute-start(bf16[1024,256]{1,0:T(8,128)(2,1)} %later_product.3), channel_id=1, source_target_pairs={{8,0},{24,16},{9,1},{25,17},{10,2},{26,18},{11,3},{27,19},{12,4},{... | collective-permute-start | bytes 1572872 | tf_op jit(solution)/shard_map/ppermute | solution.py:260
  96.6 4.7 %collective-permute-start.13 = (f32[264,256]{1,0:T(8,128)}, f32[264,256]{1,0:T(8,128)}, u32[]{:S(2)}, u32[]{:S(2)}) collective-permute-start(f32[264,256]{1,0:T(8,128)} %pack.1.refs_2_), channel_id=1, source_target_pairs={{8,0},{9,1},{10,2},{11,3},{12,4},{13,5},{14,6},{15,7}} | collective-permute-start | bytes 811016 | tf_op jit(solution)/shard_map/ppermute | solution.py:285
  98.0 3.4 %collective-permute-start.14 = (f32[264,256]{1,0:T(8,128)}, f32[264,256]{1,0:T(8,128)}, u32[]{:S(2)}, u32[]{:S(2)}) collective-permute-start(f32[264,256]{1,0:T(8,128)} %pack.1.refs_2_), channel_id=1, source_target_pairs={{16,0},{17,1},{18,2},{19,3},{20,4},{21,5},{22,6},{23,7}} | collective-permute-start | bytes 811016 | tf_op jit(solution)/shard_map/ppermute | solution.py:285
  99.4 8.6 %collective-permute-start.15 = (f32[264,256]{1,0:T(8,128)}, f32[264,256]{1,0:T(8,128)}, u32[]{:S(2)}, u32[]{:S(2)}) collective-permute-start(f32[264,256]{1,0:T(8,128)} %pack.1.refs_2_), channel_id=1, source_target_pairs={{24,0},{25,1},{26,2},{27,3},{28,4},{29,5},{30,6},{31,7}} | collective-permute-start | bytes 811016 | tf_op jit(solution)/shard_map/ppermute | solution.py:285
  108.0 1.0 copy-start.4
  109.0 1.0 copy-start.6
  110.1 1.0 copy-start.8
  111.1 1.0 copy-start.10
  112.2 10.4 %copy-start.25 = (bf16[1024,256]{1,0:T(8,128)(2,1)S(1)}, bf16[1024,256]{1,0:T(8,128)(2,1)}, u32[]{:S(2)}) copy-start(bf16[1024,256]{1,0:T(8,128)(2,1)} %copy-done.24) | copy-start | bytes 1572868
  115.0 1.0 copy-start.11
  116.0 8.7 %collective-permute-start.16 = (bf16[1024,256]{1,0:T(8,128)(2,1)}, bf16[1024,256]{1,0:T(8,128)(2,1)}, u32[]{:S(2)}, u32[]{:S(2)}) collective-permute-start(bf16[1024,256]{1,0:T(8,128)(2,1)} %get-tuple-element.18.own), channel_id=1, source_target_pairs={{0,1},{1,2},{2,3},{3,4},{4,5},{5,6},{6,7}} | collective-permute-start | bytes 1572872 | tf_op jit(solution)/shard_map/ppermute | solution.py:27
  117.5 7.3 %collective-permute-start.17 = (bf16[1024,256]{1,0:T(8,128)(2,1)}, bf16[1024,256]{1,0:T(8,128)(2,1)}, u32[]{:S(2)}, u32[]{:S(2)}) collective-permute-start(bf16[1024,256]{1,0:T(8,128)(2,1)} %get-tuple-element.18.own), channel_id=1, source_target_pairs={{1,0},{2,1},{3,2},{4,3},{5,4},{6,5},{7,6}} | collective-permute-start | bytes 1572872 | tf_op jit(solution)/shard_map/ppermute | solution.py:27
  121.1 3.6 %collective-permute-start.19 = (bf16[1024,256]{1,0:T(8,128)(2,1)}, bf16[1024,256]{1,0:T(8,128)(2,1)}, u32[]{:S(2)}, u32[]{:S(2)}) collective-permute-start(bf16[1024,256]{1,0:T(8,128)(2,1)} %add_convert_fusion), channel_id=1, source_target_pairs={{16,0},{17,1},{18,2},{19,3},{20,4},{21,5},{22,6},{23,7}} | collective-permute-start | bytes 1572872 | tf_op jit(solution)/shard_map/ppermute | solution.py:260
  123.4 46.1 %collective-permute-start.20 = (bf16[1024,256]{1,0:T(8,128)(2,1)}, bf16[1024,256]{1,0:T(8,128)(2,1)}, u32[]{:S(2)}, u32[]{:S(2)}) collective-permute-start(bf16[1024,256]{1,0:T(8,128)(2,1)} %broadcast_select_fusion.1), channel_id=1, source_target_pairs={{0,8},{16,24},{1,9},{17,25},{2,10},{18,26},{3,11},{19,27},{4,12},{... | collective-permute-start | bytes 1572872 | tf_op jit(solution)/shard_map/ppermute | solution.py:300
  124.7 1.2 copy-start.12
  126.0 43.6 %copy-start.23 = (bf16[1024,256]{1,0:T(8,128)(2,1)S(1)}, bf16[1024,256]{1,0:T(8,128)(2,1)}, u32[]{:S(2)}) copy-start(bf16[1024,256]{1,0:T(8,128)(2,1)} %copy-done.22) | copy-start | bytes 1572868
  127.8 58.3 %copy-start.13 = (f32[1024,256]{1,0:T(8,128)}, f32[1024,256]{1,0:T(8,128)S(1)}, u32[]{:S(2)}) copy-start(f32[1024,256]{1,0:T(8,128)S(1)} %get-tuple-element.25) | copy-start | bytes 3145732
  170.7 15.4 %collective-permute-start.21 = (bf16[1024,256]{1,0:T(8,128)(2,1)S(1)}, bf16[1024,256]{1,0:T(8,128)(2,1)S(1)}, u32[]{:S(2)}, u32[]{:S(2)}) collective-permute-start(bf16[1024,256]{1,0:T(8,128)(2,1)S(1)} %select_select_fusion.own), channel_id=1, source_target_pairs={{0,1},{1,2},{2,3},{3,4},{4,5},{5,6},{6,7},{8,9},{9,10},{10,11},{11... | collective-permute-start | bytes 1572872 | tf_op jit(solution)/shard_map/ppermute | solution.py:27
  172.6 13.5 %collective-permute-start.22 = (bf16[1024,256]{1,0:T(8,128)(2,1)S(1)}, bf16[1024,256]{1,0:T(8,128)(2,1)S(1)}, u32[]{:S(2)}, u32[]{:S(2)}) collective-permute-start(bf16[1024,256]{1,0:T(8,128)(2,1)S(1)} %select_select_fusion.own), channel_id=1, source_target_pairs={{1,0},{2,1},{3,2},{4,3},{5,4},{6,5},{7,6},{9,8},{10,9},{11,10},{12... | collective-permute-start | bytes 1572872 | tf_op jit(solution)/shard_map/ppermute | solution.py:27
  178.0 26.1 %collective-permute-start.26 = (f32[256,256]{1,0:T(8,128)S(1)}, f32[256,256]{1,0:T(8,128)S(1)}, u32[]{:S(2)}, u32[]{:S(2)}) collective-permute-start(f32[256,256]{1,0:T(8,128)S(1)} %get-tuple-element.30), channel_id=1, source_target_pairs={{0,24},{1,25},{2,26},{3,27},{4,28},{5,29},{6,30},{7,31}} | collective-permute-start | bytes 786440 | tf_op jit(solution)/shard_map/ppermute | solution.py:307
  179.3 26.1 %collective-permute-start.27 = (f32[256,256]{1,0:T(8,128)}, f32[256,256]{1,0:T(8,128)}, u32[]{:S(2)}, u32[]{:S(2)}) collective-permute-start(f32[256,256]{1,0:T(8,128)} %get-tuple-element.29), channel_id=1, source_target_pairs={{0,16},{1,17},{2,18},{3,19},{4,20},{5,21},{6,22},{7,23}} | collective-permute-start | bytes 786440 | tf_op jit(solution)/shard_map/ppermute | solution.py:307
  180.7 24.7 %collective-permute-start.28 = (f32[256,256]{1,0:T(8,128)}, f32[256,256]{1,0:T(8,128)}, u32[]{:S(2)}, u32[]{:S(2)}) collective-permute-start(f32[256,256]{1,0:T(8,128)} %get-tuple-element.28), channel_id=1, source_target_pairs={{0,8},{1,9},{2,10},{3,11},{4,12},{5,13},{6,14},{7,15}} | collective-permute-start | bytes 786440 | tf_op jit(solution)/shard_map/ppermute | solution.py:307
  189.4 0.7 copy-start.16
  190.1 16.8 %collective-permute-start.23 = (bf16[256,256]{1,0:T(8,128)(2,1)}, bf16[256,256]{1,0:T(8,128)(2,1)S(1)}, u32[]{:S(2)}, u32[]{:S(2)}) collective-permute-start(bf16[256,256]{1,0:T(8,128)(2,1)} %get-tuple-element.22), channel_id=1, source_target_pairs={{0,8},{8,16},{16,24},{24,0},{1,9},{9,17},{17,25},{25,1},{2,10},{10... | collective-permute-start | bytes 393224 | tf_op jit(solution)/shard_map/ppermute | solution.py:252
  204.1 7.3 %collective-permute-start.24 = (bf16[256,256]{1,0:T(8,128)(2,1)}, bf16[256,256]{1,0:T(8,128)(2,1)S(1)}, u32[]{:S(2)}, u32[]{:S(2)}) collective-permute-start(bf16[256,256]{1,0:T(8,128)(2,1)} %get-tuple-element.23), channel_id=1, source_target_pairs={{0,16},{8,24},{16,0},{24,8},{1,17},{9,25},{17,1},{25,9},{2,18},{10... | collective-permute-start | bytes 393224 | tf_op jit(solution)/shard_map/ppermute | solution.py:252
  204.1 0.7 copy-start.26
  204.8 12.5 %collective-permute-start.25 = (bf16[256,256]{1,0:T(8,128)(2,1)S(1)}, bf16[256,256]{1,0:T(8,128)(2,1)S(1)}, u32[]{:S(2)}, u32[]{:S(2)}) collective-permute-start(bf16[256,256]{1,0:T(8,128)(2,1)S(1)} %get-tuple-element.24), channel_id=1, source_target_pairs={{0,24},{8,0},{16,8},{24,16},{1,25},{9,1},{17,9},{25,17},{2,26},{10... | collective-permute-start | bytes 393224 | tf_op jit(solution)/shard_map/ppermute | solution.py:252

commit v5 on v1

v5 whole, which is shorter than its diff:
```python
import functools

import jax
import jax.numpy as jnp
from jax import lax
from jax.experimental import pallas as pl
from jax.experimental.pallas import tpu as pltpu
from jax.sharding import PartitionSpec as P


STEPS = 4
NEWTON = 3

damping = 0.5
time_step = 0.25
creep_square = 0.01

ANY = pl.BlockSpec(memory_space=pl.ANY)
VMEM = pl.BlockSpec(memory_space=pltpu.VMEM)
PARAMS = pltpu.CompilerParams(vmem_limit_bytes=32 * 1024 * 1024)


def exchange(value, planes):
    count = lax.axis_size("elem")
    up = [(i * count + j, i * count + j + 1) for i in planes for j in range(count - 1)]
    down = [(j, i) for i, j in up]
    axes = ("lag", "elem")
    return lax.ppermute(value, axes, up), lax.ppermute(value, axes, down)


def fetch(picks, live, below, own, above, sources, sems):
    slots = sems.shape[0]
    block = sources.shape[0] // slots
    per = own.shape[0] // block
    alive = live[0]
    for k in range(slots):
        spot = sources.at[pl.ds(k * block, block)]
        pick = picks[0, 0, k]
        start = pl.multiple_of(lax.rem(pick, per) * block, block)
        for which, ref in enumerate((below, own, above)):

            @pl.when((k < alive) & (lax.div(pick, per) == which))
            def _():
                pltpu.make_async_copy(ref.at[pl.ds(start, block)], spot, sems.at[k]).start()

    for k in range(slots):
        spot = sources.at[pl.ds(k * block, block)]

        @pl.when(k >= alive)
        def _():
            spot[...] = jnp.zeros(spot.shape, spot.dtype)

        @pl.when(k < alive)
        def _():
            pltpu.make_async_copy(own.at[pl.ds(0, block)], spot, sems.at[k]).wait()


def rows_kernel(lags, rows, picks, live, tile, below, own, above, *refs):
    outs, sources, sems = refs[:lags], refs[lags], refs[lags + 1]
    me = lax.axis_index("lag")
    fetch(picks, live, below, own, above, sources, sems)
    for d in range(lags):
        first = pl.multiple_of(lax.rem(me + d, lags) * rows, rows)
        part = jnp.dot(tile[0, pl.ds(first, rows), :], sources[...], preferred_element_type=jnp.float32)
        outs[d][...] = part.astype(outs[d].dtype)


def product_by_rows(picks, live, tile, below, own, above, lags):
    rows, cols = own.shape[0] // lags, own.shape[1]
    kinds = [jnp.float32] + [jnp.bfloat16] * (lags - 1)
    return pl.pallas_call(
        functools.partial(rows_kernel, lags, rows),
        grid_spec=pltpu.PrefetchScalarGridSpec(
            num_scalar_prefetch=2,
            grid=(1,),
            in_specs=[VMEM] + [ANY] * 3,
            out_specs=[VMEM] * lags,
            scratch_shapes=[pltpu.VMEM((tile.shape[2], cols), own.dtype), pltpu.SemaphoreType.DMA((picks.shape[2],))],
        ),
        out_shape=[jax.ShapeDtypeStruct((rows, cols), kind) for kind in kinds],
        compiler_params=PARAMS,
        cost_estimate=pl.CostEstimate(
            flops=2 * tile.size * cols, bytes_accessed=2 * (tile.size + 4 * own.size), transcendentals=0
        ),
        name="product_by_rows",
    )(picks, live, tile, below, own, above)


def newton(load, state, ratio, strength):
    scale = 0.5 * jnp.exp(ratio * state)
    product = strength * scale
    velocity = load / (product + damping)
    for _ in range(NEWTON):
        scaled = scale * velocity
        magnitude = jnp.abs(scaled)
        root = jnp.sqrt(magnitude * magnitude + 1.0)
        positive = jnp.log(magnitude + root)
        arc = jnp.where(scaled < 0.0, -positive, positive)
        residual = strength * arc + damping * velocity - load
        velocity = velocity - residual / (product / root + damping)
    return velocity


def evolved(state, speed_of):
    return state + time_step * (jnp.exp(-state) - jnp.sqrt(speed_of * speed_of + creep_square))


def scatter_sum(parts):
    lags = len(parts)
    total = parts[0]
    for d in range(1, lags):
        route = [(i, (i + d) % lags) for i in range(lags)]
        total = total + lax.ppermute(parts[d], "lag", route).astype(jnp.float32)
    return total


def settle_friction(shear_load, state, coef_a, coef_b, sigma):
    velocity = newton(shear_load, state, coef_b / coef_a, sigma * coef_a)
    return velocity.astype(jnp.bfloat16), evolved(state, velocity)


def shards(kernel_tiles, shell_index, cone_blocks, history, prestress, log_state, fric_a, fric_b, normal_stress):
    lags = lax.axis_size("lag")
    me = lax.axis_index("lag")
    local = (shell_index, cone_blocks, kernel_tiles)
    field, state = history[0], log_state[0, 0]
    columns = [c[0, 0][:, None] for c in (fric_a, fric_b, normal_stress)]
    for step in range(STEPS):
        below, above = exchange(field, range(lags))
        if step + 1 < STEPS:
            older = lax.ppermute(field, "lag", [(i, i + 1) for i in range(lags - 1)])
        parts = product_by_rows(*local, below, field, above, lags)
        traction = scatter_sum(parts)
        rates, state = settle_friction(prestress[0, 0] + traction, state, *columns)
        if step + 1 < STEPS:
            newest = lax.all_gather(rates, "lag", axis=0, tiled=True)
            field = jnp.where(me == 0, newest, older)
    return rates[None, None], state[None, None]


def solution(mesh):
    in_specs = (
        P("lag", "elem", None),
        P("lag", "elem", None),
        P("lag"),
        P("lag", "elem", None),
        P("elem", "lag", None, None),
        P("elem", "lag", None, None),
        P("elem", "lag", None),
        P("elem", "lag", None),
        P("elem", "lag", None),
    )
    out_specs = (P("elem", "lag", None, None), P("elem", "lag", None, None))
    return jax.shard_map(shards, mesh=mesh, in_specs=in_specs, out_specs=out_specs, check_vma=False)
```

time: 186 us -> 187 us (level)
  transfers between devices with their start and end apart: 23 -> 23, of which waited for: 14 -> 16; matrix products, arithmetic and copies ran while one was open for 2% -> 2% of each run, Pallas kernels for 1% -> 1%
where the time goes in v5:
time: 187 us; the launch traced here: 186 us
  blocking collectives  62.2 us (33%)
  waiting for transfers between devices  60.3 us (32%)
  starting transfers between devices  45.6 us (24%)
  Pallas kernels  6.7 us (4%)
  other arithmetic  6.18 us (3%)
  local copies, waits for them, and re-layouts  3.59 us (2%)
    all_gather x3, blocking collectives, shards(): newest = lax.all_gather(rates, 'lag', axis=0, tiled=True)  62.2 us
    ppermute x12, waiting for transfers between devices, scatter_sum(): total = total + lax.ppermute(parts[d], 'lag', route).astype(jnp.float32)  34.3 us
    ppermute x8, waiting for transfers between devices, exchange(): return (lax.ppermute(value, axes, up), lax.ppermute(value, axes, down))  26 us
    ppermute x8, starting transfers between devices, exchange(): return (lax.ppermute(value, axes, up), lax.ppermute(value, axes, down))  22.3 us
    ppermute x12, starting transfers between devices, scatter_sum(): total = total + lax.ppermute(parts[d], 'lag', route).astype(jnp.float32)  13.2 us
    ppermute x3, starting transfers between devices, shards(): older = lax.ppermute(field, 'lag', [(i, i + 1) for i in range(lags - 1)])  10.2 us
    pallas_call x4, Pallas kernels, product_by_rows(): pl.pallas_call(functools.partial(rows_kernel, lags, rows), grid_spec=pltp...  6.7 us
  transfers between devices with their start and end apart: 23, of which 16 were waited for; matrix products, arithmetic and copies ran while one was open for 2% of the time, Pallas kernels for 1%

profile of v5, /device:TPU:2, one launch (start us, length us, event | category | flops | bytes accessed | tf_op | source)
XLA Modules:
  0.0 186.1 jit_solution(15978885827462279747)
XLA Ops:
  0.6 1.9 %collective-permute-start = (bf16[1024,256]{1,0:T(8,128)(2,1)}, bf16[1024,256]{1,0:T(8,128)(2,1)S(1)}, u32[]{:S(2)}, u32[]{:S(2)}) collective-permute-start(bf16[1024,256]{1,0:T(8,128)(2,1)} %bitcast.43), channel_id=1, source_target_pairs={{0,1},{1,2},{2,3},{3,4},{4,5},{5,6},{6,7},{8,9},{9,10},{10,11},{11... | collective-permute-start | bytes 1572872 | tf_op jit(solution)/shard_map/ppermute | solution.py:28
  2.6 3.6 %collective-permute-start.1 = (bf16[1024,256]{1,0:T(8,128)(2,1)}, bf16[1024,256]{1,0:T(8,128)(2,1)S(1)}, u32[]{:S(2)}, u32[]{:S(2)}) collective-permute-start(bf16[1024,256]{1,0:T(8,128)(2,1)} %bitcast.44), channel_id=1, source_target_pairs={{1,0},{2,1},{3,2},{4,3},{5,4},{6,5},{7,6},{9,8},{10,9},{11,10},{12... | collective-permute-start | bytes 1572872 | tf_op jit(solution)/shard_map/ppermute | solution.py:28
  6.2 3.5 %collective-permute-start.5 = (bf16[1024,256]{1,0:T(8,128)(2,1)}, bf16[1024,256]{1,0:T(8,128)(2,1)S(1)}, u32[]{:S(2)}, u32[]{:S(2)}) collective-permute-start(bf16[1024,256]{1,0:T(8,128)(2,1)} %bitcast.45), channel_id=1, source_target_pairs={{0,8},{8,16},{16,24},{1,9},{9,17},{17,25},{2,10},{10,18},{18,26},{... | collective-permute-start | bytes 1572872 | tf_op jit(solution)/shard_map/ppermute | solution.py:131
  10.4 0.7 fusion.71
  11.1 0.2 collective-permute-done.below
  11.3 4.7 %collective-permute-done.1.above = bf16[1024,256]{1,0:T(8,128)(2,1)S(1)} collective-permute-done((bf16[1024,256]{1,0:T(8,128)(2,1)}, bf16[1024,256]{1,0:T(8,128)(2,1)S(1)}, u32[]{:S(2)}, u32[]{:S(2)}) %collective-permute-start.1) | collective-permute-done | bytes 524320 | tf_op jit(solution)/shard_map/ppermute | solution.py:28
  16.1 1.9 %copy-done = bf16[1,1024,1536]{2,1,0:T(8,128)(2,1)S(1)} copy-done((bf16[1,1024,1536]{2,1,0:T(8,128)(2,1)S(1)}, bf16[1,1024,1536]{2,1,0:T(8,128)(2,1)}, u32[]{:S(2)}) %copy-start) | copy-done | bytes 3145752
  18.0 1.0 copy-done.1
  19.0 0.7 copy-done.2
  19.7 1.7 product_by_rows.4
  21.4 3.7 %collective-permute-start.4 = (bf16[256,256]{1,0:T(8,128)(2,1)S(1)}, bf16[256,256]{1,0:T(8,128)(2,1)S(1)}, u32[]{:S(2)}, u32[]{:S(2)}) collective-permute-start(bf16[256,256]{1,0:T(8,128)(2,1)S(1)} %get-tuple-element.21), channel_id=1, source_target_pairs={{0,24},{8,0},{16,8},{24,16},{1,25},{9,1},{17,9},{25,17},{2,26},{10... | collective-permute-start | bytes 393224 | tf_op jit(solution)/shard_map/ppermute | solution.py:113
  25.0 0.0 collective-permute-start.3
  25.0 1.0 collective-permute-start.2
  26.0 2.2 %collective-permute-done.4 = bf16[256,256]{1,0:T(8,128)(2,1)S(1)} collective-permute-done((bf16[256,256]{1,0:T(8,128)(2,1)S(1)}, bf16[256,256]{1,0:T(8,128)(2,1)S(1)}, u32[]{:S(2)}, u32[]{:S(2)}) %collective-permute-start.4) | collective-permute-done | bytes 131104 | tf_op jit(solution)/shard_map/ppermute | solution.py:113
  28.3 9.3 %collective-permute-done.3 = bf16[256,256]{1,0:T(8,128)(2,1)S(1)} collective-permute-done((bf16[256,256]{1,0:T(8,128)(2,1)S(1)}, bf16[256,256]{1,0:T(8,128)(2,1)S(1)}, u32[]{:S(2)}, u32[]{:S(2)}) %collective-permute-start.3) | collective-permute-done | bytes 131104 | tf_op jit(solution)/shard_map/ppermute | solution.py:113
  37.5 0.0 collective-permute-done.2
  37.5 1.0 fusion.69
  38.5 16.2 %all_gather.9 = bf16[1024,256]{1,0:T(8,128)(2,1)S(1)} all-gather(bf16[256,256]{1,0:T(8,128)(2,1)S(1)} %get-tuple-element.41), channel_id=1, replica_groups=mesh['lag'=4,'elem'=8] {'lag'}, dimensions={0}, use_global_device_ids=true | all-gather | bytes 655360 | tf_op jit(solution)/shard_map/all_gather | solution.py:136
  54.7 0.0 collective-permute-done.5
  54.7 0.1 broadcast_select_fusion.2.own
  54.8 1.9 %collective-permute-start.6 = (bf16[1024,256]{1,0:T(8,128)(2,1)S(1)}, bf16[1024,256]{1,0:T(8,128)(2,1)S(1)}, u32[]{:S(2)}, u32[]{:S(2)}) collective-permute-start(bf16[1024,256]{1,0:T(8,128)(2,1)S(1)} %broadcast_select_fusion.2.own), channel_id=1, source_target_pairs={{0,1},{1,2},{2,3},{3,4},{4,5},{5,6},{6,7},{8,9},{9,10},{10,11},{11... | collective-permute-start | bytes 1572872 | tf_op jit(solution)/shard_map/ppermute | solution.py:28
  56.7 3.6 %collective-permute-start.7 = (bf16[1024,256]{1,0:T(8,128)(2,1)S(1)}, bf16[1024,256]{1,0:T(8,128)(2,1)S(1)}, u32[]{:S(2)}, u32[]{:S(2)}) collective-permute-start(bf16[1024,256]{1,0:T(8,128)(2,1)S(1)} %broadcast_select_fusion.2.own), channel_id=1, source_target_pairs={{1,0},{2,1},{3,2},{4,3},{5,4},{6,5},{7,6},{9,8},{10,9},{11,10},{12... | collective-permute-start | bytes 1572872 | tf_op jit(solution)/shard_map/ppermute | solution.py:28
  60.4 4.9 %collective-permute-done.6.below = bf16[1024,256]{1,0:T(8,128)(2,1)S(1)} collective-permute-done((bf16[1024,256]{1,0:T(8,128)(2,1)S(1)}, bf16[1024,256]{1,0:T(8,128)(2,1)S(1)}, u32[]{:S(2)}, u32[]{:S(2)}) %collective-permute-start.6) | collective-permute-done | bytes 524320 | tf_op jit(solution)/shard_map/ppermute | solution.py:28
  65.3 2.7 %collective-permute-done.7.above = bf16[1024,256]{1,0:T(8,128)(2,1)S(1)} collective-permute-done((bf16[1024,256]{1,0:T(8,128)(2,1)S(1)}, bf16[1024,256]{1,0:T(8,128)(2,1)S(1)}, u32[]{:S(2)}, u32[]{:S(2)}) %collective-permute-start.7) | collective-permute-done | bytes 524320 | tf_op jit(solution)/shard_map/ppermute | solution.py:28
  67.9 1.7 product_by_rows.5
  69.6 0.8 collective-permute-start.10
  70.4 0.1 collective-permute-start.9
  70.5 1.9 %collective-permute-start.8 = (bf16[256,256]{1,0:T(8,128)(2,1)S(1)}, bf16[256,256]{1,0:T(8,128)(2,1)S(1)}, u32[]{:S(2)}, u32[]{:S(2)}) collective-permute-start(bf16[256,256]{1,0:T(8,128)(2,1)S(1)} %get-tuple-element.23), channel_id=1, source_target_pairs={{0,8},{8,16},{16,24},{24,0},{1,9},{9,17},{17,25},{25,1},{2,10},{10... | collective-permute-start | bytes 393224 | tf_op jit(solution)/shard_map/ppermute | solution.py:113
  72.4 3.4 %collective-permute-start.11 = (bf16[1024,256]{1,0:T(8,128)(2,1)S(1)}, bf16[1024,256]{1,0:T(8,128)(2,1)S(1)}, u32[]{:S(2)}, u32[]{:S(2)}) collective-permute-start(bf16[1024,256]{1,0:T(8,128)(2,1)S(1)} %broadcast_select_fusion.2.own), channel_id=1, source_target_pairs={{0,8},{8,16},{16,24},{1,9},{9,17},{17,25},{2,10},{10,18},{18,26},{... | collective-permute-start | bytes 1572872 | tf_op jit(solution)/shard_map/ppermute | solution.py:131
  75.8 0.2 collective-permute-done.10
  76.0 6.2 %collective-permute-done.9 = bf16[256,256]{1,0:T(8,128)(2,1)S(1)} collective-permute-done((bf16[256,256]{1,0:T(8,128)(2,1)S(1)}, bf16[256,256]{1,0:T(8,128)(2,1)S(1)}, u32[]{:S(2)}, u32[]{:S(2)}) %collective-permute-start.9) | collective-permute-done | bytes 131104 | tf_op jit(solution)/shard_map/ppermute | solution.py:113
  82.3 0.0 collective-permute-done.8
  82.3 1.1 fusion.67
  83.4 23.1 %all_gather.10 = bf16[1024,256]{1,0:T(8,128)(2,1)S(1)} all-gather(bf16[256,256]{1,0:T(8,128)(2,1)S(1)} %get-tuple-element.38), channel_id=1, replica_groups=mesh['lag'=4,'elem'=8] {'lag'}, dimensions={0}, use_global_device_ids=true | all-gather | bytes 655360 | tf_op jit(solution)/shard_map/all_gather | solution.py:136
  106.4 0.0 collective-permute-done.11
  106.4 0.1 broadcast_select_fusion.1.own
  106.5 1.9 %collective-permute-start.12 = (bf16[1024,256]{1,0:T(8,128)(2,1)S(1)}, bf16[1024,256]{1,0:T(8,128)(2,1)S(1)}, u32[]{:S(2)}, u32[]{:S(2)}) collective-permute-start(bf16[1024,256]{1,0:T(8,128)(2,1)S(1)} %broadcast_select_fusion.1.own), channel_id=1, source_target_pairs={{0,1},{1,2},{2,3},{3,4},{4,5},{5,6},{6,7},{8,9},{9,10},{10,11},{11... | collective-permute-start | bytes 1572872 | tf_op jit(solution)/shard_map/ppermute | solution.py:28
  108.4 3.6 %collective-permute-start.13 = (bf16[1024,256]{1,0:T(8,128)(2,1)S(1)}, bf16[1024,256]{1,0:T(8,128)(2,1)S(1)}, u32[]{:S(2)}, u32[]{:S(2)}) collective-permute-start(bf16[1024,256]{1,0:T(8,128)(2,1)S(1)} %broadcast_select_fusion.1.own), channel_id=1, source_target_pairs={{1,0},{2,1},{3,2},{4,3},{5,4},{6,5},{7,6},{9,8},{10,9},{11,10},{12... | collective-permute-start | bytes 1572872 | tf_op jit(solution)/shard_map/ppermute | solution.py:28
  112.1 4.9 %collective-permute-done.12.below = bf16[1024,256]{1,0:T(8,128)(2,1)S(1)} collective-permute-done((bf16[1024,256]{1,0:T(8,128)(2,1)S(1)}, bf16[1024,256]{1,0:T(8,128)(2,1)S(1)}, u32[]{:S(2)}, u32[]{:S(2)}) %collective-permute-start.12) | collective-permute-done | bytes 524320 | tf_op jit(solution)/shard_map/ppermute | solution.py:28
  117.0 1.8 collective-permute-done.13.above
  118.8 1.7 product_by_rows.6
  120.5 0.7 collective-permute-start.16
  121.2 0.3 collective-permute-start.15
  121.5 1.8 collective-permute-start.14
  123.3 3.3 %collective-permute-start.17 = (bf16[1024,256]{1,0:T(8,128)(2,1)S(1)}, bf16[1024,256]{1,0:T(8,128)(2,1)S(1)}, u32[]{:S(2)}, u32[]{:S(2)}) collective-permute-start(bf16[1024,256]{1,0:T(8,128)(2,1)S(1)} %broadcast_select_fusion.1.own), channel_id=1, source_target_pairs={{0,8},{8,16},{16,24},{1,9},{9,17},{17,25},{2,10},{10,18},{18,26},{... | collective-permute-start | bytes 1572872 | tf_op jit(solution)/shard_map/ppermute | solution.py:131
  126.6 0.3 collective-permute-done.16
  126.9 6.2 %collective-permute-done.15 = bf16[256,256]{1,0:T(8,128)(2,1)S(1)} collective-permute-done((bf16[256,256]{1,0:T(8,128)(2,1)S(1)}, bf16[256,256]{1,0:T(8,128)(2,1)S(1)}, u32[]{:S(2)}, u32[]{:S(2)}) %collective-permute-start.15) | collective-permute-done | bytes 131104 | tf_op jit(solution)/shard_map/ppermute | solution.py:113
  133.2 0.0 collective-permute-done.14
  133.2 1.1 fusion.65
  134.3 23.0 %all_gather.11 = bf16[1024,256]{1,0:T(8,128)(2,1)S(1)} all-gather(bf16[256,256]{1,0:T(8,128)(2,1)S(1)} %get-tuple-element.36), channel_id=1, replica_groups=mesh['lag'=4,'elem'=8] {'lag'}, dimensions={0}, use_global_device_ids=true | all-gather | bytes 655360 | tf_op jit(solution)/shard_map/all_gather | solution.py:136
  157.2 0.0 collective-permute-done.17
  157.2 0.1 broadcast_select_fusion.own
  157.3 1.9 %collective-permute-start.18 = (bf16[1024,256]{1,0:T(8,128)(2,1)S(1)}, bf16[1024,256]{1,0:T(8,128)(2,1)S(1)}, u32[]{:S(2)}, u32[]{:S(2)}) collective-permute-start(bf16[1024,256]{1,0:T(8,128)(2,1)S(1)} %broadcast_select_fusion.own), channel_id=1, source_target_pairs={{0,1},{1,2},{2,3},{3,4},{4,5},{5,6},{6,7},{8,9},{9,10},{10,11},{11... | collective-permute-start | bytes 1572872 | tf_op jit(solution)/shard_map/ppermute | solution.py:28
  159.2 3.6 %collective-permute-start.19 = (bf16[1024,256]{1,0:T(8,128)(2,1)S(1)}, bf16[1024,256]{1,0:T(8,128)(2,1)S(1)}, u32[]{:S(2)}, u32[]{:S(2)}) collective-permute-start(bf16[1024,256]{1,0:T(8,128)(2,1)S(1)} %broadcast_select_fusion.own), channel_id=1, source_target_pairs={{1,0},{2,1},{3,2},{4,3},{5,4},{6,5},{7,6},{9,8},{10,9},{11,10},{12... | collective-permute-start | bytes 1572872 | tf_op jit(solution)/shard_map/ppermute | solution.py:28
  162.9 4.9 %collective-permute-done.18.below = bf16[1024,256]{1,0:T(8,128)(2,1)S(1)} collective-permute-done((bf16[1024,256]{1,0:T(8,128)(2,1)S(1)}, bf16[1024,256]{1,0:T(8,128)(2,1)S(1)}, u32[]{:S(2)}, u32[]{:S(2)}) %collective-permute-start.18) | collective-permute-done | bytes 524320 | tf_op jit(solution)/shard_map/ppermute | solution.py:28
  167.8 1.8 collective-permute-done.19.above
  169.5 1.7 product_by_rows.7
  171.2 0.6 collective-permute-start.22
  171.8 0.5 collective-permute-start.21
  172.3 1.8 collective-permute-start.20
  174.1 2.8 %collective-permute-done.22 = bf16[256,256]{1,0:T(8,128)(2,1)S(1)} collective-permute-done((bf16[256,256]{1,0:T(8,128)(2,1)S(1)}, bf16[256,256]{1,0:T(8,128)(2,1)S(1)}, u32[]{:S(2)}, u32[]{:S(2)}) %collective-permute-start.22) | collective-permute-done | bytes 131104 | tf_op jit(solution)/shard_map/ppermute | solution.py:113
  176.9 7.0 %collective-permute-done.21 = bf16[256,256]{1,0:T(8,128)(2,1)S(1)} collective-permute-done((bf16[256,256]{1,0:T(8,128)(2,1)S(1)}, bf16[256,256]{1,0:T(8,128)(2,1)S(1)}, u32[]{:S(2)}, u32[]{:S(2)}) %collective-permute-start.21) | collective-permute-done | bytes 131104 | tf_op jit(solution)/shard_map/ppermute | solution.py:113
  183.9 0.0 collective-permute-done.20
  183.9 2.1 %add_bitcast_fusion = (f32[1,1,256,256]{3,2,1,0:T(8,128)}, bf16[256,256]{1,0:T(8,128)(2,1)}) fusion(f32[256,256]{1,0:T(8,128)S(1)} %get-tuple-element.37, f32[256,256]{1,0:T(8,128)S(1)} %get-tuple-element.40, f32[256,256]{1,0:T(8,128)S(1)} %get-tuple-element.39, f32[256]{0:T(256)S(1)} %bitcast.52, f32[256]{0:T(256)S(1)} %broadcast_multiply_fusion, ...), kind=kLoop, calls=%fused_computation.86 | loop fusion | flops 5177344 | bytes 2100224 | tf_op jit(solution)/shard_map/broadcast_in_dim | solution.py:138
  (8 shorter events, 0.0 us)
Async XLA Ops:
  0.6 10.7 %collective-permute-start = (bf16[1024,256]{1,0:T(8,128)(2,1)}, bf16[1024,256]{1,0:T(8,128)(2,1)S(1)}, u32[]{:S(2)}, u32[]{:S(2)}) collective-permute-start(bf16[1024,256]{1,0:T(8,128)(2,1)} %bitcast.43), channel_id=1, source_target_pairs={{0,1},{1,2},{2,3},{3,4},{4,5},{5,6},{6,7},{8,9},{9,10},{10,11},{11... | collective-permute-start | bytes 1572872 | tf_op jit(solution)/shard_map/ppermute | solution.py:28
  2.6 13.5 %collective-permute-start.1 = (bf16[1024,256]{1,0:T(8,128)(2,1)}, bf16[1024,256]{1,0:T(8,128)(2,1)S(1)}, u32[]{:S(2)}, u32[]{:S(2)}) collective-permute-start(bf16[1024,256]{1,0:T(8,128)(2,1)} %bitcast.44), channel_id=1, source_target_pairs={{1,0},{2,1},{3,2},{4,3},{5,4},{6,5},{7,6},{9,8},{10,9},{11,10},{12... | collective-permute-start | bytes 1572872 | tf_op jit(solution)/shard_map/ppermute | solution.py:28
  6.2 48.5 %collective-permute-start.5 = (bf16[1024,256]{1,0:T(8,128)(2,1)}, bf16[1024,256]{1,0:T(8,128)(2,1)S(1)}, u32[]{:S(2)}, u32[]{:S(2)}) collective-permute-start(bf16[1024,256]{1,0:T(8,128)(2,1)} %bitcast.45), channel_id=1, source_target_pairs={{0,8},{8,16},{16,24},{1,9},{9,17},{17,25},{2,10},{10,18},{18,26},{... | collective-permute-start | bytes 1572872 | tf_op jit(solution)/shard_map/ppermute | solution.py:131
  16.1 1.9 %copy-start = (bf16[1,1024,1536]{2,1,0:T(8,128)(2,1)S(1)}, bf16[1,1024,1536]{2,1,0:T(8,128)(2,1)}, u32[]{:S(2)}) copy-start(bf16[1,1024,1536]{2,1,0:T(8,128)(2,1)} %tile.7) | copy-start | bytes 9437188
  18.0 1.0 copy-start.1
  19.0 0.7 copy-start.2
  19.7 17.8 %copy-start.3 = (f32[1,1,256,256]{3,2,1,0:T(8,128)S(1)}, f32[1,1,256,256]{3,2,1,0:T(8,128)}, u32[]{:S(2)}) copy-start(f32[1,1,256,256]{3,2,1,0:T(8,128)} %param.13) | copy-start | bytes 786436
  19.7 17.8 %copy-start.4 = (f32[1,1,256,256]{3,2,1,0:T(8,128)S(1)}, f32[1,1,256,256]{3,2,1,0:T(8,128)}, u32[]{:S(2)}) copy-start(f32[1,1,256,256]{3,2,1,0:T(8,128)} %param.14) | copy-start | bytes 786436
  21.4 6.9 %collective-permute-start.4 = (bf16[256,256]{1,0:T(8,128)(2,1)S(1)}, bf16[256,256]{1,0:T(8,128)(2,1)S(1)}, u32[]{:S(2)}, u32[]{:S(2)}) collective-permute-start(bf16[256,256]{1,0:T(8,128)(2,1)S(1)} %get-tuple-element.21), channel_id=1, source_target_pairs={{0,24},{8,0},{16,8},{24,16},{1,25},{9,1},{17,9},{25,17},{2,26},{10... | collective-permute-start | bytes 393224 | tf_op jit(solution)/shard_map/ppermute | solution.py:113
  25.0 12.5 %collective-permute-start.3 = (bf16[256,256]{1,0:T(8,128)(2,1)S(1)}, bf16[256,256]{1,0:T(8,128)(2,1)S(1)}, u32[]{:S(2)}, u32[]{:S(2)}) collective-permute-start(bf16[256,256]{1,0:T(8,128)(2,1)S(1)} %get-tuple-element.20), channel_id=1, source_target_pairs={{0,16},{8,24},{16,0},{24,8},{1,17},{9,25},{17,1},{25,9},{2,18},{10... | collective-permute-start | bytes 393224 | tf_op jit(solution)/shard_map/ppermute | solution.py:113
  25.0 12.5 %collective-permute-start.2 = (bf16[256,256]{1,0:T(8,128)(2,1)S(1)}, bf16[256,256]{1,0:T(8,128)(2,1)S(1)}, u32[]{:S(2)}, u32[]{:S(2)}) collective-permute-start(bf16[256,256]{1,0:T(8,128)(2,1)S(1)} %get-tuple-element.19), channel_id=1, source_target_pairs={{0,8},{8,16},{16,24},{24,0},{1,9},{9,17},{17,25},{25,1},{2,10},{10... | collective-permute-start | bytes 393224 | tf_op jit(solution)/shard_map/ppermute | solution.py:113
  54.8 10.5 %collective-permute-start.6 = (bf16[1024,256]{1,0:T(8,128)(2,1)S(1)}, bf16[1024,256]{1,0:T(8,128)(2,1)S(1)}, u32[]{:S(2)}, u32[]{:S(2)}) collective-permute-start(bf16[1024,256]{1,0:T(8,128)(2,1)S(1)} %broadcast_select_fusion.2.own), channel_id=1, source_target_pairs={{0,1},{1,2},{2,3},{3,4},{4,5},{5,6},{6,7},{8,9},{9,10},{10,11},{11... | collective-permute-start | bytes 1572872 | tf_op jit(solution)/shard_map/ppermute | solution.py:28
  56.7 11.2 %collective-permute-start.7 = (bf16[1024,256]{1,0:T(8,128)(2,1)S(1)}, bf16[1024,256]{1,0:T(8,128)(2,1)S(1)}, u32[]{:S(2)}, u32[]{:S(2)}) collective-permute-start(bf16[1024,256]{1,0:T(8,128)(2,1)S(1)} %broadcast_select_fusion.2.own), channel_id=1, source_target_pairs={{1,0},{2,1},{3,2},{4,3},{5,4},{6,5},{7,6},{9,8},{10,9},{11,10},{12... | collective-permute-start | bytes 1572872 | tf_op jit(solution)/shard_map/ppermute | solution.py:28
  69.6 6.4 %collective-permute-start.10 = (bf16[256,256]{1,0:T(8,128)(2,1)S(1)}, bf16[256,256]{1,0:T(8,128)(2,1)S(1)}, u32[]{:S(2)}, u32[]{:S(2)}) collective-permute-start(bf16[256,256]{1,0:T(8,128)(2,1)S(1)} %get-tuple-element.25), channel_id=1, source_target_pairs={{0,24},{8,0},{16,8},{24,16},{1,25},{9,1},{17,9},{25,17},{2,26},{10... | collective-permute-start | bytes 393224 | tf_op jit(solution)/shard_map/ppermute | solution.py:113
  70.4 11.9 %collective-permute-start.9 = (bf16[256,256]{1,0:T(8,128)(2,1)S(1)}, bf16[256,256]{1,0:T(8,128)(2,1)S(1)}, u32[]{:S(2)}, u32[]{:S(2)}) collective-permute-start(bf16[256,256]{1,0:T(8,128)(2,1)S(1)} %get-tuple-element.24), channel_id=1, source_target_pairs={{0,16},{8,24},{16,0},{24,8},{1,17},{9,25},{17,1},{25,9},{2,18},{10... | collective-permute-start | bytes 393224 | tf_op jit(solution)/shard_map/ppermute | solution.py:113
  70.5 11.8 %collective-permute-start.8 = (bf16[256,256]{1,0:T(8,128)(2,1)S(1)}, bf16[256,256]{1,0:T(8,128)(2,1)S(1)}, u32[]{:S(2)}, u32[]{:S(2)}) collective-permute-start(bf16[256,256]{1,0:T(8,128)(2,1)S(1)} %get-tuple-element.23), channel_id=1, source_target_pairs={{0,8},{8,16},{16,24},{24,0},{1,9},{9,17},{17,25},{25,1},{2,10},{10... | collective-permute-start | bytes 393224 | tf_op jit(solution)/shard_map/ppermute | solution.py:113
  72.4 34.0 %collective-permute-start.11 = (bf16[1024,256]{1,0:T(8,128)(2,1)S(1)}, bf16[1024,256]{1,0:T(8,128)(2,1)S(1)}, u32[]{:S(2)}, u32[]{:S(2)}) collective-permute-start(bf16[1024,256]{1,0:T(8,128)(2,1)S(1)} %broadcast_select_fusion.2.own), channel_id=1, source_target_pairs={{0,8},{8,16},{16,24},{1,9},{9,17},{17,25},{2,10},{10,18},{18,26},{... | collective-permute-start | bytes 1572872 | tf_op jit(solution)/shard_map/ppermute | solution.py:131
  106.5 10.5 %collective-permute-start.12 = (bf16[1024,256]{1,0:T(8,128)(2,1)S(1)}, bf16[1024,256]{1,0:T(8,128)(2,1)S(1)}, u32[]{:S(2)}, u32[]{:S(2)}) collective-permute-start(bf16[1024,256]{1,0:T(8,128)(2,1)S(1)} %broadcast_select_fusion.1.own), channel_id=1, source_target_pairs={{0,1},{1,2},{2,3},{3,4},{4,5},{5,6},{6,7},{8,9},{9,10},{10,11},{11... | collective-permute-start | bytes 1572872 | tf_op jit(solution)/shard_map/ppermute | solution.py:28
  108.4 10.4 %collective-permute-start.13 = (bf16[1024,256]{1,0:T(8,128)(2,1)S(1)}, bf16[1024,256]{1,0:T(8,128)(2,1)S(1)}, u32[]{:S(2)}, u32[]{:S(2)}) collective-permute-start(bf16[1024,256]{1,0:T(8,128)(2,1)S(1)} %broadcast_select_fusion.1.own), channel_id=1, source_target_pairs={{1,0},{2,1},{3,2},{4,3},{5,4},{6,5},{7,6},{9,8},{10,9},{11,10},{12... | collective-permute-start | bytes 1572872 | tf_op jit(solution)/shard_map/ppermute | solution.py:28
  120.5 6.4 %collective-permute-start.16 = (bf16[256,256]{1,0:T(8,128)(2,1)S(1)}, bf16[256,256]{1,0:T(8,128)(2,1)S(1)}, u32[]{:S(2)}, u32[]{:S(2)}) collective-permute-start(bf16[256,256]{1,0:T(8,128)(2,1)S(1)} %get-tuple-element.29), channel_id=1, source_target_pairs={{0,24},{8,0},{16,8},{24,16},{1,25},{9,1},{17,9},{25,17},{2,26},{10... | collective-permute-start | bytes 393224 | tf_op jit(solution)/shard_map/ppermute | solution.py:113
  121.2 12.0 %collective-permute-start.15 = (bf16[256,256]{1,0:T(8,128)(2,1)S(1)}, bf16[256,256]{1,0:T(8,128)(2,1)S(1)}, u32[]{:S(2)}, u32[]{:S(2)}) collective-permute-start(bf16[256,256]{1,0:T(8,128)(2,1)S(1)} %get-tuple-element.28), channel_id=1, source_target_pairs={{0,16},{8,24},{16,0},{24,8},{1,17},{9,25},{17,1},{25,9},{2,18},{10... | collective-permute-start | bytes 393224 | tf_op jit(solution)/shard_map/ppermute | solution.py:113
  121.5 11.7 %collective-permute-start.14 = (bf16[256,256]{1,0:T(8,128)(2,1)S(1)}, bf16[256,256]{1,0:T(8,128)(2,1)S(1)}, u32[]{:S(2)}, u32[]{:S(2)}) collective-permute-start(bf16[256,256]{1,0:T(8,128)(2,1)S(1)} %get-tuple-element.27), channel_id=1, source_target_pairs={{0,8},{8,16},{16,24},{24,0},{1,9},{9,17},{17,25},{25,1},{2,10},{10... | collective-permute-start | bytes 393224 | tf_op jit(solution)/shard_map/ppermute | solution.py:113
  123.3 33.9 %collective-permute-start.17 = (bf16[1024,256]{1,0:T(8,128)(2,1)S(1)}, bf16[1024,256]{1,0:T(8,128)(2,1)S(1)}, u32[]{:S(2)}, u32[]{:S(2)}) collective-permute-start(bf16[1024,256]{1,0:T(8,128)(2,1)S(1)} %broadcast_select_fusion.1.own), channel_id=1, source_target_pairs={{0,8},{8,16},{16,24},{1,9},{9,17},{17,25},{2,10},{10,18},{18,26},{... | collective-permute-start | bytes 1572872 | tf_op jit(solution)/shard_map/ppermute | solution.py:131
  157.3 10.5 %collective-permute-start.18 = (bf16[1024,256]{1,0:T(8,128)(2,1)S(1)}, bf16[1024,256]{1,0:T(8,128)(2,1)S(1)}, u32[]{:S(2)}, u32[]{:S(2)}) collective-permute-start(bf16[1024,256]{1,0:T(8,128)(2,1)S(1)} %broadcast_select_fusion.own), channel_id=1, source_target_pairs={{0,1},{1,2},{2,3},{3,4},{4,5},{5,6},{6,7},{8,9},{9,10},{10,11},{11... | collective-permute-start | bytes 1572872 | tf_op jit(solution)/shard_map/ppermute | solution.py:28
  159.2 10.3 %collective-permute-start.19 = (bf16[1024,256]{1,0:T(8,128)(2,1)S(1)}, bf16[1024,256]{1,0:T(8,128)(2,1)S(1)}, u32[]{:S(2)}, u32[]{:S(2)}) collective-permute-start(bf16[1024,256]{1,0:T(8,128)(2,1)S(1)} %broadcast_select_fusion.own), channel_id=1, source_target_pairs={{1,0},{2,1},{3,2},{4,3},{5,4},{6,5},{7,6},{9,8},{10,9},{11,10},{12... | collective-permute-start | bytes 1572872 | tf_op jit(solution)/shard_map/ppermute | solution.py:28
  171.2 5.7 %collective-permute-start.22 = (bf16[256,256]{1,0:T(8,128)(2,1)S(1)}, bf16[256,256]{1,0:T(8,128)(2,1)S(1)}, u32[]{:S(2)}, u32[]{:S(2)}) collective-permute-start(bf16[256,256]{1,0:T(8,128)(2,1)S(1)} %get-tuple-element.33), channel_id=1, source_target_pairs={{0,24},{8,0},{16,8},{24,16},{1,25},{9,1},{17,9},{25,17},{2,26},{10... | collective-permute-start | bytes 393224 | tf_op jit(solution)/shard_map/ppermute | solution.py:113
  171.8 12.1 %collective-permute-start.21 = (bf16[256,256]{1,0:T(8,128)(2,1)S(1)}, bf16[256,256]{1,0:T(8,128)(2,1)S(1)}, u32[]{:S(2)}, u32[]{:S(2)}) collective-permute-start(bf16[256,256]{1,0:T(8,128)(2,1)S(1)} %get-tuple-element.32), channel_id=1, source_target_pairs={{0,16},{8,24},{16,0},{24,8},{1,17},{9,25},{17,1},{25,9},{2,18},{10... | collective-permute-start | bytes 393224 | tf_op jit(solution)/shard_map/ppermute | solution.py:113
  172.3 11.6 %collective-permute-start.20 = (bf16[256,256]{1,0:T(8,128)(2,1)S(1)}, bf16[256,256]{1,0:T(8,128)(2,1)S(1)}, u32[]{:S(2)}, u32[]{:S(2)}) collective-permute-start(bf16[256,256]{1,0:T(8,128)(2,1)S(1)} %get-tuple-element.31), channel_id=1, source_target_pairs={{0,8},{8,16},{16,24},{24,0},{1,9},{9,17},{17,25},{25,1},{2,10},{10... | collective-permute-start | bytes 393224 | tf_op jit(solution)/shard_map/ppermute | solution.py:113

commit v6 on v5

--- a/solution.py
+++ b/solution.py
@@ -28,20 +28,17 @@
     return lax.ppermute(value, axes, up), lax.ppermute(value, axes, down)
 
 
-def fetch(picks, live, below, own, above, sources, sems):
+def fetch(where, picks, live, refs, sources, sems):
     slots = sems.shape[0]
     block = sources.shape[0] // slots
-    per = own.shape[0] // block
     alive = live[0]
     for k in range(slots):
         spot = sources.at[pl.ds(k * block, block)]
-        pick = picks[0, 0, k]
-        start = pl.multiple_of(lax.rem(pick, per) * block, block)
-        for which, ref in enumerate((below, own, above)):
+        for p, (which, first) in enumerate(where):
 
-            @pl.when((k < alive) & (lax.div(pick, per) == which))
+            @pl.when((k < alive) & (picks[0, 0, k] == p))
             def _():
-                pltpu.make_async_copy(ref.at[pl.ds(start, block)], spot, sems.at[k]).start()
+                pltpu.make_async_copy(refs[which].at[pl.ds(first, block)], spot, sems.at[k]).start()
 
     for k in range(slots):
         spot = sources.at[pl.ds(k * block, block)]
@@ -52,38 +49,45 @@
 
         @pl.when(k < alive)
         def _():
-            pltpu.make_async_copy(own.at[pl.ds(0, block)], spot, sems.at[k]).wait()
+            pltpu.make_async_copy(refs[0].at[pl.ds(0, block)], spot, sems.at[k]).wait()
 
 
-def rows_kernel(lags, rows, picks, live, tile, below, own, above, *refs):
-    outs, sources, sems = refs[:lags], refs[lags], refs[lags + 1]
+def rows_kernel(lags, rows, where, count, picks, live, tile, *refs):
+    window, outs, sources, sems = refs[:count], refs[count : count + lags], refs[-2], refs[-1]
     me = lax.axis_index("lag")
-    fetch(picks, live, below, own, above, sources, sems)
+    fetch(where, picks, live, window, sources, sems)
     for d in range(lags):
         first = pl.multiple_of(lax.rem(me + d, lags) * rows, rows)
         part = jnp.dot(tile[0, pl.ds(first, rows), :], sources[...], preferred_element_type=jnp.float32)
         outs[d][...] = part.astype(outs[d].dtype)
 
 
-def product_by_rows(picks, live, tile, below, own, above, lags):
-    rows, cols = own.shape[0] // lags, own.shape[1]
+def product_by_rows(picks, live, tile, window, lags):
+    rows, cols = tile.shape[1] // lags, window[0].shape[1]
+    block = tile.shape[2] // picks.shape[2]
+    where = [(i, first) for i, part in enumerate(window) for first in range(0, part.shape[0], block)]
     kinds = [jnp.float32] + [jnp.bfloat16] * (lags - 1)
     return pl.pallas_call(
-        functools.partial(rows_kernel, lags, rows),
+        functools.partial(rows_kernel, lags, rows, where, len(window)),
         grid_spec=pltpu.PrefetchScalarGridSpec(
             num_scalar_prefetch=2,
             grid=(1,),
-            in_specs=[VMEM] + [ANY] * 3,
+            in_specs=[VMEM] + [ANY] * len(window),
             out_specs=[VMEM] * lags,
-            scratch_shapes=[pltpu.VMEM((tile.shape[2], cols), own.dtype), pltpu.SemaphoreType.DMA((picks.shape[2],))],
+            scratch_shapes=[
+                pltpu.VMEM((tile.shape[2], cols), window[0].dtype),
+                pltpu.SemaphoreType.DMA((picks.shape[2],)),
+            ],
         ),
         out_shape=[jax.ShapeDtypeStruct((rows, cols), kind) for kind in kinds],
         compiler_params=PARAMS,
         cost_estimate=pl.CostEstimate(
-            flops=2 * tile.size * cols, bytes_accessed=2 * (tile.size + 4 * own.size), transcendentals=0
+            flops=2 * tile.size * cols,
+            bytes_accessed=2 * (tile.size + sum(part.size for part in window)),
+            transcendentals=0,
         ),
         name="product_by_rows",
-    )(picks, live, tile, below, own, above)
+    )(picks, live, tile, *window)
 
 
 def newton(load, state, ratio, strength):
@@ -123,18 +127,26 @@
     lags = lax.axis_size("lag")
     me = lax.axis_index("lag")
     local = (shell_index, cone_blocks, kernel_tiles)
-    field, state = history[0], log_state[0, 0]
+    pieces, state = [history[0]], log_state[0, 0]
+    parts = history.shape[1] * shell_index.shape[2] // kernel_tiles.shape[2]
     columns = [c[0, 0][:, None] for c in (fric_a, fric_b, normal_stress)]
     for step in range(STEPS):
-        below, above = exchange(field, range(lags))
+        sides = [exchange(piece, range(lags)) for piece in pieces]
+        window = [side[0] for side in sides] + pieces + [side[1] for side in sides]
         if step + 1 < STEPS:
+            field = jnp.concatenate(pieces, 0)
             older = lax.ppermute(field, "lag", [(i, i + 1) for i in range(lags - 1)])
-        parts = product_by_rows(*local, below, field, above, lags)
-        traction = scatter_sum(parts)
+        traction = scatter_sum(product_by_rows(*local, window, lags))
         rates, state = settle_friction(prestress[0, 0] + traction, state, *columns)
         if step + 1 < STEPS:
-            newest = lax.all_gather(rates, "lag", axis=0, tiled=True)
-            field = jnp.where(me == 0, newest, older)
+            newest = [rates] + [lax.ppermute(rates, "lag", [(d, 0)]) for d in range(1, lags)]
+            size, height = lags // parts, older.shape[0] // parts
+            pieces, me_now = [], me
+            for i in range(parts):
+                new = jnp.concatenate(newest[i * size : (i + 1) * size], 0)
+                piece = jnp.where(me_now == 0, new, older[i * height : (i + 1) * height])
+                piece, older, me_now = lax.optimization_barrier((piece, older, me_now))
+                pieces.append(piece)
     return rates[None, None], state[None, None]
 
 

time: 187 us -> 180 us (0.963)
  the two profiles are of different devices: /device:TPU:2 before, /device:TPU:12 now
where the time goes in v6:
time: 180 us; the launch traced here: 179 us
  starting transfers between devices  80.7 us (45%)
  waiting for transfers between devices  71.5 us (40%)
  other arithmetic  13 us (7%)
  Pallas kernels  7.06 us (4%)
  local copies, waits for them, and re-layouts  5.28 us (3%)
    ppermute x14, starting transfers between devices, exchange(): return (lax.ppermute(value, axes, up), lax.ppermute(value, axes, down))  37.8 us
    ppermute x12, waiting for transfers between devices, scatter_sum(): total = total + lax.ppermute(parts[d], 'lag', route).astype(jnp.float32)  28.9 us
    ppermute x14, waiting for transfers between devices, exchange(): return (lax.ppermute(value, axes, up), lax.ppermute(value, axes, down))  26.7 us
    ppermute x12, starting transfers between devices, scatter_sum(): total = total + lax.ppermute(parts[d], 'lag', route).astype(jnp.float32)  18.8 us
    ppermute x9, waiting for transfers between devices, shards(): lax.ppermute(rates, 'lag', [(d, 0)])  15.9 us
    ppermute x9, starting transfers between devices, shards(): lax.ppermute(rates, 'lag', [(d, 0)])  12.8 us
    ppermute x3, starting transfers between devices, shards(): older = lax.ppermute(field, 'lag', [(i, i + 1) for i in range(lags - 1)])  11.3 us
    pallas_call x4, Pallas kernels, product_by_rows(): pl.pallas_call(functools.partial(rows_kernel, lags, rows, where, len(wind...  7.06 us
  transfers between devices with their start and end apart: 38, of which 24 were waited for; matrix products, arithmetic and copies ran while one was open for 4% of the time, Pallas kernels for 1%

profile of v6, /device:TPU:12, one launch (start us, length us, event | category | flops | bytes accessed | tf_op | source)
XLA Modules:
  0.0 179.3 jit_solution(12812864761247951584)
XLA Ops:
  0.6 2.8 %collective-permute-start.1 = (bf16[1024,256]{1,0:T(8,128)(2,1)}, bf16[1024,256]{1,0:T(8,128)(2,1)S(1)}, u32[]{:S(2)}, u32[]{:S(2)}) collective-permute-start(bf16[1024,256]{1,0:T(8,128)(2,1)} %bitcast.43), channel_id=1, source_target_pairs={{1,0},{2,1},{3,2},{4,3},{5,4},{6,5},{7,6},{9,8},{10,9},{11,10},{12... | collective-permute-start | bytes 1572872 | tf_op jit(solution)/shard_map/ppermute | solution.py:28
  3.4 1.9 %collective-permute-start = (bf16[1024,256]{1,0:T(8,128)(2,1)}, bf16[1024,256]{1,0:T(8,128)(2,1)S(1)}, u32[]{:S(2)}, u32[]{:S(2)}) collective-permute-start(bf16[1024,256]{1,0:T(8,128)(2,1)} %bitcast.44), channel_id=1, source_target_pairs={{0,1},{1,2},{2,3},{3,4},{4,5},{5,6},{6,7},{8,9},{9,10},{10,11},{11... | collective-permute-start | bytes 1572872 | tf_op jit(solution)/shard_map/ppermute | solution.py:28
  5.4 3.5 %collective-permute-start.6 = (bf16[1024,256]{1,0:T(8,128)(2,1)}, bf16[1024,256]{1,0:T(8,128)(2,1)}, u32[]{:S(2)}, u32[]{:S(2)}) collective-permute-start(bf16[1024,256]{1,0:T(8,128)(2,1)} %bitcast.45), channel_id=1, source_target_pairs={{0,8},{8,16},{16,24},{1,9},{9,17},{17,25},{2,10},{10,18},{18,26},{... | collective-permute-start | bytes 1572872 | tf_op jit(solution)/shard_map/ppermute | solution.py:138
  10.2 3.8 %collective-permute-done.1.refs_2_ = bf16[1024,256]{1,0:T(8,128)(2,1)S(1)} collective-permute-done((bf16[1024,256]{1,0:T(8,128)(2,1)}, bf16[1024,256]{1,0:T(8,128)(2,1)S(1)}, u32[]{:S(2)}, u32[]{:S(2)}) %collective-permute-start.1) | collective-permute-done | bytes 524320 | tf_op jit(solution)/shard_map/ppermute | solution.py:28
  14.1 2.9 %collective-permute-done.refs_0_ = bf16[1024,256]{1,0:T(8,128)(2,1)S(1)} collective-permute-done((bf16[1024,256]{1,0:T(8,128)(2,1)}, bf16[1024,256]{1,0:T(8,128)(2,1)S(1)}, u32[]{:S(2)}, u32[]{:S(2)}) %collective-permute-start) | collective-permute-done | bytes 524320 | tf_op jit(solution)/shard_map/ppermute | solution.py:28
  17.0 1.9 %copy-done = bf16[1,1024,1536]{2,1,0:T(8,128)(2,1)S(1)} copy-done((bf16[1,1024,1536]{2,1,0:T(8,128)(2,1)S(1)}, bf16[1,1024,1536]{2,1,0:T(8,128)(2,1)}, u32[]{:S(2)}) %copy-start) | copy-done | bytes 3145752
  20.6 1.8 product_by_rows.4
  22.3 1.6 collective-permute-start.2
  24.0 1.2 collective-permute-start.3
  25.2 1.8 %collective-permute-start.4 = (bf16[256,256]{1,0:T(8,128)(2,1)S(1)}, bf16[256,256]{1,0:T(8,128)(2,1)S(1)}, u32[]{:S(2)}, u32[]{:S(2)}) collective-permute-start(bf16[256,256]{1,0:T(8,128)(2,1)S(1)} %get-tuple-element.33), channel_id=1, source_target_pairs={{0,24},{8,0},{16,8},{24,16},{1,25},{9,1},{17,9},{25,17},{2,26},{10... | collective-permute-start | bytes 393224 | tf_op jit(solution)/shard_map/ppermute | solution.py:117
  27.0 6.1 %collective-permute-done.2 = bf16[256,256]{1,0:T(8,128)(2,1)S(1)} collective-permute-done((bf16[256,256]{1,0:T(8,128)(2,1)S(1)}, bf16[256,256]{1,0:T(8,128)(2,1)S(1)}, u32[]{:S(2)}, u32[]{:S(2)}) %collective-permute-start.2) | collective-permute-done | bytes 131104 | tf_op jit(solution)/shard_map/ppermute | solution.py:117
  33.1 1.4 collective-permute-done.3
  34.5 1.8 collective-permute-done.4
  36.3 1.7 fusion.69
  38.0 1.9 %collective-permute-start.5 = (bf16[256,256]{1,0:T(8,128)(2,1)S(1)}, bf16[256,256]{1,0:T(8,128)(2,1)}, u32[]{:S(2)}, u32[]{:S(2)}) collective-permute-start(bf16[256,256]{1,0:T(8,128)(2,1)S(1)} %get-tuple-element.65), channel_id=1, source_target_pairs={{8,0},{9,1},{10,2},{11,3},{12,4},{13,5},{14,6},{15,7}} | collective-permute-start | bytes 393224 | tf_op jit(solution)/shard_map/ppermute | solution.py:142
  39.9 1.3 collective-permute-start.9
  41.2 1.3 collective-permute-start.8
  42.5 5.6 %collective-permute-done.5 = bf16[256,256]{1,0:T(8,128)(2,1)} collective-permute-done((bf16[256,256]{1,0:T(8,128)(2,1)S(1)}, bf16[256,256]{1,0:T(8,128)(2,1)}, u32[]{:S(2)}, u32[]{:S(2)}) %collective-permute-start.5) | collective-permute-done | bytes 131104 | tf_op jit(solution)/shard_map/ppermute | solution.py:142
  50.4 1.9 %collective-permute-start.12 = (bf16[512,256]{1,0:T(8,128)(2,1)S(1)}, bf16[512,256]{1,0:T(8,128)(2,1)S(1)}, u32[]{:S(2)}, u32[]{:S(2)}) collective-permute-start(bf16[512,256]{1,0:T(8,128)(2,1)S(1)} %maximum_select_fusion.refs_3_), channel_id=1, source_target_pairs={{1,0},{2,1},{3,2},{4,3},{5,4},{6,5},{7,6},{9,8},{10,9},{11,10},{12... | collective-permute-start | bytes 786440 | tf_op jit(solution)/shard_map/ppermute | solution.py:28
  52.4 2.4 %collective-permute-start.10 = (bf16[512,256]{1,0:T(8,128)(2,1)S(1)}, bf16[512,256]{1,0:T(8,128)(2,1)S(1)}, u32[]{:S(2)}, u32[]{:S(2)}) collective-permute-start(bf16[512,256]{1,0:T(8,128)(2,1)S(1)} %maximum_select_fusion.refs_3_), channel_id=1, source_target_pairs={{0,1},{1,2},{2,3},{3,4},{4,5},{5,6},{6,7},{8,9},{9,10},{10,11},{11... | collective-permute-start | bytes 786440 | tf_op jit(solution)/shard_map/ppermute | solution.py:28
  54.8 4.1 %collective-permute-start.11 = (bf16[512,256]{1,0:T(8,128)(2,1)S(1)}, bf16[512,256]{1,0:T(8,128)(2,1)S(1)}, u32[]{:S(2)}, u32[]{:S(2)}) collective-permute-start(bf16[512,256]{1,0:T(8,128)(2,1)S(1)} %slice_select_fusion.2.refs_2_), channel_id=1, source_target_pairs={{1,0},{2,1},{3,2},{4,3},{5,4},{6,5},{7,6},{9,8},{10,9},{11,10},{12... | collective-permute-start | bytes 786440 | tf_op jit(solution)/shard_map/ppermute | solution.py:28
  58.8 1.9 %collective-permute-start.7 = (bf16[512,256]{1,0:T(8,128)(2,1)S(1)}, bf16[512,256]{1,0:T(8,128)(2,1)S(1)}, u32[]{:S(2)}, u32[]{:S(2)}) collective-permute-start(bf16[512,256]{1,0:T(8,128)(2,1)S(1)} %slice_select_fusion.2.refs_2_), channel_id=1, source_target_pairs={{0,1},{1,2},{2,3},{3,4},{4,5},{5,6},{6,7},{8,9},{9,10},{10,11},{11... | collective-permute-start | bytes 786440 | tf_op jit(solution)/shard_map/ppermute | solution.py:28
  60.8 2.2 %collective-permute-done.10.refs_1_ = bf16[512,256]{1,0:T(8,128)(2,1)S(1)} collective-permute-done((bf16[512,256]{1,0:T(8,128)(2,1)S(1)}, bf16[512,256]{1,0:T(8,128)(2,1)S(1)}, u32[]{:S(2)}, u32[]{:S(2)}) %collective-permute-start.10) | collective-permute-done | bytes 262176 | tf_op jit(solution)/shard_map/ppermute | solution.py:28
  63.0 1.7 collective-permute-done.11.refs_4_
  64.7 2.8 %collective-permute-done.7.refs_0_ = bf16[512,256]{1,0:T(8,128)(2,1)S(1)} collective-permute-done((bf16[512,256]{1,0:T(8,128)(2,1)S(1)}, bf16[512,256]{1,0:T(8,128)(2,1)S(1)}, u32[]{:S(2)}, u32[]{:S(2)}) %collective-permute-start.7) | collective-permute-done | bytes 262176 | tf_op jit(solution)/shard_map/ppermute | solution.py:28
  67.4 1.8 product_by_rows.5
  69.3 4.9 %collective-permute-start.14 = (bf16[256,256]{1,0:T(8,128)(2,1)S(1)}, bf16[256,256]{1,0:T(8,128)(2,1)S(1)}, u32[]{:S(2)}, u32[]{:S(2)}) collective-permute-start(bf16[256,256]{1,0:T(8,128)(2,1)S(1)} %get-tuple-element.40), channel_id=1, source_target_pairs={{0,16},{8,24},{16,0},{24,8},{1,17},{9,25},{17,1},{25,9},{2,18},{10... | collective-permute-start | bytes 393224 | tf_op jit(solution)/shard_map/ppermute | solution.py:117
  74.2 3.9 %collective-permute-start.17 = (bf16[1024,256]{1,0:T(8,128)(2,1)S(1)}, bf16[1024,256]{1,0:T(8,128)(2,1)S(1)}, u32[]{:S(2)}, u32[]{:S(2)}) collective-permute-start(bf16[1024,256]{1,0:T(8,128)(2,1)S(1)} %pad_maximum_fusion), channel_id=1, source_target_pairs={{0,8},{8,16},{16,24},{1,9},{9,17},{17,25},{2,10},{10,18},{18,26},{... | collective-permute-start | bytes 1572872 | tf_op jit(solution)/shard_map/ppermute | solution.py:138
  78.2 2.8 %collective-permute-done.14 = bf16[256,256]{1,0:T(8,128)(2,1)S(1)} collective-permute-done((bf16[256,256]{1,0:T(8,128)(2,1)S(1)}, bf16[256,256]{1,0:T(8,128)(2,1)S(1)}, u32[]{:S(2)}, u32[]{:S(2)}) %collective-permute-start.14) | collective-permute-done | bytes 131104 | tf_op jit(solution)/shard_map/ppermute | solution.py:117
  81.0 2.4 %collective-permute-done.15 = bf16[256,256]{1,0:T(8,128)(2,1)S(1)} collective-permute-done((bf16[256,256]{1,0:T(8,128)(2,1)S(1)}, bf16[256,256]{1,0:T(8,128)(2,1)S(1)}, u32[]{:S(2)}, u32[]{:S(2)}) %collective-permute-start.15) | collective-permute-done | bytes 131104 | tf_op jit(solution)/shard_map/ppermute | solution.py:117
  83.4 1.8 fusion.67
  85.2 1.5 collective-permute-start.16
  86.6 1.3 collective-permute-start.20
  88.0 1.3 collective-permute-start.19
  89.3 5.2 %collective-permute-done.16 = bf16[256,256]{1,0:T(8,128)(2,1)S(1)} collective-permute-done((bf16[256,256]{1,0:T(8,128)(2,1)S(1)}, bf16[256,256]{1,0:T(8,128)(2,1)S(1)}, u32[]{:S(2)}, u32[]{:S(2)}) %collective-permute-start.16) | collective-permute-done | bytes 131104 | tf_op jit(solution)/shard_map/ppermute | solution.py:142
  96.6 2.6 %collective-permute-start.23 = (bf16[512,256]{1,0:T(8,128)(2,1)S(1)}, bf16[512,256]{1,0:T(8,128)(2,1)S(1)}, u32[]{:S(2)}, u32[]{:S(2)}) collective-permute-start(bf16[512,256]{1,0:T(8,128)(2,1)S(1)} %maximum_select_fusion.1.refs_3_), channel_id=1, source_target_pairs={{1,0},{2,1},{3,2},{4,3},{5,4},{6,5},{7,6},{9,8},{10,9},{11,10},{12... | collective-permute-start | bytes 786440 | tf_op jit(solution)/shard_map/ppermute | solution.py:28
  99.2 1.9 %collective-permute-start.21 = (bf16[512,256]{1,0:T(8,128)(2,1)S(1)}, bf16[512,256]{1,0:T(8,128)(2,1)S(1)}, u32[]{:S(2)}, u32[]{:S(2)}) collective-permute-start(bf16[512,256]{1,0:T(8,128)(2,1)S(1)} %maximum_select_fusion.1.refs_3_), channel_id=1, source_target_pairs={{0,1},{1,2},{2,3},{3,4},{4,5},{5,6},{6,7},{8,9},{9,10},{10,11},{11... | collective-permute-start | bytes 786440 | tf_op jit(solution)/shard_map/ppermute | solution.py:28
  101.2 4.5 %collective-permute-start.22 = (bf16[512,256]{1,0:T(8,128)(2,1)S(1)}, bf16[512,256]{1,0:T(8,128)(2,1)S(1)}, u32[]{:S(2)}, u32[]{:S(2)}) collective-permute-start(bf16[512,256]{1,0:T(8,128)(2,1)S(1)} %slice_select_fusion.1.refs_2_), channel_id=1, source_target_pairs={{1,0},{2,1},{3,2},{4,3},{5,4},{6,5},{7,6},{9,8},{10,9},{11,10},{12... | collective-permute-start | bytes 786440 | tf_op jit(solution)/shard_map/ppermute | solution.py:28
  105.7 1.9 %collective-permute-start.18 = (bf16[512,256]{1,0:T(8,128)(2,1)S(1)}, bf16[512,256]{1,0:T(8,128)(2,1)S(1)}, u32[]{:S(2)}, u32[]{:S(2)}) collective-permute-start(bf16[512,256]{1,0:T(8,128)(2,1)S(1)} %slice_select_fusion.1.refs_2_), channel_id=1, source_target_pairs={{0,1},{1,2},{2,3},{3,4},{4,5},{5,6},{6,7},{8,9},{9,10},{10,11},{11... | collective-permute-start | bytes 786440 | tf_op jit(solution)/shard_map/ppermute | solution.py:28
  107.6 1.9 %collective-permute-done.21.refs_1_ = bf16[512,256]{1,0:T(8,128)(2,1)S(1)} collective-permute-done((bf16[512,256]{1,0:T(8,128)(2,1)S(1)}, bf16[512,256]{1,0:T(8,128)(2,1)S(1)}, u32[]{:S(2)}, u32[]{:S(2)}) %collective-permute-start.21) | collective-permute-done | bytes 262176 | tf_op jit(solution)/shard_map/ppermute | solution.py:28
  109.5 2.7 %collective-permute-done.22.refs_4_ = bf16[512,256]{1,0:T(8,128)(2,1)S(1)} collective-permute-done((bf16[512,256]{1,0:T(8,128)(2,1)S(1)}, bf16[512,256]{1,0:T(8,128)(2,1)S(1)}, u32[]{:S(2)}, u32[]{:S(2)}) %collective-permute-start.22) | collective-permute-done | bytes 262176 | tf_op jit(solution)/shard_map/ppermute | solution.py:28
  112.2 2.0 %collective-permute-done.18.refs_0_ = bf16[512,256]{1,0:T(8,128)(2,1)S(1)} collective-permute-done((bf16[512,256]{1,0:T(8,128)(2,1)S(1)}, bf16[512,256]{1,0:T(8,128)(2,1)S(1)}, u32[]{:S(2)}, u32[]{:S(2)}) %collective-permute-start.18) | collective-permute-done | bytes 262176 | tf_op jit(solution)/shard_map/ppermute | solution.py:28
  114.3 1.8 product_by_rows.6
  116.1 4.5 %collective-permute-start.25 = (bf16[256,256]{1,0:T(8,128)(2,1)S(1)}, bf16[256,256]{1,0:T(8,128)(2,1)S(1)}, u32[]{:S(2)}, u32[]{:S(2)}) collective-permute-start(bf16[256,256]{1,0:T(8,128)(2,1)S(1)} %get-tuple-element.48), channel_id=1, source_target_pairs={{0,16},{8,24},{16,0},{24,8},{1,17},{9,25},{17,1},{25,9},{2,18},{10... | collective-permute-start | bytes 393224 | tf_op jit(solution)/shard_map/ppermute | solution.py:117
  120.7 3.9 %collective-permute-start.28 = (bf16[1024,256]{1,0:T(8,128)(2,1)S(1)}, bf16[1024,256]{1,0:T(8,128)(2,1)S(1)}, u32[]{:S(2)}, u32[]{:S(2)}) collective-permute-start(bf16[1024,256]{1,0:T(8,128)(2,1)S(1)} %pad_maximum_fusion.1), channel_id=1, source_target_pairs={{0,8},{8,16},{16,24},{1,9},{9,17},{17,25},{2,10},{10,18},{18,26},{... | collective-permute-start | bytes 1572872 | tf_op jit(solution)/shard_map/ppermute | solution.py:138
  124.7 3.0 %collective-permute-done.25 = bf16[256,256]{1,0:T(8,128)(2,1)S(1)} collective-permute-done((bf16[256,256]{1,0:T(8,128)(2,1)S(1)}, bf16[256,256]{1,0:T(8,128)(2,1)S(1)}, u32[]{:S(2)}, u32[]{:S(2)}) %collective-permute-start.25) | collective-permute-done | bytes 131104 | tf_op jit(solution)/shard_map/ppermute | solution.py:117
  127.7 2.2 %collective-permute-done.26 = bf16[256,256]{1,0:T(8,128)(2,1)S(1)} collective-permute-done((bf16[256,256]{1,0:T(8,128)(2,1)S(1)}, bf16[256,256]{1,0:T(8,128)(2,1)S(1)}, u32[]{:S(2)}, u32[]{:S(2)}) %collective-permute-start.26) | collective-permute-done | bytes 131104 | tf_op jit(solution)/shard_map/ppermute | solution.py:117
  129.9 1.8 fusion.65
  131.7 1.5 collective-permute-start.27
  133.2 1.3 collective-permute-start.31
  134.5 1.3 collective-permute-start.30
  135.8 5.2 %collective-permute-done.27 = bf16[256,256]{1,0:T(8,128)(2,1)S(1)} collective-permute-done((bf16[256,256]{1,0:T(8,128)(2,1)S(1)}, bf16[256,256]{1,0:T(8,128)(2,1)S(1)}, u32[]{:S(2)}, u32[]{:S(2)}) %collective-permute-start.27) | collective-permute-done | bytes 131104 | tf_op jit(solution)/shard_map/ppermute | solution.py:142
  143.1 3.4 %collective-permute-start.34 = (bf16[512,256]{1,0:T(8,128)(2,1)S(1)}, bf16[512,256]{1,0:T(8,128)(2,1)S(1)}, u32[]{:S(2)}, u32[]{:S(2)}) collective-permute-start(bf16[512,256]{1,0:T(8,128)(2,1)S(1)} %maximum_select_fusion.2.refs_3_), channel_id=1, source_target_pairs={{1,0},{2,1},{3,2},{4,3},{5,4},{6,5},{7,6},{9,8},{10,9},{11,10},{12... | collective-permute-start | bytes 786440 | tf_op jit(solution)/shard_map/ppermute | solution.py:28
  146.5 1.9 %collective-permute-start.32 = (bf16[512,256]{1,0:T(8,128)(2,1)S(1)}, bf16[512,256]{1,0:T(8,128)(2,1)S(1)}, u32[]{:S(2)}, u32[]{:S(2)}) collective-permute-start(bf16[512,256]{1,0:T(8,128)(2,1)S(1)} %maximum_select_fusion.2.refs_3_), channel_id=1, source_target_pairs={{0,1},{1,2},{2,3},{3,4},{4,5},{5,6},{6,7},{8,9},{9,10},{10,11},{11... | collective-permute-start | bytes 786440 | tf_op jit(solution)/shard_map/ppermute | solution.py:28
  148.5 4.5 %collective-permute-start.33 = (bf16[512,256]{1,0:T(8,128)(2,1)S(1)}, bf16[512,256]{1,0:T(8,128)(2,1)S(1)}, u32[]{:S(2)}, u32[]{:S(2)}) collective-permute-start(bf16[512,256]{1,0:T(8,128)(2,1)S(1)} %slice_select_fusion.refs_2_), channel_id=1, source_target_pairs={{1,0},{2,1},{3,2},{4,3},{5,4},{6,5},{7,6},{9,8},{10,9},{11,10},{12... | collective-permute-start | bytes 786440 | tf_op jit(solution)/shard_map/ppermute | solution.py:28
  153.0 1.9 %collective-permute-start.29 = (bf16[512,256]{1,0:T(8,128)(2,1)S(1)}, bf16[512,256]{1,0:T(8,128)(2,1)S(1)}, u32[]{:S(2)}, u32[]{:S(2)}) collective-permute-start(bf16[512,256]{1,0:T(8,128)(2,1)S(1)} %slice_select_fusion.refs_2_), channel_id=1, source_target_pairs={{0,1},{1,2},{2,3},{3,4},{4,5},{5,6},{6,7},{8,9},{9,10},{10,11},{11... | collective-permute-start | bytes 786440 | tf_op jit(solution)/shard_map/ppermute | solution.py:28
  155.0 3.0 %collective-permute-done.32.refs_1_ = bf16[512,256]{1,0:T(8,128)(2,1)S(1)} collective-permute-done((bf16[512,256]{1,0:T(8,128)(2,1)S(1)}, bf16[512,256]{1,0:T(8,128)(2,1)S(1)}, u32[]{:S(2)}, u32[]{:S(2)}) %collective-permute-start.32) | collective-permute-done | bytes 262176 | tf_op jit(solution)/shard_map/ppermute | solution.py:28
  159.0 2.6 %collective-permute-done.29.refs_0_ = bf16[512,256]{1,0:T(8,128)(2,1)S(1)} collective-permute-done((bf16[512,256]{1,0:T(8,128)(2,1)S(1)}, bf16[512,256]{1,0:T(8,128)(2,1)S(1)}, u32[]{:S(2)}, u32[]{:S(2)}) %collective-permute-start.29) | collective-permute-done | bytes 262176 | tf_op jit(solution)/shard_map/ppermute | solution.py:28
  161.6 1.8 product_by_rows.7
  163.5 4.5 %collective-permute-start.36 = (bf16[256,256]{1,0:T(8,128)(2,1)S(1)}, bf16[256,256]{1,0:T(8,128)(2,1)S(1)}, u32[]{:S(2)}, u32[]{:S(2)}) collective-permute-start(bf16[256,256]{1,0:T(8,128)(2,1)S(1)} %get-tuple-element.56), channel_id=1, source_target_pairs={{0,16},{8,24},{16,0},{24,8},{1,17},{9,25},{17,1},{25,9},{2,18},{10... | collective-permute-start | bytes 393224 | tf_op jit(solution)/shard_map/ppermute | solution.py:117
  168.0 2.0 %collective-permute-done.35 = bf16[256,256]{1,0:T(8,128)(2,1)S(1)} collective-permute-done((bf16[256,256]{1,0:T(8,128)(2,1)S(1)}, bf16[256,256]{1,0:T(8,128)(2,1)S(1)}, u32[]{:S(2)}, u32[]{:S(2)}) %collective-permute-start.35) | collective-permute-done | bytes 131104 | tf_op jit(solution)/shard_map/ppermute | solution.py:117
  169.9 4.4 %collective-permute-done.36 = bf16[256,256]{1,0:T(8,128)(2,1)S(1)} collective-permute-done((bf16[256,256]{1,0:T(8,128)(2,1)S(1)}, bf16[256,256]{1,0:T(8,128)(2,1)S(1)}, u32[]{:S(2)}, u32[]{:S(2)}) %collective-permute-start.36) | collective-permute-done | bytes 131104 | tf_op jit(solution)/shard_map/ppermute | solution.py:117
  174.4 2.8 %collective-permute-done.37 = bf16[256,256]{1,0:T(8,128)(2,1)S(1)} collective-permute-done((bf16[256,256]{1,0:T(8,128)(2,1)S(1)}, bf16[256,256]{1,0:T(8,128)(2,1)S(1)}, u32[]{:S(2)}, u32[]{:S(2)}) %collective-permute-start.37) | collective-permute-done | bytes 131104 | tf_op jit(solution)/shard_map/ppermute | solution.py:117
  177.2 2.1 %add_bitcast_fusion = (f32[1,1,256,256]{3,2,1,0:T(8,128)}, bf16[256,256]{1,0:T(8,128)(2,1)}) fusion(f32[256,256]{1,0:T(8,128)S(1)} %copy-done.16, f32[256,256]{1,0:T(8,128)S(1)} %copy-done.12, f32[256,256]{1,0:T(8,128)S(1)} %copy-done.10, f32[256]{0:T(256)S(1)} %bitcast.52, f32[256]{0:T(256)S(1)} %broadcast_multiply_fusion, f32[256]{0:T(256)S(1)} %bitcast.56, ...), kind=kLoop, calls=%fused_computation.91 | loop fusion | flops 5177344 | bytes 2100224 | tf_op jit(solution)/shard_map/broadcast_in_dim | solution.py:150
  (68 shorter events, 10.3 us)
Async XLA Ops:
  0.6 13.4 %collective-permute-start.1 = (bf16[1024,256]{1,0:T(8,128)(2,1)}, bf16[1024,256]{1,0:T(8,128)(2,1)S(1)}, u32[]{:S(2)}, u32[]{:S(2)}) collective-permute-start(bf16[1024,256]{1,0:T(8,128)(2,1)} %bitcast.43), channel_id=1, source_target_pairs={{1,0},{2,1},{3,2},{4,3},{5,4},{6,5},{7,6},{9,8},{10,9},{11,10},{12... | collective-permute-start | bytes 1572872 | tf_op jit(solution)/shard_map/ppermute | solution.py:28
  3.4 13.5 %collective-permute-start = (bf16[1024,256]{1,0:T(8,128)(2,1)}, bf16[1024,256]{1,0:T(8,128)(2,1)S(1)}, u32[]{:S(2)}, u32[]{:S(2)}) collective-permute-start(bf16[1024,256]{1,0:T(8,128)(2,1)} %bitcast.44), channel_id=1, source_target_pairs={{0,1},{1,2},{2,3},{3,4},{4,5},{5,6},{6,7},{8,9},{9,10},{10,11},{11... | collective-permute-start | bytes 1572872 | tf_op jit(solution)/shard_map/ppermute | solution.py:28
  5.4 37.2 %collective-permute-start.6 = (bf16[1024,256]{1,0:T(8,128)(2,1)}, bf16[1024,256]{1,0:T(8,128)(2,1)}, u32[]{:S(2)}, u32[]{:S(2)}) collective-permute-start(bf16[1024,256]{1,0:T(8,128)(2,1)} %bitcast.45), channel_id=1, source_target_pairs={{0,8},{8,16},{16,24},{1,9},{9,17},{17,25},{2,10},{10,18},{18,26},{... | collective-permute-start | bytes 1572872 | tf_op jit(solution)/shard_map/ppermute | solution.py:138
  9.5 57.9 %copy-start.4 = (s32[1,1,3]{2,1,0:T(1,128)S(1)}, s32[1,1,3]{2,1,0:T(1,128)}, u32[]{:S(2)}) copy-start(s32[1,1,3]{2,1,0:T(1,128)} %picks.7) | copy-start | bytes 40
  17.0 1.9 %copy-start = (bf16[1,1024,1536]{2,1,0:T(8,128)(2,1)S(1)}, bf16[1,1024,1536]{2,1,0:T(8,128)(2,1)}, u32[]{:S(2)}) copy-start(bf16[1,1024,1536]{2,1,0:T(8,128)(2,1)} %tile.7) | copy-start | bytes 9437188
  18.8 1.0 copy-start.2
  19.9 0.7 copy-start.3
  20.5 15.7 %copy-start.5 = (f32[1,1,256,256]{3,2,1,0:T(8,128)S(1)}, f32[1,1,256,256]{3,2,1,0:T(8,128)}, u32[]{:S(2)}) copy-start(f32[1,1,256,256]{3,2,1,0:T(8,128)} %param.13) | copy-start | bytes 786436
  20.5 15.7 %copy-start.13 = (f32[1,1,256,256]{3,2,1,0:T(8,128)S(1)}, f32[1,1,256,256]{3,2,1,0:T(8,128)}, u32[]{:S(2)}) copy-start(f32[1,1,256,256]{3,2,1,0:T(8,128)} %param.14) | copy-start | bytes 786436
  20.5 46.9 %copy-start.1 = (bf16[1,1024,1536]{2,1,0:T(8,128)(2,1)S(1)}, bf16[1,1024,1536]{2,1,0:T(8,128)(2,1)}, u32[]{:S(2)}) copy-start(bf16[1,1024,1536]{2,1,0:T(8,128)(2,1)} %tile.7) | copy-start | bytes 9437188
  22.3 10.8 %collective-permute-start.2 = (bf16[256,256]{1,0:T(8,128)(2,1)S(1)}, bf16[256,256]{1,0:T(8,128)(2,1)S(1)}, u32[]{:S(2)}, u32[]{:S(2)}) collective-permute-start(bf16[256,256]{1,0:T(8,128)(2,1)S(1)} %get-tuple-element.31), channel_id=1, source_target_pairs={{0,8},{8,16},{16,24},{24,0},{1,9},{9,17},{17,25},{25,1},{2,10},{10... | collective-permute-start | bytes 393224 | tf_op jit(solution)/shard_map/ppermute | solution.py:117
  24.0 10.5 %collective-permute-start.3 = (bf16[256,256]{1,0:T(8,128)(2,1)S(1)}, bf16[256,256]{1,0:T(8,128)(2,1)S(1)}, u32[]{:S(2)}, u32[]{:S(2)}) collective-permute-start(bf16[256,256]{1,0:T(8,128)(2,1)S(1)} %get-tuple-element.32), channel_id=1, source_target_pairs={{0,16},{8,24},{16,0},{24,8},{1,17},{9,25},{17,1},{25,9},{2,18},{10... | collective-permute-start | bytes 393224 | tf_op jit(solution)/shard_map/ppermute | solution.py:117
  25.2 11.1 %collective-permute-start.4 = (bf16[256,256]{1,0:T(8,128)(2,1)S(1)}, bf16[256,256]{1,0:T(8,128)(2,1)S(1)}, u32[]{:S(2)}, u32[]{:S(2)}) collective-permute-start(bf16[256,256]{1,0:T(8,128)(2,1)S(1)} %get-tuple-element.33), channel_id=1, source_target_pairs={{0,24},{8,0},{16,8},{24,16},{1,25},{9,1},{17,9},{25,17},{2,26},{10... | collective-permute-start | bytes 393224 | tf_op jit(solution)/shard_map/ppermute | solution.py:117
  38.0 10.1 %collective-permute-start.5 = (bf16[256,256]{1,0:T(8,128)(2,1)S(1)}, bf16[256,256]{1,0:T(8,128)(2,1)}, u32[]{:S(2)}, u32[]{:S(2)}) collective-permute-start(bf16[256,256]{1,0:T(8,128)(2,1)S(1)} %get-tuple-element.65), channel_id=1, source_target_pairs={{8,0},{9,1},{10,2},{11,3},{12,4},{13,5},{14,6},{15,7}} | collective-permute-start | bytes 393224 | tf_op jit(solution)/shard_map/ppermute | solution.py:142
  39.9 9.3 %collective-permute-start.9 = (bf16[256,256]{1,0:T(8,128)(2,1)S(1)}, bf16[256,256]{1,0:T(8,128)(2,1)}, u32[]{:S(2)}, u32[]{:S(2)}) collective-permute-start(bf16[256,256]{1,0:T(8,128)(2,1)S(1)} %get-tuple-element.65), channel_id=1, source_target_pairs={{24,0},{25,1},{26,2},{27,3},{28,4},{29,5},{30,6},{31,7}} | collective-permute-start | bytes 393224 | tf_op jit(solution)/shard_map/ppermute | solution.py:142
  41.2 8.0 %collective-permute-start.8 = (bf16[256,256]{1,0:T(8,128)(2,1)S(1)}, bf16[256,256]{1,0:T(8,128)(2,1)}, u32[]{:S(2)}, u32[]{:S(2)}) collective-permute-start(bf16[256,256]{1,0:T(8,128)(2,1)S(1)} %get-tuple-element.65), channel_id=1, source_target_pairs={{16,0},{17,1},{18,2},{19,3},{20,4},{21,5},{22,6},{23,7}} | collective-permute-start | bytes 393224 | tf_op jit(solution)/shard_map/ppermute | solution.py:142
  49.2 34.2 %copy-start.6 = (f32[1,1,256,256]{3,2,1,0:T(8,128)S(1)}, f32[1,1,256,256]{3,2,1,0:T(8,128)}, u32[]{:S(2)}) copy-start(f32[1,1,256,256]{3,2,1,0:T(8,128)} %param.13) | copy-start | bytes 786436
  49.2 34.2 %copy-start.14 = (f32[1,1,256,256]{3,2,1,0:T(8,128)S(1)}, f32[1,1,256,256]{3,2,1,0:T(8,128)}, u32[]{:S(2)}) copy-start(f32[1,1,256,256]{3,2,1,0:T(8,128)} %param.14) | copy-start | bytes 786436
  49.2 34.2 %copy-start.15 = (f32[256,256]{1,0:T(8,128)S(1)}, f32[256,256]{1,0:T(8,128)}, u32[]{:S(2)}) copy-start(f32[256,256]{1,0:T(8,128)} %get-tuple-element.66) | copy-start | bytes 786436
  50.4 10.3 %collective-permute-start.12 = (bf16[512,256]{1,0:T(8,128)(2,1)S(1)}, bf16[512,256]{1,0:T(8,128)(2,1)S(1)}, u32[]{:S(2)}, u32[]{:S(2)}) collective-permute-start(bf16[512,256]{1,0:T(8,128)(2,1)S(1)} %maximum_select_fusion.refs_3_), channel_id=1, source_target_pairs={{1,0},{2,1},{3,2},{4,3},{5,4},{6,5},{7,6},{9,8},{10,9},{11,10},{12... | collective-permute-start | bytes 786440 | tf_op jit(solution)/shard_map/ppermute | solution.py:28
  52.4 10.6 %collective-permute-start.10 = (bf16[512,256]{1,0:T(8,128)(2,1)S(1)}, bf16[512,256]{1,0:T(8,128)(2,1)S(1)}, u32[]{:S(2)}, u32[]{:S(2)}) collective-permute-start(bf16[512,256]{1,0:T(8,128)(2,1)S(1)} %maximum_select_fusion.refs_3_), channel_id=1, source_target_pairs={{0,1},{1,2},{2,3},{3,4},{4,5},{5,6},{6,7},{8,9},{9,10},{10,11},{11... | collective-permute-start | bytes 786440 | tf_op jit(solution)/shard_map/ppermute | solution.py:28
  54.8 9.9 %collective-permute-start.11 = (bf16[512,256]{1,0:T(8,128)(2,1)S(1)}, bf16[512,256]{1,0:T(8,128)(2,1)S(1)}, u32[]{:S(2)}, u32[]{:S(2)}) collective-permute-start(bf16[512,256]{1,0:T(8,128)(2,1)S(1)} %slice_select_fusion.2.refs_2_), channel_id=1, source_target_pairs={{1,0},{2,1},{3,2},{4,3},{5,4},{6,5},{7,6},{9,8},{10,9},{11,10},{12... | collective-permute-start | bytes 786440 | tf_op jit(solution)/shard_map/ppermute | solution.py:28
  58.8 8.6 %collective-permute-start.7 = (bf16[512,256]{1,0:T(8,128)(2,1)S(1)}, bf16[512,256]{1,0:T(8,128)(2,1)S(1)}, u32[]{:S(2)}, u32[]{:S(2)}) collective-permute-start(bf16[512,256]{1,0:T(8,128)(2,1)S(1)} %slice_select_fusion.2.refs_2_), channel_id=1, source_target_pairs={{0,1},{1,2},{2,3},{3,4},{4,5},{5,6},{6,7},{8,9},{9,10},{10,11},{11... | collective-permute-start | bytes 786440 | tf_op jit(solution)/shard_map/ppermute | solution.py:28
  69.2 9.0 %collective-permute-start.13 = (bf16[256,256]{1,0:T(8,128)(2,1)S(1)}, bf16[256,256]{1,0:T(8,128)(2,1)S(1)}, u32[]{:S(2)}, u32[]{:S(2)}) collective-permute-start(bf16[256,256]{1,0:T(8,128)(2,1)S(1)} %get-tuple-element.39), channel_id=1, source_target_pairs={{0,8},{8,16},{16,24},{24,0},{1,9},{9,17},{17,25},{25,1},{2,10},{10... | collective-permute-start | bytes 393224 | tf_op jit(solution)/shard_map/ppermute | solution.py:117
  69.3 11.7 %collective-permute-start.14 = (bf16[256,256]{1,0:T(8,128)(2,1)S(1)}, bf16[256,256]{1,0:T(8,128)(2,1)S(1)}, u32[]{:S(2)}, u32[]{:S(2)}) collective-permute-start(bf16[256,256]{1,0:T(8,128)(2,1)S(1)} %get-tuple-element.40), channel_id=1, source_target_pairs={{0,16},{8,24},{16,0},{24,8},{1,17},{9,25},{17,1},{25,9},{2,18},{10... | collective-permute-start | bytes 393224 | tf_op jit(solution)/shard_map/ppermute | solution.py:117
  74.2 9.2 %collective-permute-start.15 = (bf16[256,256]{1,0:T(8,128)(2,1)S(1)}, bf16[256,256]{1,0:T(8,128)(2,1)S(1)}, u32[]{:S(2)}, u32[]{:S(2)}) collective-permute-start(bf16[256,256]{1,0:T(8,128)(2,1)S(1)} %get-tuple-element.41), channel_id=1, source_target_pairs={{0,24},{8,0},{16,8},{24,16},{1,25},{9,1},{17,9},{25,17},{2,26},{10... | collective-permute-start | bytes 393224 | tf_op jit(solution)/shard_map/ppermute | solution.py:117
  74.2 20.2 %collective-permute-start.17 = (bf16[1024,256]{1,0:T(8,128)(2,1)S(1)}, bf16[1024,256]{1,0:T(8,128)(2,1)S(1)}, u32[]{:S(2)}, u32[]{:S(2)}) collective-permute-start(bf16[1024,256]{1,0:T(8,128)(2,1)S(1)} %pad_maximum_fusion), channel_id=1, source_target_pairs={{0,8},{8,16},{16,24},{1,9},{9,17},{17,25},{2,10},{10,18},{18,26},{... | collective-permute-start | bytes 1572872 | tf_op jit(solution)/shard_map/ppermute | solution.py:138
  85.2 9.3 %collective-permute-start.16 = (bf16[256,256]{1,0:T(8,128)(2,1)S(1)}, bf16[256,256]{1,0:T(8,128)(2,1)S(1)}, u32[]{:S(2)}, u32[]{:S(2)}) collective-permute-start(bf16[256,256]{1,0:T(8,128)(2,1)S(1)} %get-tuple-element.62), channel_id=1, source_target_pairs={{8,0},{9,1},{10,2},{11,3},{12,4},{13,5},{14,6},{15,7}} | collective-permute-start | bytes 393224 | tf_op jit(solution)/shard_map/ppermute | solution.py:142
  86.6 8.7 %collective-permute-start.20 = (bf16[256,256]{1,0:T(8,128)(2,1)S(1)}, bf16[256,256]{1,0:T(8,128)(2,1)}, u32[]{:S(2)}, u32[]{:S(2)}) collective-permute-start(bf16[256,256]{1,0:T(8,128)(2,1)S(1)} %get-tuple-element.62), channel_id=1, source_target_pairs={{24,0},{25,1},{26,2},{27,3},{28,4},{29,5},{30,6},{31,7}} | collective-permute-start | bytes 393224 | tf_op jit(solution)/shard_map/ppermute | solution.py:142
  88.0 7.4 %collective-permute-start.19 = (bf16[256,256]{1,0:T(8,128)(2,1)S(1)}, bf16[256,256]{1,0:T(8,128)(2,1)}, u32[]{:S(2)}, u32[]{:S(2)}) collective-permute-start(bf16[256,256]{1,0:T(8,128)(2,1)S(1)} %get-tuple-element.62), channel_id=1, source_target_pairs={{16,0},{17,1},{18,2},{19,3},{20,4},{21,5},{22,6},{23,7}} | collective-permute-start | bytes 393224 | tf_op jit(solution)/shard_map/ppermute | solution.py:142
  94.4 0.8 copy-start.18
  95.3 34.5 %copy-start.7 = (f32[1,1,256,256]{3,2,1,0:T(8,128)S(1)}, f32[1,1,256,256]{3,2,1,0:T(8,128)}, u32[]{:S(2)}) copy-start(f32[1,1,256,256]{3,2,1,0:T(8,128)} %param.13) | copy-start | bytes 786436
  95.3 34.5 %copy-start.9 = (f32[256,256]{1,0:T(8,128)S(1)}, f32[256,256]{1,0:T(8,128)}, u32[]{:S(2)}) copy-start(f32[256,256]{1,0:T(8,128)} %get-tuple-element.63) | copy-start | bytes 786436
  95.4 34.5 %copy-start.11 = (f32[256,256]{1,0:T(8,128)S(1)}, f32[256,256]{1,0:T(8,128)}, u32[]{:S(2)}) copy-start(f32[256,256]{1,0:T(8,128)} %get-tuple-element.64) | copy-start | bytes 786436
  96.6 11.0 %collective-permute-start.23 = (bf16[512,256]{1,0:T(8,128)(2,1)S(1)}, bf16[512,256]{1,0:T(8,128)(2,1)S(1)}, u32[]{:S(2)}, u32[]{:S(2)}) collective-permute-start(bf16[512,256]{1,0:T(8,128)(2,1)S(1)} %maximum_select_fusion.1.refs_3_), channel_id=1, source_target_pairs={{1,0},{2,1},{3,2},{4,3},{5,4},{6,5},{7,6},{9,8},{10,9},{11,10},{12... | collective-permute-start | bytes 786440 | tf_op jit(solution)/shard_map/ppermute | solution.py:28
  99.2 10.3 %collective-permute-start.21 = (bf16[512,256]{1,0:T(8,128)(2,1)S(1)}, bf16[512,256]{1,0:T(8,128)(2,1)S(1)}, u32[]{:S(2)}, u32[]{:S(2)}) collective-permute-start(bf16[512,256]{1,0:T(8,128)(2,1)S(1)} %maximum_select_fusion.1.refs_3_), channel_id=1, source_target_pairs={{0,1},{1,2},{2,3},{3,4},{4,5},{5,6},{6,7},{8,9},{9,10},{10,11},{11... | collective-permute-start | bytes 786440 | tf_op jit(solution)/shard_map/ppermute | solution.py:28
  101.2 11.1 %collective-permute-start.22 = (bf16[512,256]{1,0:T(8,128)(2,1)S(1)}, bf16[512,256]{1,0:T(8,128)(2,1)S(1)}, u32[]{:S(2)}, u32[]{:S(2)}) collective-permute-start(bf16[512,256]{1,0:T(8,128)(2,1)S(1)} %slice_select_fusion.1.refs_2_), channel_id=1, source_target_pairs={{1,0},{2,1},{3,2},{4,3},{5,4},{6,5},{7,6},{9,8},{10,9},{11,10},{12... | collective-permute-start | bytes 786440 | tf_op jit(solution)/shard_map/ppermute | solution.py:28
  105.7 8.6 %collective-permute-start.18 = (bf16[512,256]{1,0:T(8,128)(2,1)S(1)}, bf16[512,256]{1,0:T(8,128)(2,1)S(1)}, u32[]{:S(2)}, u32[]{:S(2)}) collective-permute-start(bf16[512,256]{1,0:T(8,128)(2,1)S(1)} %slice_select_fusion.1.refs_2_), channel_id=1, source_target_pairs={{0,1},{1,2},{2,3},{3,4},{4,5},{5,6},{6,7},{8,9},{9,10},{10,11},{11... | collective-permute-start | bytes 786440 | tf_op jit(solution)/shard_map/ppermute | solution.py:28
  116.1 8.6 %collective-permute-start.24 = (bf16[256,256]{1,0:T(8,128)(2,1)S(1)}, bf16[256,256]{1,0:T(8,128)(2,1)S(1)}, u32[]{:S(2)}, u32[]{:S(2)}) collective-permute-start(bf16[256,256]{1,0:T(8,128)(2,1)S(1)} %get-tuple-element.47), channel_id=1, source_target_pairs={{0,8},{8,16},{16,24},{24,0},{1,9},{9,17},{17,25},{25,1},{2,10},{10... | collective-permute-start | bytes 393224 | tf_op jit(solution)/shard_map/ppermute | solution.py:117
  116.1 11.5 %collective-permute-start.25 = (bf16[256,256]{1,0:T(8,128)(2,1)S(1)}, bf16[256,256]{1,0:T(8,128)(2,1)S(1)}, u32[]{:S(2)}, u32[]{:S(2)}) collective-permute-start(bf16[256,256]{1,0:T(8,128)(2,1)S(1)} %get-tuple-element.48), channel_id=1, source_target_pairs={{0,16},{8,24},{16,0},{24,8},{1,17},{9,25},{17,1},{25,9},{2,18},{10... | collective-permute-start | bytes 393224 | tf_op jit(solution)/shard_map/ppermute | solution.py:117
  120.7 9.2 %collective-permute-start.26 = (bf16[256,256]{1,0:T(8,128)(2,1)S(1)}, bf16[256,256]{1,0:T(8,128)(2,1)S(1)}, u32[]{:S(2)}, u32[]{:S(2)}) collective-permute-start(bf16[256,256]{1,0:T(8,128)(2,1)S(1)} %get-tuple-element.49), channel_id=1, source_target_pairs={{0,24},{8,0},{16,8},{24,16},{1,25},{9,1},{17,9},{25,17},{2,26},{10... | collective-permute-start | bytes 393224 | tf_op jit(solution)/shard_map/ppermute | solution.py:117
  120.7 20.2 %collective-permute-start.28 = (bf16[1024,256]{1,0:T(8,128)(2,1)S(1)}, bf16[1024,256]{1,0:T(8,128)(2,1)S(1)}, u32[]{:S(2)}, u32[]{:S(2)}) collective-permute-start(bf16[1024,256]{1,0:T(8,128)(2,1)S(1)} %pad_maximum_fusion.1), channel_id=1, source_target_pairs={{0,8},{8,16},{16,24},{1,9},{9,17},{17,25},{2,10},{10,18},{18,26},{... | collective-permute-start | bytes 1572872 | tf_op jit(solution)/shard_map/ppermute | solution.py:138
  131.7 9.3 %collective-permute-start.27 = (bf16[256,256]{1,0:T(8,128)(2,1)S(1)}, bf16[256,256]{1,0:T(8,128)(2,1)S(1)}, u32[]{:S(2)}, u32[]{:S(2)}) collective-permute-start(bf16[256,256]{1,0:T(8,128)(2,1)S(1)} %get-tuple-element.60), channel_id=1, source_target_pairs={{8,0},{9,1},{10,2},{11,3},{12,4},{13,5},{14,6},{15,7}} | collective-permute-start | bytes 393224 | tf_op jit(solution)/shard_map/ppermute | solution.py:142
  133.2 8.7 %collective-permute-start.31 = (bf16[256,256]{1,0:T(8,128)(2,1)S(1)}, bf16[256,256]{1,0:T(8,128)(2,1)}, u32[]{:S(2)}, u32[]{:S(2)}) collective-permute-start(bf16[256,256]{1,0:T(8,128)(2,1)S(1)} %get-tuple-element.60), channel_id=1, source_target_pairs={{24,0},{25,1},{26,2},{27,3},{28,4},{29,5},{30,6},{31,7}} | collective-permute-start | bytes 393224 | tf_op jit(solution)/shard_map/ppermute | solution.py:142
  134.5 7.4 %collective-permute-start.30 = (bf16[256,256]{1,0:T(8,128)(2,1)S(1)}, bf16[256,256]{1,0:T(8,128)(2,1)}, u32[]{:S(2)}, u32[]{:S(2)}) collective-permute-start(bf16[256,256]{1,0:T(8,128)(2,1)S(1)} %get-tuple-element.60), channel_id=1, source_target_pairs={{16,0},{17,1},{18,2},{19,3},{20,4},{21,5},{22,6},{23,7}} | collective-permute-start | bytes 393224 | tf_op jit(solution)/shard_map/ppermute | solution.py:142
  140.9 0.8 copy-start.17
  141.8 35.4 %copy-start.8 = (f32[1,1,256,256]{3,2,1,0:T(8,128)S(1)}, f32[1,1,256,256]{3,2,1,0:T(8,128)}, u32[]{:S(2)}) copy-start(f32[1,1,256,256]{3,2,1,0:T(8,128)} %param.13) | copy-start | bytes 786436
  141.8 35.4 %copy-start.10 = (f32[256,256]{1,0:T(8,128)S(1)}, f32[256,256]{1,0:T(8,128)}, u32[]{:S(2)}) copy-start(f32[256,256]{1,0:T(8,128)} %get-tuple-element.63) | copy-start | bytes 786436
  141.9 35.3 %copy-start.12 = (f32[256,256]{1,0:T(8,128)S(1)}, f32[256,256]{1,0:T(8,128)}, u32[]{:S(2)}) copy-start(f32[256,256]{1,0:T(8,128)} %get-tuple-element.64) | copy-start | bytes 786436
  141.9 35.3 %copy-start.16 = (f32[256,256]{1,0:T(8,128)S(1)}, f32[256,256]{1,0:T(8,128)}, u32[]{:S(2)}) copy-start(f32[256,256]{1,0:T(8,128)} %get-tuple-element.61) | copy-start | bytes 786436
  143.1 11.8 %collective-permute-start.34 = (bf16[512,256]{1,0:T(8,128)(2,1)S(1)}, bf16[512,256]{1,0:T(8,128)(2,1)S(1)}, u32[]{:S(2)}, u32[]{:S(2)}) collective-permute-start(bf16[512,256]{1,0:T(8,128)(2,1)S(1)} %maximum_select_fusion.2.refs_3_), channel_id=1, source_target_pairs={{1,0},{2,1},{3,2},{4,3},{5,4},{6,5},{7,6},{9,8},{10,9},{11,10},{12... | collective-permute-start | bytes 786440 | tf_op jit(solution)/shard_map/ppermute | solution.py:28
  146.5 11.4 %collective-permute-start.32 = (bf16[512,256]{1,0:T(8,128)(2,1)S(1)}, bf16[512,256]{1,0:T(8,128)(2,1)S(1)}, u32[]{:S(2)}, u32[]{:S(2)}) collective-permute-start(bf16[512,256]{1,0:T(8,128)(2,1)S(1)} %maximum_select_fusion.2.refs_3_), channel_id=1, source_target_pairs={{0,1},{1,2},{2,3},{3,4},{4,5},{5,6},{6,7},{8,9},{9,10},{10,11},{11... | collective-permute-start | bytes 786440 | tf_op jit(solution)/shard_map/ppermute | solution.py:28
  148.5 10.6 %collective-permute-start.33 = (bf16[512,256]{1,0:T(8,128)(2,1)S(1)}, bf16[512,256]{1,0:T(8,128)(2,1)S(1)}, u32[]{:S(2)}, u32[]{:S(2)}) collective-permute-start(bf16[512,256]{1,0:T(8,128)(2,1)S(1)} %slice_select_fusion.refs_2_), channel_id=1, source_target_pairs={{1,0},{2,1},{3,2},{4,3},{5,4},{6,5},{7,6},{9,8},{10,9},{11,10},{12... | collective-permute-start | bytes 786440 | tf_op jit(solution)/shard_map/ppermute | solution.py:28
  153.0 8.6 %collective-permute-start.29 = (bf16[512,256]{1,0:T(8,128)(2,1)S(1)}, bf16[512,256]{1,0:T(8,128)(2,1)S(1)}, u32[]{:S(2)}, u32[]{:S(2)}) collective-permute-start(bf16[512,256]{1,0:T(8,128)(2,1)S(1)} %slice_select_fusion.refs_2_), channel_id=1, source_target_pairs={{0,1},{1,2},{2,3},{3,4},{4,5},{5,6},{6,7},{8,9},{9,10},{10,11},{11... | collective-permute-start | bytes 786440 | tf_op jit(solution)/shard_map/ppermute | solution.py:28
  163.4 6.6 %collective-permute-start.35 = (bf16[256,256]{1,0:T(8,128)(2,1)S(1)}, bf16[256,256]{1,0:T(8,128)(2,1)S(1)}, u32[]{:S(2)}, u32[]{:S(2)}) collective-permute-start(bf16[256,256]{1,0:T(8,128)(2,1)S(1)} %get-tuple-element.55), channel_id=1, source_target_pairs={{0,8},{8,16},{16,24},{24,0},{1,9},{9,17},{17,25},{25,1},{2,10},{10... | collective-permute-start | bytes 393224 | tf_op jit(solution)/shard_map/ppermute | solution.py:117
  163.5 10.9 %collective-permute-start.36 = (bf16[256,256]{1,0:T(8,128)(2,1)S(1)}, bf16[256,256]{1,0:T(8,128)(2,1)S(1)}, u32[]{:S(2)}, u32[]{:S(2)}) collective-permute-start(bf16[256,256]{1,0:T(8,128)(2,1)S(1)} %get-tuple-element.56), channel_id=1, source_target_pairs={{0,16},{8,24},{16,0},{24,8},{1,17},{9,25},{17,1},{25,9},{2,18},{10... | collective-permute-start | bytes 393224 | tf_op jit(solution)/shard_map/ppermute | solution.py:117
  168.0 9.2 %collective-permute-start.37 = (bf16[256,256]{1,0:T(8,128)(2,1)S(1)}, bf16[256,256]{1,0:T(8,128)(2,1)S(1)}, u32[]{:S(2)}, u32[]{:S(2)}) collective-permute-start(bf16[256,256]{1,0:T(8,128)(2,1)S(1)} %get-tuple-element.57), channel_id=1, source_target_pairs={{0,24},{8,0},{16,8},{24,16},{1,25},{9,1},{17,9},{25,17},{2,26},{10... | collective-permute-start | bytes 393224 | tf_op jit(solution)/shard_map/ppermute | solution.py:117

commit v7 on v5

v7 whole, which is shorter than its diff:
```python
import functools

import jax
import jax.numpy as jnp
from jax import lax
from jax.experimental import pallas as pl
from jax.experimental.pallas import tpu as pltpu
from jax.sharding import PartitionSpec as P


STEPS = 4
NEWTON = 3

damping = 0.5
time_step = 0.25
creep_square = 0.01

ANY = pl.BlockSpec(memory_space=pl.ANY)
VMEM = pl.BlockSpec(memory_space=pltpu.VMEM)
PARAMS = pltpu.CompilerParams(vmem_limit_bytes=32 * 1024 * 1024)


def exchange(value, planes):
    count = lax.axis_size("elem")
    up = [(i * count + j, i * count + j + 1) for i in planes for j in range(count - 1)]
    down = [(j, i) for i, j in up]
    axes = ("lag", "elem")
    return lax.ppermute(value, axes, up), lax.ppermute(value, axes, down)


def fetch(windows, picks, live, sources, sems):
    slots = sems.shape[0]
    block = sources.shape[0] // slots
    alive = live[0]
    for k in range(slots):
        spot = sources.at[pl.ds(k * block, block)]
        pick = picks[0, 0, k]
        for holds, refs in windows:
            per = refs[1].shape[0] // block
            start = pl.multiple_of(lax.rem(pick, per) * block, block)
            for which, ref in enumerate(refs):

                @pl.when(holds & (k < alive) & (lax.div(pick, per) == which))
                def _():
                    pltpu.make_async_copy(ref.at[pl.ds(start, block)], spot, sems.at[k]).start()

    for k in range(slots):
        spot = sources.at[pl.ds(k * block, block)]

        @pl.when(k >= alive)
        def _():
            spot[...] = jnp.zeros(spot.shape, spot.dtype)

        @pl.when(k < alive)
        def _():
            pltpu.make_async_copy(windows[0][1][1].at[pl.ds(0, block)], spot, sems.at[k]).wait()


def rows_kernel(lags, rows, least, count, picks, live, tile, *refs):
    window, outs, sources, sems = refs[: 3 * count], refs[3 * count : 3 * count + lags], refs[-2], refs[-1]
    me = lax.axis_index("lag")
    windows = [window[3 * i : 3 * i + 3] for i in range(count)]
    holds = [me == least + i for i in range(count - 1)] + [me >= least + count - 1]

    @pl.when(me >= least)
    def _():
        fetch(list(zip(holds, windows)), picks, live, sources, sems)
        for d in range(lags):
            first = pl.multiple_of(lax.rem(me + d, lags) * rows, rows)
            part = jnp.dot(tile[0, pl.ds(first, rows), :], sources[...], preferred_element_type=jnp.float32)
            outs[d][...] = part.astype(outs[d].dtype)

    if least:

        @pl.when(me < least)
        def _():
            outs[0][...] = jnp.zeros(outs[0].shape, outs[0].dtype)


def product_by_rows(picks, live, tile, least, windows, lags):
    rows, cols = tile.shape[1] // lags, windows[0][0].shape[1]
    kinds = [jnp.float32] + [jnp.bfloat16] * (lags - 1)
    return pl.pallas_call(
        functools.partial(rows_kernel, lags, rows, least, len(windows)),
        grid_spec=pltpu.PrefetchScalarGridSpec(
            num_scalar_prefetch=2,
            grid=(1,),
            in_specs=[VMEM] + [ANY] * (3 * len(windows)),
            out_specs=[VMEM] * lags,
            scratch_shapes=[
                pltpu.VMEM((tile.shape[2], cols), windows[0][0].dtype),
                pltpu.SemaphoreType.DMA((picks.shape[2],)),
            ],
        ),
        out_shape=[jax.ShapeDtypeStruct((rows, cols), kind) for kind in kinds],
        compiler_params=PARAMS,
        cost_estimate=pl.CostEstimate(
            flops=2 * tile.size * cols, bytes_accessed=2 * (tile.size + 4 * rows * lags * cols), transcendentals=0
        ),
        name="product_by_rows",
    )(picks, live, tile, *[part for window in windows for part in window])


def own_kernel(lags, picks, live, tile, *refs):
    moved, window, out = refs[: lags - 1], refs[lags - 1 : lags + 2], refs[lags + 2]
    mine, sources, tile_sem, sems = refs[lags + 3 :]
    me = lax.axis_index("lag")
    rows = mine.shape[0]
    for d, ref in enumerate([tile.at[0, pl.ds(0, rows)], *moved]):

        @pl.when(me == d)
        def _():
            pltpu.make_async_copy(ref, mine, tile_sem).start()

    fetch([(me >= 0, window)], picks, live, sources, sems)
    pltpu.make_async_copy(tile.at[0, pl.ds(0, rows)], mine, tile_sem).wait()
    out[...] = jnp.dot(mine[...], sources[...], preferred_element_type=jnp.float32)


def own_product(picks, live, tile, moved, window):
    rows, cols = moved[0].shape[0], window[0].shape[1]
    return pl.pallas_call(
        functools.partial(own_kernel, len(moved) + 1),
        grid_spec=pltpu.PrefetchScalarGridSpec(
            num_scalar_prefetch=2,
            grid=(1,),
            in_specs=[ANY] * (4 + len(moved)),
            out_specs=VMEM,
            scratch_shapes=[
                pltpu.VMEM(moved[0].shape, tile.dtype),
                pltpu.VMEM((tile.shape[2], cols), window[0].dtype),
                pltpu.SemaphoreType.DMA(()),
                pltpu.SemaphoreType.DMA((picks.shape[2],)),
            ],
        ),
        out_shape=jax.ShapeDtypeStruct((rows, cols), jnp.float32),
        compiler_params=PARAMS,
        cost_estimate=pl.CostEstimate(
            flops=2 * moved[0].size * cols, bytes_accessed=2 * (moved[0].size + 3 * window[0].size), transcendentals=0
        ),
        name="own_product",
    )(picks, live, tile, *moved, *window)


def newton(load, state, ratio, strength):
    scale = 0.5 * jnp.exp(ratio * state)
    product = strength * scale
    velocity = load / (product + damping)
    for _ in range(NEWTON):
        scaled = scale * velocity
        magnitude = jnp.abs(scaled)
        root = jnp.sqrt(magnitude * magnitude + 1.0)
        positive = jnp.log(magnitude + root)
        arc = jnp.where(scaled < 0.0, -positive, positive)
        residual = strength * arc + damping * velocity - load
        velocity = velocity - residual / (product / root + damping)
    return velocity


def evolved(state, speed_of):
    return state + time_step * (jnp.exp(-state) - jnp.sqrt(speed_of * speed_of + creep_square))


def scatter_sum(parts, least):
    lags = len(parts)
    total = parts[0]
    for d in range(1, lags):
        route = [(i, (i + d) % lags) for i in range(least, lags)]
        total = total + lax.ppermute(parts[d], "lag", route).astype(jnp.float32)
    return total


def settle_friction(shear_load, state, coef_a, coef_b, sigma):
    velocity = newton(shear_load, state, coef_b / coef_a, sigma * coef_a)
    return velocity.astype(jnp.bfloat16), evolved(state, velocity)


def shards(kernel_tiles, shell_index, cone_blocks, history, prestress, log_state, fric_a, fric_b, normal_stress):
    lags = lax.axis_size("lag")
    local = (shell_index, cone_blocks, kernel_tiles)
    field, state, rows = history[0], log_state[0, 0], prestress.shape[2]
    columns = [c[0, 0][:, None] for c in (fric_a, fric_b, normal_stress)]

    def window_of(own, least):
        below, above = exchange(own, range(least, lags))
        return below, own, above

    window = window_of(field, 0)
    shifted = lax.ppermute(field, "lag", [(i, i + 1) for i in range(lags - 1)])
    moved = [lax.ppermute(kernel_tiles[0, d * rows : (d + 1) * rows], "lag", [(0, d)]) for d in range(1, lags)]
    table = jnp.concatenate([shell_index[0, 0], cone_blocks])
    table = lax.all_gather(table, "lag", axis=0, tiled=False)[0]
    newest = (table[None, None, :-1], table[-1:], kernel_tiles, moved)
    traction = scatter_sum(product_by_rows(*local, 0, [window], lags), 0)
    rates, state = settle_friction(prestress[0, 0] + traction, state, *columns)

    known = []
    for step in range(1, STEPS):
        windows = known + [window_of(shifted, step)]
        first = lax.all_gather(rates, "lag", axis=0, tiled=True)
        window = window_of(first, 0)
        parts = product_by_rows(*local, 1, windows, lags)
        traction = scatter_sum(parts, 1)
        if step + 1 < STEPS:
            shifted = lax.ppermute(shifted, "lag", [(i, i + 1) for i in range(step, lags - 1)])
        traction = traction + own_product(*newest, window)
        rates, state = settle_friction(prestress[0, 0] + traction, state, *columns)
        known = [window] + known
    return rates[None, None], state[None, None]


def solution(mesh):
    in_specs = (
        P("lag", "elem", None),
        P("lag", "elem", None),
        P("lag"),
        P("lag", "elem", None),
        P("elem", "lag", None, None),
        P("elem", "lag", None, None),
        P("elem", "lag", None),
        P("elem", "lag", None),
        P("elem", "lag", None),
    )
    out_specs = (P("elem", "lag", None, None), P("elem", "lag", None, None))
    return jax.shard_map(shards, mesh=mesh, in_specs=in_specs, out_specs=out_specs, check_vma=False)
```

time: 187 us -> 240 us (1.28)
  blocking collectives: 62.2 us -> 103 us
  starting transfers between devices: 45.6 us -> 60 us
  waiting for transfers between devices: 60.3 us -> 48.9 us
  local copies, waits for them, and re-layouts: 3.59 us -> 8.83 us
  Pallas kernels: 6.7 us -> 9.86 us
    all_gather x3, blocking collectives: 62.2 us -> 96.2 us  [shards(): first = lax.all_gather(rates, 'lag', axis=0, tiled=True)]
    ppermute x3 -> x6, waiting for transfers between devices: 0.01 us -> 19.5 us  [the longest x1 19.4 us: shards(): shifted = lax.ppermute(field, 'lag', [(i, i + 1) for i in range(lags - 1)])]
    ppermute x8 -> x14, waiting for transfers between devices: 26 us -> 8.11 us  [exchange(): return (lax.ppermute(value, axes, up), lax.ppermute(value, axes, down))]
    ppermute x12, waiting for transfers between devices: 34.3 us -> 21.3 us  [scatter_sum(): total = total + lax.ppermute(parts[d], 'lag', route).astype(jnp.float32)]
    ppermute x3 -> x6, starting transfers between devices: 10.2 us -> 17.1 us  [the longest x3 12.9 us: shards(): lax.ppermute(kernel_tiles[0, d * rows:(d + 1) * rows], 'lag', [(0, d)])]
    unnamed x0 -> x1, blocking collectives: none -> 6.6 us
    ppermute x8 -> x14, starting transfers between devices: 22.3 us -> 26.6 us  [exchange(): return (lax.ppermute(value, axes, up), lax.ppermute(value, axes, down))]
    pallas_call x4 -> x7, Pallas kernels: 6.7 us -> 9.86 us  [the longest x3 6.37 us: own_product(): pl.pallas_call(functools.partial(own_kernel, len(moved) + 1), grid_spec=p...]
  transfers between devices with their start and end apart: 23 -> 32, of which waited for: 16 -> 10; matrix products, arithmetic and copies ran while one was open for 2% -> 3% of each run, Pallas kernels for 1% -> 4%
where the time goes in v7:
time: 240 us; the launch traced here: 239 us
  blocking collectives  103 us (43%)
  starting transfers between devices  60 us (25%)
  waiting for transfers between devices  48.9 us (20%)
  Pallas kernels  9.86 us (4%)
  local copies, waits for them, and re-layouts  8.83 us (4%)
  other arithmetic  6.24 us (3%)
  between operations  2.51 us (1%)
    all_gather x3, blocking collectives, shards(): first = lax.all_gather(rates, 'lag', axis=0, tiled=True)  96.2 us
    ppermute x14, starting transfers between devices, exchange(): return (lax.ppermute(value, axes, up), lax.ppermute(value, axes, down))  26.6 us
    ppermute x12, waiting for transfers between devices, scatter_sum(): total = total + lax.ppermute(parts[d], 'lag', route).astype(jnp.float32)  21.3 us
    ppermute x1, waiting for transfers between devices, shards(): shifted = lax.ppermute(field, 'lag', [(i, i + 1) for i in range(lags - 1)])  19.4 us
    ppermute x12, starting transfers between devices, scatter_sum(): total = total + lax.ppermute(parts[d], 'lag', route).astype(jnp.float32)  16.3 us
    ppermute x3, starting transfers between devices, shards(): lax.ppermute(kernel_tiles[0, d * rows:(d + 1) * rows], 'lag', [(0, d)])  12.9 us
    ppermute x14, waiting for transfers between devices, exchange(): return (lax.ppermute(value, axes, up), lax.ppermute(value, axes, down))  8.11 us
    unnamed x1, blocking collectives  6.6 us
  transfers between devices with their start and end apart: 32, of which 10 were waited for; matrix products, arithmetic and copies ran while one was open for 3% of the time, Pallas kernels for 4%

profile of v7, /device:TPU:2, one launch (start us, length us, event | category | flops | bytes accessed | tf_op | source)
XLA Modules:
  0.0 239.2 jit_solution(5290614892770693261)
XLA Ops:
  0.7 2.2 collective-permute-start.9
  2.9 3.6 %collective-permute-start.10 = (bf16[1024,256]{1,0:T(8,128)(2,1)}, bf16[1024,256]{1,0:T(8,128)(2,1)S(1)}, u32[]{:S(2)}, u32[]{:S(2)}) collective-permute-start(bf16[1024,256]{1,0:T(8,128)(2,1)} %bitcast.55), channel_id=1, source_target_pairs={{1,0},{2,1},{3,2},{4,3},{5,4},{6,5},{7,6},{9,8},{10,9},{11,10},{12... | collective-permute-start | bytes 1572872 | tf_op jit(solution)/shard_map/ppermute | solution.py:28
  6.5 2.9 %slice_bitcast_fusion = (bf16[256,1536]{1,0:T(8,128)(2,1)}, bf16[256,1536]{1,0:T(8,128)(2,1)}, bf16[256,1536]{1,0:T(8,128)(2,1)S(1)}) fusion(bf16[1,1024,1536]{2,1,0:T(8,128)(2,1)} %tile.13), kind=kLoop, calls=%fused_computation | loop fusion | bytes 4718592 | tf_op jit(solution)/shard_map/squeeze | solution.py:190
  9.4 3.6 %collective-permute-start.6 = (bf16[256,1536]{1,0:T(8,128)(2,1)S(1)}, bf16[256,1536]{1,0:T(8,128)(2,1)S(1)}, u32[]{:S(2)}, u32[]{:S(2)}) collective-permute-start(bf16[256,1536]{1,0:T(8,128)(2,1)S(1)} %get-tuple-element.45), channel_id=1, source_target_pairs={{0,8},{1,9},{2,10},{3,11},{4,12},{5,13},{6,14},{7,15}} | collective-permute-start | bytes 2359304 | tf_op jit(solution)/shard_map/ppermute | solution.py:190
  13.1 2.1 collective-permute-start
  15.9 0.5 collective-permute-done.10.refs_2_
  16.4 1.7 product_by_rows.5
  18.1 3.7 %collective-permute-start.13 = (bf16[256,256]{1,0:T(8,128)(2,1)S(1)}, bf16[256,256]{1,0:T(8,128)(2,1)S(1)}, u32[]{:S(2)}, u32[]{:S(2)}) collective-permute-start(bf16[256,256]{1,0:T(8,128)(2,1)S(1)} %get-tuple-element.25), channel_id=1, source_target_pairs={{0,24},{8,0},{16,8},{24,16},{1,25},{9,1},{17,9},{25,17},{2,26},{10... | collective-permute-start | bytes 393224 | tf_op jit(solution)/shard_map/ppermute | solution.py:169
  21.8 1.0 collective-permute-start.11
  22.8 19.4 %collective-permute-done.refs_1_ = bf16[1024,256]{1,0:T(8,128)(2,1)} collective-permute-done((bf16[1024,256]{1,0:T(8,128)(2,1)S(1)}, bf16[1024,256]{1,0:T(8,128)(2,1)}, u32[]{:S(2)}, u32[]{:S(2)}) %collective-permute-start) | collective-permute-done | bytes 524320 | tf_op jit(solution)/shard_map/ppermute | solution.py:189
  42.2 2.2 collective-permute-start.7
  44.4 0.6 collective-permute-done.13
  45.0 7.1 %collective-permute-start.8 = (bf16[256,1536]{1,0:T(8,128)(2,1)}, bf16[256,1536]{1,0:T(8,128)(2,1)}, u32[]{:S(2)}, u32[]{:S(2)}) collective-permute-start(bf16[256,1536]{1,0:T(8,128)(2,1)} %get-tuple-element.43), channel_id=1, source_target_pairs={{0,24},{1,25},{2,26},{3,27},{4,28},{5,29},{6,30},{7,31}} | collective-permute-start | bytes 2359304 | tf_op jit(solution)/shard_map/ppermute | solution.py:190
  52.1 0.7 collective-permute-start.1
  52.8 0.7 collective-permute-start.2
  53.5 0.9 copy-done.1
  54.4 1.4 collective-permute-start.18
  55.8 1.7 fusion.69
  57.5 51.6 %all_gather.17.refs_4_.refs_1_ = bf16[1024,256]{1,0:T(8,128)(2,1)} all-gather(bf16[256,256]{1,0:T(8,128)(2,1)S(1)} %get-tuple-element.41), channel_id=1, replica_groups=mesh['lag'=4,'elem'=8] {'lag'}, dimensions={0}, use_global_device_ids=true | all-gather | bytes 655360 | tf_op jit(solution)/shard_map/all_gather | solution.py:200
  109.2 0.8 copy-done.4
  110.0 1.9 collective-permute-start.14
  111.9 0.8 copy-done.6
  112.8 3.6 %collective-permute-start.15 = (bf16[1024,256]{1,0:T(8,128)(2,1)}, bf16[1024,256]{1,0:T(8,128)(2,1)}, u32[]{:S(2)}, u32[]{:S(2)}) collective-permute-start(bf16[1024,256]{1,0:T(8,128)(2,1)} %all_gather.17.refs_4_.refs_1_), channel_id=1, source_target_pairs={{1,0},{2,1},{3,2},{4,3},{5,4},{6,5},{7,6},{9,8},{10,9},{11,10},{12... | collective-permute-start | bytes 1572872 | tf_op jit(solution)/shard_map/ppermute | solution.py:28
  116.4 0.6 dynamic-slice
  117.8 6.6 %all-reduce = s32[16]{0:T(128)S(1)} all-reduce(s32[16]{0:T(128)S(1)} %add_dynamic-update-slice_fusion), channel_id=2, replica_groups=mesh['lag'=4,'elem'=8] {'lag'}, use_global_device_ids=true, to_apply=%add | all-reduce | flops 16 | bytes 128
  124.5 1.0 copy-done.5
  125.6 1.0 copy-done.7
  126.6 0.6 product_by_rows.4
  127.2 1.3 collective-permute-start.5
  128.5 1.3 collective-permute-start.4
  129.8 1.3 collective-permute-start.3
  131.2 0.6 slice.23
  131.7 0.7 collective-permute-start.25
  132.4 0.7 collective-permute-start.26
  133.2 2.8 %own_product.3 = f32[256,256]{1,0:T(8,128)S(1)} custom-call(s32[1,1,3]{2,1,0:T(1,128)S(1)} %slice_bitcast_fusion.3.picks, s32[1]{0:T(128)} %bitcast.5.live, bf16[1,1024,1536]{2,1,0:T(8,128)(2,1)S(1)} %copy-done, bf16[256,1536]{1,0:T(8,128)(2,1)S(1)} %copy-done.2, bf16[256,1536]{1,0:T(8,128)(2,1)} %collective-permute-done.7.refs_1_, ...), custom_call_target="tpu_custom_call" | custom-call | flops 201326592 | bytes 2359296 | tf_op jit(solution)/shard_map/own_product/pallas_call | solution.py:122
  136.0 0.7 collective-permute-start.19
  136.7 5.8 %collective-permute-done.4 = bf16[256,256]{1,0:T(8,128)(2,1)S(1)} collective-permute-done((bf16[256,256]{1,0:T(8,128)(2,1)S(1)}, bf16[256,256]{1,0:T(8,128)(2,1)S(1)}, u32[]{:S(2)}, u32[]{:S(2)}) %collective-permute-start.4) | collective-permute-done | bytes 131104 | tf_op jit(solution)/shard_map/ppermute | solution.py:169
  142.5 1.1 fusion.67
  143.6 29.7 %all_gather.18.refs_1_.refs_4_ = bf16[1024,256]{1,0:T(8,128)(2,1)S(1)} all-gather(bf16[256,256]{1,0:T(8,128)(2,1)S(1)} %get-tuple-element.38), channel_id=1, replica_groups=mesh['lag'=4,'elem'=8] {'lag'}, dimensions={0}, use_global_device_ids=true | all-gather | bytes 655360 | tf_op jit(solution)/shard_map/all_gather | solution.py:200
  173.4 1.9 collective-permute-start.16
  175.3 3.6 %collective-permute-start.17 = (bf16[1024,256]{1,0:T(8,128)(2,1)S(1)}, bf16[1024,256]{1,0:T(8,128)(2,1)S(1)}, u32[]{:S(2)}, u32[]{:S(2)}) collective-permute-start(bf16[1024,256]{1,0:T(8,128)(2,1)S(1)} %all_gather.18.refs_1_.refs_4_), channel_id=1, source_target_pairs={{1,0},{2,1},{3,2},{4,3},{5,4},{6,5},{7,6},{9,8},{10,9},{11,10},{12... | collective-permute-start | bytes 1572872 | tf_op jit(solution)/shard_map/ppermute | solution.py:28
  179.0 0.6 product_by_rows.7
  179.6 1.3 collective-permute-start.29
  180.9 1.3 collective-permute-start.28
  182.2 1.3 collective-permute-start.27
  183.5 0.4 collective-permute-done.16.refs_0_.refs_3_
  183.9 0.7 collective-permute-start.20
  184.5 2.4 %collective-permute-done.17.refs_2_.refs_5_ = bf16[1024,256]{1,0:T(8,128)(2,1)S(1)} collective-permute-done((bf16[1024,256]{1,0:T(8,128)(2,1)S(1)}, bf16[1024,256]{1,0:T(8,128)(2,1)S(1)}, u32[]{:S(2)}, u32[]{:S(2)}) %collective-permute-start.17) | collective-permute-done | bytes 524320 | tf_op jit(solution)/shard_map/ppermute | solution.py:28
  186.9 0.7 collective-permute-start.21
  187.6 1.8 own_product.4
  189.4 8.0 %collective-permute-done.28 = bf16[256,256]{1,0:T(8,128)(2,1)S(1)} collective-permute-done((bf16[256,256]{1,0:T(8,128)(2,1)S(1)}, bf16[256,256]{1,0:T(8,128)(2,1)S(1)}, u32[]{:S(2)}, u32[]{:S(2)}) %collective-permute-start.28) | collective-permute-done | bytes 131104 | tf_op jit(solution)/shard_map/ppermute | solution.py:169
  197.5 1.1 fusion.65
  198.6 14.9 %all_gather.19.refs_4_ = bf16[1024,256]{1,0:T(8,128)(2,1)S(1)} all-gather(bf16[256,256]{1,0:T(8,128)(2,1)S(1)} %get-tuple-element.36), channel_id=1, replica_groups=mesh['lag'=4,'elem'=8] {'lag'}, dimensions={0}, use_global_device_ids=true | all-gather | bytes 655360 | tf_op jit(solution)/shard_map/all_gather | solution.py:200
  213.5 1.9 collective-permute-start.30
  215.4 3.6 %collective-permute-start.31 = (bf16[1024,256]{1,0:T(8,128)(2,1)S(1)}, bf16[1024,256]{1,0:T(8,128)(2,1)S(1)}, u32[]{:S(2)}, u32[]{:S(2)}) collective-permute-start(bf16[1024,256]{1,0:T(8,128)(2,1)S(1)} %all_gather.19.refs_4_), channel_id=1, source_target_pairs={{1,0},{2,1},{3,2},{4,3},{5,4},{6,5},{7,6},{9,8},{10,9},{11,10},{12... | collective-permute-start | bytes 1572872 | tf_op jit(solution)/shard_map/ppermute | solution.py:28
  219.0 0.6 product_by_rows.6
  219.7 1.3 collective-permute-start.24
  221.0 1.3 collective-permute-start.23
  222.3 1.3 collective-permute-start.22
  223.6 0.4 collective-permute-done.30.refs_3_
  223.9 4.5 %collective-permute-done.31.refs_5_ = bf16[1024,256]{1,0:T(8,128)(2,1)S(1)} collective-permute-done((bf16[1024,256]{1,0:T(8,128)(2,1)S(1)}, bf16[1024,256]{1,0:T(8,128)(2,1)S(1)}, u32[]{:S(2)}, u32[]{:S(2)}) %collective-permute-start.31) | collective-permute-done | bytes 524320 | tf_op jit(solution)/shard_map/ppermute | solution.py:28
  228.4 1.8 own_product.5
  230.2 6.9 %collective-permute-done.23 = bf16[256,256]{1,0:T(8,128)(2,1)S(1)} collective-permute-done((bf16[256,256]{1,0:T(8,128)(2,1)S(1)}, bf16[256,256]{1,0:T(8,128)(2,1)S(1)}, u32[]{:S(2)}, u32[]{:S(2)}) %collective-permute-start.23) | collective-permute-done | bytes 131104 | tf_op jit(solution)/shard_map/ppermute | solution.py:169
  237.1 2.1 add_bitcast_fusion
  (58 shorter events, 0.4 us)
Async XLA Ops:
  0.6 12.5 %copy-start.3 = (bf16[1,1024,256]{2,1,0:T(8,128)(2,1)S(1)}, bf16[1,1024,256]{2,1,0:T(8,128)(2,1)}, u32[]{:S(2)}) copy-start(bf16[1,1024,256]{2,1,0:T(8,128)(2,1)} %param.12) | copy-start | bytes 1572868
  0.6 15.8 %copy-start = (bf16[1,1024,1536]{2,1,0:T(8,128)(2,1)S(1)}, bf16[1,1024,1536]{2,1,0:T(8,128)(2,1)}, u32[]{:S(2)}) copy-start(bf16[1,1024,1536]{2,1,0:T(8,128)(2,1)} %tile.13) | copy-start | bytes 9437188
  0.7 15.2 %copy-start.13 = (f32[1,1,256]{2,1,0:T(1,128)S(1)}, f32[1,1,256]{2,1,0:T(1,128)}, u32[]{:S(2)}) copy-start(f32[1,1,256]{2,1,0:T(1,128)} %param.16) | copy-start | bytes 3076
  0.7 15.2 %copy-start.14 = (f32[1,1,256]{2,1,0:T(1,128)S(1)}, f32[1,1,256]{2,1,0:T(1,128)}, u32[]{:S(2)}) copy-start(f32[1,1,256]{2,1,0:T(1,128)} %param.15) | copy-start | bytes 3076
  0.7 15.2 %copy-start.15 = (f32[1,1,256]{2,1,0:T(1,128)S(1)}, f32[1,1,256]{2,1,0:T(1,128)}, u32[]{:S(2)}) copy-start(f32[1,1,256]{2,1,0:T(1,128)} %param.17) | copy-start | bytes 3076
  0.7 15.7 %copy-start.8 = (s32[1,1,3]{2,1,0:T(1,128)S(1)}, s32[1,1,3]{2,1,0:T(1,128)}, u32[]{:S(2)}) copy-start(s32[1,1,3]{2,1,0:T(1,128)} %picks.7) | copy-start | bytes 40
  0.7 15.2 %collective-permute-start.9 = (bf16[1024,256]{1,0:T(8,128)(2,1)}, bf16[1024,256]{1,0:T(8,128)(2,1)S(1)}, u32[]{:S(2)}, u32[]{:S(2)}) collective-permute-start(bf16[1024,256]{1,0:T(8,128)(2,1)} %bitcast.54), channel_id=1, source_target_pairs={{0,1},{1,2},{2,3},{3,4},{4,5},{5,6},{6,7},{8,9},{9,10},{10,11},{11... | collective-permute-start | bytes 1572872 | tf_op jit(solution)/shard_map/ppermute | solution.py:28
  2.9 13.5 %collective-permute-start.10 = (bf16[1024,256]{1,0:T(8,128)(2,1)}, bf16[1024,256]{1,0:T(8,128)(2,1)S(1)}, u32[]{:S(2)}, u32[]{:S(2)}) collective-permute-start(bf16[1024,256]{1,0:T(8,128)(2,1)} %bitcast.55), channel_id=1, source_target_pairs={{1,0},{2,1},{3,2},{4,3},{5,4},{6,5},{7,6},{9,8},{10,9},{11,10},{12... | collective-permute-start | bytes 1572872 | tf_op jit(solution)/shard_map/ppermute | solution.py:28
  9.4 46.4 %copy-start.9 = (f32[1,1,256,256]{3,2,1,0:T(8,128)S(1)}, f32[1,1,256,256]{3,2,1,0:T(8,128)}, u32[]{:S(2)}) copy-start(f32[1,1,256,256]{3,2,1,0:T(8,128)} %param.13) | copy-start | bytes 786436
  9.4 46.4 %copy-start.10 = (f32[1,1,256,256]{3,2,1,0:T(8,128)S(1)}, f32[1,1,256,256]{3,2,1,0:T(8,128)}, u32[]{:S(2)}) copy-start(f32[1,1,256,256]{3,2,1,0:T(8,128)} %param.14) | copy-start | bytes 786436
  9.4 44.0 %collective-permute-start.6 = (bf16[256,1536]{1,0:T(8,128)(2,1)S(1)}, bf16[256,1536]{1,0:T(8,128)(2,1)S(1)}, u32[]{:S(2)}, u32[]{:S(2)}) collective-permute-start(bf16[256,1536]{1,0:T(8,128)(2,1)S(1)} %get-tuple-element.45), channel_id=1, source_target_pairs={{0,8},{1,9},{2,10},{3,11},{4,12},{5,13},{6,14},{7,15}} | collective-permute-start | bytes 2359304 | tf_op jit(solution)/shard_map/ppermute | solution.py:190
  13.1 29.1 %collective-permute-start = (bf16[1024,256]{1,0:T(8,128)(2,1)S(1)}, bf16[1024,256]{1,0:T(8,128)(2,1)}, u32[]{:S(2)}, u32[]{:S(2)}) collective-permute-start(bf16[1024,256]{1,0:T(8,128)(2,1)S(1)} %bitcast.56), channel_id=1, source_target_pairs={{0,8},{8,16},{16,24},{1,9},{9,17},{17,25},{2,10},{10,18},{18,26},{... | collective-permute-start | bytes 1572872 | tf_op jit(solution)/shard_map/ppermute | solution.py:189
  15.9 100.5 %copy-start.16 = (u32[32]{0:T(128)S(1)}, u32[32]{0:T(128)}, u32[]{:S(2)}) copy-start(u32[32]{0:T(128)} %constant.21) | copy-start | bytes 388
  18.1 26.9 %collective-permute-start.13 = (bf16[256,256]{1,0:T(8,128)(2,1)S(1)}, bf16[256,256]{1,0:T(8,128)(2,1)S(1)}, u32[]{:S(2)}, u32[]{:S(2)}) collective-permute-start(bf16[256,256]{1,0:T(8,128)(2,1)S(1)} %get-tuple-element.25), channel_id=1, source_target_pairs={{0,24},{8,0},{16,8},{24,16},{1,25},{9,1},{17,9},{25,17},{2,26},{10... | collective-permute-start | bytes 393224 | tf_op jit(solution)/shard_map/ppermute | solution.py:169
  21.8 30.3 %collective-permute-start.12 = (bf16[256,256]{1,0:T(8,128)(2,1)S(1)}, bf16[256,256]{1,0:T(8,128)(2,1)S(1)}, u32[]{:S(2)}, u32[]{:S(2)}) collective-permute-start(bf16[256,256]{1,0:T(8,128)(2,1)S(1)} %get-tuple-element.24), channel_id=1, source_target_pairs={{0,16},{8,24},{16,0},{24,8},{1,17},{9,25},{17,1},{25,9},{2,18},{10... | collective-permute-start | bytes 393224 | tf_op jit(solution)/shard_map/ppermute | solution.py:169
  21.8 31.0 %collective-permute-start.11 = (bf16[256,256]{1,0:T(8,128)(2,1)S(1)}, bf16[256,256]{1,0:T(8,128)(2,1)S(1)}, u32[]{:S(2)}, u32[]{:S(2)}) collective-permute-start(bf16[256,256]{1,0:T(8,128)(2,1)S(1)} %get-tuple-element.23), channel_id=1, source_target_pairs={{0,8},{8,16},{16,24},{24,0},{1,9},{9,17},{17,25},{25,1},{2,10},{10... | collective-permute-start | bytes 393224 | tf_op jit(solution)/shard_map/ppermute | solution.py:169
  42.2 85.0 %collective-permute-start.7 = (bf16[256,1536]{1,0:T(8,128)(2,1)}, bf16[256,1536]{1,0:T(8,128)(2,1)}, u32[]{:S(2)}, u32[]{:S(2)}) collective-permute-start(bf16[256,1536]{1,0:T(8,128)(2,1)} %get-tuple-element.44), channel_id=1, source_target_pairs={{0,16},{1,17},{2,18},{3,19},{4,20},{5,21},{6,22},{7,23}} | collective-permute-start | bytes 2359304 | tf_op jit(solution)/shard_map/ppermute | solution.py:190
  45.0 83.5 %collective-permute-start.8 = (bf16[256,1536]{1,0:T(8,128)(2,1)}, bf16[256,1536]{1,0:T(8,128)(2,1)}, u32[]{:S(2)}, u32[]{:S(2)}) collective-permute-start(bf16[256,1536]{1,0:T(8,128)(2,1)} %get-tuple-element.43), channel_id=1, source_target_pairs={{0,24},{1,25},{2,26},{3,27},{4,28},{5,29},{6,30},{7,31}} | collective-permute-start | bytes 2359304 | tf_op jit(solution)/shard_map/ppermute | solution.py:190
  52.1 57.1 %collective-permute-start.1 = (bf16[1024,256]{1,0:T(8,128)(2,1)}, bf16[1024,256]{1,0:T(8,128)(2,1)S(1)}, u32[]{:S(2)}, u32[]{:S(2)}) collective-permute-start(bf16[1024,256]{1,0:T(8,128)(2,1)} %collective-permute-done.refs_1_), channel_id=1, source_target_pairs={{8,9},{9,10},{10,11},{11,12},{12,13},{13,14},{14,15},{16,17},{17,1... | collective-permute-start | bytes 1572872 | tf_op jit(solution)/shard_map/ppermute | solution.py:28
  52.8 59.1 %collective-permute-start.2 = (bf16[1024,256]{1,0:T(8,128)(2,1)}, bf16[1024,256]{1,0:T(8,128)(2,1)S(1)}, u32[]{:S(2)}, u32[]{:S(2)}) collective-permute-start(bf16[1024,256]{1,0:T(8,128)(2,1)} %collective-permute-done.refs_1_), channel_id=1, source_target_pairs={{9,8},{10,9},{11,10},{12,11},{13,12},{14,13},{15,14},{17,16},{18,1... | collective-permute-start | bytes 1572872 | tf_op jit(solution)/shard_map/ppermute | solution.py:28
  53.5 0.9 copy-start.1
  54.4 75.4 %collective-permute-start.18 = (bf16[1024,256]{1,0:T(8,128)(2,1)}, bf16[1024,256]{1,0:T(8,128)(2,1)}, u32[]{:S(2)}, u32[]{:S(2)}) collective-permute-start(bf16[1024,256]{1,0:T(8,128)(2,1)} %collective-permute-done.refs_1_), channel_id=1, source_target_pairs={{8,16},{16,24},{9,17},{17,25},{10,18},{18,26},{11,19},{19,27},{12,... | collective-permute-start | bytes 1572872 | tf_op jit(solution)/shard_map/ppermute | solution.py:205
  109.2 0.8 copy-start.4
  110.0 21.8 %collective-permute-start.14 = (bf16[1024,256]{1,0:T(8,128)(2,1)}, bf16[1024,256]{1,0:T(8,128)(2,1)}, u32[]{:S(2)}, u32[]{:S(2)}) collective-permute-start(bf16[1024,256]{1,0:T(8,128)(2,1)} %all_gather.17.refs_4_.refs_1_), channel_id=1, source_target_pairs={{0,1},{1,2},{2,3},{3,4},{4,5},{5,6},{6,7},{8,9},{9,10},{10,11},{11... | collective-permute-start | bytes 1572872 | tf_op jit(solution)/shard_map/ppermute | solution.py:28
  111.9 0.9 copy-start.6
  112.8 19.7 %collective-permute-start.15 = (bf16[1024,256]{1,0:T(8,128)(2,1)}, bf16[1024,256]{1,0:T(8,128)(2,1)}, u32[]{:S(2)}, u32[]{:S(2)}) collective-permute-start(bf16[1024,256]{1,0:T(8,128)(2,1)} %all_gather.17.refs_4_.refs_1_), channel_id=1, source_target_pairs={{1,0},{2,1},{3,2},{4,3},{5,4},{6,5},{7,6},{9,8},{10,9},{11,10},{12... | collective-permute-start | bytes 1572872 | tf_op jit(solution)/shard_map/ppermute | solution.py:28
  124.5 1.0 copy-start.5
  125.6 1.0 copy-start.7
  126.6 6.5 %copy-start.2 = (bf16[256,1536]{1,0:T(8,128)(2,1)S(1)}, bf16[256,1536]{1,0:T(8,128)(2,1)}, u32[]{:S(2)}) copy-start(bf16[256,1536]{1,0:T(8,128)(2,1)} %copy-done.1) | copy-start | bytes 2359300
  127.2 8.7 %collective-permute-start.5 = (bf16[256,256]{1,0:T(8,128)(2,1)S(1)}, bf16[256,256]{1,0:T(8,128)(2,1)S(1)}, u32[]{:S(2)}, u32[]{:S(2)}) collective-permute-start(bf16[256,256]{1,0:T(8,128)(2,1)S(1)} %get-tuple-element.21), channel_id=1, source_target_pairs={{8,0},{16,8},{24,16},{9,1},{17,9},{25,17},{10,2},{18,10},{26,18},{... | collective-permute-start | bytes 393224 | tf_op jit(solution)/shard_map/ppermute | solution.py:169
  128.5 14.0 %collective-permute-start.4 = (bf16[256,256]{1,0:T(8,128)(2,1)S(1)}, bf16[256,256]{1,0:T(8,128)(2,1)S(1)}, u32[]{:S(2)}, u32[]{:S(2)}) collective-permute-start(bf16[256,256]{1,0:T(8,128)(2,1)S(1)} %get-tuple-element.20), channel_id=1, source_target_pairs={{8,24},{16,0},{24,8},{9,25},{17,1},{25,9},{10,26},{18,2},{26,10},{... | collective-permute-start | bytes 393224 | tf_op jit(solution)/shard_map/ppermute | solution.py:169
  129.8 12.7 %collective-permute-start.3 = (bf16[256,256]{1,0:T(8,128)(2,1)S(1)}, bf16[256,256]{1,0:T(8,128)(2,1)S(1)}, u32[]{:S(2)}, u32[]{:S(2)}) collective-permute-start(bf16[256,256]{1,0:T(8,128)(2,1)S(1)} %get-tuple-element.19), channel_id=1, source_target_pairs={{8,16},{16,24},{24,0},{9,17},{17,25},{25,1},{10,18},{18,26},{26,2}... | collective-permute-start | bytes 393224 | tf_op jit(solution)/shard_map/ppermute | solution.py:169
  131.7 47.2 %collective-permute-start.25 = (bf16[1024,256]{1,0:T(8,128)(2,1)}, bf16[1024,256]{1,0:T(8,128)(2,1)S(1)}, u32[]{:S(2)}, u32[]{:S(2)}) collective-permute-start(bf16[1024,256]{1,0:T(8,128)(2,1)} %collective-permute-done.18.refs_4_), channel_id=1, source_target_pairs={{16,17},{17,18},{18,19},{19,20},{20,21},{21,22},{22,23},{24,25},{2... | collective-permute-start | bytes 1572872 | tf_op jit(solution)/shard_map/ppermute | solution.py:28
  132.4 46.5 %collective-permute-start.26 = (bf16[1024,256]{1,0:T(8,128)(2,1)}, bf16[1024,256]{1,0:T(8,128)(2,1)S(1)}, u32[]{:S(2)}, u32[]{:S(2)}) collective-permute-start(bf16[1024,256]{1,0:T(8,128)(2,1)} %collective-permute-done.18.refs_4_), channel_id=1, source_target_pairs={{17,16},{18,17},{19,18},{20,19},{21,20},{22,21},{23,22},{25,24},{2... | collective-permute-start | bytes 1572872 | tf_op jit(solution)/shard_map/ppermute | solution.py:28
  133.1 9.3 %copy-start.11 = (f32[1,1,256,256]{3,2,1,0:T(8,128)S(1)}, f32[1,1,256,256]{3,2,1,0:T(8,128)}, u32[]{:S(2)}) copy-start(f32[1,1,256,256]{3,2,1,0:T(8,128)} %param.14) | copy-start | bytes 786436
  133.2 9.3 %copy-start.12 = (f32[256,256]{1,0:T(8,128)S(1)}, f32[256,256]{1,0:T(8,128)}, u32[]{:S(2)}) copy-start(f32[256,256]{1,0:T(8,128)} %get-tuple-element.42) | copy-start | bytes 786436
  136.0 46.2 %collective-permute-start.19 = (bf16[1024,256]{1,0:T(8,128)(2,1)}, bf16[1024,256]{1,0:T(8,128)(2,1)S(1)}, u32[]{:S(2)}, u32[]{:S(2)}) collective-permute-start(bf16[1024,256]{1,0:T(8,128)(2,1)} %collective-permute-done.18.refs_4_), channel_id=1, source_target_pairs={{16,24},{17,25},{18,26},{19,27},{20,28},{21,29},{22,30},{23,31}} | collective-permute-start | bytes 1572872 | tf_op jit(solution)/shard_map/ppermute | solution.py:205
  173.4 10.5 %collective-permute-start.16 = (bf16[1024,256]{1,0:T(8,128)(2,1)S(1)}, bf16[1024,256]{1,0:T(8,128)(2,1)S(1)}, u32[]{:S(2)}, u32[]{:S(2)}) collective-permute-start(bf16[1024,256]{1,0:T(8,128)(2,1)S(1)} %all_gather.18.refs_1_.refs_4_), channel_id=1, source_target_pairs={{0,1},{1,2},{2,3},{3,4},{4,5},{5,6},{6,7},{8,9},{9,10},{10,11},{11... | collective-permute-start | bytes 1572872 | tf_op jit(solution)/shard_map/ppermute | solution.py:28
  175.3 11.7 %collective-permute-start.17 = (bf16[1024,256]{1,0:T(8,128)(2,1)S(1)}, bf16[1024,256]{1,0:T(8,128)(2,1)S(1)}, u32[]{:S(2)}, u32[]{:S(2)}) collective-permute-start(bf16[1024,256]{1,0:T(8,128)(2,1)S(1)} %all_gather.18.refs_1_.refs_4_), channel_id=1, source_target_pairs={{1,0},{2,1},{3,2},{4,3},{5,4},{6,5},{7,6},{9,8},{10,9},{11,10},{12... | collective-permute-start | bytes 1572872 | tf_op jit(solution)/shard_map/ppermute | solution.py:28
  179.6 9.9 %collective-permute-start.29 = (bf16[256,256]{1,0:T(8,128)(2,1)S(1)}, bf16[256,256]{1,0:T(8,128)(2,1)S(1)}, u32[]{:S(2)}, u32[]{:S(2)}) collective-permute-start(bf16[256,256]{1,0:T(8,128)(2,1)S(1)} %get-tuple-element.33), channel_id=1, source_target_pairs={{8,0},{16,8},{24,16},{9,1},{17,9},{25,17},{10,2},{18,10},{26,18},{... | collective-permute-start | bytes 393224 | tf_op jit(solution)/shard_map/ppermute | solution.py:169
  180.9 16.6 %collective-permute-start.28 = (bf16[256,256]{1,0:T(8,128)(2,1)S(1)}, bf16[256,256]{1,0:T(8,128)(2,1)S(1)}, u32[]{:S(2)}, u32[]{:S(2)}) collective-permute-start(bf16[256,256]{1,0:T(8,128)(2,1)S(1)} %get-tuple-element.32), channel_id=1, source_target_pairs={{8,24},{16,0},{24,8},{9,25},{17,1},{25,9},{10,26},{18,2},{26,10},{... | collective-permute-start | bytes 393224 | tf_op jit(solution)/shard_map/ppermute | solution.py:169
  182.2 15.3 %collective-permute-start.27 = (bf16[256,256]{1,0:T(8,128)(2,1)S(1)}, bf16[256,256]{1,0:T(8,128)(2,1)S(1)}, u32[]{:S(2)}, u32[]{:S(2)}) collective-permute-start(bf16[256,256]{1,0:T(8,128)(2,1)S(1)} %get-tuple-element.31), channel_id=1, source_target_pairs={{8,16},{16,24},{24,0},{9,17},{17,25},{25,1},{10,18},{18,26},{26,2}... | collective-permute-start | bytes 393224 | tf_op jit(solution)/shard_map/ppermute | solution.py:169
  183.9 35.2 %collective-permute-start.20 = (bf16[1024,256]{1,0:T(8,128)(2,1)S(1)}, bf16[1024,256]{1,0:T(8,128)(2,1)S(1)}, u32[]{:S(2)}, u32[]{:S(2)}) collective-permute-start(bf16[1024,256]{1,0:T(8,128)(2,1)S(1)} %collective-permute-done.19.refs_7_), channel_id=1, source_target_pairs={{24,25},{25,26},{26,27},{27,28},{28,29},{29,30},{30,31}} | collective-permute-start | bytes 1572872 | tf_op jit(solution)/shard_map/ppermute | solution.py:28
  186.9 32.1 %collective-permute-start.21 = (bf16[1024,256]{1,0:T(8,128)(2,1)S(1)}, bf16[1024,256]{1,0:T(8,128)(2,1)S(1)}, u32[]{:S(2)}, u32[]{:S(2)}) collective-permute-start(bf16[1024,256]{1,0:T(8,128)(2,1)S(1)} %collective-permute-done.19.refs_7_), channel_id=1, source_target_pairs={{25,24},{26,25},{27,26},{28,27},{29,28},{30,29},{31,30}} | collective-permute-start | bytes 1572872 | tf_op jit(solution)/shard_map/ppermute | solution.py:28
  213.5 10.5 %collective-permute-start.30 = (bf16[1024,256]{1,0:T(8,128)(2,1)S(1)}, bf16[1024,256]{1,0:T(8,128)(2,1)S(1)}, u32[]{:S(2)}, u32[]{:S(2)}) collective-permute-start(bf16[1024,256]{1,0:T(8,128)(2,1)S(1)} %all_gather.19.refs_4_), channel_id=1, source_target_pairs={{0,1},{1,2},{2,3},{3,4},{4,5},{5,6},{6,7},{8,9},{9,10},{10,11},{11... | collective-permute-start | bytes 1572872 | tf_op jit(solution)/shard_map/ppermute | solution.py:28
  215.4 13.0 %collective-permute-start.31 = (bf16[1024,256]{1,0:T(8,128)(2,1)S(1)}, bf16[1024,256]{1,0:T(8,128)(2,1)S(1)}, u32[]{:S(2)}, u32[]{:S(2)}) collective-permute-start(bf16[1024,256]{1,0:T(8,128)(2,1)S(1)} %all_gather.19.refs_4_), channel_id=1, source_target_pairs={{1,0},{2,1},{3,2},{4,3},{5,4},{6,5},{7,6},{9,8},{10,9},{11,10},{12... | collective-permute-start | bytes 1572872 | tf_op jit(solution)/shard_map/ppermute | solution.py:28
  219.7 10.5 %collective-permute-start.24 = (bf16[256,256]{1,0:T(8,128)(2,1)S(1)}, bf16[256,256]{1,0:T(8,128)(2,1)S(1)}, u32[]{:S(2)}, u32[]{:S(2)}) collective-permute-start(bf16[256,256]{1,0:T(8,128)(2,1)S(1)} %get-tuple-element.29), channel_id=1, source_target_pairs={{8,0},{16,8},{24,16},{9,1},{17,9},{25,17},{10,2},{18,10},{26,18},{... | collective-permute-start | bytes 393224 | tf_op jit(solution)/shard_map/ppermute | solution.py:169
  221.0 16.1 %collective-permute-start.23 = (bf16[256,256]{1,0:T(8,128)(2,1)S(1)}, bf16[256,256]{1,0:T(8,128)(2,1)S(1)}, u32[]{:S(2)}, u32[]{:S(2)}) collective-permute-start(bf16[256,256]{1,0:T(8,128)(2,1)S(1)} %get-tuple-element.28), channel_id=1, source_target_pairs={{8,24},{16,0},{24,8},{9,25},{17,1},{25,9},{10,26},{18,2},{26,10},{... | collective-permute-start | bytes 393224 | tf_op jit(solution)/shard_map/ppermute | solution.py:169
  222.3 14.8 %collective-permute-start.22 = (bf16[256,256]{1,0:T(8,128)(2,1)S(1)}, bf16[256,256]{1,0:T(8,128)(2,1)S(1)}, u32[]{:S(2)}, u32[]{:S(2)}) collective-permute-start(bf16[256,256]{1,0:T(8,128)(2,1)S(1)} %get-tuple-element.27), channel_id=1, source_target_pairs={{8,16},{16,24},{24,0},{9,17},{17,25},{25,1},{10,18},{18,26},{26,2}... | collective-permute-start | bytes 393224 | tf_op jit(solution)/shard_map/ppermute | solution.py:169

commit v8 on v5

--- a/solution.py
+++ b/solution.py
@@ -8,7 +8,6 @@
 from jax.sharding import PartitionSpec as P
 
 
-STEPS = 4
 NEWTON = 3
 
 damping = 0.5
@@ -84,6 +83,80 @@
         ),
         name="product_by_rows",
     )(picks, live, tile, below, own, above)
+
+
+def block_kernel(chunks, planes, high_too, picks, live, tile, below, own, above, stress, *refs):
+    outs, sources, sems = refs[:-2], refs[-2], refs[-1]
+    me = lax.axis_index("lag")
+    rows, height = own.shape[0] // chunks, stress.shape[2]
+    mine = pl.ds(pl.multiple_of(me * height, height), height)
+
+    def write(out):
+        for d in range(chunks):
+            spot = pl.ds(d * rows, rows)
+            part = jnp.dot(tile[0, spot, :], sources[...], preferred_element_type=jnp.float32)
+            out[spot, :] = part.astype(out.dtype)
+        part = jnp.dot(tile[0, mine, :], sources[...], preferred_element_type=jnp.float32)
+        out[mine, :] = (part + stress[0, 0]).astype(out.dtype)
+
+    @pl.when((me >= planes[0]) & (me <= planes[-1]))
+    def _():
+        fetch(picks, live, below, own, above, sources, sems)
+        if high_too:
+
+            @pl.when(me == 0)
+            def _():
+                write(outs[0])
+
+            @pl.when(me > 0)
+            def _():
+                write(outs[1])
+
+        else:
+            write(outs[0])
+
+
+def block_product(picks, live, tile, window, stress, planes, kinds):
+    below, own, above = window
+    chunks = max(1, tile.shape[1] // 256)
+    return pl.pallas_call(
+        functools.partial(block_kernel, chunks, (planes[0], planes[-1]), len(kinds) > 1),
+        grid_spec=pltpu.PrefetchScalarGridSpec(
+            num_scalar_prefetch=2,
+            grid=(1,),
+            in_specs=[VMEM] + [ANY] * 3 + [VMEM],
+            out_specs=[VMEM] * len(kinds),
+            scratch_shapes=[
+                pltpu.VMEM((tile.shape[2], own.shape[1]), own.dtype),
+                pltpu.SemaphoreType.DMA((picks.shape[2],)),
+            ],
+        ),
+        out_shape=[jax.ShapeDtypeStruct(own.shape, kind) for kind in kinds],
+        compiler_params=PARAMS,
+        cost_estimate=pl.CostEstimate(
+            flops=2 * tile.size * own.shape[1], bytes_accessed=2 * (tile.size + 4 * own.size), transcendentals=0
+        ),
+        name="block_product",
+    )(picks, live, tile, below, own, above, stress)
+
+
+def pack_kernel(state, coef_a, coef_b, sigma, tile, field, out):
+    rows = state.shape[2]
+    out[pl.ds(0, rows), :] = state[0, 0]
+    out[pl.ds(rows, 8), :] = jnp.zeros((8, out.shape[1]), out.dtype)
+    out[pl.ds(rows, 1), pl.ds(0, rows)] = coef_b[0] / coef_a[0]
+    out[pl.ds(rows + 1, 1), pl.ds(0, rows)] = sigma[0] * coef_a[0]
+
+
+def pack(state, coef_a, coef_b, sigma, tile, field):
+    return pl.pallas_call(
+        pack_kernel,
+        in_specs=[VMEM] * 4 + [ANY] * 2,
+        out_specs=VMEM,
+        out_shape=jax.ShapeDtypeStruct((state.shape[2] + 8, state.shape[3]), jnp.float32),
+        compiler_params=PARAMS,
+        name="pack",
+    )(state, coef_a, coef_b, sigma, tile, field)
 
 
 def newton(load, state, ratio, strength):
@@ -114,27 +187,82 @@
     return total
 
 
-def settle_friction(shear_load, state, coef_a, coef_b, sigma):
-    velocity = newton(shear_load, state, coef_b / coef_a, sigma * coef_a)
+def settle_friction(shear_load, state, ratio, strength):
+    velocity = newton(shear_load, state, ratio, strength)
     return velocity.astype(jnp.bfloat16), evolved(state, velocity)
+
+
+def tree_to_first(value, lags, least):
+    received, stride = [], 1
+    while stride < lags:
+        route = [(i + stride, i) for i in range(0, lags - stride, 2 * stride) if i + stride >= least]
+        arrived = lax.ppermute(value, "lag", route)
+        if route[0][1] == 0:
+            received.append(arrived)
+        stride *= 2
+        if stride < lags:
+            total = value.astype(jnp.float32) + arrived.astype(jnp.float32)
+            value = lax.optimization_barrier(total.astype(jnp.bfloat16))
+    return received
 
 
 def shards(kernel_tiles, shell_index, cone_blocks, history, prestress, log_state, fric_a, fric_b, normal_stress):
     lags = lax.axis_size("lag")
     me = lax.axis_index("lag")
+    every, rest = list(range(lags)), list(range(1, lags))
     local = (shell_index, cone_blocks, kernel_tiles)
-    field, state = history[0], log_state[0, 0]
-    columns = [c[0, 0][:, None] for c in (fric_a, fric_b, normal_stress)]
-    for step in range(STEPS):
-        below, above = exchange(field, range(lags))
-        if step + 1 < STEPS:
-            older = lax.ppermute(field, "lag", [(i, i + 1) for i in range(lags - 1)])
-        parts = product_by_rows(*local, below, field, above, lags)
-        traction = scatter_sum(parts)
-        rates, state = settle_friction(prestress[0, 0] + traction, state, *columns)
-        if step + 1 < STEPS:
-            newest = lax.all_gather(rates, "lag", axis=0, tiled=True)
-            field = jnp.where(me == 0, newest, older)
+    field = history[0]
+    rows = prestress.shape[2]
+
+    def window_of(own, planes):
+        below, above = exchange(own, planes)
+        return below, own, above
+
+    def block_load(high, *received):
+        load = high
+        for part in received:
+            load = load + part.astype(jnp.float32)
+        return load
+
+    below, own, above = window_of(field, every)
+    packed = pack(log_state, fric_a, fric_b, normal_stress, kernel_tiles, field)
+    packed = [packed] + [lax.ppermute(packed, "lag", [(d, 0)]) for d in rest]
+    once = lax.ppermute(field, "lag", [(i, i + 1) for i in every[:-1]])
+    traction = scatter_sum(product_by_rows(*local, below, own, above, lags))
+    coef_a, coef_b, sigma = (c[0, 0][:, None] for c in (fric_a, fric_b, normal_stress))
+    row_pair = (coef_b / coef_a, sigma * coef_a)
+    rates, _ = settle_friction(prestress[0, 0] + traction, log_state[0, 0], *row_pair)
+    first = lax.all_gather(rates, "lag", axis=0, tiled=True)
+    packed, first = lax.optimization_barrier((packed, first))
+    state = jnp.concatenate([g[:rows] for g in packed], 0)
+    ratio, strength = (jnp.concatenate([g[rows + k, :rows] for g in packed])[:, None] for k in range(2))
+    state = evolved(state, first.astype(jnp.float32))
+
+    kinds = [jnp.float32, jnp.bfloat16]
+    (low,) = block_product(*local, window_of(once, rest), prestress, rest, kinds[1:])
+    base_1 = tree_to_first(low, lags, 1)
+    twice = lax.ppermute(once, "lag", [(i, i + 1) for i in rest[:-1]])
+    (low,) = block_product(*local, window_of(twice, rest[1:]), prestress, rest[1:], kinds[1:])
+    base_2 = tree_to_first(low, lags, 2)
+
+    window = window_of(first, [0, 1])
+    high, low = block_product(*local, window, prestress, [0, 1], kinds)
+    base_2 = base_2 + [lax.ppermute(low, "lag", [(1, 0)])]
+    second, state = settle_friction(block_load(high, *base_1), state, ratio, strength)
+    window = window_of(second, [0])
+    (high,) = block_product(*local, window, prestress, [0], kinds[:1])
+    third, state = settle_friction(block_load(high, *base_2), state, ratio, strength)
+
+    source = jnp.where(me == 0, second, twice)
+    moved = lax.ppermute(source, "lag", [(0, 1)] + [(i, i + 1) for i in every[2:-1]])
+    last = jnp.where(me == 0, third, jnp.where(me == 2, first, moved))
+    below, own, above = window_of(last, every)
+    mine = state[:rows]
+    for d in rest:
+        piece = lax.ppermute(state[d * rows : (d + 1) * rows], "lag", [(0, d)])
+        mine = jnp.where(me == d, piece, mine)
+    traction = scatter_sum(product_by_rows(*local, below, own, above, lags))
+    rates, state = settle_friction(prestress[0, 0] + traction, mine, *row_pair)
     return rates[None, None], state[None, None]
 
 

time: 187 us -> 182 us (0.973)
  blocking collectives: 62.2 us -> 37.8 us
  waiting for transfers between devices: 60.3 us -> 41.2 us
  other arithmetic: 6.18 us -> 20.8 us
  starting transfers between devices: 45.6 us -> 60 us
  Pallas kernels: 6.7 us -> 11.5 us
  local copies, waits for them, and re-layouts: 3.59 us -> 7.42 us
    ppermute x12 -> x6, waiting for transfers between devices: 34.3 us -> 8.65 us  [scatter_sum(): total = total + lax.ppermute(parts[d], 'lag', route).astype(jnp.float32)]
    all_gather x3 -> x1, blocking collectives: 62.2 us -> 37.8 us  [shards(): first = lax.all_gather(rates, 'lag', axis=0, tiled=True)]
    ppermute x3 -> x14, waiting for transfers between devices: 0.01 us -> 16.9 us  [the longest x4 8.3 us: tree_to_first(): arrived = lax.ppermute(value, 'lag', route)]
    ppermute x3 -> x14, starting transfers between devices: 10.2 us -> 21.7 us  [the longest x3 5.28 us: shards(): piece = lax.ppermute(state[d * rows:(d + 1) * rows], 'lag', [(0, d)])]
    ppermute x8 -> x12, waiting for transfers between devices: 26 us -> 15.6 us  [exchange(): return (lax.ppermute(value, axes, up), lax.ppermute(value, axes, down))]
    add x0 -> x1, other arithmetic: none -> 7.64 us  [evolved(): state + time_step * (jnp.exp(-state) - jnp.sqrt(speed_of * speed_of + cre...]
    pallas_call x0 -> x5, Pallas kernels: none -> 6.87 us  [the longest x4 6.84 us: block_product(): pl.pallas_call(functools.partial(block_kernel, chunks, (planes[0], planes...]
    select_n x3 -> x2, other arithmetic: 0.17 us -> 6.39 us  [the longest x1 6.32 us: shards(): source = jnp.where(me == 0, second, twice)]
  transfers between devices with their start and end apart: 23 -> 32, of which waited for: 16 -> 14; matrix products, arithmetic and copies ran while one was open for 2% -> 10% of each run, Pallas kernels for 1% -> 6%
where the time goes in v8:
time: 182 us; the launch traced here: 181 us
  starting transfers between devices  60 us (33%)
  waiting for transfers between devices  41.2 us (23%)
  blocking collectives  37.8 us (21%)
  other arithmetic  20.8 us (11%)
  Pallas kernels  11.5 us (6%)
  local copies, waits for them, and re-layouts  7.42 us (4%)
  between operations  1.97 us (1%)
    all_gather x1, blocking collectives, shards(): first = lax.all_gather(rates, 'lag', axis=0, tiled=True)  37.8 us
    ppermute x12, starting transfers between devices, exchange(): return (lax.ppermute(value, axes, up), lax.ppermute(value, axes, down))  26.5 us
    ppermute x12, waiting for transfers between devices, exchange(): return (lax.ppermute(value, axes, up), lax.ppermute(value, axes, down))  15.6 us
    ppermute x6, starting transfers between devices, scatter_sum(): total = total + lax.ppermute(parts[d], 'lag', route).astype(jnp.float32)  11.8 us
    ppermute x6, waiting for transfers between devices, scatter_sum(): total = total + lax.ppermute(parts[d], 'lag', route).astype(jnp.float32)  8.65 us
    ppermute x4, waiting for transfers between devices, tree_to_first(): arrived = lax.ppermute(value, 'lag', route)  8.3 us
    add x1, other arithmetic, evolved(): state + time_step * (jnp.exp(-state) - jnp.sqrt(speed_of * speed_of + cre...  7.64 us
    pallas_call x4, Pallas kernels, block_product(): pl.pallas_call(functools.partial(block_kernel, chunks, (planes[0], planes...  6.84 us
  transfers between devices with their start and end apart: 32, of which 14 were waited for; matrix products, arithmetic and copies ran while one was open for 10% of the time, Pallas kernels for 6%

profile of v8, /device:TPU:2, one launch (start us, length us, event | category | flops | bytes accessed | tf_op | source)
XLA Modules:
  0.0 180.7 jit_solution(365769223097773171)
XLA Ops:
  0.7 4.4 %collective-permute-start.10 = (bf16[1024,256]{1,0:T(8,128)(2,1)}, bf16[1024,256]{1,0:T(8,128)(2,1)}, u32[]{:S(2)}, u32[]{:S(2)}) collective-permute-start(bf16[1024,256]{1,0:T(8,128)(2,1)} %bitcast.34), channel_id=1, source_target_pairs={{0,8},{8,16},{16,24},{1,9},{9,17},{17,25},{2,10},{10,18},{18,26},{... | collective-permute-start | bytes 1572872 | tf_op jit(solution)/shard_map/ppermute | solution.py:230
  5.1 1.9 %collective-permute-start.3 = (bf16[1024,256]{1,0:T(8,128)(2,1)}, bf16[1024,256]{1,0:T(8,128)(2,1)S(1)}, u32[]{:S(2)}, u32[]{:S(2)}) collective-permute-start(bf16[1024,256]{1,0:T(8,128)(2,1)} %bitcast.35), channel_id=1, source_target_pairs={{0,1},{1,2},{2,3},{3,4},{4,5},{5,6},{6,7},{8,9},{9,10},{10,11},{11... | collective-permute-start | bytes 1572872 | tf_op jit(solution)/shard_map/ppermute | solution.py:27
  7.0 3.6 %collective-permute-start.4 = (bf16[1024,256]{1,0:T(8,128)(2,1)}, bf16[1024,256]{1,0:T(8,128)(2,1)S(1)}, u32[]{:S(2)}, u32[]{:S(2)}) collective-permute-start(bf16[1024,256]{1,0:T(8,128)(2,1)} %bitcast.36), channel_id=1, source_target_pairs={{1,0},{2,1},{3,2},{4,3},{5,4},{6,5},{7,6},{9,8},{10,9},{11,10},{12... | collective-permute-start | bytes 1572872 | tf_op jit(solution)/shard_map/ppermute | solution.py:27
  11.3 4.5 %collective-permute-done.10.own = bf16[1024,256]{1,0:T(8,128)(2,1)} collective-permute-done((bf16[1024,256]{1,0:T(8,128)(2,1)}, bf16[1024,256]{1,0:T(8,128)(2,1)}, u32[]{:S(2)}, u32[]{:S(2)}) %collective-permute-start.10) | collective-permute-done | bytes 524320 | tf_op jit(solution)/shard_map/ppermute | solution.py:230
  15.8 1.5 collective-permute-start.11
  17.2 1.5 collective-permute-start.12
  18.7 0.7 fusion.74
  19.4 1.1 collective-permute-done.4.above
  20.5 1.9 %copy-done = bf16[1,1024,1536]{2,1,0:T(8,128)(2,1)S(1)} copy-done((bf16[1,1024,1536]{2,1,0:T(8,128)(2,1)S(1)}, bf16[1,1024,1536]{2,1,0:T(8,128)(2,1)}, u32[]{:S(2)}) %copy-start) | copy-done | bytes 3145752
  22.4 1.0 copy-done.5
  23.5 0.7 copy-done.14
  24.1 2.3 %product_by_rows.2 = (f32[256,256]{1,0:T(8,128)S(1)}, bf16[256,256]{1,0:T(8,128)(2,1)}, bf16[256,256]{1,0:T(8,128)(2,1)}, bf16[256,256]{1,0:T(8,128)(2,1)S(1)}) custom-call(s32[1,1,3]{2,1,0:T(1,128)S(1)} %copy-done.14, s32[1]{0:T(128)S(6)} %copy.11.live, bf16[1,1024,1536]{2,1,0:T(8,128)(2,1)S(1)} %copy-done, ...), custom_call_target="tpu_custom_call" | custom-call | flops 805306368 | bytes 5242880 | tf_op jit(solution)/shard_map/product_by_rows/pallas_call | solution.py:70
  26.5 0.7 copy-done.11
  27.2 4.0 %collective-permute-start.5 = (bf16[256,256]{1,0:T(8,128)(2,1)}, bf16[256,256]{1,0:T(8,128)(2,1)}, u32[]{:S(2)}, u32[]{:S(2)}) collective-permute-start(bf16[256,256]{1,0:T(8,128)(2,1)} %get-tuple-element.18), channel_id=1, source_target_pairs={{0,8},{8,16},{16,24},{24,0},{1,9},{9,17},{17,25},{25,1},{2,10},{10... | collective-permute-start | bytes 393224 | tf_op jit(solution)/shard_map/ppermute | solution.py:186
  31.2 2.6 %collective-permute-start.6 = (bf16[256,256]{1,0:T(8,128)(2,1)}, bf16[256,256]{1,0:T(8,128)(2,1)}, u32[]{:S(2)}, u32[]{:S(2)}) collective-permute-start(bf16[256,256]{1,0:T(8,128)(2,1)} %get-tuple-element.19), channel_id=1, source_target_pairs={{0,16},{8,24},{16,0},{24,8},{1,17},{9,25},{17,1},{25,9},{2,18},{10... | collective-permute-start | bytes 393224 | tf_op jit(solution)/shard_map/ppermute | solution.py:186
  33.8 1.3 collective-permute-start.7
  35.2 0.7 copy-done.7
  35.9 1.4 collective-permute-start
  37.4 1.3 collective-permute-start.1
  38.7 0.6 block_product.5
  39.3 1.3 collective-permute-start.2
  40.6 2.2 %collective-permute-done.6 = bf16[256,256]{1,0:T(8,128)(2,1)} collective-permute-done((bf16[256,256]{1,0:T(8,128)(2,1)}, bf16[256,256]{1,0:T(8,128)(2,1)}, u32[]{:S(2)}, u32[]{:S(2)}) %collective-permute-start.6) | collective-permute-done | bytes 131104 | tf_op jit(solution)/shard_map/ppermute | solution.py:186
  42.8 0.7 collective-permute-start.17
  43.5 1.3 collective-permute-start.13
  44.8 2.0 %fusion.65 = bf16[256,256]{1,0:T(8,128)(2,1)S(1)} fusion(f32[1,1,256,256]{3,2,1,0:T(8,128)S(1)} %copy-done.10, bf16[256,256]{1,0:T(8,128)(2,1)} %collective-permute-done.7, bf16[256,256]{1,0:T(8,128)(2,1)} %collective-permute-done.6, f32[256,256]{1,0:T(8,128)S(1)} %copy-done.12, bf16[256,256]{1,0:T(8,128)(2,1)} %collective-permute-done.5, ...), kind=kLoop, calls=%fused_computation.99 | loop fusion | flops 3997696 | bytes 1313792 | tf_op jit(solution)/shard_map/convert_element_type | solution.py:192
  46.9 37.8 %all_gather.3.own = bf16[1024,256]{1,0:T(8,128)(2,1)S(1)} all-gather(bf16[256,256]{1,0:T(8,128)(2,1)S(1)} %fusion.65), channel_id=1, replica_groups=mesh['lag'=4,'elem'=8] {'lag'}, dimensions={0}, use_global_device_ids=true | all-gather | bytes 655360 | tf_op jit(solution)/shard_map/all_gather | solution.py:235
  84.7 1.9 %collective-permute-start.8 = (bf16[1024,256]{1,0:T(8,128)(2,1)S(1)}, bf16[1024,256]{1,0:T(8,128)(2,1)S(1)}, u32[]{:S(2)}, u32[]{:S(2)}) collective-permute-start(bf16[1024,256]{1,0:T(8,128)(2,1)S(1)} %all_gather.3.own), channel_id=1, source_target_pairs={{0,1},{1,2},{2,3},{3,4},{4,5},{5,6},{6,7},{8,9},{9,10},{10,11},{11... | collective-permute-start | bytes 1572872 | tf_op jit(solution)/shard_map/ppermute | solution.py:27
  86.6 3.6 %collective-permute-start.9 = (bf16[1024,256]{1,0:T(8,128)(2,1)S(1)}, bf16[1024,256]{1,0:T(8,128)(2,1)S(1)}, u32[]{:S(2)}, u32[]{:S(2)}) collective-permute-start(bf16[1024,256]{1,0:T(8,128)(2,1)S(1)} %all_gather.3.own), channel_id=1, source_target_pairs={{1,0},{2,1},{3,2},{4,3},{5,4},{6,5},{7,6},{9,8},{10,9},{11,10},{12... | collective-permute-start | bytes 1572872 | tf_op jit(solution)/shard_map/ppermute | solution.py:27
  90.4 0.7 collective-permute-start.18
  91.1 0.7 collective-permute-start.19
  92.0 1.3 collective-permute-start.14
  93.3 1.8 %collective-permute-done.8.below = bf16[1024,256]{1,0:T(8,128)(2,1)S(1)} collective-permute-done((bf16[1024,256]{1,0:T(8,128)(2,1)S(1)}, bf16[1024,256]{1,0:T(8,128)(2,1)S(1)}, u32[]{:S(2)}, u32[]{:S(2)}) %collective-permute-start.8) | collective-permute-done | bytes 524320 | tf_op jit(solution)/shard_map/ppermute | solution.py:27
  95.2 4.2 %collective-permute-done.9.above = bf16[1024,256]{1,0:T(8,128)(2,1)S(1)} collective-permute-done((bf16[1024,256]{1,0:T(8,128)(2,1)S(1)}, bf16[1024,256]{1,0:T(8,128)(2,1)S(1)}, u32[]{:S(2)}, u32[]{:S(2)}) %collective-permute-start.9) | collective-permute-done | bytes 524320 | tf_op jit(solution)/shard_map/ppermute | solution.py:27
  99.3 2.7 %block_product.4 = (f32[1024,256]{1,0:T(8,128)S(1)}, bf16[1024,256]{1,0:T(8,128)(2,1)}) custom-call(s32[1,1,3]{2,1,0:T(1,128)S(1)} %copy-done.15, s32[1]{0:T(128)S(6)} %copy.11.live, bf16[1,1024,1536]{2,1,0:T(8,128)(2,1)S(1)} %copy-done.1, bf16[1024,256]{1,0:T(8,128)(2,1)S(1)} %collective-permute-done.8.below, bf16[1024,256]{1,0:T(8,128)(2,1)S(1)} %all_gather.3.own, ...), custom_call_target="tpu_custom_call" | custom-call | flops 805306368 | bytes 5242880 | tf_op jit(solution)/shard_map/block_product/pallas_call | solution.py:122
  102.0 1.3 collective-permute-start.22
  103.9 0.7 collective-permute-start.20
  104.6 3.4 %collective-permute-done.14 = bf16[1024,256]{1,0:T(8,128)(2,1)S(1)} collective-permute-done((bf16[1024,256]{1,0:T(8,128)(2,1)S(1)}, bf16[1024,256]{1,0:T(8,128)(2,1)S(1)}, u32[]{:S(2)}, u32[]{:S(2)}) %collective-permute-start.14) | collective-permute-done | bytes 524320 | tf_op jit(solution)/shard_map/ppermute | solution.py:199
  108.1 6.3 %broadcast_select_fusion = (bf16[1024,256]{1,0:T(8,128)(2,1)}, bf16[1024,256]{1,0:T(8,128)(2,1)}, f32[1024,256]{1,0:T(8,128)}) fusion(bf16[1024,256]{1,0:T(8,128)(2,1)S(1)} %collective-permute-done.17.own, pred[]{:T(512)S(6)} %eq.14, f32[1024]{0:T(1024)S(1)} %get-tuple-element.51, f32[1024]{0:T(1024)S(1)} %get-tuple-element.50, ...), kind=kLoop, calls=%fused_computation.51 | loop fusion | flops 18087936 | bytes 6303745 | tf_op jit(solution)/shard_map/jit(_where)/select_n | solution.py:256
  114.4 1.9 %collective-permute-start.15 = (bf16[1024,256]{1,0:T(8,128)(2,1)}, bf16[1024,256]{1,0:T(8,128)(2,1)}, u32[]{:S(2)}, u32[]{:S(2)}) collective-permute-start(bf16[1024,256]{1,0:T(8,128)(2,1)} %get-tuple-element.37.own), channel_id=1, source_target_pairs={{0,1},{1,2},{2,3},{3,4},{4,5},{5,6},{6,7}} | collective-permute-start | bytes 1572872 | tf_op jit(solution)/shard_map/ppermute | solution.py:27
  116.3 3.6 %collective-permute-start.16 = (bf16[1024,256]{1,0:T(8,128)(2,1)}, bf16[1024,256]{1,0:T(8,128)(2,1)}, u32[]{:S(2)}, u32[]{:S(2)}) collective-permute-start(bf16[1024,256]{1,0:T(8,128)(2,1)} %get-tuple-element.37.own), channel_id=1, source_target_pairs={{1,0},{2,1},{3,2},{4,3},{5,4},{6,5},{7,6}} | collective-permute-start | bytes 1572872 | tf_op jit(solution)/shard_map/ppermute | solution.py:27
  120.0 1.0 add_convert_fusion
  120.9 1.3 collective-permute-start.21
  122.3 1.5 collective-permute-start.23
  123.8 1.4 collective-permute-done.15.below
  125.2 4.7 %collective-permute-done.16.above = bf16[1024,256]{1,0:T(8,128)(2,1)} collective-permute-done((bf16[1024,256]{1,0:T(8,128)(2,1)}, bf16[1024,256]{1,0:T(8,128)(2,1)}, u32[]{:S(2)}, u32[]{:S(2)}) %collective-permute-start.16) | collective-permute-done | bytes 524320 | tf_op jit(solution)/shard_map/ppermute | solution.py:27
  129.9 3.0 %block_product.6 = f32[1024,256]{1,0:T(8,128)S(1)} custom-call(s32[1,1,3]{2,1,0:T(1,128)S(1)} %copy-done.15, s32[1]{0:T(128)S(6)} %copy.11.live, bf16[1,1024,1536]{2,1,0:T(8,128)(2,1)S(1)} %copy-done.1, bf16[1024,256]{1,0:T(8,128)(2,1)} %collective-permute-done.15.below, bf16[1024,256]{1,0:T(8,128)(2,1)} %get-tuple-element.37.own, ...), custom_call_target="tpu_custom_call" | custom-call | flops 805306368 | bytes 5242880 | tf_op jit(solution)/shard_map/block_product/pallas_call | solution.py:122
  132.9 4.9 %collective-permute-done.21 = bf16[1024,256]{1,0:T(8,128)(2,1)} collective-permute-done((bf16[1024,256]{1,0:T(8,128)(2,1)}, bf16[1024,256]{1,0:T(8,128)(2,1)}, u32[]{:S(2)}, u32[]{:S(2)}) %collective-permute-start.21) | collective-permute-done | bytes 524320 | tf_op jit(solution)/shard_map/ppermute | solution.py:199
  137.9 7.6 %multiply_add_fusion = (f32[1024,256]{1,0:T(8,128)S(1)}, bf16[1024,256]{1,0:T(8,128)(2,1)S(1)}) fusion(f32[1024,256]{1,0:T(8,128)S(1)} %copy-done.28, bf16[1024,256]{1,0:T(8,128)(2,1)S(1)} %copy-done.4, f32[256,256]{1,0:T(8,128)S(1)} %copy-done.26, f32[256,256]{1,0:T(8,128)S(1)} %copy-done.24, f32[256,256]{1,0:T(8,128)S(1)} %copy-done.22, ...), kind=kLoop, calls=%fused_computation.41 | loop fusion | flops 20971520 | bytes 6303744 | tf_op jit(solution)/shard_map/add | solution.py:178
  145.6 1.9 %collective-permute-start.24 = (bf16[1024,256]{1,0:T(8,128)(2,1)S(1)}, bf16[1024,256]{1,0:T(8,128)(2,1)S(1)}, u32[]{:S(2)}, u32[]{:S(2)}) collective-permute-start(bf16[1024,256]{1,0:T(8,128)(2,1)S(1)} %select_select_fusion.own), channel_id=1, source_target_pairs={{0,1},{1,2},{2,3},{3,4},{4,5},{5,6},{6,7},{8,9},{9,10},{10,11},{11... | collective-permute-start | bytes 1572872 | tf_op jit(solution)/shard_map/ppermute | solution.py:27
  147.5 3.6 %collective-permute-start.25 = (bf16[1024,256]{1,0:T(8,128)(2,1)S(1)}, bf16[1024,256]{1,0:T(8,128)(2,1)S(1)}, u32[]{:S(2)}, u32[]{:S(2)}) collective-permute-start(bf16[1024,256]{1,0:T(8,128)(2,1)S(1)} %select_select_fusion.own), channel_id=1, source_target_pairs={{1,0},{2,1},{3,2},{4,3},{5,4},{6,5},{7,6},{9,8},{10,9},{11,10},{12... | collective-permute-start | bytes 1572872 | tf_op jit(solution)/shard_map/ppermute | solution.py:27
  151.2 0.9 fusion.69
  152.0 1.3 collective-permute-start.29
  153.3 2.0 %collective-permute-start.30 = (f32[256,256]{1,0:T(8,128)}, f32[256,256]{1,0:T(8,128)}, u32[]{:S(2)}, u32[]{:S(2)}) collective-permute-start(f32[256,256]{1,0:T(8,128)} %get-tuple-element.40), channel_id=1, source_target_pairs={{0,16},{1,17},{2,18},{3,19},{4,20},{5,21},{6,22},{7,23}} | collective-permute-start | bytes 786440 | tf_op jit(solution)/shard_map/ppermute | solution.py:262
  155.3 2.0 %collective-permute-start.31 = (f32[256,256]{1,0:T(8,128)}, f32[256,256]{1,0:T(8,128)}, u32[]{:S(2)}, u32[]{:S(2)}) collective-permute-start(f32[256,256]{1,0:T(8,128)} %get-tuple-element.39), channel_id=1, source_target_pairs={{0,8},{1,9},{2,10},{3,11},{4,12},{5,13},{6,14},{7,15}} | collective-permute-start | bytes 786440 | tf_op jit(solution)/shard_map/ppermute | solution.py:262
  157.3 2.3 %collective-permute-done.25.above = bf16[1024,256]{1,0:T(8,128)(2,1)S(1)} collective-permute-done((bf16[1024,256]{1,0:T(8,128)(2,1)S(1)}, bf16[1024,256]{1,0:T(8,128)(2,1)S(1)}, u32[]{:S(2)}, u32[]{:S(2)}) %collective-permute-start.25) | collective-permute-done | bytes 524320 | tf_op jit(solution)/shard_map/ppermute | solution.py:27
  159.7 2.3 %product_by_rows.3 = (f32[256,256]{1,0:T(8,128)S(1)}, bf16[256,256]{1,0:T(8,128)(2,1)}, bf16[256,256]{1,0:T(8,128)(2,1)}, bf16[256,256]{1,0:T(8,128)(2,1)S(1)}) custom-call(s32[1,1,3]{2,1,0:T(1,128)S(1)} %copy-done.15, s32[1]{0:T(128)S(6)} %copy.11.live, bf16[1,1024,1536]{2,1,0:T(8,128)(2,1)S(1)} %copy-done.1, ...), custom_call_target="tpu_custom_call" | custom-call | flops 805306368 | bytes 5242880 | tf_op jit(solution)/shard_map/product_by_rows/pallas_call | solution.py:70
  162.0 0.7 copy-done.13
  162.7 0.7 copy-done.29
  163.4 3.8 %collective-permute-start.28 = (bf16[256,256]{1,0:T(8,128)(2,1)S(1)}, bf16[256,256]{1,0:T(8,128)(2,1)S(1)}, u32[]{:S(2)}, u32[]{:S(2)}) collective-permute-start(bf16[256,256]{1,0:T(8,128)(2,1)S(1)} %get-tuple-element.31), channel_id=1, source_target_pairs={{0,24},{8,0},{16,8},{24,16},{1,25},{9,1},{17,9},{25,17},{2,26},{10... | collective-permute-start | bytes 393224 | tf_op jit(solution)/shard_map/ppermute | solution.py:186
  167.3 4.1 %collective-permute-done.31 = f32[256,256]{1,0:T(8,128)} collective-permute-done((f32[256,256]{1,0:T(8,128)}, f32[256,256]{1,0:T(8,128)}, u32[]{:S(2)}, u32[]{:S(2)}) %collective-permute-start.31) | collective-permute-done | bytes 262176 | tf_op jit(solution)/shard_map/ppermute | solution.py:262
  171.3 2.8 %collective-permute-done.26 = bf16[256,256]{1,0:T(8,128)(2,1)S(1)} collective-permute-done((bf16[256,256]{1,0:T(8,128)(2,1)}, bf16[256,256]{1,0:T(8,128)(2,1)S(1)}, u32[]{:S(2)}, u32[]{:S(2)}) %collective-permute-start.26) | collective-permute-done | bytes 131104 | tf_op jit(solution)/shard_map/ppermute | solution.py:186
  174.2 2.3 %collective-permute-done.27 = bf16[256,256]{1,0:T(8,128)(2,1)S(1)} collective-permute-done((bf16[256,256]{1,0:T(8,128)(2,1)}, bf16[256,256]{1,0:T(8,128)(2,1)S(1)}, u32[]{:S(2)}, u32[]{:S(2)}) %collective-permute-start.27) | collective-permute-done | bytes 131104 | tf_op jit(solution)/shard_map/ppermute | solution.py:186
  176.5 1.3 collective-permute-done.28
  177.8 2.9 %add_bitcast_fusion = (f32[1,1,256,256]{3,2,1,0:T(8,128)}, bf16[256,256]{1,0:T(8,128)(2,1)}) fusion(f32[256]{0:T(256)S(1)} %bitcast.42, f32[256]{0:T(256)S(1)} %broadcast_multiply_fusion.1, f32[256]{0:T(256)S(1)} %bitcast.44, bf16[256,256]{1,0:T(8,128)(2,1)S(1)} %collective-permute-done.28, bf16[256,256]{1,0:T(8,128)(2,1)S(1)} %collective-permute-done.27, ...), kind=kLoop, calls=%fused_computation.95 | loop fusion | flops 4587520 | bytes 2362371 | tf_op jit(solution)/shard_map/broadcast_in_dim | solution.py:266
  (86 shorter events, 1.1 us)
Async XLA Ops:
  0.6 34.5 %copy-start.17 = (f32[1,1,256]{2,1,0:T(1,128)S(1)}, f32[1,1,256]{2,1,0:T(1,128)}, u32[]{:S(2)}) copy-start(f32[1,1,256]{2,1,0:T(1,128)} %coef_a.1) | copy-start | bytes 3076
  0.6 34.5 %copy-start.16 = (f32[1,1,256]{2,1,0:T(1,128)S(1)}, f32[1,1,256]{2,1,0:T(1,128)}, u32[]{:S(2)}) copy-start(f32[1,1,256]{2,1,0:T(1,128)} %coef_b.1) | copy-start | bytes 3076
  0.7 34.5 %copy-start.18 = (f32[1,1,256]{2,1,0:T(1,128)S(1)}, f32[1,1,256]{2,1,0:T(1,128)}, u32[]{:S(2)}) copy-start(f32[1,1,256]{2,1,0:T(1,128)} %sigma.1) | copy-start | bytes 3076
  0.7 15.1 %collective-permute-start.10 = (bf16[1024,256]{1,0:T(8,128)(2,1)}, bf16[1024,256]{1,0:T(8,128)(2,1)}, u32[]{:S(2)}, u32[]{:S(2)}) collective-permute-start(bf16[1024,256]{1,0:T(8,128)(2,1)} %bitcast.34), channel_id=1, source_target_pairs={{0,8},{8,16},{16,24},{1,9},{9,17},{17,25},{2,10},{10,18},{18,26},{... | collective-permute-start | bytes 1572872 | tf_op jit(solution)/shard_map/ppermute | solution.py:230
  5.1 14.3 %collective-permute-start.3 = (bf16[1024,256]{1,0:T(8,128)(2,1)}, bf16[1024,256]{1,0:T(8,128)(2,1)S(1)}, u32[]{:S(2)}, u32[]{:S(2)}) collective-permute-start(bf16[1024,256]{1,0:T(8,128)(2,1)} %bitcast.35), channel_id=1, source_target_pairs={{0,1},{1,2},{2,3},{3,4},{4,5},{5,6},{6,7},{8,9},{9,10},{10,11},{11... | collective-permute-start | bytes 1572872 | tf_op jit(solution)/shard_map/ppermute | solution.py:27
  7.0 13.5 %collective-permute-start.4 = (bf16[1024,256]{1,0:T(8,128)(2,1)}, bf16[1024,256]{1,0:T(8,128)(2,1)S(1)}, u32[]{:S(2)}, u32[]{:S(2)}) collective-permute-start(bf16[1024,256]{1,0:T(8,128)(2,1)} %bitcast.36), channel_id=1, source_target_pairs={{1,0},{2,1},{3,2},{4,3},{5,4},{6,5},{7,6},{9,8},{10,9},{11,10},{12... | collective-permute-start | bytes 1572872 | tf_op jit(solution)/shard_map/ppermute | solution.py:27
  15.8 20.2 %collective-permute-start.11 = (bf16[1024,256]{1,0:T(8,128)(2,1)}, bf16[1024,256]{1,0:T(8,128)(2,1)}, u32[]{:S(2)}, u32[]{:S(2)}) collective-permute-start(bf16[1024,256]{1,0:T(8,128)(2,1)} %collective-permute-done.10.own), channel_id=1, source_target_pairs={{8,9},{9,10},{10,11},{11,12},{12,13},{13,14},{14,15},{16,17},{17,1... | collective-permute-start | bytes 1572872 | tf_op jit(solution)/shard_map/ppermute | solution.py:27
  17.2 20.2 %collective-permute-start.12 = (bf16[1024,256]{1,0:T(8,128)(2,1)}, bf16[1024,256]{1,0:T(8,128)(2,1)}, u32[]{:S(2)}, u32[]{:S(2)}) collective-permute-start(bf16[1024,256]{1,0:T(8,128)(2,1)} %collective-permute-done.10.own), channel_id=1, source_target_pairs={{9,8},{10,9},{11,10},{12,11},{13,12},{14,13},{15,14},{17,16},{18,1... | collective-permute-start | bytes 1572872 | tf_op jit(solution)/shard_map/ppermute | solution.py:27
  20.5 1.9 %copy-start = (bf16[1,1024,1536]{2,1,0:T(8,128)(2,1)S(1)}, bf16[1,1024,1536]{2,1,0:T(8,128)(2,1)}, u32[]{:S(2)}) copy-start(bf16[1,1024,1536]{2,1,0:T(8,128)(2,1)} %tile.13) | copy-start | bytes 9437188
  22.4 1.0 copy-start.5
  23.5 0.7 copy-start.14
  24.1 11.0 %copy-start.1 = (bf16[1,1024,1536]{2,1,0:T(8,128)(2,1)S(1)}, bf16[1,1024,1536]{2,1,0:T(8,128)(2,1)}, u32[]{:S(2)}) copy-start(bf16[1,1024,1536]{2,1,0:T(8,128)(2,1)} %tile.13) | copy-start | bytes 9437188
  24.1 11.0 %copy-start.6 = (bf16[1,1024,256]{2,1,0:T(8,128)(2,1)S(1)}, bf16[1,1024,256]{2,1,0:T(8,128)(2,1)}, u32[]{:S(2)}) copy-start(bf16[1,1024,256]{2,1,0:T(8,128)(2,1)} %param.12) | copy-start | bytes 1572868
  24.1 11.0 %copy-start.9 = (f32[1,1,256,256]{3,2,1,0:T(8,128)S(1)}, f32[1,1,256,256]{3,2,1,0:T(8,128)}, u32[]{:S(2)}) copy-start(f32[1,1,256,256]{3,2,1,0:T(8,128)} %state.1) | copy-start | bytes 786436
  26.5 0.7 copy-start.11
  27.2 11.5 %copy-start.2 = (f32[1,1,256,256]{3,2,1,0:T(8,128)S(1)}, f32[1,1,256,256]{3,2,1,0:T(8,128)}, u32[]{:S(2)}) copy-start(f32[1,1,256,256]{3,2,1,0:T(8,128)} %stress.7) | copy-start | bytes 786436
  27.2 11.5 %copy-start.15 = (s32[1,1,3]{2,1,0:T(1,128)S(1)}, s32[1,1,3]{2,1,0:T(1,128)}, u32[]{:S(2)}) copy-start(s32[1,1,3]{2,1,0:T(1,128)} %picks.11) | copy-start | bytes 40
  27.2 12.1 %collective-permute-start.5 = (bf16[256,256]{1,0:T(8,128)(2,1)}, bf16[256,256]{1,0:T(8,128)(2,1)}, u32[]{:S(2)}, u32[]{:S(2)}) collective-permute-start(bf16[256,256]{1,0:T(8,128)(2,1)} %get-tuple-element.18), channel_id=1, source_target_pairs={{0,8},{8,16},{16,24},{24,0},{1,9},{9,17},{17,25},{25,1},{2,10},{10... | collective-permute-start | bytes 393224 | tf_op jit(solution)/shard_map/ppermute | solution.py:186
  31.2 11.6 %collective-permute-start.6 = (bf16[256,256]{1,0:T(8,128)(2,1)}, bf16[256,256]{1,0:T(8,128)(2,1)}, u32[]{:S(2)}, u32[]{:S(2)}) collective-permute-start(bf16[256,256]{1,0:T(8,128)(2,1)} %get-tuple-element.19), channel_id=1, source_target_pairs={{0,16},{8,24},{16,0},{24,8},{1,17},{9,25},{17,1},{25,9},{2,18},{10... | collective-permute-start | bytes 393224 | tf_op jit(solution)/shard_map/ppermute | solution.py:186
  33.8 9.7 %collective-permute-start.7 = (bf16[256,256]{1,0:T(8,128)(2,1)S(1)}, bf16[256,256]{1,0:T(8,128)(2,1)}, u32[]{:S(2)}, u32[]{:S(2)}) collective-permute-start(bf16[256,256]{1,0:T(8,128)(2,1)S(1)} %get-tuple-element.20), channel_id=1, source_target_pairs={{0,24},{8,0},{16,8},{24,16},{1,25},{9,1},{17,9},{25,17},{2,26},{10... | collective-permute-start | bytes 393224 | tf_op jit(solution)/shard_map/ppermute | solution.py:186
  35.2 0.7 copy-start.7
  35.9 3.4 %copy-start.8 = (f32[264,256]{1,0:T(8,128)S(1)}, f32[264,256]{1,0:T(8,128)}, u32[]{:S(2)}) copy-start(f32[264,256]{1,0:T(8,128)} %copy-done.7) | copy-start | bytes 811012
  35.9 8.9 %copy-start.10 = (f32[1,1,256,256]{3,2,1,0:T(8,128)S(1)}, f32[1,1,256,256]{3,2,1,0:T(8,128)}, u32[]{:S(2)}) copy-start(f32[1,1,256,256]{3,2,1,0:T(8,128)} %state.1) | copy-start | bytes 786436
  35.9 8.9 %copy-start.12 = (f32[256,256]{1,0:T(8,128)S(1)}, f32[256,256]{1,0:T(8,128)}, u32[]{:S(2)}) copy-start(f32[256,256]{1,0:T(8,128)} %copy-done.11) | copy-start | bytes 786436
  35.9 48.7 %collective-permute-start = (f32[264,256]{1,0:T(8,128)}, f32[264,256]{1,0:T(8,128)S(1)}, u32[]{:S(2)}, u32[]{:S(2)}) collective-permute-start(f32[264,256]{1,0:T(8,128)} %copy-done.7), channel_id=1, source_target_pairs={{8,0},{9,1},{10,2},{11,3},{12,4},{13,5},{14,6},{15,7}} | collective-permute-start | bytes 811016 | tf_op jit(solution)/shard_map/ppermute | solution.py:229
  37.4 47.3 %collective-permute-start.1 = (f32[264,256]{1,0:T(8,128)}, f32[264,256]{1,0:T(8,128)S(1)}, u32[]{:S(2)}, u32[]{:S(2)}) collective-permute-start(f32[264,256]{1,0:T(8,128)} %copy-done.7), channel_id=1, source_target_pairs={{16,0},{17,1},{18,2},{19,3},{20,4},{21,5},{22,6},{23,7}} | collective-permute-start | bytes 811016 | tf_op jit(solution)/shard_map/ppermute | solution.py:229
  39.3 45.4 %collective-permute-start.2 = (f32[264,256]{1,0:T(8,128)S(1)}, f32[264,256]{1,0:T(8,128)S(1)}, u32[]{:S(2)}, u32[]{:S(2)}) collective-permute-start(f32[264,256]{1,0:T(8,128)S(1)} %copy-done.8), channel_id=1, source_target_pairs={{24,0},{25,1},{26,2},{27,3},{28,4},{29,5},{30,6},{31,7}} | collective-permute-start | bytes 811016 | tf_op jit(solution)/shard_map/ppermute | solution.py:229
  42.8 47.6 %collective-permute-start.17 = (bf16[1024,256]{1,0:T(8,128)(2,1)}, bf16[1024,256]{1,0:T(8,128)(2,1)S(1)}, u32[]{:S(2)}, u32[]{:S(2)}) collective-permute-start(bf16[1024,256]{1,0:T(8,128)(2,1)} %collective-permute-done.10.own), channel_id=1, source_target_pairs={{8,16},{16,24},{9,17},{17,25},{10,18},{18,26},{11,19},{19,27},{12,... | collective-permute-start | bytes 1572872 | tf_op jit(solution)/shard_map/ppermute | solution.py:244
  43.5 48.3 %collective-permute-start.13 = (bf16[1024,256]{1,0:T(8,128)(2,1)S(1)}, bf16[1024,256]{1,0:T(8,128)(2,1)S(1)}, u32[]{:S(2)}, u32[]{:S(2)}) collective-permute-start(bf16[1024,256]{1,0:T(8,128)(2,1)S(1)} %block_product.5), channel_id=1, source_target_pairs={{8,0},{24,16},{9,1},{25,17},{10,2},{26,18},{11,3},{27,19},{12,4},{... | collective-permute-start | bytes 1572872 | tf_op jit(solution)/shard_map/ppermute | solution.py:199
  84.6 23.4 %copy-start.3 = (bf16[1024,256]{1,0:T(8,128)(2,1)}, bf16[1024,256]{1,0:T(8,128)(2,1)S(1)}, u32[]{:S(2)}) copy-start(bf16[1024,256]{1,0:T(8,128)(2,1)S(1)} %all_gather.3.own) | copy-start | bytes 1572868
  84.7 10.5 %collective-permute-start.8 = (bf16[1024,256]{1,0:T(8,128)(2,1)S(1)}, bf16[1024,256]{1,0:T(8,128)(2,1)S(1)}, u32[]{:S(2)}, u32[]{:S(2)}) collective-permute-start(bf16[1024,256]{1,0:T(8,128)(2,1)S(1)} %all_gather.3.own), channel_id=1, source_target_pairs={{0,1},{1,2},{2,3},{3,4},{4,5},{5,6},{6,7},{8,9},{9,10},{10,11},{11... | collective-permute-start | bytes 1572872 | tf_op jit(solution)/shard_map/ppermute | solution.py:27
  86.6 12.7 %collective-permute-start.9 = (bf16[1024,256]{1,0:T(8,128)(2,1)S(1)}, bf16[1024,256]{1,0:T(8,128)(2,1)S(1)}, u32[]{:S(2)}, u32[]{:S(2)}) collective-permute-start(bf16[1024,256]{1,0:T(8,128)(2,1)S(1)} %all_gather.3.own), channel_id=1, source_target_pairs={{1,0},{2,1},{3,2},{4,3},{5,4},{6,5},{7,6},{9,8},{10,9},{11,10},{12... | collective-permute-start | bytes 1572872 | tf_op jit(solution)/shard_map/ppermute | solution.py:27
  90.3 17.8 %copy-start.19 = (f32[256,256]{1,0:T(8,128)}, f32[256,256]{1,0:T(8,128)S(1)}, u32[]{:S(2)}) copy-start(f32[256,256]{1,0:T(8,128)S(1)} %slice.52) | copy-start | bytes 786436
  90.3 17.7 %copy-start.21 = (f32[256,256]{1,0:T(8,128)}, f32[256,256]{1,0:T(8,128)S(1)}, u32[]{:S(2)}) copy-start(f32[256,256]{1,0:T(8,128)S(1)} %slice.53) | copy-start | bytes 786436
  90.3 17.7 %copy-start.23 = (f32[256,256]{1,0:T(8,128)}, f32[256,256]{1,0:T(8,128)S(1)}, u32[]{:S(2)}) copy-start(f32[256,256]{1,0:T(8,128)S(1)} %slice.54) | copy-start | bytes 786436
  90.4 17.7 %copy-start.25 = (f32[256,256]{1,0:T(8,128)}, f32[256,256]{1,0:T(8,128)S(1)}, u32[]{:S(2)}) copy-start(f32[256,256]{1,0:T(8,128)S(1)} %slice.55) | copy-start | bytes 786436
  90.4 12.9 %collective-permute-start.18 = (bf16[1024,256]{1,0:T(8,128)(2,1)S(1)}, bf16[1024,256]{1,0:T(8,128)(2,1)S(1)}, u32[]{:S(2)}, u32[]{:S(2)}) collective-permute-start(bf16[1024,256]{1,0:T(8,128)(2,1)S(1)} %collective-permute-done.17.own), channel_id=1, source_target_pairs={{16,17},{17,18},{18,19},{19,20},{20,21},{21,22},{22,23},{24,25},{2... | collective-permute-start | bytes 1572872 | tf_op jit(solution)/shard_map/ppermute | solution.py:27
  91.1 12.2 %collective-permute-start.19 = (bf16[1024,256]{1,0:T(8,128)(2,1)S(1)}, bf16[1024,256]{1,0:T(8,128)(2,1)S(1)}, u32[]{:S(2)}, u32[]{:S(2)}) collective-permute-start(bf16[1024,256]{1,0:T(8,128)(2,1)S(1)} %collective-permute-done.17.own), channel_id=1, source_target_pairs={{17,16},{18,17},{19,18},{20,19},{21,20},{22,21},{23,22},{25,24},{2... | collective-permute-start | bytes 1572872 | tf_op jit(solution)/shard_map/ppermute | solution.py:27
  92.0 16.1 %collective-permute-start.14 = (bf16[1024,256]{1,0:T(8,128)(2,1)S(1)}, bf16[1024,256]{1,0:T(8,128)(2,1)S(1)}, u32[]{:S(2)}, u32[]{:S(2)}) collective-permute-start(bf16[1024,256]{1,0:T(8,128)(2,1)S(1)} %fusion.1), channel_id=1, source_target_pairs={{16,0},{17,1},{18,2},{19,3},{20,4},{21,5},{22,6},{23,7}} | collective-permute-start | bytes 1572872 | tf_op jit(solution)/shard_map/ppermute | solution.py:199
  102.0 30.9 %collective-permute-start.22 = (bf16[1024,256]{1,0:T(8,128)(2,1)}, bf16[1024,256]{1,0:T(8,128)(2,1)}, u32[]{:S(2)}, u32[]{:S(2)}) collective-permute-start(bf16[1024,256]{1,0:T(8,128)(2,1)} %get-tuple-element.27), channel_id=1, source_target_pairs={{8,0},{9,1},{10,2},{11,3},{12,4},{13,5},{14,6},{15,7}} | collective-permute-start | bytes 1572872 | tf_op jit(solution)/shard_map/ppermute | solution.py:250
  103.9 16.0 %collective-permute-start.20 = (bf16[1024,256]{1,0:T(8,128)(2,1)S(1)}, bf16[1024,256]{1,0:T(8,128)(2,1)S(1)}, u32[]{:S(2)}, u32[]{:S(2)}) collective-permute-start(bf16[1024,256]{1,0:T(8,128)(2,1)S(1)} %block_product.7), channel_id=1, source_target_pairs={{24,16},{25,17},{26,18},{27,19},{28,20},{29,21},{30,22},{31,23}} | collective-permute-start | bytes 1572872 | tf_op jit(solution)/shard_map/ppermute | solution.py:199
  114.4 10.8 %collective-permute-start.15 = (bf16[1024,256]{1,0:T(8,128)(2,1)}, bf16[1024,256]{1,0:T(8,128)(2,1)}, u32[]{:S(2)}, u32[]{:S(2)}) collective-permute-start(bf16[1024,256]{1,0:T(8,128)(2,1)} %get-tuple-element.37.own), channel_id=1, source_target_pairs={{0,1},{1,2},{2,3},{3,4},{4,5},{5,6},{6,7}} | collective-permute-start | bytes 1572872 | tf_op jit(solution)/shard_map/ppermute | solution.py:27
  116.3 13.6 %collective-permute-start.16 = (bf16[1024,256]{1,0:T(8,128)(2,1)}, bf16[1024,256]{1,0:T(8,128)(2,1)}, u32[]{:S(2)}, u32[]{:S(2)}) collective-permute-start(bf16[1024,256]{1,0:T(8,128)(2,1)} %get-tuple-element.37.own), channel_id=1, source_target_pairs={{1,0},{2,1},{3,2},{4,3},{5,4},{6,5},{7,6}} | collective-permute-start | bytes 1572872 | tf_op jit(solution)/shard_map/ppermute | solution.py:27
  120.9 16.9 %collective-permute-start.21 = (bf16[1024,256]{1,0:T(8,128)(2,1)}, bf16[1024,256]{1,0:T(8,128)(2,1)}, u32[]{:S(2)}, u32[]{:S(2)}) collective-permute-start(bf16[1024,256]{1,0:T(8,128)(2,1)} %add_convert_fusion), channel_id=1, source_target_pairs={{16,0},{17,1},{18,2},{19,3},{20,4},{21,5},{22,6},{23,7}} | collective-permute-start | bytes 1572872 | tf_op jit(solution)/shard_map/ppermute | solution.py:199
  122.2 15.6 %copy-start.4 = (bf16[1024,256]{1,0:T(8,128)(2,1)S(1)}, bf16[1024,256]{1,0:T(8,128)(2,1)}, u32[]{:S(2)}) copy-start(bf16[1024,256]{1,0:T(8,128)(2,1)} %copy-done.3) | copy-start | bytes 1572868
  122.2 15.6 %copy-start.20 = (f32[256,256]{1,0:T(8,128)S(1)}, f32[256,256]{1,0:T(8,128)}, u32[]{:S(2)}) copy-start(f32[256,256]{1,0:T(8,128)} %copy-done.19) | copy-start | bytes 786436
  122.2 15.6 %copy-start.22 = (f32[256,256]{1,0:T(8,128)S(1)}, f32[256,256]{1,0:T(8,128)}, u32[]{:S(2)}) copy-start(f32[256,256]{1,0:T(8,128)} %copy-done.21) | copy-start | bytes 786436
  122.3 15.6 %copy-start.24 = (f32[256,256]{1,0:T(8,128)S(1)}, f32[256,256]{1,0:T(8,128)}, u32[]{:S(2)}) copy-start(f32[256,256]{1,0:T(8,128)} %copy-done.23) | copy-start | bytes 786436
  122.3 15.6 %copy-start.26 = (f32[256,256]{1,0:T(8,128)S(1)}, f32[256,256]{1,0:T(8,128)}, u32[]{:S(2)}) copy-start(f32[256,256]{1,0:T(8,128)} %copy-done.25) | copy-start | bytes 786436
  122.3 15.6 %copy-start.28 = (f32[1024,256]{1,0:T(8,128)S(1)}, f32[1024,256]{1,0:T(8,128)}, u32[]{:S(2)}) copy-start(f32[1024,256]{1,0:T(8,128)} %get-tuple-element.38) | copy-start | bytes 3145732
  122.3 23.2 %collective-permute-start.23 = (bf16[1024,256]{1,0:T(8,128)(2,1)}, bf16[1024,256]{1,0:T(8,128)(2,1)S(1)}, u32[]{:S(2)}, u32[]{:S(2)}) collective-permute-start(bf16[1024,256]{1,0:T(8,128)(2,1)} %get-tuple-element.36), channel_id=1, source_target_pairs={{0,8},{16,24},{1,9},{17,25},{2,10},{18,26},{3,11},{19,27},{4,12},{... | collective-permute-start | bytes 1572872 | tf_op jit(solution)/shard_map/ppermute | solution.py:257
  145.5 11.8 %copy-start.27 = (f32[1024,256]{1,0:T(8,128)}, f32[1024,256]{1,0:T(8,128)S(1)}, u32[]{:S(2)}) copy-start(f32[1024,256]{1,0:T(8,128)S(1)} %get-tuple-element.34) | copy-start | bytes 3145732
  145.6 11.7 %collective-permute-start.24 = (bf16[1024,256]{1,0:T(8,128)(2,1)S(1)}, bf16[1024,256]{1,0:T(8,128)(2,1)S(1)}, u32[]{:S(2)}, u32[]{:S(2)}) collective-permute-start(bf16[1024,256]{1,0:T(8,128)(2,1)S(1)} %select_select_fusion.own), channel_id=1, source_target_pairs={{0,1},{1,2},{2,3},{3,4},{4,5},{5,6},{6,7},{8,9},{9,10},{10,11},{11... | collective-permute-start | bytes 1572872 | tf_op jit(solution)/shard_map/ppermute | solution.py:27
  147.5 12.1 %collective-permute-start.25 = (bf16[1024,256]{1,0:T(8,128)(2,1)S(1)}, bf16[1024,256]{1,0:T(8,128)(2,1)S(1)}, u32[]{:S(2)}, u32[]{:S(2)}) collective-permute-start(bf16[1024,256]{1,0:T(8,128)(2,1)S(1)} %select_select_fusion.own), channel_id=1, source_target_pairs={{1,0},{2,1},{3,2},{4,3},{5,4},{6,5},{7,6},{9,8},{10,9},{11,10},{12... | collective-permute-start | bytes 1572872 | tf_op jit(solution)/shard_map/ppermute | solution.py:27
  152.0 10.7 %collective-permute-start.29 = (f32[256,256]{1,0:T(8,128)S(1)}, f32[256,256]{1,0:T(8,128)S(1)}, u32[]{:S(2)}, u32[]{:S(2)}) collective-permute-start(f32[256,256]{1,0:T(8,128)S(1)} %get-tuple-element.41), channel_id=1, source_target_pairs={{0,24},{1,25},{2,26},{3,27},{4,28},{5,29},{6,30},{7,31}} | collective-permute-start | bytes 786440 | tf_op jit(solution)/shard_map/ppermute | solution.py:262
  153.3 13.9 %collective-permute-start.30 = (f32[256,256]{1,0:T(8,128)}, f32[256,256]{1,0:T(8,128)}, u32[]{:S(2)}, u32[]{:S(2)}) collective-permute-start(f32[256,256]{1,0:T(8,128)} %get-tuple-element.40), channel_id=1, source_target_pairs={{0,16},{1,17},{2,18},{3,19},{4,20},{5,21},{6,22},{7,23}} | collective-permute-start | bytes 786440 | tf_op jit(solution)/shard_map/ppermute | solution.py:262
  155.3 16.0 %collective-permute-start.31 = (f32[256,256]{1,0:T(8,128)}, f32[256,256]{1,0:T(8,128)}, u32[]{:S(2)}, u32[]{:S(2)}) collective-permute-start(f32[256,256]{1,0:T(8,128)} %get-tuple-element.39), channel_id=1, source_target_pairs={{0,8},{1,9},{2,10},{3,11},{4,12},{5,13},{6,14},{7,15}} | collective-permute-start | bytes 786440 | tf_op jit(solution)/shard_map/ppermute | solution.py:262
  162.0 0.7 copy-start.13
  162.7 11.4 %collective-permute-start.26 = (bf16[256,256]{1,0:T(8,128)(2,1)}, bf16[256,256]{1,0:T(8,128)(2,1)S(1)}, u32[]{:S(2)}, u32[]{:S(2)}) collective-permute-start(bf16[256,256]{1,0:T(8,128)(2,1)} %get-tuple-element.29), channel_id=1, source_target_pairs={{0,8},{8,16},{16,24},{24,0},{1,9},{9,17},{17,25},{25,1},{2,10},{10... | collective-permute-start | bytes 393224 | tf_op jit(solution)/shard_map/ppermute | solution.py:186
  162.7 13.8 %collective-permute-start.27 = (bf16[256,256]{1,0:T(8,128)(2,1)}, bf16[256,256]{1,0:T(8,128)(2,1)S(1)}, u32[]{:S(2)}, u32[]{:S(2)}) collective-permute-start(bf16[256,256]{1,0:T(8,128)(2,1)} %get-tuple-element.30), channel_id=1, source_target_pairs={{0,16},{8,24},{16,0},{24,8},{1,17},{9,25},{17,1},{25,9},{2,18},{10... | collective-permute-start | bytes 393224 | tf_op jit(solution)/shard_map/ppermute | solution.py:186
  162.7 0.7 copy-start.29
  163.4 14.4 %collective-permute-start.28 = (bf16[256,256]{1,0:T(8,128)(2,1)S(1)}, bf16[256,256]{1,0:T(8,128)(2,1)S(1)}, u32[]{:S(2)}, u32[]{:S(2)}) collective-permute-start(bf16[256,256]{1,0:T(8,128)(2,1)S(1)} %get-tuple-element.31), channel_id=1, source_target_pairs={{0,24},{8,0},{16,8},{24,16},{1,25},{9,1},{17,9},{25,17},{2,26},{10... | collective-permute-start | bytes 393224 | tf_op jit(solution)/shard_map/ppermute | solution.py:186

commit v9 on v8

--- a/solution.py
+++ b/solution.py
@@ -140,7 +140,7 @@
     )(picks, live, tile, below, own, above, stress)
 
 
-def pack_kernel(state, coef_a, coef_b, sigma, tile, field, out):
+def pack_kernel(state, coef_a, coef_b, sigma, out):
     rows = state.shape[2]
     out[pl.ds(0, rows), :] = state[0, 0]
     out[pl.ds(rows, 8), :] = jnp.zeros((8, out.shape[1]), out.dtype)
@@ -148,15 +148,26 @@
     out[pl.ds(rows + 1, 1), pl.ds(0, rows)] = sigma[0] * coef_a[0]
 
 
-def pack(state, coef_a, coef_b, sigma, tile, field):
+def pack(state, coef_a, coef_b, sigma):
     return pl.pallas_call(
         pack_kernel,
-        in_specs=[VMEM] * 4 + [ANY] * 2,
+        in_specs=[VMEM] * 4,
         out_specs=VMEM,
         out_shape=jax.ShapeDtypeStruct((state.shape[2] + 8, state.shape[3]), jnp.float32),
         compiler_params=PARAMS,
         name="pack",
-    )(state, coef_a, coef_b, sigma, tile, field)
+    )(state, coef_a, coef_b, sigma)
+
+
+def touch(*arrays):
+    pl.pallas_call(
+        lambda *refs: refs[-1].__setitem__(Ellipsis, jnp.zeros(refs[-1].shape, refs[-1].dtype)),
+        in_specs=[ANY] * len(arrays),
+        out_specs=VMEM,
+        out_shape=jax.ShapeDtypeStruct((8, 128), jnp.float32),
+        compiler_params=pltpu.CompilerParams(vmem_limit_bytes=32 * 1024 * 1024, has_side_effects=True),
+        name="touch",
+    )(*arrays)
 
 
 def newton(load, state, ratio, strength):
@@ -225,24 +236,25 @@
         return load
 
     below, own, above = window_of(field, every)
-    packed = pack(log_state, fric_a, fric_b, normal_stress, kernel_tiles, field)
+    packed = pack(log_state, fric_a, fric_b, normal_stress)
     packed = [packed] + [lax.ppermute(packed, "lag", [(d, 0)]) for d in rest]
     once = lax.ppermute(field, "lag", [(i, i + 1) for i in every[:-1]])
+    touch(kernel_tiles, field)
     traction = scatter_sum(product_by_rows(*local, below, own, above, lags))
     coef_a, coef_b, sigma = (c[0, 0][:, None] for c in (fric_a, fric_b, normal_stress))
     row_pair = (coef_b / coef_a, sigma * coef_a)
     rates, _ = settle_friction(prestress[0, 0] + traction, log_state[0, 0], *row_pair)
     first = lax.all_gather(rates, "lag", axis=0, tiled=True)
-    packed, first = lax.optimization_barrier((packed, first))
-    state = jnp.concatenate([g[:rows] for g in packed], 0)
-    ratio, strength = (jnp.concatenate([g[rows + k, :rows] for g in packed])[:, None] for k in range(2))
-    state = evolved(state, first.astype(jnp.float32))
-
     kinds = [jnp.float32, jnp.bfloat16]
     (low,) = block_product(*local, window_of(once, rest), prestress, rest, kinds[1:])
     base_1 = tree_to_first(low, lags, 1)
     twice = lax.ppermute(once, "lag", [(i, i + 1) for i in rest[:-1]])
-    (low,) = block_product(*local, window_of(twice, rest[1:]), prestress, rest[1:], kinds[1:])
+    window_2 = window_of(twice, rest[1:])
+    packed, _ = lax.optimization_barrier((packed, window_2[0]))
+    state = jnp.concatenate([g[:rows] for g in packed], 0)
+    ratio, strength = (jnp.concatenate([g[rows + k, :rows] for g in packed])[:, None] for k in range(2))
+    state = evolved(state, first.astype(jnp.float32))
+    (low,) = block_product(*local, window_2, prestress, rest[1:], kinds[1:])
     base_2 = tree_to_first(low, lags, 2)
 
     window = window_of(first, [0, 1])

time: 182 us -> 193 us (1.060)
  waiting for transfers between devices: 41.2 us -> 58.4 us
  blocking collectives: 37.8 us -> 24 us
  local copies, waits for them, and re-layouts: 7.42 us -> 11.8 us
  Pallas kernels: 11.5 us -> 13.9 us
  starting transfers between devices: 60 us -> 57.7 us
    all_gather x1, blocking collectives: 37.8 us -> 24 us  [shards(): first = lax.all_gather(rates, 'lag', axis=0, tiled=True)]
    ppermute x3, waiting for transfers between devices: 0.01 us -> 12.4 us  [shards(): packed = [packed] + [lax.ppermute(packed, 'lag', [(d, 0)]) for d in rest]]
    ppermute x4, waiting for transfers between devices: 8.3 us -> 19.9 us  [tree_to_first(): arrived = lax.ppermute(value, 'lag', route)]
    ppermute x12, waiting for transfers between devices: 15.6 us -> 9.87 us  [exchange(): return (lax.ppermute(value, axes, up), lax.ppermute(value, axes, down))]
    ppermute x1, waiting for transfers between devices: 4.46 us -> 0.01 us  [shards(): once = lax.ppermute(field, 'lag', [(i, i + 1) for i in every[:-1]])]
    ppermute x6, waiting for transfers between devices: 8.65 us -> 11.9 us  [scatter_sum(): total = total + lax.ppermute(parts[d], 'lag', route).astype(jnp.float32)]
    slice x4, local copies, waits for them, and re-layouts: 0.08 us -> 3.18 us  [shards(): state = jnp.concatenate([g[:rows] for g in packed], 0)]
    ppermute x6, starting transfers between devices: 11.8 us -> 9.45 us  [scatter_sum(): total = total + lax.ppermute(parts[d], 'lag', route).astype(jnp.float32)]
  transfers between devices with their start and end apart: 32 -> 32, of which waited for: 14 -> 15; matrix products, arithmetic and copies ran while one was open for 10% -> 13% of each run, Pallas kernels for 6% -> 7%
where the time goes in v9:
time: 193 us; the launch traced here: 190 us
  waiting for transfers between devices  58.4 us (30%)
  starting transfers between devices  57.7 us (30%)
  blocking collectives  24 us (12%)
  other arithmetic  22.3 us (12%)
  Pallas kernels  13.9 us (7%)
  local copies, waits for them, and re-layouts  11.8 us (6%)
    ppermute x12, starting transfers between devices, exchange(): return (lax.ppermute(value, axes, up), lax.ppermute(value, axes, down))  25.9 us
    all_gather x1, blocking collectives, shards(): first = lax.all_gather(rates, 'lag', axis=0, tiled=True)  24 us
    ppermute x4, waiting for transfers between devices, tree_to_first(): arrived = lax.ppermute(value, 'lag', route)  19.9 us
    ppermute x3, waiting for transfers between devices, shards(): packed = [packed] + [lax.ppermute(packed, 'lag', [(d, 0)]) for d in rest]  12.4 us
    ppermute x6, waiting for transfers between devices, scatter_sum(): total = total + lax.ppermute(parts[d], 'lag', route).astype(jnp.float32)  11.9 us
    ppermute x12, waiting for transfers between devices, exchange(): return (lax.ppermute(value, axes, up), lax.ppermute(value, axes, down))  9.87 us
    ppermute x6, starting transfers between devices, scatter_sum(): total = total + lax.ppermute(parts[d], 'lag', route).astype(jnp.float32)  9.45 us
    pallas_call x4, Pallas kernels, block_product(): pl.pallas_call(functools.partial(block_kernel, chunks, (planes[0], planes...  8.53 us
  transfers between devices with their start and end apart: 32, of which 15 were waited for; matrix products, arithmetic and copies ran while one was open for 13% of the time, Pallas kernels for 7%

profile of v9, /device:TPU:2, one launch (start us, length us, event | category | flops | bytes accessed | tf_op | source)
XLA Modules:
  0.0 190.0 jit_solution(4991893330893445107)
XLA Ops:
  0.6 1.9 %collective-permute-start = (bf16[1024,256]{1,0:T(8,128)(2,1)}, bf16[1024,256]{1,0:T(8,128)(2,1)S(1)}, u32[]{:S(2)}, u32[]{:S(2)}) collective-permute-start(bf16[1024,256]{1,0:T(8,128)(2,1)} %bitcast.34), channel_id=1, source_target_pairs={{0,1},{1,2},{2,3},{3,4},{4,5},{5,6},{6,7},{8,9},{9,10},{10,11},{11... | collective-permute-start | bytes 1572872 | tf_op jit(solution)/shard_map/ppermute | solution.py:27
  2.6 3.6 %collective-permute-start.1 = (bf16[1024,256]{1,0:T(8,128)(2,1)}, bf16[1024,256]{1,0:T(8,128)(2,1)S(1)}, u32[]{:S(2)}, u32[]{:S(2)}) collective-permute-start(bf16[1024,256]{1,0:T(8,128)(2,1)} %bitcast.35), channel_id=1, source_target_pairs={{1,0},{2,1},{3,2},{4,3},{5,4},{6,5},{7,6},{9,8},{10,9},{11,10},{12... | collective-permute-start | bytes 1572872 | tf_op jit(solution)/shard_map/ppermute | solution.py:27
  6.2 3.5 %collective-permute-start.7 = (bf16[1024,256]{1,0:T(8,128)(2,1)}, bf16[1024,256]{1,0:T(8,128)(2,1)S(1)}, u32[]{:S(2)}, u32[]{:S(2)}) collective-permute-start(bf16[1024,256]{1,0:T(8,128)(2,1)} %bitcast.36), channel_id=1, source_target_pairs={{0,8},{8,16},{16,24},{1,9},{9,17},{17,25},{2,10},{10,18},{18,26},{... | collective-permute-start | bytes 1572872 | tf_op jit(solution)/shard_map/ppermute | solution.py:241
  10.4 0.7 fusion.74
  11.3 4.7 %collective-permute-done.1.above = bf16[1024,256]{1,0:T(8,128)(2,1)S(1)} collective-permute-done((bf16[1024,256]{1,0:T(8,128)(2,1)}, bf16[1024,256]{1,0:T(8,128)(2,1)S(1)}, u32[]{:S(2)}, u32[]{:S(2)}) %collective-permute-start.1) | collective-permute-done | bytes 524320 | tf_op jit(solution)/shard_map/ppermute | solution.py:27
  16.1 1.9 copy-done
  18.0 1.0 copy-done.3
  19.7 1.7 product_by_rows.2
  21.4 1.6 collective-permute-start.2
  23.0 2.6 %collective-permute-start.3 = (bf16[256,256]{1,0:T(8,128)(2,1)S(1)}, bf16[256,256]{1,0:T(8,128)(2,1)S(1)}, u32[]{:S(2)}, u32[]{:S(2)}) collective-permute-start(bf16[256,256]{1,0:T(8,128)(2,1)S(1)} %get-tuple-element.18), channel_id=1, source_target_pairs={{0,16},{8,24},{16,0},{24,8},{1,17},{9,25},{17,1},{25,9},{2,18},{10... | collective-permute-start | bytes 393224 | tf_op jit(solution)/shard_map/ppermute | solution.py:197
  25.6 1.3 collective-permute-start.4
  26.9 1.5 collective-permute-start.15
  29.8 5.5 %collective-permute-done.3 = bf16[256,256]{1,0:T(8,128)(2,1)S(1)} collective-permute-done((bf16[256,256]{1,0:T(8,128)(2,1)S(1)}, bf16[256,256]{1,0:T(8,128)(2,1)S(1)}, u32[]{:S(2)}, u32[]{:S(2)}) %collective-permute-start.3) | collective-permute-done | bytes 131104 | tf_op jit(solution)/shard_map/ppermute | solution.py:197
  35.3 1.0 fusion.65
  36.3 24.0 %all_gather.3.own = bf16[1024,256]{1,0:T(8,128)(2,1)} all-gather(bf16[256,256]{1,0:T(8,128)(2,1)S(1)} %fusion.65), channel_id=1, replica_groups=mesh['lag'=4,'elem'=8] {'lag'}, dimensions={0}, use_global_device_ids=true | all-gather | bytes 655360 | tf_op jit(solution)/shard_map/all_gather | solution.py:247
  60.3 2.2 %collective-permute-start.5 = (bf16[1024,256]{1,0:T(8,128)(2,1)}, bf16[1024,256]{1,0:T(8,128)(2,1)S(1)}, u32[]{:S(2)}, u32[]{:S(2)}) collective-permute-start(bf16[1024,256]{1,0:T(8,128)(2,1)} %all_gather.3.own), channel_id=1, source_target_pairs={{0,1},{1,2},{2,3},{3,4},{4,5},{5,6},{6,7},{8,9},{9,10},{10,11},{11... | collective-permute-start | bytes 1572872 | tf_op jit(solution)/shard_map/ppermute | solution.py:27
  62.5 3.5 %collective-permute-start.6 = (bf16[1024,256]{1,0:T(8,128)(2,1)}, bf16[1024,256]{1,0:T(8,128)(2,1)}, u32[]{:S(2)}, u32[]{:S(2)}) collective-permute-start(bf16[1024,256]{1,0:T(8,128)(2,1)} %all_gather.3.own), channel_id=1, source_target_pairs={{1,0},{2,1},{3,2},{4,3},{5,4},{6,5},{7,6},{9,8},{10,9},{11,10},{12... | collective-permute-start | bytes 1572872 | tf_op jit(solution)/shard_map/ppermute | solution.py:27
  66.7 1.3 collective-permute-start.12
  68.0 1.5 collective-permute-start.16
  69.5 1.4 block_product.5
  70.9 1.3 collective-permute-start.10
  72.2 5.1 %collective-permute-done.12 = f32[264,256]{1,0:T(8,128)S(1)} collective-permute-done((f32[264,256]{1,0:T(8,128)}, f32[264,256]{1,0:T(8,128)S(1)}, u32[]{:S(2)}, u32[]{:S(2)}) %collective-permute-start.12) | collective-permute-done | bytes 270368 | tf_op jit(solution)/shard_map/ppermute | solution.py:240
  77.3 1.3 collective-permute-start.13
  78.6 0.8 copy-done.6
  79.4 1.3 collective-permute-start.14
  81.4 1.0 copy-done.7
  82.5 3.6 %block_product.4 = (f32[1024,256]{1,0:T(8,128)S(1)}, bf16[1024,256]{1,0:T(8,128)(2,1)}) custom-call(s32[1,1,3]{2,1,0:T(1,128)S(1)} %copy-done.10, s32[1]{0:T(128)S(6)} %copy.11.live, bf16[1,1024,1536]{2,1,0:T(8,128)(2,1)S(1)} %copy-done.1, bf16[1024,256]{1,0:T(8,128)(2,1)S(1)} %copy-done.7, bf16[1024,256]{1,0:T(8,128)(2,1)} %all_gather.3.own, ...), custom_call_target="tpu_custom_call" | custom-call | flops 805306368 | bytes 5242880 | tf_op jit(solution)/shard_map/block_product/pallas_call | solution.py:122
  86.1 7.3 %collective-permute-done.13 = f32[264,256]{1,0:T(8,128)} collective-permute-done((f32[264,256]{1,0:T(8,128)}, f32[264,256]{1,0:T(8,128)}, u32[]{:S(2)}, u32[]{:S(2)}) %collective-permute-start.13) | collective-permute-done | bytes 270368 | tf_op jit(solution)/shard_map/ppermute | solution.py:240
  93.3 1.3 collective-permute-start.22
  94.7 6.2 %collective-permute-done.10 = bf16[1024,256]{1,0:T(8,128)(2,1)} collective-permute-done((bf16[1024,256]{1,0:T(8,128)(2,1)}, bf16[1024,256]{1,0:T(8,128)(2,1)}, u32[]{:S(2)}, u32[]{:S(2)}) %collective-permute-start.10) | collective-permute-done | bytes 524320 | tf_op jit(solution)/shard_map/ppermute | solution.py:210
  100.8 1.3 fusion.1
  102.2 1.3 collective-permute-start.11
  103.5 1.0 slice.52
  104.5 1.1 slice.54
  105.6 1.1 slice.55
  106.7 0.8 fusion.70
  108.8 0.8 fusion.72
  109.6 7.6 %collective-permute-done.11 = bf16[1024,256]{1,0:T(8,128)(2,1)S(1)} collective-permute-done((bf16[1024,256]{1,0:T(8,128)(2,1)S(1)}, bf16[1024,256]{1,0:T(8,128)(2,1)S(1)}, u32[]{:S(2)}, u32[]{:S(2)}) %collective-permute-start.11) | collective-permute-done | bytes 524320 | tf_op jit(solution)/shard_map/ppermute | solution.py:210
  117.2 7.4 %broadcast_select_fusion = (bf16[1024,256]{1,0:T(8,128)(2,1)}, bf16[1024,256]{1,0:T(8,128)(2,1)}, f32[1024,256]{1,0:T(8,128)}) fusion(bf16[1024,256]{1,0:T(8,128)(2,1)} %collective-permute-done.15.own, pred[]{:T(512)S(6)} %eq.14, f32[1024]{0:T(1024)S(1)} %get-tuple-element.49, f32[1024]{0:T(1024)S(1)} %get-tuple-element.48, ...), kind=kLoop, calls=%fused_computation.51 | loop fusion | flops 18087936 | bytes 6303745 | tf_op jit(solution)/shard_map/jit(_where)/select_n | solution.py:268
  124.6 1.9 %collective-permute-start.17 = (bf16[1024,256]{1,0:T(8,128)(2,1)}, bf16[1024,256]{1,0:T(8,128)(2,1)}, u32[]{:S(2)}, u32[]{:S(2)}) collective-permute-start(bf16[1024,256]{1,0:T(8,128)(2,1)} %get-tuple-element.35.own), channel_id=1, source_target_pairs={{0,1},{1,2},{2,3},{3,4},{4,5},{5,6},{6,7}} | collective-permute-start | bytes 1572872 | tf_op jit(solution)/shard_map/ppermute | solution.py:27
  126.5 3.6 %collective-permute-start.18 = (bf16[1024,256]{1,0:T(8,128)(2,1)}, bf16[1024,256]{1,0:T(8,128)(2,1)}, u32[]{:S(2)}, u32[]{:S(2)}) collective-permute-start(bf16[1024,256]{1,0:T(8,128)(2,1)} %get-tuple-element.35.own), channel_id=1, source_target_pairs={{1,0},{2,1},{3,2},{4,3},{5,4},{6,5},{7,6}} | collective-permute-start | bytes 1572872 | tf_op jit(solution)/shard_map/ppermute | solution.py:27
  130.2 0.9 add_convert_fusion
  131.1 1.3 collective-permute-start.21
  132.5 1.5 collective-permute-start.23
  133.9 1.5 collective-permute-done.17.below
  135.4 2.4 %collective-permute-done.18.above = bf16[1024,256]{1,0:T(8,128)(2,1)} collective-permute-done((bf16[1024,256]{1,0:T(8,128)(2,1)}, bf16[1024,256]{1,0:T(8,128)(2,1)}, u32[]{:S(2)}, u32[]{:S(2)}) %collective-permute-start.18) | collective-permute-done | bytes 524320 | tf_op jit(solution)/shard_map/ppermute | solution.py:27
  137.8 3.0 %block_product.6 = f32[1024,256]{1,0:T(8,128)S(1)} custom-call(s32[1,1,3]{2,1,0:T(1,128)S(1)} %copy-done.10, s32[1]{0:T(128)S(6)} %copy.11.live, bf16[1,1024,1536]{2,1,0:T(8,128)(2,1)S(1)} %copy-done.1, bf16[1024,256]{1,0:T(8,128)(2,1)} %collective-permute-done.17.below, bf16[1024,256]{1,0:T(8,128)(2,1)} %get-tuple-element.35.own, ...), custom_call_target="tpu_custom_call" | custom-call | flops 805306368 | bytes 5242880 | tf_op jit(solution)/shard_map/block_product/pallas_call | solution.py:122
  140.8 6.1 %collective-permute-done.21 = bf16[1024,256]{1,0:T(8,128)(2,1)} collective-permute-done((bf16[1024,256]{1,0:T(8,128)(2,1)}, bf16[1024,256]{1,0:T(8,128)(2,1)}, u32[]{:S(2)}, u32[]{:S(2)}) %collective-permute-start.21) | collective-permute-done | bytes 524320 | tf_op jit(solution)/shard_map/ppermute | solution.py:210
  146.9 7.7 %multiply_add_fusion = (f32[1024,256]{1,0:T(8,128)S(1)}, bf16[1024,256]{1,0:T(8,128)(2,1)S(1)}) fusion(f32[1024,256]{1,0:T(8,128)S(1)} %copy-done.23, bf16[1024,256]{1,0:T(8,128)(2,1)} %all_gather.3.own, f32[256,256]{1,0:T(8,128)S(1)} %copy-done.21, f32[256,256]{1,0:T(8,128)S(1)} %copy-done.19, f32[256,256]{1,0:T(8,128)S(1)} %copy-done.17, ...), kind=kLoop, calls=%fused_computation.41 | loop fusion | flops 20971520 | bytes 6303744 | tf_op jit(solution)/shard_map/add | solution.py:189
  154.7 1.9 %collective-permute-start.24 = (bf16[1024,256]{1,0:T(8,128)(2,1)S(1)}, bf16[1024,256]{1,0:T(8,128)(2,1)S(1)}, u32[]{:S(2)}, u32[]{:S(2)}) collective-permute-start(bf16[1024,256]{1,0:T(8,128)(2,1)S(1)} %select_select_fusion.own), channel_id=1, source_target_pairs={{0,1},{1,2},{2,3},{3,4},{4,5},{5,6},{6,7},{8,9},{9,10},{10,11},{11... | collective-permute-start | bytes 1572872 | tf_op jit(solution)/shard_map/ppermute | solution.py:27
  156.7 3.6 %collective-permute-start.25 = (bf16[1024,256]{1,0:T(8,128)(2,1)S(1)}, bf16[1024,256]{1,0:T(8,128)(2,1)S(1)}, u32[]{:S(2)}, u32[]{:S(2)}) collective-permute-start(bf16[1024,256]{1,0:T(8,128)(2,1)S(1)} %select_select_fusion.own), channel_id=1, source_target_pairs={{1,0},{2,1},{3,2},{4,3},{5,4},{6,5},{7,6},{9,8},{10,9},{11,10},{12... | collective-permute-start | bytes 1572872 | tf_op jit(solution)/shard_map/ppermute | solution.py:27
  160.3 0.8 fusion.69
  161.2 1.3 collective-permute-start.29
  162.5 2.9 %collective-permute-start.30 = (f32[256,256]{1,0:T(8,128)}, f32[256,256]{1,0:T(8,128)}, u32[]{:S(2)}, u32[]{:S(2)}) collective-permute-start(f32[256,256]{1,0:T(8,128)} %get-tuple-element.38), channel_id=1, source_target_pairs={{0,16},{1,17},{2,18},{3,19},{4,20},{5,21},{6,22},{7,23}} | collective-permute-start | bytes 786440 | tf_op jit(solution)/shard_map/ppermute | solution.py:274
  165.4 2.0 %collective-permute-start.31 = (f32[256,256]{1,0:T(8,128)}, f32[256,256]{1,0:T(8,128)}, u32[]{:S(2)}, u32[]{:S(2)}) collective-permute-start(f32[256,256]{1,0:T(8,128)} %get-tuple-element.37), channel_id=1, source_target_pairs={{0,8},{1,9},{2,10},{3,11},{4,12},{5,13},{6,14},{7,15}} | collective-permute-start | bytes 786440 | tf_op jit(solution)/shard_map/ppermute | solution.py:274
  167.4 1.1 collective-permute-done.25.above
  168.5 2.3 %product_by_rows.3 = (f32[256,256]{1,0:T(8,128)S(1)}, bf16[256,256]{1,0:T(8,128)(2,1)}, bf16[256,256]{1,0:T(8,128)(2,1)}, bf16[256,256]{1,0:T(8,128)(2,1)S(1)}) custom-call(s32[1,1,3]{2,1,0:T(1,128)S(1)} %copy-done.10, s32[1]{0:T(128)S(6)} %copy.11.live, bf16[1,1024,1536]{2,1,0:T(8,128)(2,1)S(1)} %copy-done.1, ...), custom_call_target="tpu_custom_call" | custom-call | flops 805306368 | bytes 5242880 | tf_op jit(solution)/shard_map/product_by_rows/pallas_call | solution.py:70
  171.6 0.9 collective-permute-start.27
  172.5 2.9 %collective-permute-start.28 = (bf16[256,256]{1,0:T(8,128)(2,1)S(1)}, bf16[256,256]{1,0:T(8,128)(2,1)}, u32[]{:S(2)}, u32[]{:S(2)}) collective-permute-start(bf16[256,256]{1,0:T(8,128)(2,1)S(1)} %get-tuple-element.29), channel_id=1, source_target_pairs={{0,24},{8,0},{16,8},{24,16},{1,25},{9,1},{17,9},{25,17},{2,26},{10... | collective-permute-start | bytes 393224 | tf_op jit(solution)/shard_map/ppermute | solution.py:197
  176.1 4.4 %collective-permute-done.31 = f32[256,256]{1,0:T(8,128)} collective-permute-done((f32[256,256]{1,0:T(8,128)}, f32[256,256]{1,0:T(8,128)}, u32[]{:S(2)}, u32[]{:S(2)}) %collective-permute-start.31) | collective-permute-done | bytes 262176 | tf_op jit(solution)/shard_map/ppermute | solution.py:274
  180.5 2.8 %collective-permute-done.26 = bf16[256,256]{1,0:T(8,128)(2,1)} collective-permute-done((bf16[256,256]{1,0:T(8,128)(2,1)}, bf16[256,256]{1,0:T(8,128)(2,1)}, u32[]{:S(2)}, u32[]{:S(2)}) %collective-permute-start.26) | collective-permute-done | bytes 131104 | tf_op jit(solution)/shard_map/ppermute | solution.py:197
  183.3 2.3 %collective-permute-done.27 = bf16[256,256]{1,0:T(8,128)(2,1)} collective-permute-done((bf16[256,256]{1,0:T(8,128)(2,1)}, bf16[256,256]{1,0:T(8,128)(2,1)}, u32[]{:S(2)}, u32[]{:S(2)}) %collective-permute-start.27) | collective-permute-done | bytes 131104 | tf_op jit(solution)/shard_map/ppermute | solution.py:197
  185.6 1.3 collective-permute-done.28
  186.9 3.1 %add_bitcast_fusion = (f32[1,1,256,256]{3,2,1,0:T(8,128)}, bf16[256,256]{1,0:T(8,128)(2,1)}) fusion(f32[256]{0:T(256)S(1)} %bitcast.42, f32[256]{0:T(256)S(1)} %broadcast_multiply_fusion.1, f32[256]{0:T(256)S(1)} %bitcast.44, bf16[256,256]{1,0:T(8,128)(2,1)} %collective-permute-done.28, bf16[256,256]{1,0:T(8,128)(2,1)} %collective-permute-done.27, ...), kind=kLoop, calls=%fused_computation.95 | loop fusion | flops 4587520 | bytes 2362371 | tf_op jit(solution)/shard_map/broadcast_in_dim | solution.py:278
  (81 shorter events, 6.6 us)
Async XLA Ops:
  0.6 10.7 %collective-permute-start = (bf16[1024,256]{1,0:T(8,128)(2,1)}, bf16[1024,256]{1,0:T(8,128)(2,1)S(1)}, u32[]{:S(2)}, u32[]{:S(2)}) collective-permute-start(bf16[1024,256]{1,0:T(8,128)(2,1)} %bitcast.34), channel_id=1, source_target_pairs={{0,1},{1,2},{2,3},{3,4},{4,5},{5,6},{6,7},{8,9},{9,10},{10,11},{11... | collective-permute-start | bytes 1572872 | tf_op jit(solution)/shard_map/ppermute | solution.py:27
  2.6 13.5 %collective-permute-start.1 = (bf16[1024,256]{1,0:T(8,128)(2,1)}, bf16[1024,256]{1,0:T(8,128)(2,1)S(1)}, u32[]{:S(2)}, u32[]{:S(2)}) collective-permute-start(bf16[1024,256]{1,0:T(8,128)(2,1)} %bitcast.35), channel_id=1, source_target_pairs={{1,0},{2,1},{3,2},{4,3},{5,4},{6,5},{7,6},{9,8},{10,9},{11,10},{12... | collective-permute-start | bytes 1572872 | tf_op jit(solution)/shard_map/ppermute | solution.py:27
  6.2 20.7 %collective-permute-start.7 = (bf16[1024,256]{1,0:T(8,128)(2,1)}, bf16[1024,256]{1,0:T(8,128)(2,1)S(1)}, u32[]{:S(2)}, u32[]{:S(2)}) collective-permute-start(bf16[1024,256]{1,0:T(8,128)(2,1)} %bitcast.36), channel_id=1, source_target_pairs={{0,8},{8,16},{16,24},{1,9},{9,17},{17,25},{2,10},{10,18},{18,26},{... | collective-permute-start | bytes 1572872 | tf_op jit(solution)/shard_map/ppermute | solution.py:241
  10.4 55.6 %copy-start.11 = (f32[1,1,256]{2,1,0:T(1,128)S(1)}, f32[1,1,256]{2,1,0:T(1,128)}, u32[]{:S(2)}) copy-start(f32[1,1,256]{2,1,0:T(1,128)} %coef_b.1) | copy-start | bytes 3076
  10.4 55.6 %copy-start.12 = (f32[1,1,256]{2,1,0:T(1,128)S(1)}, f32[1,1,256]{2,1,0:T(1,128)}, u32[]{:S(2)}) copy-start(f32[1,1,256]{2,1,0:T(1,128)} %coef_a.1) | copy-start | bytes 3076
  10.4 55.6 %copy-start.13 = (f32[1,1,256]{2,1,0:T(1,128)S(1)}, f32[1,1,256]{2,1,0:T(1,128)}, u32[]{:S(2)}) copy-start(f32[1,1,256]{2,1,0:T(1,128)} %sigma.1) | copy-start | bytes 3076
  16.1 1.9 copy-start
  18.0 1.0 copy-start.3
  19.0 0.7 copy-start.9
  19.7 15.6 %copy-start.2 = (f32[1,1,256,256]{3,2,1,0:T(8,128)S(1)}, f32[1,1,256,256]{3,2,1,0:T(8,128)}, u32[]{:S(2)}) copy-start(f32[1,1,256,256]{3,2,1,0:T(8,128)} %stress.7) | copy-start | bytes 786436
  19.7 15.6 %copy-start.5 = (f32[1,1,256,256]{3,2,1,0:T(8,128)S(1)}, f32[1,1,256,256]{3,2,1,0:T(8,128)}, u32[]{:S(2)}) copy-start(f32[1,1,256,256]{3,2,1,0:T(8,128)} %state.1) | copy-start | bytes 786436
  19.7 49.8 %copy-start.1 = (bf16[1,1024,1536]{2,1,0:T(8,128)(2,1)S(1)}, bf16[1,1024,1536]{2,1,0:T(8,128)(2,1)}, u32[]{:S(2)}) copy-start(bf16[1,1024,1536]{2,1,0:T(8,128)(2,1)} %tile.11) | copy-start | bytes 9437188
  21.4 7.7 %collective-permute-start.2 = (bf16[256,256]{1,0:T(8,128)(2,1)S(1)}, bf16[256,256]{1,0:T(8,128)(2,1)S(1)}, u32[]{:S(2)}, u32[]{:S(2)}) collective-permute-start(bf16[256,256]{1,0:T(8,128)(2,1)S(1)} %get-tuple-element.17), channel_id=1, source_target_pairs={{0,8},{8,16},{16,24},{24,0},{1,9},{9,17},{17,25},{25,1},{2,10},{10... | collective-permute-start | bytes 393224 | tf_op jit(solution)/shard_map/ppermute | solution.py:197
  23.0 12.3 %collective-permute-start.3 = (bf16[256,256]{1,0:T(8,128)(2,1)S(1)}, bf16[256,256]{1,0:T(8,128)(2,1)S(1)}, u32[]{:S(2)}, u32[]{:S(2)}) collective-permute-start(bf16[256,256]{1,0:T(8,128)(2,1)S(1)} %get-tuple-element.18), channel_id=1, source_target_pairs={{0,16},{8,24},{16,0},{24,8},{1,17},{9,25},{17,1},{25,9},{2,18},{10... | collective-permute-start | bytes 393224 | tf_op jit(solution)/shard_map/ppermute | solution.py:197
  25.6 9.7 %collective-permute-start.4 = (bf16[256,256]{1,0:T(8,128)(2,1)S(1)}, bf16[256,256]{1,0:T(8,128)(2,1)S(1)}, u32[]{:S(2)}, u32[]{:S(2)}) collective-permute-start(bf16[256,256]{1,0:T(8,128)(2,1)S(1)} %get-tuple-element.19), channel_id=1, source_target_pairs={{0,24},{8,0},{16,8},{24,16},{1,25},{9,1},{17,9},{25,17},{2,26},{10... | collective-permute-start | bytes 393224 | tf_op jit(solution)/shard_map/ppermute | solution.py:197
  26.9 39.8 %collective-permute-start.15 = (bf16[1024,256]{1,0:T(8,128)(2,1)S(1)}, bf16[1024,256]{1,0:T(8,128)(2,1)}, u32[]{:S(2)}, u32[]{:S(2)}) collective-permute-start(bf16[1024,256]{1,0:T(8,128)(2,1)S(1)} %collective-permute-done.7.own), channel_id=1, source_target_pairs={{8,16},{16,24},{9,17},{17,25},{10,18},{18,26},{11,19},{19,27},{12,... | collective-permute-start | bytes 1572872 | tf_op jit(solution)/shard_map/ppermute | solution.py:251
  28.4 39.6 %collective-permute-start.8 = (bf16[1024,256]{1,0:T(8,128)(2,1)S(1)}, bf16[1024,256]{1,0:T(8,128)(2,1)S(1)}, u32[]{:S(2)}, u32[]{:S(2)}) collective-permute-start(bf16[1024,256]{1,0:T(8,128)(2,1)S(1)} %collective-permute-done.7.own), channel_id=1, source_target_pairs={{8,9},{9,10},{10,11},{11,12},{12,13},{13,14},{14,15},{16,17},{17,1... | collective-permute-start | bytes 1572872 | tf_op jit(solution)/shard_map/ppermute | solution.py:27
  29.1 40.4 %collective-permute-start.9 = (bf16[1024,256]{1,0:T(8,128)(2,1)S(1)}, bf16[1024,256]{1,0:T(8,128)(2,1)S(1)}, u32[]{:S(2)}, u32[]{:S(2)}) collective-permute-start(bf16[1024,256]{1,0:T(8,128)(2,1)S(1)} %collective-permute-done.7.own), channel_id=1, source_target_pairs={{9,8},{10,9},{11,10},{12,11},{13,12},{14,13},{15,14},{17,16},{18,1... | collective-permute-start | bytes 1572872 | tf_op jit(solution)/shard_map/ppermute | solution.py:27
  60.3 21.2 %copy-start.10 = (s32[1,1,3]{2,1,0:T(1,128)S(1)}, s32[1,1,3]{2,1,0:T(1,128)}, u32[]{:S(2)}) copy-start(s32[1,1,3]{2,1,0:T(1,128)} %picks.11) | copy-start | bytes 40
  60.3 18.3 %collective-permute-start.5 = (bf16[1024,256]{1,0:T(8,128)(2,1)}, bf16[1024,256]{1,0:T(8,128)(2,1)S(1)}, u32[]{:S(2)}, u32[]{:S(2)}) collective-permute-start(bf16[1024,256]{1,0:T(8,128)(2,1)} %all_gather.3.own), channel_id=1, source_target_pairs={{0,1},{1,2},{2,3},{3,4},{4,5},{5,6},{6,7},{8,9},{9,10},{10,11},{11... | collective-permute-start | bytes 1572872 | tf_op jit(solution)/shard_map/ppermute | solution.py:27
  62.5 18.2 %collective-permute-start.6 = (bf16[1024,256]{1,0:T(8,128)(2,1)}, bf16[1024,256]{1,0:T(8,128)(2,1)}, u32[]{:S(2)}, u32[]{:S(2)}) collective-permute-start(bf16[1024,256]{1,0:T(8,128)(2,1)} %all_gather.3.own), channel_id=1, source_target_pairs={{1,0},{2,1},{3,2},{4,3},{5,4},{6,5},{7,6},{9,8},{10,9},{11,10},{12... | collective-permute-start | bytes 1572872 | tf_op jit(solution)/shard_map/ppermute | solution.py:27
  66.7 10.6 %collective-permute-start.12 = (f32[264,256]{1,0:T(8,128)}, f32[264,256]{1,0:T(8,128)S(1)}, u32[]{:S(2)}, u32[]{:S(2)}) collective-permute-start(f32[264,256]{1,0:T(8,128)} %pack.1), channel_id=1, source_target_pairs={{8,0},{9,1},{10,2},{11,3},{12,4},{13,5},{14,6},{15,7}} | collective-permute-start | bytes 811016 | tf_op jit(solution)/shard_map/ppermute | solution.py:240
  68.0 26.6 %collective-permute-start.16 = (bf16[1024,256]{1,0:T(8,128)(2,1)}, bf16[1024,256]{1,0:T(8,128)(2,1)}, u32[]{:S(2)}, u32[]{:S(2)}) collective-permute-start(bf16[1024,256]{1,0:T(8,128)(2,1)} %collective-permute-done.15.own), channel_id=1, source_target_pairs={{16,17},{17,18},{18,19},{19,20},{20,21},{21,22},{22,23},{24,25},{2... | collective-permute-start | bytes 1572872 | tf_op jit(solution)/shard_map/ppermute | solution.py:27
  70.9 29.9 %collective-permute-start.10 = (bf16[1024,256]{1,0:T(8,128)(2,1)}, bf16[1024,256]{1,0:T(8,128)(2,1)}, u32[]{:S(2)}, u32[]{:S(2)}) collective-permute-start(bf16[1024,256]{1,0:T(8,128)(2,1)} %block_product.5), channel_id=1, source_target_pairs={{8,0},{24,16},{9,1},{25,17},{10,2},{26,18},{11,3},{27,19},{12,4},{... | collective-permute-start | bytes 1572872 | tf_op jit(solution)/shard_map/ppermute | solution.py:210
  77.3 1.3 copy-start.25
  77.3 16.0 %collective-permute-start.13 = (f32[264,256]{1,0:T(8,128)}, f32[264,256]{1,0:T(8,128)}, u32[]{:S(2)}, u32[]{:S(2)}) collective-permute-start(f32[264,256]{1,0:T(8,128)} %pack.1), channel_id=1, source_target_pairs={{16,0},{17,1},{18,2},{19,3},{20,4},{21,5},{22,6},{23,7}} | collective-permute-start | bytes 811016 | tf_op jit(solution)/shard_map/ppermute | solution.py:240
  78.6 0.8 copy-start.6
  79.4 15.2 %collective-permute-start.14 = (f32[264,256]{1,0:T(8,128)}, f32[264,256]{1,0:T(8,128)}, u32[]{:S(2)}, u32[]{:S(2)}) collective-permute-start(f32[264,256]{1,0:T(8,128)} %pack.1), channel_id=1, source_target_pairs={{24,0},{25,1},{26,2},{27,3},{28,4},{29,5},{30,6},{31,7}} | collective-permute-start | bytes 811016 | tf_op jit(solution)/shard_map/ppermute | solution.py:240
  80.7 26.8 %collective-permute-start.19 = (bf16[1024,256]{1,0:T(8,128)(2,1)}, bf16[1024,256]{1,0:T(8,128)(2,1)S(1)}, u32[]{:S(2)}, u32[]{:S(2)}) collective-permute-start(bf16[1024,256]{1,0:T(8,128)(2,1)} %collective-permute-done.15.own), channel_id=1, source_target_pairs={{17,16},{18,17},{19,18},{20,19},{21,20},{22,21},{23,22},{25,24},{2... | collective-permute-start | bytes 1572872 | tf_op jit(solution)/shard_map/ppermute | solution.py:27
  81.4 1.0 copy-start.7
  82.5 22.0 %copy-start.26 = (f32[264,256]{1,0:T(8,128)S(1)}, f32[264,256]{1,0:T(8,128)}, u32[]{:S(2)}) copy-start(f32[264,256]{1,0:T(8,128)} %copy-done.25) | copy-start | bytes 811012
  93.3 47.4 %collective-permute-start.22 = (bf16[1024,256]{1,0:T(8,128)(2,1)}, bf16[1024,256]{1,0:T(8,128)(2,1)}, u32[]{:S(2)}, u32[]{:S(2)}) collective-permute-start(bf16[1024,256]{1,0:T(8,128)(2,1)} %get-tuple-element.25), channel_id=1, source_target_pairs={{8,0},{9,1},{10,2},{11,3},{12,4},{13,5},{14,6},{15,7}} | collective-permute-start | bytes 1572872 | tf_op jit(solution)/shard_map/ppermute | solution.py:262
  102.2 15.1 %collective-permute-start.11 = (bf16[1024,256]{1,0:T(8,128)(2,1)S(1)}, bf16[1024,256]{1,0:T(8,128)(2,1)S(1)}, u32[]{:S(2)}, u32[]{:S(2)}) collective-permute-start(bf16[1024,256]{1,0:T(8,128)(2,1)S(1)} %fusion.1), channel_id=1, source_target_pairs={{16,0},{17,1},{18,2},{19,3},{20,4},{21,5},{22,6},{23,7}} | collective-permute-start | bytes 1572872 | tf_op jit(solution)/shard_map/ppermute | solution.py:210
  104.4 12.8 %copy-start.14 = (f32[256,256]{1,0:T(8,128)}, f32[256,256]{1,0:T(8,128)S(1)}, u32[]{:S(2)}) copy-start(f32[256,256]{1,0:T(8,128)S(1)} %slice.52) | copy-start | bytes 786436
  104.5 26.6 %copy-start.16 = (f32[256,256]{1,0:T(8,128)}, f32[256,256]{1,0:T(8,128)S(1)}, u32[]{:S(2)}) copy-start(f32[256,256]{1,0:T(8,128)S(1)} %slice.53) | copy-start | bytes 786436
  105.6 25.5 %copy-start.18 = (f32[256,256]{1,0:T(8,128)}, f32[256,256]{1,0:T(8,128)S(1)}, u32[]{:S(2)}) copy-start(f32[256,256]{1,0:T(8,128)S(1)} %slice.54) | copy-start | bytes 786436
  106.7 24.4 %copy-start.20 = (f32[256,256]{1,0:T(8,128)}, f32[256,256]{1,0:T(8,128)S(1)}, u32[]{:S(2)}) copy-start(f32[256,256]{1,0:T(8,128)S(1)} %slice.55) | copy-start | bytes 786436
  108.1 22.1 %collective-permute-start.20 = (bf16[1024,256]{1,0:T(8,128)(2,1)S(1)}, bf16[1024,256]{1,0:T(8,128)(2,1)S(1)}, u32[]{:S(2)}, u32[]{:S(2)}) collective-permute-start(bf16[1024,256]{1,0:T(8,128)(2,1)S(1)} %block_product.7), channel_id=1, source_target_pairs={{24,16},{25,17},{26,18},{27,19},{28,20},{29,21},{30,22},{31,23}} | collective-permute-start | bytes 1572872 | tf_op jit(solution)/shard_map/ppermute | solution.py:210
  124.6 10.8 %collective-permute-start.17 = (bf16[1024,256]{1,0:T(8,128)(2,1)}, bf16[1024,256]{1,0:T(8,128)(2,1)}, u32[]{:S(2)}, u32[]{:S(2)}) collective-permute-start(bf16[1024,256]{1,0:T(8,128)(2,1)} %get-tuple-element.35.own), channel_id=1, source_target_pairs={{0,1},{1,2},{2,3},{3,4},{4,5},{5,6},{6,7}} | collective-permute-start | bytes 1572872 | tf_op jit(solution)/shard_map/ppermute | solution.py:27
  126.5 11.2 %collective-permute-start.18 = (bf16[1024,256]{1,0:T(8,128)(2,1)}, bf16[1024,256]{1,0:T(8,128)(2,1)}, u32[]{:S(2)}, u32[]{:S(2)}) collective-permute-start(bf16[1024,256]{1,0:T(8,128)(2,1)} %get-tuple-element.35.own), channel_id=1, source_target_pairs={{1,0},{2,1},{3,2},{4,3},{5,4},{6,5},{7,6}} | collective-permute-start | bytes 1572872 | tf_op jit(solution)/shard_map/ppermute | solution.py:27
  131.1 15.7 %collective-permute-start.21 = (bf16[1024,256]{1,0:T(8,128)(2,1)}, bf16[1024,256]{1,0:T(8,128)(2,1)}, u32[]{:S(2)}, u32[]{:S(2)}) collective-permute-start(bf16[1024,256]{1,0:T(8,128)(2,1)} %add_convert_fusion), channel_id=1, source_target_pairs={{16,0},{17,1},{18,2},{19,3},{20,4},{21,5},{22,6},{23,7}} | collective-permute-start | bytes 1572872 | tf_op jit(solution)/shard_map/ppermute | solution.py:210
  132.4 14.4 %copy-start.15 = (f32[256,256]{1,0:T(8,128)S(1)}, f32[256,256]{1,0:T(8,128)}, u32[]{:S(2)}) copy-start(f32[256,256]{1,0:T(8,128)} %copy-done.14) | copy-start | bytes 786436
  132.4 14.4 %copy-start.17 = (f32[256,256]{1,0:T(8,128)S(1)}, f32[256,256]{1,0:T(8,128)}, u32[]{:S(2)}) copy-start(f32[256,256]{1,0:T(8,128)} %copy-done.16) | copy-start | bytes 786436
  132.5 14.4 %copy-start.19 = (f32[256,256]{1,0:T(8,128)S(1)}, f32[256,256]{1,0:T(8,128)}, u32[]{:S(2)}) copy-start(f32[256,256]{1,0:T(8,128)} %copy-done.18) | copy-start | bytes 786436
  132.5 14.4 %copy-start.21 = (f32[256,256]{1,0:T(8,128)S(1)}, f32[256,256]{1,0:T(8,128)}, u32[]{:S(2)}) copy-start(f32[256,256]{1,0:T(8,128)} %copy-done.20) | copy-start | bytes 786436
  132.5 14.4 %copy-start.23 = (f32[1024,256]{1,0:T(8,128)S(1)}, f32[1024,256]{1,0:T(8,128)}, u32[]{:S(2)}) copy-start(f32[1024,256]{1,0:T(8,128)} %get-tuple-element.36) | copy-start | bytes 3145732
  132.5 22.1 %collective-permute-start.23 = (bf16[1024,256]{1,0:T(8,128)(2,1)}, bf16[1024,256]{1,0:T(8,128)(2,1)S(1)}, u32[]{:S(2)}, u32[]{:S(2)}) collective-permute-start(bf16[1024,256]{1,0:T(8,128)(2,1)} %get-tuple-element.34), channel_id=1, source_target_pairs={{0,8},{16,24},{1,9},{17,25},{2,10},{18,26},{3,11},{19,27},{4,12},{... | collective-permute-start | bytes 1572872 | tf_op jit(solution)/shard_map/ppermute | solution.py:269
  154.6 12.8 %copy-start.22 = (f32[1024,256]{1,0:T(8,128)}, f32[1024,256]{1,0:T(8,128)S(1)}, u32[]{:S(2)}) copy-start(f32[1024,256]{1,0:T(8,128)S(1)} %get-tuple-element.32) | copy-start | bytes 3145732
  154.7 12.7 %collective-permute-start.24 = (bf16[1024,256]{1,0:T(8,128)(2,1)S(1)}, bf16[1024,256]{1,0:T(8,128)(2,1)S(1)}, u32[]{:S(2)}, u32[]{:S(2)}) collective-permute-start(bf16[1024,256]{1,0:T(8,128)(2,1)S(1)} %select_select_fusion.own), channel_id=1, source_target_pairs={{0,1},{1,2},{2,3},{3,4},{4,5},{5,6},{6,7},{8,9},{9,10},{10,11},{11... | collective-permute-start | bytes 1572872 | tf_op jit(solution)/shard_map/ppermute | solution.py:27
  156.7 11.9 %collective-permute-start.25 = (bf16[1024,256]{1,0:T(8,128)(2,1)S(1)}, bf16[1024,256]{1,0:T(8,128)(2,1)S(1)}, u32[]{:S(2)}, u32[]{:S(2)}) collective-permute-start(bf16[1024,256]{1,0:T(8,128)(2,1)S(1)} %select_select_fusion.own), channel_id=1, source_target_pairs={{1,0},{2,1},{3,2},{4,3},{5,4},{6,5},{7,6},{9,8},{10,9},{11,10},{12... | collective-permute-start | bytes 1572872 | tf_op jit(solution)/shard_map/ppermute | solution.py:27
  160.3 15.1 %copy-start.4 = (bf16[1,1024,256]{2,1,0:T(8,128)(2,1)S(1)}, bf16[1,1024,256]{2,1,0:T(8,128)(2,1)}, u32[]{:S(2)}) copy-start(bf16[1,1024,256]{2,1,0:T(8,128)(2,1)} %param.12) | copy-start | bytes 1572868
  161.2 11.3 %collective-permute-start.29 = (f32[256,256]{1,0:T(8,128)S(1)}, f32[256,256]{1,0:T(8,128)S(1)}, u32[]{:S(2)}, u32[]{:S(2)}) collective-permute-start(f32[256,256]{1,0:T(8,128)S(1)} %get-tuple-element.39), channel_id=1, source_target_pairs={{0,24},{1,25},{2,26},{3,27},{4,28},{5,29},{6,30},{7,31}} | collective-permute-start | bytes 786440 | tf_op jit(solution)/shard_map/ppermute | solution.py:274
  162.5 13.6 %collective-permute-start.30 = (f32[256,256]{1,0:T(8,128)}, f32[256,256]{1,0:T(8,128)}, u32[]{:S(2)}, u32[]{:S(2)}) collective-permute-start(f32[256,256]{1,0:T(8,128)} %get-tuple-element.38), channel_id=1, source_target_pairs={{0,16},{1,17},{2,18},{3,19},{4,20},{5,21},{6,22},{7,23}} | collective-permute-start | bytes 786440 | tf_op jit(solution)/shard_map/ppermute | solution.py:274
  165.4 15.1 %collective-permute-start.31 = (f32[256,256]{1,0:T(8,128)}, f32[256,256]{1,0:T(8,128)}, u32[]{:S(2)}, u32[]{:S(2)}) collective-permute-start(f32[256,256]{1,0:T(8,128)} %get-tuple-element.37), channel_id=1, source_target_pairs={{0,8},{1,9},{2,10},{3,11},{4,12},{5,13},{6,14},{7,15}} | collective-permute-start | bytes 786440 | tf_op jit(solution)/shard_map/ppermute | solution.py:274
  170.9 0.7 copy-start.8
  171.6 11.7 %collective-permute-start.26 = (bf16[256,256]{1,0:T(8,128)(2,1)}, bf16[256,256]{1,0:T(8,128)(2,1)}, u32[]{:S(2)}, u32[]{:S(2)}) collective-permute-start(bf16[256,256]{1,0:T(8,128)(2,1)} %get-tuple-element.27), channel_id=1, source_target_pairs={{0,8},{8,16},{16,24},{24,0},{1,9},{9,17},{17,25},{25,1},{2,10},{10... | collective-permute-start | bytes 393224 | tf_op jit(solution)/shard_map/ppermute | solution.py:197
  171.6 14.0 %collective-permute-start.27 = (bf16[256,256]{1,0:T(8,128)(2,1)}, bf16[256,256]{1,0:T(8,128)(2,1)}, u32[]{:S(2)}, u32[]{:S(2)}) collective-permute-start(bf16[256,256]{1,0:T(8,128)(2,1)} %get-tuple-element.28), channel_id=1, source_target_pairs={{0,16},{8,24},{16,0},{24,8},{1,17},{9,25},{17,1},{25,9},{2,18},{10... | collective-permute-start | bytes 393224 | tf_op jit(solution)/shard_map/ppermute | solution.py:197
  172.5 2.9 %copy-start.24 = (f32[256,256]{1,0:T(8,128)}, f32[256,256]{1,0:T(8,128)S(1)}, u32[]{:S(2)}) copy-start(f32[256,256]{1,0:T(8,128)S(1)} %collective-permute-done.29) | copy-start | bytes 786436
  172.5 14.4 %collective-permute-start.28 = (bf16[256,256]{1,0:T(8,128)(2,1)S(1)}, bf16[256,256]{1,0:T(8,128)(2,1)}, u32[]{:S(2)}, u32[]{:S(2)}) collective-permute-start(bf16[256,256]{1,0:T(8,128)(2,1)S(1)} %get-tuple-element.29), channel_id=1, source_target_pairs={{0,24},{8,0},{16,8},{24,16},{1,25},{9,1},{17,9},{25,17},{2,26},{10... | collective-permute-start | bytes 393224 | tf_op jit(solution)/shard_map/ppermute | solution.py:197

commit v10 on v9

--- a/solution.py
+++ b/solution.py
@@ -159,6 +159,31 @@
     )(state, coef_a, coef_b, sigma)
 
 
+def unpack_kernel(lags, *refs):
+    packed, state, columns = refs[:lags], refs[lags], refs[lags + 1]
+    rows = state.shape[0] // lags
+
+    @pl.when(lax.axis_index("lag") == 0)
+    def _():
+        for d, ref in enumerate(packed):
+            spot = pl.ds(d * rows, rows)
+            state[spot, :] = ref[pl.ds(0, rows), :]
+            columns[spot, :] = jnp.transpose(ref[pl.ds(rows, 8), :])[:rows]
+
+
+def unpack(packed):
+    lags, (height, cols) = len(packed), packed[0].shape
+    rows = (height - 8) * lags
+    return pl.pallas_call(
+        functools.partial(unpack_kernel, lags),
+        in_specs=[VMEM] * lags,
+        out_specs=[VMEM] * 2,
+        out_shape=[jax.ShapeDtypeStruct((rows, cols), jnp.float32), jax.ShapeDtypeStruct((rows, 8), jnp.float32)],
+        compiler_params=PARAMS,
+        name="unpack",
+    )(*packed)
+
+
 def touch(*arrays):
     pl.pallas_call(
         lambda *refs: refs[-1].__setitem__(Ellipsis, jnp.zeros(refs[-1].shape, refs[-1].dtype)),
@@ -250,20 +275,29 @@
     base_1 = tree_to_first(low, lags, 1)
     twice = lax.ppermute(once, "lag", [(i, i + 1) for i in rest[:-1]])
     window_2 = window_of(twice, rest[1:])
-    packed, _ = lax.optimization_barrier((packed, window_2[0]))
-    state = jnp.concatenate([g[:rows] for g in packed], 0)
-    ratio, strength = (jnp.concatenate([g[rows + k, :rows] for g in packed])[:, None] for k in range(2))
-    state = evolved(state, first.astype(jnp.float32))
+    state, columns = unpack(packed)
     (low,) = block_product(*local, window_2, prestress, rest[1:], kinds[1:])
     base_2 = tree_to_first(low, lags, 2)
 
     window = window_of(first, [0, 1])
     high, low = block_product(*local, window, prestress, [0, 1], kinds)
     base_2 = base_2 + [lax.ppermute(low, "lag", [(1, 0)])]
-    second, state = settle_friction(block_load(high, *base_1), state, ratio, strength)
+
+    def on_first(step, *values):
+        like = (jax.ShapeDtypeStruct(field.shape, jnp.bfloat16), jax.ShapeDtypeStruct(field.shape, jnp.float32))
+        return lax.cond(me == 0, step, lambda *_: tuple(jnp.zeros(x.shape, x.dtype) for x in like), *values)
+
+    def second_step(high, start, first, columns, *received):
+        begun = evolved(start, first.astype(jnp.float32))
+        return settle_friction(block_load(high, *received), begun, columns[:, 0:1], columns[:, 1:2])
+
+    def third_step(high, start, columns, *received):
+        return settle_friction(block_load(high, *received), start, columns[:, 0:1], columns[:, 1:2])
+
+    second, state = on_first(second_step, high, state, first, columns, *base_1)
     window = window_of(second, [0])
     (high,) = block_product(*local, window, prestress, [0], kinds[:1])
-    third, state = settle_friction(block_load(high, *base_2), state, ratio, strength)
+    third, state = on_first(third_step, high, state, columns, *base_2)
 
     source = jnp.where(me == 0, second, twice)
     moved = lax.ppermute(source, "lag", [(0, 1)] + [(i, i + 1) for i in every[2:-1]])

time: 193 us -> 208 us (1.078)
  blocking collectives: 24 us -> 33.5 us
  waiting for transfers between devices: 58.4 us -> 51.3 us
  starting transfers between devices: 57.7 us -> 63.2 us
  other arithmetic: 22.3 us -> 26.1 us
  Pallas kernels: 13.9 us -> 17.7 us
    ppermute x4, waiting for transfers between devices: 19.9 us -> 5.05 us  [tree_to_first(): arrived = lax.ppermute(value, 'lag', route)]
    ppermute x3, waiting for transfers between devices: 12.4 us -> 22.8 us  [shards(): packed = [packed] + [lax.ppermute(packed, 'lag', [(d, 0)]) for d in rest]]
    all_gather x1, blocking collectives: 24 us -> 33.5 us  [shards(): first = lax.all_gather(rates, 'lag', axis=0, tiled=True)]
    ppermute x6, starting transfers between devices: 9.45 us -> 17.2 us  [scatter_sum(): total = total + lax.ppermute(parts[d], 'lag', route).astype(jnp.float32)]
    add x1 -> x2, other arithmetic: 7.69 us -> 15 us  [evolved(): state + time_step * (jnp.exp(-state) - jnp.sqrt(speed_of * speed_of + cre...]
    ppermute x1, waiting for transfers between devices: 0.01 us -> 7.1 us  [shards(): once = lax.ppermute(field, 'lag', [(i, i + 1) for i in every[:-1]])]
    ppermute x12, waiting for transfers between devices: 9.87 us -> 3.06 us  [exchange(): return (lax.ppermute(value, axes, up), lax.ppermute(value, axes, down))]
    select_n x1, other arithmetic: 7.36 us -> 1.92 us  [shards(): source = jnp.where(me == 0, second, twice)]
  transfers between devices with their start and end apart: 32 -> 32, of which waited for: 15 -> 10; matrix products, arithmetic and copies ran while one was open for 13% -> 13% of each run, Pallas kernels for 7% -> 9%
where the time goes in v10:
time: 208 us; the launch traced here: 206 us
  starting transfers between devices  63.2 us (30%)
  waiting for transfers between devices  51.3 us (25%)
  blocking collectives  33.5 us (16%)
  other arithmetic  26.1 us (13%)
  Pallas kernels  17.7 us (9%)
  local copies, waits for them, and re-layouts  12.1 us (6%)
    all_gather x1, blocking collectives, shards(): first = lax.all_gather(rates, 'lag', axis=0, tiled=True)  33.5 us
    ppermute x12, starting transfers between devices, exchange(): return (lax.ppermute(value, axes, up), lax.ppermute(value, axes, down))  23.8 us
    ppermute x3, waiting for transfers between devices, shards(): packed = [packed] + [lax.ppermute(packed, 'lag', [(d, 0)]) for d in rest]  22.8 us
    ppermute x6, starting transfers between devices, scatter_sum(): total = total + lax.ppermute(parts[d], 'lag', route).astype(jnp.float32)  17.2 us
    add x2, other arithmetic, evolved(): state + time_step * (jnp.exp(-state) - jnp.sqrt(speed_of * speed_of + cre...  15 us
    pallas_call x4, Pallas kernels, block_product(): pl.pallas_call(functools.partial(block_kernel, chunks, (planes[0], planes...  9.97 us
    ppermute x6, waiting for transfers between devices, scatter_sum(): total = total + lax.ppermute(parts[d], 'lag', route).astype(jnp.float32)  8.54 us
    unnamed x38, local copies, waits for them, and re-layouts  7.63 us
  transfers between devices with their start and end apart: 32, of which 10 were waited for; matrix products, arithmetic and copies ran while one was open for 13% of the time, Pallas kernels for 9%

profile of v10, /device:TPU:2, one launch (start us, length us, event | category | flops | bytes accessed | tf_op | source)
XLA Modules:
  0.0 205.6 jit_solution(1303876604405322506)
XLA Ops:
  0.7 3.6 %collective-permute-start = (bf16[1024,256]{1,0:T(8,128)(2,1)}, bf16[1024,256]{1,0:T(8,128)(2,1)S(1)}, u32[]{:S(2)}, u32[]{:S(2)}) collective-permute-start(bf16[1024,256]{1,0:T(8,128)(2,1)} %bitcast.30), channel_id=1, source_target_pairs={{0,8},{8,16},{16,24},{1,9},{9,17},{17,25},{2,10},{10,18},{18,26},{... | collective-permute-start | bytes 1572872 | tf_op jit(solution)/shard_map/ppermute | solution.py:266
  4.3 1.9 collective-permute-start.10
  6.3 2.4 %collective-permute-start.9 = (bf16[1024,256]{1,0:T(8,128)(2,1)}, bf16[1024,256]{1,0:T(8,128)(2,1)S(1)}, u32[]{:S(2)}, u32[]{:S(2)}) collective-permute-start(bf16[1024,256]{1,0:T(8,128)(2,1)} %bitcast.32), channel_id=1, source_target_pairs={{0,1},{1,2},{2,3},{3,4},{4,5},{5,6},{6,7},{8,9},{9,10},{10,11},{11... | collective-permute-start | bytes 1572872 | tf_op jit(solution)/shard_map/ppermute | solution.py:27
  8.7 7.1 %collective-permute-done.own = bf16[1024,256]{1,0:T(8,128)(2,1)S(1)} collective-permute-done((bf16[1024,256]{1,0:T(8,128)(2,1)}, bf16[1024,256]{1,0:T(8,128)(2,1)S(1)}, u32[]{:S(2)}, u32[]{:S(2)}) %collective-permute-start) | collective-permute-done | bytes 524320 | tf_op jit(solution)/shard_map/ppermute | solution.py:266
  18.5 0.7 fusion.68
  19.3 1.9 copy-done
  21.1 1.0 copy-done.4
  22.8 1.7 product_by_rows.2
  24.5 9.4 %collective-permute-start.11 = (bf16[256,256]{1,0:T(8,128)(2,1)S(1)}, bf16[256,256]{1,0:T(8,128)(2,1)S(1)}, u32[]{:S(2)}, u32[]{:S(2)}) collective-permute-start(bf16[256,256]{1,0:T(8,128)(2,1)S(1)} %get-tuple-element.52), channel_id=1, source_target_pairs={{0,8},{8,16},{16,24},{24,0},{1,9},{9,17},{17,25},{25,1},{2,10},{10... | collective-permute-start | bytes 393224 | tf_op jit(solution)/shard_map/ppermute | solution.py:222
  34.0 1.1 collective-permute-start.12
  35.0 2.8 %collective-permute-start.13 = (bf16[256,256]{1,0:T(8,128)(2,1)S(1)}, bf16[256,256]{1,0:T(8,128)(2,1)S(1)}, u32[]{:S(2)}, u32[]{:S(2)}) collective-permute-start(bf16[256,256]{1,0:T(8,128)(2,1)S(1)} %get-tuple-element.54), channel_id=1, source_target_pairs={{0,24},{8,0},{16,8},{24,16},{1,25},{9,1},{17,9},{25,17},{2,26},{10... | collective-permute-start | bytes 393224 | tf_op jit(solution)/shard_map/ppermute | solution.py:222
  37.9 0.7 pack.1.refs_0_
  38.6 1.3 collective-permute-start.17
  40.5 1.3 collective-permute-start.18
  41.8 1.5 collective-permute-done.12
  43.4 1.3 collective-permute-start.8
  44.7 0.7 collective-permute-start.2
  45.4 0.7 collective-permute-start.3
  46.1 1.0 fusion.61
  47.1 33.5 %all_gather.3.own = bf16[1024,256]{1,0:T(8,128)(2,1)} all-gather(bf16[256,256]{1,0:T(8,128)(2,1)S(1)} %fusion.61), channel_id=1, replica_groups=mesh['lag'=4,'elem'=8] {'lag'}, dimensions={0}, use_global_device_ids=true | all-gather | bytes 655360 | tf_op jit(solution)/shard_map/all_gather | solution.py:272
  80.6 1.9 collective-permute-start.14
  82.5 3.6 %collective-permute-start.15 = (bf16[1024,256]{1,0:T(8,128)(2,1)}, bf16[1024,256]{1,0:T(8,128)(2,1)}, u32[]{:S(2)}, u32[]{:S(2)}) collective-permute-start(bf16[1024,256]{1,0:T(8,128)(2,1)} %all_gather.3.own), channel_id=1, source_target_pairs={{1,0},{2,1},{3,2},{4,3},{5,4},{6,5},{7,6},{9,8},{10,9},{11,10},{12... | collective-permute-start | bytes 1572872 | tf_op jit(solution)/shard_map/ppermute | solution.py:27
  86.2 0.9 add_convert_fusion
  87.1 1.3 collective-permute-start.16
  88.4 1.4 block_product.4
  90.5 1.5 collective-permute-start.4
  92.0 0.7 copy-done.9
  92.7 1.3 collective-permute-start.19
  94.0 22.8 %collective-permute-done.19.refs_3_ = f32[264,256]{1,0:T(8,128)} collective-permute-done((f32[264,256]{1,0:T(8,128)}, f32[264,256]{1,0:T(8,128)}, u32[]{:S(2)}, u32[]{:S(2)}) %collective-permute-start.19) | collective-permute-done | bytes 270368 | tf_op jit(solution)/shard_map/ppermute | solution.py:265
  116.8 1.0 copy-done.8
  117.7 1.0 copy-done.10
  118.7 2.5 %unpack.1 = (f32[1024,256]{1,0:T(8,128)}, f32[1024,8]{1,0:T(8,128)}) custom-call(f32[264,256]{1,0:T(8,128)} %pack.1.refs_0_, f32[264,256]{1,0:T(8,128)S(1)} %copy-done.8, f32[264,256]{1,0:T(8,128)S(1)} %copy-done.10, f32[264,256]{1,0:T(8,128)} %collective-permute-done.19.refs_3_), custom_call_target="tpu_custom_call" | custom-call | tf_op jit(solution)/shard_map/unpack/pallas_call | solution.py:177
  121.2 4.0 %block_product.6 = (f32[1024,256]{1,0:T(8,128)}, bf16[1024,256]{1,0:T(8,128)(2,1)}) custom-call(s32[1,1,3]{2,1,0:T(1,128)S(1)} %copy-done.13, s32[1]{0:T(128)S(6)} %copy.21.live, bf16[1,1024,1536]{2,1,0:T(8,128)(2,1)S(1)} %copy-done.1, bf16[1024,256]{1,0:T(8,128)(2,1)} %collective-permute-done.14.below, bf16[1024,256]{1,0:T(8,128)(2,1)} %all_gather.3.own, ...), custom_call_target="tpu_custom_call" | custom-call | flops 805306368 | bytes 5242880 | tf_op jit(solution)/shard_map/block_product/pallas_call | solution.py:122
  125.1 1.3 collective-permute-start.22
  126.5 9.0 %conditional.2 = (bf16[1024,256]{1,0:T(8,128)(2,1)}, f32[1024,256]{1,0:T(8,128)}) conditional(s32[]{:T(128)} %convert_element_type.67, () %tuple.25, (bf16[1024,256]{1,0:T(8,128)(2,1)}, f32[1024,256]{1,0:T(8,128)}, bf16[1024,256]{1,0:T(8,128)(2,1)}, f32[1024,8]{1,0:T(8,128)}, f32[1024,256]{1,0:T(8,128)}, /*index=5*/bf16[1024,256]{1,0:T(8,128)(2,1)}) %tuple.46), branch_computations={%region_0.1_spmd, %region_1.2_spmd} | conditional | flops 18613248 | bytes 5345296 | solution.py:288
  126.5 1.2 copy.11
  127.7 7.7 %multiply_add_fusion = (f32[1024,256]{1,0:T(8,128)}, bf16[1024,256]{1,0:T(8,128)(2,1)}) fusion(f32[1024,256]{1,0:T(8,128)} %get-tuple-element.26, bf16[1024,256]{1,0:T(8,128)(2,1)} %get-tuple-element.27, f32[1024]{0:T(1024)S(1)} %bitcast.39, f32[1024]{0:T(1024)S(1)} %broadcast_multiply_fusion, f32[1024]{0:T(1024)S(1)} %bitcast.46, ...), kind=kLoop, calls=%fused_computation.18 | loop fusion | flops 18612224 | bytes 5255168 | tf_op jit(solution)/shard_map/cond/branch_1_fun/add | solution.py:214
  135.4 1.9 collective-permute-start.20
  137.4 3.6 %collective-permute-start.21 = (bf16[1024,256]{1,0:T(8,128)(2,1)}, bf16[1024,256]{1,0:T(8,128)(2,1)}, u32[]{:S(2)}, u32[]{:S(2)}) collective-permute-start(bf16[1024,256]{1,0:T(8,128)(2,1)} %get-tuple-element.58.own), channel_id=1, source_target_pairs={{1,0},{2,1},{3,2},{4,3},{5,4},{6,5},{7,6}} | collective-permute-start | bytes 1572872 | tf_op jit(solution)/shard_map/ppermute | solution.py:27
  141.0 2.1 %add_convert_fusion.1 = bf16[1024,256]{1,0:T(8,128)(2,1)} fusion(bf16[1024,256]{1,0:T(8,128)(2,1)} %collective-permute-done.4, bf16[1024,256]{1,0:T(8,128)(2,1)} %block_product.4), kind=kLoop, calls=%fused_computation.48 | loop fusion | flops 1048576 | bytes 1572864 | tf_op jit(solution)/shard_map/convert_element_type | solution.py:241
  143.1 1.3 collective-permute-start.5
  144.4 1.9 broadcast_select_fusion
  146.4 2.1 %collective-permute-start.23 = (bf16[1024,256]{1,0:T(8,128)(2,1)}, bf16[1024,256]{1,0:T(8,128)(2,1)}, u32[]{:S(2)}, u32[]{:S(2)}) collective-permute-start(bf16[1024,256]{1,0:T(8,128)(2,1)} %broadcast_select_fusion), channel_id=1, source_target_pairs={{0,8},{16,24},{1,9},{17,25},{2,10},{18,26},{3,11},{19,27},{4,12},{... | collective-permute-start | bytes 1572872 | tf_op jit(solution)/shard_map/ppermute | solution.py:303
  148.5 1.3 collective-permute-done.21.above
  149.8 4.0 %block_product.7 = f32[1024,256]{1,0:T(8,128)} custom-call(s32[1,1,3]{2,1,0:T(1,128)S(1)} %copy-done.13, s32[1]{0:T(128)S(6)} %copy.21.live, bf16[1,1024,1536]{2,1,0:T(8,128)(2,1)S(1)} %copy-done.1, bf16[1024,256]{1,0:T(8,128)(2,1)} %collective-permute-done.20.below, bf16[1024,256]{1,0:T(8,128)(2,1)} %get-tuple-element.58.own, ...), custom_call_target="tpu_custom_call" | custom-call | flops 805306368 | bytes 5242880 | tf_op jit(solution)/shard_map/block_product/pallas_call | solution.py:122
  153.8 5.0 %collective-permute-done.5 = bf16[1024,256]{1,0:T(8,128)(2,1)} collective-permute-done((bf16[1024,256]{1,0:T(8,128)(2,1)}, bf16[1024,256]{1,0:T(8,128)(2,1)}, u32[]{:S(2)}, u32[]{:S(2)}) %collective-permute-start.5) | collective-permute-done | bytes 524320 | tf_op jit(solution)/shard_map/ppermute | solution.py:235
  158.8 8.5 %conditional.3 = (bf16[1024,256]{1,0:T(8,128)(2,1)}, f32[1024,256]{1,0:T(8,128)}) conditional(s32[]{:T(128)} %convert_element_type.67, () %tuple.24, (bf16[1024,256]{1,0:T(8,128)(2,1)}, f32[1024,256]{1,0:T(8,128)}, bf16[1024,256]{1,0:T(8,128)(2,1)}, f32[1024,8]{1,0:T(8,128)}, f32[1024,256]{1,0:T(8,128)}) %tuple.27), branch_computations={%region_2.3_spmd, %region_3.4_spmd} | conditional | flops 16778240 | bytes 4821008 | solution.py:288
  158.9 1.2 copy.12
  160.1 7.2 %multiply_add_fusion.2 = (f32[1024,256]{1,0:T(8,128)}, bf16[1024,256]{1,0:T(8,128)(2,1)}) fusion(f32[1024,256]{1,0:T(8,128)} %get-tuple-element.32, f32[1024]{0:T(1024)S(1)} %bitcast.37, f32[1024]{0:T(1024)S(1)} %broadcast_multiply_fusion.1, f32[1024]{0:T(1024)S(1)} %bitcast.43, bf16[1024,256]{1,0:T(8,128)(2,1)} %get-tuple-element.30, ...), kind=kLoop, calls=%fused_computation.42 | loop fusion | flops 16777216 | bytes 4730880 | tf_op jit(solution)/shard_map/cond/branch_1_fun/add | solution.py:214
  167.3 1.3 select_select_fusion.own
  168.6 1.9 collective-permute-start.24
  170.5 3.6 %collective-permute-start.25 = (bf16[1024,256]{1,0:T(8,128)(2,1)S(1)}, bf16[1024,256]{1,0:T(8,128)(2,1)S(1)}, u32[]{:S(2)}, u32[]{:S(2)}) collective-permute-start(bf16[1024,256]{1,0:T(8,128)(2,1)S(1)} %select_select_fusion.own), channel_id=1, source_target_pairs={{1,0},{2,1},{3,2},{4,3},{5,4},{6,5},{7,6},{9,8},{10,9},{11,10},{12... | collective-permute-start | bytes 1572872 | tf_op jit(solution)/shard_map/ppermute | solution.py:27
  174.2 2.0 fusion.67
  176.2 1.3 collective-permute-start.29
  177.5 2.0 collective-permute-start.30
  179.5 2.0 collective-permute-start.31
  181.5 1.7 collective-permute-done.25.above
  183.2 2.3 %product_by_rows.3 = (f32[256,256]{1,0:T(8,128)S(1)}, bf16[256,256]{1,0:T(8,128)(2,1)}, bf16[256,256]{1,0:T(8,128)(2,1)}, bf16[256,256]{1,0:T(8,128)(2,1)S(1)}) custom-call(s32[1,1,3]{2,1,0:T(1,128)S(1)} %copy-done.13, s32[1]{0:T(128)S(6)} %copy.21.live, bf16[1,1024,1536]{2,1,0:T(8,128)(2,1)S(1)} %copy-done.1, ...), custom_call_target="tpu_custom_call" | custom-call | flops 805306368 | bytes 5242880 | tf_op jit(solution)/shard_map/product_by_rows/pallas_call | solution.py:70
  186.3 3.9 %collective-permute-start.28 = (bf16[256,256]{1,0:T(8,128)(2,1)S(1)}, bf16[256,256]{1,0:T(8,128)(2,1)}, u32[]{:S(2)}, u32[]{:S(2)}) collective-permute-start(bf16[256,256]{1,0:T(8,128)(2,1)S(1)} %get-tuple-element.65), channel_id=1, source_target_pairs={{0,24},{8,0},{16,8},{24,16},{1,25},{9,1},{17,9},{25,17},{2,26},{10... | collective-permute-start | bytes 393224 | tf_op jit(solution)/shard_map/ppermute | solution.py:222
  190.8 4.8 %collective-permute-done.31 = f32[256,256]{1,0:T(8,128)} collective-permute-done((f32[256,256]{1,0:T(8,128)}, f32[256,256]{1,0:T(8,128)}, u32[]{:S(2)}, u32[]{:S(2)}) %collective-permute-start.31) | collective-permute-done | bytes 262176 | tf_op jit(solution)/shard_map/ppermute | solution.py:308
  195.5 2.8 %collective-permute-done.26 = bf16[256,256]{1,0:T(8,128)(2,1)} collective-permute-done((bf16[256,256]{1,0:T(8,128)(2,1)}, bf16[256,256]{1,0:T(8,128)(2,1)}, u32[]{:S(2)}, u32[]{:S(2)}) %collective-permute-start.26) | collective-permute-done | bytes 131104 | tf_op jit(solution)/shard_map/ppermute | solution.py:222
  198.4 2.8 %collective-permute-done.27 = bf16[256,256]{1,0:T(8,128)(2,1)} collective-permute-done((bf16[256,256]{1,0:T(8,128)(2,1)}, bf16[256,256]{1,0:T(8,128)(2,1)}, u32[]{:S(2)}, u32[]{:S(2)}) %collective-permute-start.27) | collective-permute-done | bytes 131104 | tf_op jit(solution)/shard_map/ppermute | solution.py:222
  201.2 1.4 collective-permute-done.28
  202.6 3.1 %add_bitcast_fusion = (f32[1,1,256,256]{3,2,1,0:T(8,128)}, bf16[256,256]{1,0:T(8,128)(2,1)}) fusion(f32[256]{0:T(256)S(1)} %bitcast.42, f32[256]{0:T(256)S(1)} %broadcast_multiply_fusion.2, f32[256]{0:T(256)S(1)} %bitcast.45, bf16[256,256]{1,0:T(8,128)(2,1)} %collective-permute-done.28, bf16[256,256]{1,0:T(8,128)(2,1)} %collective-permute-done.27, ...), kind=kLoop, calls=%fused_computation.91 | loop fusion | flops 4587520 | bytes 2362371 | tf_op jit(solution)/shard_map/broadcast_in_dim | solution.py:312
  (67 shorter events, 5.4 us)
Async XLA Ops:
  0.6 37.2 %copy-start.15 = (f32[1,1,256]{2,1,0:T(1,128)S(1)}, f32[1,1,256]{2,1,0:T(1,128)}, u32[]{:S(2)}) copy-start(f32[1,1,256]{2,1,0:T(1,128)} %coef_a.1) | copy-start | bytes 3076
  0.6 37.2 %copy-start.14 = (f32[1,1,256]{2,1,0:T(1,128)S(1)}, f32[1,1,256]{2,1,0:T(1,128)}, u32[]{:S(2)}) copy-start(f32[1,1,256]{2,1,0:T(1,128)} %coef_b.1) | copy-start | bytes 3076
  0.7 37.2 %copy-start.16 = (f32[1,1,256]{2,1,0:T(1,128)S(1)}, f32[1,1,256]{2,1,0:T(1,128)}, u32[]{:S(2)}) copy-start(f32[1,1,256]{2,1,0:T(1,128)} %sigma.1) | copy-start | bytes 3076
  0.7 39.2 %copy-start.13 = (s32[1,1,3]{2,1,0:T(1,128)S(1)}, s32[1,1,3]{2,1,0:T(1,128)}, u32[]{:S(2)}) copy-start(s32[1,1,3]{2,1,0:T(1,128)} %picks.11) | copy-start | bytes 40
  0.7 15.1 %collective-permute-start = (bf16[1024,256]{1,0:T(8,128)(2,1)}, bf16[1024,256]{1,0:T(8,128)(2,1)S(1)}, u32[]{:S(2)}, u32[]{:S(2)}) collective-permute-start(bf16[1024,256]{1,0:T(8,128)(2,1)} %bitcast.30), channel_id=1, source_target_pairs={{0,8},{8,16},{16,24},{1,9},{9,17},{17,25},{2,10},{10,18},{18,26},{... | collective-permute-start | bytes 1572872 | tf_op jit(solution)/shard_map/ppermute | solution.py:266
  4.3 14.9 %collective-permute-start.10 = (bf16[1024,256]{1,0:T(8,128)(2,1)}, bf16[1024,256]{1,0:T(8,128)(2,1)S(1)}, u32[]{:S(2)}, u32[]{:S(2)}) collective-permute-start(bf16[1024,256]{1,0:T(8,128)(2,1)} %bitcast.31), channel_id=1, source_target_pairs={{1,0},{2,1},{3,2},{4,3},{5,4},{6,5},{7,6},{9,8},{10,9},{11,10},{12... | collective-permute-start | bytes 1572872 | tf_op jit(solution)/shard_map/ppermute | solution.py:27
  6.3 13.0 %collective-permute-start.9 = (bf16[1024,256]{1,0:T(8,128)(2,1)}, bf16[1024,256]{1,0:T(8,128)(2,1)S(1)}, u32[]{:S(2)}, u32[]{:S(2)}) collective-permute-start(bf16[1024,256]{1,0:T(8,128)(2,1)} %bitcast.32), channel_id=1, source_target_pairs={{0,1},{1,2},{2,3},{3,4},{4,5},{5,6},{6,7},{8,9},{9,10},{10,11},{11... | collective-permute-start | bytes 1572872 | tf_op jit(solution)/shard_map/ppermute | solution.py:27
  15.8 19.2 %collective-permute-start.6 = (bf16[1024,256]{1,0:T(8,128)(2,1)S(1)}, bf16[1024,256]{1,0:T(8,128)(2,1)S(1)}, u32[]{:S(2)}, u32[]{:S(2)}) collective-permute-start(bf16[1024,256]{1,0:T(8,128)(2,1)S(1)} %collective-permute-done.own), channel_id=1, source_target_pairs={{8,9},{9,10},{10,11},{11,12},{12,13},{13,14},{14,15},{16,17},{17,1... | collective-permute-start | bytes 1572872 | tf_op jit(solution)/shard_map/ppermute | solution.py:27
  17.1 21.5 %collective-permute-start.7 = (bf16[1024,256]{1,0:T(8,128)(2,1)S(1)}, bf16[1024,256]{1,0:T(8,128)(2,1)S(1)}, u32[]{:S(2)}, u32[]{:S(2)}) collective-permute-start(bf16[1024,256]{1,0:T(8,128)(2,1)S(1)} %collective-permute-done.own), channel_id=1, source_target_pairs={{9,8},{10,9},{11,10},{12,11},{13,12},{14,13},{15,14},{17,16},{18,1... | collective-permute-start | bytes 1572872 | tf_op jit(solution)/shard_map/ppermute | solution.py:27
  17.8 26.8 %collective-permute-start.1 = (bf16[1024,256]{1,0:T(8,128)(2,1)S(1)}, bf16[1024,256]{1,0:T(8,128)(2,1)S(1)}, u32[]{:S(2)}, u32[]{:S(2)}) collective-permute-start(bf16[1024,256]{1,0:T(8,128)(2,1)S(1)} %collective-permute-done.own), channel_id=1, source_target_pairs={{8,16},{16,24},{9,17},{17,25},{10,18},{18,26},{11,19},{19,27},{12,... | collective-permute-start | bytes 1572872 | tf_op jit(solution)/shard_map/ppermute | solution.py:276
  19.2 1.9 copy-start
  21.1 1.0 copy-start.4
  22.2 0.7 copy-start.12
  22.8 15.0 %copy-start.6 = (f32[1,1,256,256]{3,2,1,0:T(8,128)S(1)}, f32[1,1,256,256]{3,2,1,0:T(8,128)}, u32[]{:S(2)}) copy-start(f32[1,1,256,256]{3,2,1,0:T(8,128)} %state.1) | copy-start | bytes 786436
  22.8 17.1 %copy-start.1 = (bf16[1,1024,1536]{2,1,0:T(8,128)(2,1)S(1)}, bf16[1,1024,1536]{2,1,0:T(8,128)(2,1)}, u32[]{:S(2)}) copy-start(bf16[1,1024,1536]{2,1,0:T(8,128)(2,1)} %tile.11) | copy-start | bytes 9437188
  22.8 17.1 %copy-start.2 = (f32[1,1,256,256]{3,2,1,0:T(8,128)S(1)}, f32[1,1,256,256]{3,2,1,0:T(8,128)}, u32[]{:S(2)}) copy-start(f32[1,1,256,256]{3,2,1,0:T(8,128)} %stress.7) | copy-start | bytes 786436
  24.5 16.0 %collective-permute-start.11 = (bf16[256,256]{1,0:T(8,128)(2,1)S(1)}, bf16[256,256]{1,0:T(8,128)(2,1)S(1)}, u32[]{:S(2)}, u32[]{:S(2)}) collective-permute-start(bf16[256,256]{1,0:T(8,128)(2,1)S(1)} %get-tuple-element.52), channel_id=1, source_target_pairs={{0,8},{8,16},{16,24},{24,0},{1,9},{9,17},{17,25},{25,1},{2,10},{10... | collective-permute-start | bytes 393224 | tf_op jit(solution)/shard_map/ppermute | solution.py:222
  34.0 9.4 %collective-permute-start.12 = (bf16[256,256]{1,0:T(8,128)(2,1)S(1)}, bf16[256,256]{1,0:T(8,128)(2,1)S(1)}, u32[]{:S(2)}, u32[]{:S(2)}) collective-permute-start(bf16[256,256]{1,0:T(8,128)(2,1)S(1)} %get-tuple-element.53), channel_id=1, source_target_pairs={{0,16},{8,24},{16,0},{24,8},{1,17},{9,25},{17,1},{25,9},{2,18},{10... | collective-permute-start | bytes 393224 | tf_op jit(solution)/shard_map/ppermute | solution.py:222
  35.0 10.4 %collective-permute-start.13 = (bf16[256,256]{1,0:T(8,128)(2,1)S(1)}, bf16[256,256]{1,0:T(8,128)(2,1)S(1)}, u32[]{:S(2)}, u32[]{:S(2)}) collective-permute-start(bf16[256,256]{1,0:T(8,128)(2,1)S(1)} %get-tuple-element.54), channel_id=1, source_target_pairs={{0,24},{8,0},{16,8},{24,16},{1,25},{9,1},{17,9},{25,17},{2,26},{10... | collective-permute-start | bytes 393224 | tf_op jit(solution)/shard_map/ppermute | solution.py:222
  38.6 51.2 %collective-permute-start.17 = (f32[264,256]{1,0:T(8,128)}, f32[264,256]{1,0:T(8,128)S(1)}, u32[]{:S(2)}, u32[]{:S(2)}) collective-permute-start(f32[264,256]{1,0:T(8,128)} %pack.1.refs_0_), channel_id=1, source_target_pairs={{8,0},{9,1},{10,2},{11,3},{12,4},{13,5},{14,6},{15,7}} | collective-permute-start | bytes 811016 | tf_op jit(solution)/shard_map/ppermute | solution.py:265
  40.5 51.5 %collective-permute-start.18 = (f32[264,256]{1,0:T(8,128)}, f32[264,256]{1,0:T(8,128)S(1)}, u32[]{:S(2)}, u32[]{:S(2)}) collective-permute-start(f32[264,256]{1,0:T(8,128)} %pack.1.refs_0_), channel_id=1, source_target_pairs={{16,0},{17,1},{18,2},{19,3},{20,4},{21,5},{22,6},{23,7}} | collective-permute-start | bytes 811016 | tf_op jit(solution)/shard_map/ppermute | solution.py:265
  43.4 37.2 %collective-permute-start.8 = (bf16[1024,256]{1,0:T(8,128)(2,1)S(1)}, bf16[1024,256]{1,0:T(8,128)(2,1)S(1)}, u32[]{:S(2)}, u32[]{:S(2)}) collective-permute-start(bf16[1024,256]{1,0:T(8,128)(2,1)S(1)} %block_product.5), channel_id=1, source_target_pairs={{8,0},{24,16},{9,1},{25,17},{10,2},{26,18},{11,3},{27,19},{12,4},{... | collective-permute-start | bytes 1572872 | tf_op jit(solution)/shard_map/ppermute | solution.py:235
  44.7 45.2 %copy-start.3 = (bf16[1024,256]{1,0:T(8,128)(2,1)}, bf16[1024,256]{1,0:T(8,128)(2,1)S(1)}, u32[]{:S(2)}) copy-start(bf16[1024,256]{1,0:T(8,128)(2,1)S(1)} %collective-permute-done.1.own) | copy-start | bytes 1572868
  44.7 37.9 %collective-permute-start.2 = (bf16[1024,256]{1,0:T(8,128)(2,1)S(1)}, bf16[1024,256]{1,0:T(8,128)(2,1)S(1)}, u32[]{:S(2)}, u32[]{:S(2)}) collective-permute-start(bf16[1024,256]{1,0:T(8,128)(2,1)S(1)} %collective-permute-done.1.own), channel_id=1, source_target_pairs={{16,17},{17,18},{18,19},{19,20},{20,21},{21,22},{22,23},{24,25},{2... | collective-permute-start | bytes 1572872 | tf_op jit(solution)/shard_map/ppermute | solution.py:27
  45.4 41.7 %collective-permute-start.3 = (bf16[1024,256]{1,0:T(8,128)(2,1)S(1)}, bf16[1024,256]{1,0:T(8,128)(2,1)S(1)}, u32[]{:S(2)}, u32[]{:S(2)}) collective-permute-start(bf16[1024,256]{1,0:T(8,128)(2,1)S(1)} %collective-permute-done.1.own), channel_id=1, source_target_pairs={{17,16},{18,17},{19,18},{20,19},{21,20},{22,21},{23,22},{25,24},{2... | collective-permute-start | bytes 1572872 | tf_op jit(solution)/shard_map/ppermute | solution.py:27
  80.6 6.5 %copy-start.17 = (bf16[1024,256]{1,0:T(8,128)(2,1)}, bf16[1024,256]{1,0:T(8,128)(2,1)S(1)}, u32[]{:S(2)}) copy-start(bf16[1024,256]{1,0:T(8,128)(2,1)S(1)} %collective-permute-done.8) | copy-start | bytes 1572868
  80.6 40.6 %collective-permute-start.14 = (bf16[1024,256]{1,0:T(8,128)(2,1)}, bf16[1024,256]{1,0:T(8,128)(2,1)}, u32[]{:S(2)}, u32[]{:S(2)}) collective-permute-start(bf16[1024,256]{1,0:T(8,128)(2,1)} %all_gather.3.own), channel_id=1, source_target_pairs={{0,1},{1,2},{2,3},{3,4},{4,5},{5,6},{6,7},{8,9},{9,10},{10,11},{11... | collective-permute-start | bytes 1572872 | tf_op jit(solution)/shard_map/ppermute | solution.py:27
  82.5 38.6 %collective-permute-start.15 = (bf16[1024,256]{1,0:T(8,128)(2,1)}, bf16[1024,256]{1,0:T(8,128)(2,1)}, u32[]{:S(2)}, u32[]{:S(2)}) collective-permute-start(bf16[1024,256]{1,0:T(8,128)(2,1)} %all_gather.3.own), channel_id=1, source_target_pairs={{1,0},{2,1},{3,2},{4,3},{5,4},{6,5},{7,6},{9,8},{10,9},{11,10},{12... | collective-permute-start | bytes 1572872 | tf_op jit(solution)/shard_map/ppermute | solution.py:27
  87.1 39.3 %collective-permute-start.16 = (bf16[1024,256]{1,0:T(8,128)(2,1)}, bf16[1024,256]{1,0:T(8,128)(2,1)}, u32[]{:S(2)}, u32[]{:S(2)}) collective-permute-start(bf16[1024,256]{1,0:T(8,128)(2,1)} %add_convert_fusion), channel_id=1, source_target_pairs={{16,0},{17,1},{18,2},{19,3},{20,4},{21,5},{22,6},{23,7}} | collective-permute-start | bytes 1572872 | tf_op jit(solution)/shard_map/ppermute | solution.py:235
  89.8 0.7 copy-start.7
  90.5 50.5 %collective-permute-start.4 = (bf16[1024,256]{1,0:T(8,128)(2,1)}, bf16[1024,256]{1,0:T(8,128)(2,1)}, u32[]{:S(2)}, u32[]{:S(2)}) collective-permute-start(bf16[1024,256]{1,0:T(8,128)(2,1)} %block_product.4), channel_id=1, source_target_pairs={{24,16},{25,17},{26,18},{27,19},{28,20},{29,21},{30,22},{31,23}} | collective-permute-start | bytes 1572872 | tf_op jit(solution)/shard_map/ppermute | solution.py:235
  92.0 0.7 copy-start.9
  92.7 24.1 %collective-permute-start.19 = (f32[264,256]{1,0:T(8,128)}, f32[264,256]{1,0:T(8,128)}, u32[]{:S(2)}, u32[]{:S(2)}) collective-permute-start(f32[264,256]{1,0:T(8,128)} %pack.1.refs_0_), channel_id=1, source_target_pairs={{24,0},{25,1},{26,2},{27,3},{28,4},{29,5},{30,6},{31,7}} | collective-permute-start | bytes 811016 | tf_op jit(solution)/shard_map/ppermute | solution.py:265
  116.8 1.0 copy-start.8
  117.7 1.0 copy-start.10
  125.1 28.7 %collective-permute-start.22 = (bf16[1024,256]{1,0:T(8,128)(2,1)}, bf16[1024,256]{1,0:T(8,128)(2,1)}, u32[]{:S(2)}, u32[]{:S(2)}) collective-permute-start(bf16[1024,256]{1,0:T(8,128)(2,1)} %get-tuple-element.59), channel_id=1, source_target_pairs={{8,0},{9,1},{10,2},{11,3},{12,4},{13,5},{14,6},{15,7}} | collective-permute-start | bytes 1572872 | tf_op jit(solution)/shard_map/ppermute | solution.py:284
  135.4 13.0 %collective-permute-start.20 = (bf16[1024,256]{1,0:T(8,128)(2,1)}, bf16[1024,256]{1,0:T(8,128)(2,1)}, u32[]{:S(2)}, u32[]{:S(2)}) collective-permute-start(bf16[1024,256]{1,0:T(8,128)(2,1)} %get-tuple-element.58.own), channel_id=1, source_target_pairs={{0,1},{1,2},{2,3},{3,4},{4,5},{5,6},{6,7}} | collective-permute-start | bytes 1572872 | tf_op jit(solution)/shard_map/ppermute | solution.py:27
  137.4 12.4 %collective-permute-start.21 = (bf16[1024,256]{1,0:T(8,128)(2,1)}, bf16[1024,256]{1,0:T(8,128)(2,1)}, u32[]{:S(2)}, u32[]{:S(2)}) collective-permute-start(bf16[1024,256]{1,0:T(8,128)(2,1)} %get-tuple-element.58.own), channel_id=1, source_target_pairs={{1,0},{2,1},{3,2},{4,3},{5,4},{6,5},{7,6}} | collective-permute-start | bytes 1572872 | tf_op jit(solution)/shard_map/ppermute | solution.py:27
  143.1 15.7 %collective-permute-start.5 = (bf16[1024,256]{1,0:T(8,128)(2,1)}, bf16[1024,256]{1,0:T(8,128)(2,1)}, u32[]{:S(2)}, u32[]{:S(2)}) collective-permute-start(bf16[1024,256]{1,0:T(8,128)(2,1)} %add_convert_fusion.1), channel_id=1, source_target_pairs={{16,0},{17,1},{18,2},{19,3},{20,4},{21,5},{22,6},{23,7}} | collective-permute-start | bytes 1572872 | tf_op jit(solution)/shard_map/ppermute | solution.py:235
  146.4 21.0 %collective-permute-start.23 = (bf16[1024,256]{1,0:T(8,128)(2,1)}, bf16[1024,256]{1,0:T(8,128)(2,1)}, u32[]{:S(2)}, u32[]{:S(2)}) collective-permute-start(bf16[1024,256]{1,0:T(8,128)(2,1)} %broadcast_select_fusion), channel_id=1, source_target_pairs={{0,8},{16,24},{1,9},{17,25},{2,10},{18,26},{3,11},{19,27},{4,12},{... | collective-permute-start | bytes 1572872 | tf_op jit(solution)/shard_map/ppermute | solution.py:303
  168.6 12.9 %collective-permute-start.24 = (bf16[1024,256]{1,0:T(8,128)(2,1)S(1)}, bf16[1024,256]{1,0:T(8,128)(2,1)S(1)}, u32[]{:S(2)}, u32[]{:S(2)}) collective-permute-start(bf16[1024,256]{1,0:T(8,128)(2,1)S(1)} %select_select_fusion.own), channel_id=1, source_target_pairs={{0,1},{1,2},{2,3},{3,4},{4,5},{5,6},{6,7},{8,9},{9,10},{10,11},{11... | collective-permute-start | bytes 1572872 | tf_op jit(solution)/shard_map/ppermute | solution.py:27
  170.5 12.7 %collective-permute-start.25 = (bf16[1024,256]{1,0:T(8,128)(2,1)S(1)}, bf16[1024,256]{1,0:T(8,128)(2,1)S(1)}, u32[]{:S(2)}, u32[]{:S(2)}) collective-permute-start(bf16[1024,256]{1,0:T(8,128)(2,1)S(1)} %select_select_fusion.own), channel_id=1, source_target_pairs={{1,0},{2,1},{3,2},{4,3},{5,4},{6,5},{7,6},{9,8},{10,9},{11,10},{12... | collective-permute-start | bytes 1572872 | tf_op jit(solution)/shard_map/ppermute | solution.py:27
  174.2 16.0 %copy-start.5 = (bf16[1,1024,256]{2,1,0:T(8,128)(2,1)S(1)}, bf16[1,1024,256]{2,1,0:T(8,128)(2,1)}, u32[]{:S(2)}) copy-start(bf16[1,1024,256]{2,1,0:T(8,128)(2,1)} %param.16) | copy-start | bytes 1572868
  176.2 10.1 %collective-permute-start.29 = (f32[256,256]{1,0:T(8,128)S(1)}, f32[256,256]{1,0:T(8,128)S(1)}, u32[]{:S(2)}, u32[]{:S(2)}) collective-permute-start(f32[256,256]{1,0:T(8,128)S(1)} %get-tuple-element.90), channel_id=1, source_target_pairs={{0,24},{1,25},{2,26},{3,27},{4,28},{5,29},{6,30},{7,31}} | collective-permute-start | bytes 786440 | tf_op jit(solution)/shard_map/ppermute | solution.py:308
  177.5 13.3 %collective-permute-start.30 = (f32[256,256]{1,0:T(8,128)}, f32[256,256]{1,0:T(8,128)}, u32[]{:S(2)}, u32[]{:S(2)}) collective-permute-start(f32[256,256]{1,0:T(8,128)} %get-tuple-element.89), channel_id=1, source_target_pairs={{0,16},{1,17},{2,18},{3,19},{4,20},{5,21},{6,22},{7,23}} | collective-permute-start | bytes 786440 | tf_op jit(solution)/shard_map/ppermute | solution.py:308
  179.5 16.0 %collective-permute-start.31 = (f32[256,256]{1,0:T(8,128)}, f32[256,256]{1,0:T(8,128)}, u32[]{:S(2)}, u32[]{:S(2)}) collective-permute-start(f32[256,256]{1,0:T(8,128)} %get-tuple-element.88), channel_id=1, source_target_pairs={{0,8},{1,9},{2,10},{3,11},{4,12},{5,13},{6,14},{7,15}} | collective-permute-start | bytes 786440 | tf_op jit(solution)/shard_map/ppermute | solution.py:308
  185.6 0.7 copy-start.11
  186.3 12.1 %collective-permute-start.26 = (bf16[256,256]{1,0:T(8,128)(2,1)}, bf16[256,256]{1,0:T(8,128)(2,1)}, u32[]{:S(2)}, u32[]{:S(2)}) collective-permute-start(bf16[256,256]{1,0:T(8,128)(2,1)} %get-tuple-element.63), channel_id=1, source_target_pairs={{0,8},{8,16},{16,24},{24,0},{1,9},{9,17},{17,25},{25,1},{2,10},{10... | collective-permute-start | bytes 393224 | tf_op jit(solution)/shard_map/ppermute | solution.py:222
  186.3 14.9 %collective-permute-start.27 = (bf16[256,256]{1,0:T(8,128)(2,1)}, bf16[256,256]{1,0:T(8,128)(2,1)}, u32[]{:S(2)}, u32[]{:S(2)}) collective-permute-start(bf16[256,256]{1,0:T(8,128)(2,1)} %get-tuple-element.64), channel_id=1, source_target_pairs={{0,16},{8,24},{16,0},{24,8},{1,17},{9,25},{17,1},{25,9},{2,18},{10... | collective-permute-start | bytes 393224 | tf_op jit(solution)/shard_map/ppermute | solution.py:222
  186.3 3.9 %copy-start.18 = (f32[256,256]{1,0:T(8,128)}, f32[256,256]{1,0:T(8,128)S(1)}, u32[]{:S(2)}) copy-start(f32[256,256]{1,0:T(8,128)S(1)} %collective-permute-done.29) | copy-start | bytes 786436
  186.3 16.3 %collective-permute-start.28 = (bf16[256,256]{1,0:T(8,128)(2,1)S(1)}, bf16[256,256]{1,0:T(8,128)(2,1)}, u32[]{:S(2)}, u32[]{:S(2)}) collective-permute-start(bf16[256,256]{1,0:T(8,128)(2,1)S(1)} %get-tuple-element.65), channel_id=1, source_target_pairs={{0,24},{8,0},{16,8},{24,16},{1,25},{9,1},{17,9},{25,17},{2,26},{10... | collective-permute-start | bytes 393224 | tf_op jit(solution)/shard_map/ppermute | solution.py:222

commit v11 on v10

--- a/solution.py
+++ b/solution.py
@@ -182,6 +182,27 @@
         compiler_params=PARAMS,
         name="unpack",
     )(*packed)
+
+
+def assemble_kernel(*refs):
+    parts, out = refs[:-1], refs[-1]
+    me, lags = lax.axis_index("lag"), len(parts)
+    rows = parts[0].shape[0]
+    for d, part in enumerate(parts):
+        spot = pl.multiple_of(lax.rem(me + lags - d, lags) * rows, rows)
+        out[pl.ds(spot, rows), :] = part[...]
+
+
+def assemble(parts):
+    rows, cols = parts[0].shape
+    return pl.pallas_call(
+        assemble_kernel,
+        in_specs=[VMEM] * len(parts),
+        out_specs=VMEM,
+        out_shape=jax.ShapeDtypeStruct((rows * len(parts), cols), parts[0].dtype),
+        compiler_params=PARAMS,
+        name="assemble",
+    )(*parts)
 
 
 def touch(*arrays):
@@ -269,7 +290,8 @@
     coef_a, coef_b, sigma = (c[0, 0][:, None] for c in (fric_a, fric_b, normal_stress))
     row_pair = (coef_b / coef_a, sigma * coef_a)
     rates, _ = settle_friction(prestress[0, 0] + traction, log_state[0, 0], *row_pair)
-    first = lax.all_gather(rates, "lag", axis=0, tiled=True)
+    arrived = [lax.ppermute(rates, "lag", [(i, (i + d) % lags) for i in every]) for d in rest]
+    first = assemble([rates] + arrived)
     kinds = [jnp.float32, jnp.bfloat16]
     (low,) = block_product(*local, window_of(once, rest), prestress, rest, kinds[1:])
     base_1 = tree_to_first(low, lags, 1)
@@ -277,7 +299,7 @@
     window_2 = window_of(twice, rest[1:])
     state, columns = unpack(packed)
     (low,) = block_product(*local, window_2, prestress, rest[1:], kinds[1:])
-    base_2 = tree_to_first(low, lags, 2)
+    base_2 = [lax.ppermute(low, "lag", [(d, 0)]) for d in rest[1:]]
 
     window = window_of(first, [0, 1])
     high, low = block_product(*local, window, prestress, [0, 1], kinds)

time: 208 us -> 204 us (0.981)
  blocking collectives: 33.5 us -> 0 us
  starting transfers between devices: 63.2 us -> 93.3 us
  local copies, waits for them, and re-layouts: 12.1 us -> 16.7 us
  waiting for transfers between devices: 51.3 us -> 48.1 us
  other arithmetic: 26.1 us -> 24 us
    all_gather x1 -> x0, blocking collectives: 33.5 us -> none  [shards(): first = lax.all_gather(rates, 'lag', axis=0, tiled=True)]
    ppermute x12, starting transfers between devices: 23.8 us -> 43.2 us  [exchange(): return (lax.ppermute(value, axes, up), lax.ppermute(value, axes, down))]
    ppermute x3, waiting for transfers between devices: 22.8 us -> 4.69 us  [shards(): packed = [packed] + [lax.ppermute(packed, 'lag', [(d, 0)]) for d in rest]]
    ppermute x0 -> x5, starting transfers between devices: none -> 12.9 us  [the longest x3 10.3 us: shards(): lax.ppermute(rates, 'lag', [(i, (i + d) % lags) for i in every])]
    ppermute x0 -> x5, waiting for transfers between devices: none -> 11.3 us  [the longest x3 11.3 us: shards(): lax.ppermute(rates, 'lag', [(i, (i + d) % lags) for i in every])]
    ppermute x1, waiting for transfers between devices: 0.01 us -> 6.52 us  [shards(): base_2 = base_2 + [lax.ppermute(low, 'lag', [(1, 0)])]]
    ppermute x4 -> x2, waiting for transfers between devices: 5.05 us -> 0.01 us  [tree_to_first(): arrived = lax.ppermute(value, 'lag', route)]
    ppermute x6, waiting for transfers between devices: 8.54 us -> 13.5 us  [scatter_sum(): total = total + lax.ppermute(parts[d], 'lag', route).astype(jnp.float32)]
  transfers between devices with their start and end apart: 32 -> 35, of which waited for: 10 -> 13; matrix products, arithmetic and copies ran while one was open for 13% -> 12% of each run, Pallas kernels for 9% -> 8%
where the time goes in v11:
time: 204 us; the launch traced here: 200 us
  starting transfers between devices  93.3 us (46%)
  waiting for transfers between devices  48.1 us (24%)
  other arithmetic  24 us (12%)
  local copies, waits for them, and re-layouts  16.7 us (8%)
  Pallas kernels  16.6 us (8%)
    ppermute x12, starting transfers between devices, exchange(): return (lax.ppermute(value, axes, up), lax.ppermute(value, axes, down))  43.2 us
    add x2, other arithmetic, evolved(): state + time_step * (jnp.exp(-state) - jnp.sqrt(speed_of * speed_of + cre...  15 us
    ppermute x6, waiting for transfers between devices, scatter_sum(): total = total + lax.ppermute(parts[d], 'lag', route).astype(jnp.float32)  13.5 us
    ppermute x6, starting transfers between devices, scatter_sum(): total = total + lax.ppermute(parts[d], 'lag', route).astype(jnp.float32)  13.2 us
    unnamed x50, local copies, waits for them, and re-layouts  12.2 us
    ppermute x3, waiting for transfers between devices, shards(): lax.ppermute(rates, 'lag', [(i, (i + d) % lags) for i in every])  11.3 us
    ppermute x3, starting transfers between devices, shards(): lax.ppermute(rates, 'lag', [(i, (i + d) % lags) for i in every])  10.3 us
    pallas_call x4, Pallas kernels, block_product(): pl.pallas_call(functools.partial(block_kernel, chunks, (planes[0], planes...  9.72 us
  transfers between devices with their start and end apart: 35, of which 13 were waited for; matrix products, arithmetic and copies ran while one was open for 12% of the time, Pallas kernels for 8%

profile of v11, /device:TPU:2, one launch (start us, length us, event | category | flops | bytes accessed | tf_op | source)
XLA Modules:
  0.0 200.4 jit_solution(6698931744350180696)
XLA Ops:
  0.7 3.6 %collective-permute-start = (bf16[1024,256]{1,0:T(8,128)(2,1)}, bf16[1024,256]{1,0:T(8,128)(2,1)S(1)}, u32[]{:S(2)}, u32[]{:S(2)}) collective-permute-start(bf16[1024,256]{1,0:T(8,128)(2,1)} %bitcast.30), channel_id=1, source_target_pairs={{0,8},{8,16},{16,24},{1,9},{9,17},{17,25},{2,10},{10,18},{18,26},{... | collective-permute-start | bytes 1572872 | tf_op jit(solution)/shard_map/ppermute | solution.py:287
  4.3 1.9 collective-permute-start.9
  6.3 2.4 %collective-permute-start.8 = (bf16[1024,256]{1,0:T(8,128)(2,1)}, bf16[1024,256]{1,0:T(8,128)(2,1)S(1)}, u32[]{:S(2)}, u32[]{:S(2)}) collective-permute-start(bf16[1024,256]{1,0:T(8,128)(2,1)} %bitcast.32), channel_id=1, source_target_pairs={{0,1},{1,2},{2,3},{3,4},{4,5},{5,6},{6,7},{8,9},{9,10},{10,11},{11... | collective-permute-start | bytes 1572872 | tf_op jit(solution)/shard_map/ppermute | solution.py:27
  9.3 6.5 %collective-permute-done.own = bf16[1024,256]{1,0:T(8,128)(2,1)S(1)} collective-permute-done((bf16[1024,256]{1,0:T(8,128)(2,1)}, bf16[1024,256]{1,0:T(8,128)(2,1)S(1)}, u32[]{:S(2)}, u32[]{:S(2)}) %collective-permute-start) | collective-permute-done | bytes 524320 | tf_op jit(solution)/shard_map/ppermute | solution.py:287
  17.9 1.9 copy-done
  19.8 1.0 copy-done.3
  21.5 1.7 product_by_rows.2
  23.2 5.4 %collective-permute-start.10 = (bf16[256,256]{1,0:T(8,128)(2,1)S(1)}, bf16[256,256]{1,0:T(8,128)(2,1)S(1)}, u32[]{:S(2)}, u32[]{:S(2)}) collective-permute-start(bf16[256,256]{1,0:T(8,128)(2,1)S(1)} %get-tuple-element.55), channel_id=1, source_target_pairs={{0,8},{8,16},{16,24},{24,0},{1,9},{9,17},{17,25},{25,1},{2,10},{10... | collective-permute-start | bytes 393224 | tf_op jit(solution)/shard_map/ppermute | solution.py:243
  28.6 2.6 %collective-permute-start.11 = (bf16[256,256]{1,0:T(8,128)(2,1)S(1)}, bf16[256,256]{1,0:T(8,128)(2,1)S(1)}, u32[]{:S(2)}, u32[]{:S(2)}) collective-permute-start(bf16[256,256]{1,0:T(8,128)(2,1)S(1)} %get-tuple-element.56), channel_id=1, source_target_pairs={{0,16},{8,24},{16,0},{24,8},{1,17},{9,25},{17,1},{25,9},{2,18},{10... | collective-permute-start | bytes 393224 | tf_op jit(solution)/shard_map/ppermute | solution.py:243
  31.1 1.3 collective-permute-start.12
  32.6 1.3 collective-permute-start.21
  34.5 1.3 collective-permute-start.7
  35.8 5.1 %collective-permute-done.11 = bf16[256,256]{1,0:T(8,128)(2,1)S(1)} collective-permute-done((bf16[256,256]{1,0:T(8,128)(2,1)S(1)}, bf16[256,256]{1,0:T(8,128)(2,1)S(1)}, u32[]{:S(2)}, u32[]{:S(2)}) %collective-permute-start.11) | collective-permute-done | bytes 131104 | tf_op jit(solution)/shard_map/ppermute | solution.py:243
  41.0 1.0 fusion.61.refs_0_
  42.0 4.2 %collective-permute-start.15 = (bf16[256,256]{1,0:T(8,128)(2,1)S(1)}, bf16[256,256]{1,0:T(8,128)(2,1)S(1)}, u32[]{:S(2)}, u32[]{:S(2)}) collective-permute-start(bf16[256,256]{1,0:T(8,128)(2,1)S(1)} %fusion.61.refs_0_), channel_id=1, source_target_pairs={{0,24},{8,0},{16,8},{24,16},{1,25},{9,1},{17,9},{25,17},{2,26},{10... | collective-permute-start | bytes 393224 | tf_op jit(solution)/shard_map/ppermute | solution.py:293
  46.2 6.1 %collective-permute-start.14 = (bf16[256,256]{1,0:T(8,128)(2,1)S(1)}, bf16[256,256]{1,0:T(8,128)(2,1)S(1)}, u32[]{:S(2)}, u32[]{:S(2)}) collective-permute-start(bf16[256,256]{1,0:T(8,128)(2,1)S(1)} %fusion.61.refs_0_), channel_id=1, source_target_pairs={{0,16},{8,24},{16,0},{24,8},{1,17},{9,25},{17,1},{25,9},{2,18},{10... | collective-permute-start | bytes 393224 | tf_op jit(solution)/shard_map/ppermute | solution.py:293
  52.3 11.3 %collective-permute-done.15.refs_3_ = bf16[256,256]{1,0:T(8,128)(2,1)S(1)} collective-permute-done((bf16[256,256]{1,0:T(8,128)(2,1)S(1)}, bf16[256,256]{1,0:T(8,128)(2,1)S(1)}, u32[]{:S(2)}, u32[]{:S(2)}) %collective-permute-start.15) | collective-permute-done | bytes 131104 | tf_op jit(solution)/shard_map/ppermute | solution.py:293
  63.6 1.5 collective-permute-start.1
  65.0 1.3 collective-permute-start.20
  66.3 1.3 collective-permute-start.19
  68.5 2.0 %collective-permute-start.17 = (bf16[1024,256]{1,0:T(8,128)(2,1)}, bf16[1024,256]{1,0:T(8,128)(2,1)}, u32[]{:S(2)}, u32[]{:S(2)}) collective-permute-start(bf16[1024,256]{1,0:T(8,128)(2,1)} %assemble.1.own), channel_id=1, source_target_pairs={{1,0},{2,1},{3,2},{4,3},{5,4},{6,5},{7,6},{9,8},{10,9},{11,10},{12... | collective-permute-start | bytes 1572872 | tf_op jit(solution)/shard_map/ppermute | solution.py:27
  70.5 2.3 %collective-permute-start.16 = (bf16[1024,256]{1,0:T(8,128)(2,1)}, bf16[1024,256]{1,0:T(8,128)(2,1)}, u32[]{:S(2)}, u32[]{:S(2)}) collective-permute-start(bf16[1024,256]{1,0:T(8,128)(2,1)} %assemble.1.own), channel_id=1, source_target_pairs={{0,1},{1,2},{2,3},{3,4},{4,5},{5,6},{6,7},{8,9},{9,10},{10,11},{11... | collective-permute-start | bytes 1572872 | tf_op jit(solution)/shard_map/ppermute | solution.py:27
  73.8 2.5 %collective-permute-done.20.refs_2_ = f32[264,256]{1,0:T(8,128)S(1)} collective-permute-done((f32[264,256]{1,0:T(8,128)S(1)}, f32[264,256]{1,0:T(8,128)S(1)}, u32[]{:S(2)}, u32[]{:S(2)}) %collective-permute-start.20) | collective-permute-done | bytes 270368 | tf_op jit(solution)/shard_map/ppermute | solution.py:286
  77.0 1.3 collective-permute-start.18
  78.3 1.5 collective-permute-start.3
  79.8 2.2 %collective-permute-done.19.refs_1_ = f32[264,256]{1,0:T(8,128)S(1)} collective-permute-done((f32[264,256]{1,0:T(8,128)S(1)}, f32[264,256]{1,0:T(8,128)S(1)}, u32[]{:S(2)}, u32[]{:S(2)}) %collective-permute-start.19) | collective-permute-done | bytes 270368 | tf_op jit(solution)/shard_map/ppermute | solution.py:286
  82.7 1.5 collective-permute-start.2
  84.2 1.0 copy-done.6
  85.1 1.0 copy-done.11
  86.1 1.0 copy-done.13
  88.0 1.4 unpack.1
  89.3 3.8 %block_product.6 = (f32[1024,256]{1,0:T(8,128)}, bf16[1024,256]{1,0:T(8,128)(2,1)S(1)}) custom-call(s32[1,1,3]{2,1,0:T(1,128)S(1)} %copy-done.18, s32[1]{0:T(128)S(6)} %copy.21.live, bf16[1,1024,1536]{2,1,0:T(8,128)(2,1)S(1)} %copy-done.1, bf16[1024,256]{1,0:T(8,128)(2,1)} %collective-permute-done.16.below, bf16[1024,256]{1,0:T(8,128)(2,1)} %assemble.1.own, ...), custom_call_target="tpu_custom_call" | custom-call | flops 805306368 | bytes 5242880 | tf_op jit(solution)/shard_map/block_product/pallas_call | solution.py:122
  94.0 9.0 %conditional.2 = (bf16[1024,256]{1,0:T(8,128)(2,1)}, f32[1024,256]{1,0:T(8,128)}) conditional(s32[]{:T(128)} %convert_element_type.61, () %tuple.25, (bf16[1024,256]{1,0:T(8,128)(2,1)}, f32[1024,256]{1,0:T(8,128)}, bf16[1024,256]{1,0:T(8,128)(2,1)}, f32[1024,8]{1,0:T(8,128)}, f32[1024,256]{1,0:T(8,128)}, /*index=5*/bf16[1024,256]{1,0:T(8,128)(2,1)}) %tuple.46), branch_computations={%region_0.1_spmd, %region_1.2_spmd} | conditional | flops 18613248 | bytes 5345296 | solution.py:310
  94.0 1.2 copy.11
  95.2 7.7 %multiply_add_fusion = (f32[1024,256]{1,0:T(8,128)}, bf16[1024,256]{1,0:T(8,128)(2,1)}) fusion(f32[1024,256]{1,0:T(8,128)} %get-tuple-element.28, bf16[1024,256]{1,0:T(8,128)(2,1)} %get-tuple-element.29, f32[1024]{0:T(1024)S(1)} %bitcast.39, f32[1024]{0:T(1024)S(1)} %broadcast_multiply_fusion, f32[1024]{0:T(1024)S(1)} %bitcast.46, ...), kind=kLoop, calls=%fused_computation.18 | loop fusion | flops 18612224 | bytes 5255168 | tf_op jit(solution)/shard_map/cond/branch_1_fun/add | solution.py:235
  102.9 13.3 %collective-permute-start.23 = (bf16[1024,256]{1,0:T(8,128)(2,1)}, bf16[1024,256]{1,0:T(8,128)(2,1)S(1)}, u32[]{:S(2)}, u32[]{:S(2)}) collective-permute-start(bf16[1024,256]{1,0:T(8,128)(2,1)} %get-tuple-element.61.own), channel_id=1, source_target_pairs={{1,0},{2,1},{3,2},{4,3},{5,4},{6,5},{7,6}} | collective-permute-start | bytes 1572872 | tf_op jit(solution)/shard_map/ppermute | solution.py:27
  116.2 1.3 collective-permute-start.25
  117.5 1.4 block_product.4
  118.9 1.3 collective-permute-start.24
  120.2 1.3 collective-permute-start.4
  121.5 1.9 collective-permute-start.22
  123.5 1.9 broadcast_select_fusion
  126.2 6.0 %collective-permute-start.26 = (bf16[1024,256]{1,0:T(8,128)(2,1)}, bf16[1024,256]{1,0:T(8,128)(2,1)}, u32[]{:S(2)}, u32[]{:S(2)}) collective-permute-start(bf16[1024,256]{1,0:T(8,128)(2,1)} %broadcast_select_fusion), channel_id=1, source_target_pairs={{0,8},{16,24},{1,9},{17,25},{2,10},{18,26},{3,11},{19,27},{4,12},{... | collective-permute-start | bytes 1572872 | tf_op jit(solution)/shard_map/ppermute | solution.py:325
  132.4 1.0 copy-done.9
  133.4 3.9 %block_product.7 = f32[1024,256]{1,0:T(8,128)} custom-call(s32[1,1,3]{2,1,0:T(1,128)S(1)} %copy-done.18, s32[1]{0:T(128)S(6)} %copy.21.live, bf16[1,1024,1536]{2,1,0:T(8,128)(2,1)S(1)} %copy-done.1, bf16[1024,256]{1,0:T(8,128)(2,1)} %collective-permute-done.22.below, bf16[1024,256]{1,0:T(8,128)(2,1)} %get-tuple-element.61.own, ...), custom_call_target="tpu_custom_call" | custom-call | flops 805306368 | bytes 5242880 | tf_op jit(solution)/shard_map/block_product/pallas_call | solution.py:122
  137.3 6.5 %collective-permute-done.25 = bf16[1024,256]{1,0:T(8,128)(2,1)} collective-permute-done((bf16[1024,256]{1,0:T(8,128)(2,1)}, bf16[1024,256]{1,0:T(8,128)(2,1)}, u32[]{:S(2)}, u32[]{:S(2)}) %collective-permute-start.25) | collective-permute-done | bytes 524320 | tf_op jit(solution)/shard_map/ppermute | solution.py:306
  143.9 8.5 %conditional.3 = (bf16[1024,256]{1,0:T(8,128)(2,1)}, f32[1024,256]{1,0:T(8,128)}) conditional(s32[]{:T(128)} %convert_element_type.61, () %tuple.24, (bf16[1024,256]{1,0:T(8,128)(2,1)}, f32[1024,256]{1,0:T(8,128)}, bf16[1024,256]{1,0:T(8,128)(2,1)}, bf16[1024,256]{1,0:T(8,128)(2,1)}, f32[1024,8]{1,0:T(8,128)}, /*index=5*/f32[1024,256]{1,0:T(8,128)}) %tuple.27), branch_computations={%region_2.3_spmd, %region_3.4_spmd} | conditional | flops 17302528 | bytes 5345296 | solution.py:310
  143.9 1.2 copy.12
  145.1 7.3 %multiply_add_fusion.2 = (f32[1024,256]{1,0:T(8,128)}, bf16[1024,256]{1,0:T(8,128)(2,1)}) fusion(f32[1024,256]{1,0:T(8,128)} %get-tuple-element.35, f32[1024]{0:T(1024)S(1)} %bitcast.37, f32[1024]{0:T(1024)S(1)} %broadcast_multiply_fusion.1, f32[1024]{0:T(1024)S(1)} %bitcast.43, bf16[1024,256]{1,0:T(8,128)(2,1)} %get-tuple-element.33, ...), kind=kLoop, calls=%fused_computation.42 | loop fusion | flops 17301504 | bytes 5255168 | tf_op jit(solution)/shard_map/cond/branch_1_fun/add | solution.py:235
  152.4 1.3 select_select_fusion.own
  153.6 13.1 %collective-permute-start.28 = (bf16[1024,256]{1,0:T(8,128)(2,1)S(1)}, bf16[1024,256]{1,0:T(8,128)(2,1)S(1)}, u32[]{:S(2)}, u32[]{:S(2)}) collective-permute-start(bf16[1024,256]{1,0:T(8,128)(2,1)S(1)} %select_select_fusion.own), channel_id=1, source_target_pairs={{1,0},{2,1},{3,2},{4,3},{5,4},{6,5},{7,6},{9,8},{10,9},{11,10},{12... | collective-permute-start | bytes 1572872 | tf_op jit(solution)/shard_map/ppermute | solution.py:27
  166.7 1.9 collective-permute-start.27
  168.7 2.0 %fusion.67 = (f32[256,256]{1,0:T(8,128)S(1)}, f32[256,256]{1,0:T(8,128)}, f32[256,256]{1,0:T(8,128)}) fusion(f32[1024,256]{1,0:T(8,128)} %get-tuple-element.69), kind=kLoop, calls=%fused_computation.100 | loop fusion | bytes 1572864 | tf_op jit(solution)/shard_map/slice | solution.py:330
  170.7 1.3 collective-permute-start.34
  172.0 2.0 %collective-permute-start.33 = (f32[256,256]{1,0:T(8,128)}, f32[256,256]{1,0:T(8,128)}, u32[]{:S(2)}, u32[]{:S(2)}) collective-permute-start(f32[256,256]{1,0:T(8,128)} %get-tuple-element.93), channel_id=1, source_target_pairs={{0,16},{1,17},{2,18},{3,19},{4,20},{5,21},{6,22},{7,23}} | collective-permute-start | bytes 786440 | tf_op jit(solution)/shard_map/ppermute | solution.py:330
  174.0 2.0 collective-permute-start.32
  176.1 1.1 collective-permute-done.27.below
  177.2 2.3 %product_by_rows.3 = (f32[256,256]{1,0:T(8,128)S(1)}, bf16[256,256]{1,0:T(8,128)(2,1)}, bf16[256,256]{1,0:T(8,128)(2,1)}, bf16[256,256]{1,0:T(8,128)(2,1)S(1)}) custom-call(s32[1,1,3]{2,1,0:T(1,128)S(1)} %copy-done.18, s32[1]{0:T(128)S(6)} %copy.21.live, bf16[1,1024,1536]{2,1,0:T(8,128)(2,1)S(1)} %copy-done.1, ...), custom_call_target="tpu_custom_call" | custom-call | flops 805306368 | bytes 5242880 | tf_op jit(solution)/shard_map/product_by_rows/pallas_call | solution.py:70
  180.3 3.9 %collective-permute-start.31 = (bf16[256,256]{1,0:T(8,128)(2,1)S(1)}, bf16[256,256]{1,0:T(8,128)(2,1)}, u32[]{:S(2)}, u32[]{:S(2)}) collective-permute-start(bf16[256,256]{1,0:T(8,128)(2,1)S(1)} %get-tuple-element.68), channel_id=1, source_target_pairs={{0,24},{8,0},{16,8},{24,16},{1,25},{9,1},{17,9},{25,17},{2,26},{10... | collective-permute-start | bytes 393224 | tf_op jit(solution)/shard_map/ppermute | solution.py:243
  184.8 4.3 %collective-permute-done.32 = f32[256,256]{1,0:T(8,128)} collective-permute-done((f32[256,256]{1,0:T(8,128)}, f32[256,256]{1,0:T(8,128)}, u32[]{:S(2)}, u32[]{:S(2)}) %collective-permute-start.32) | collective-permute-done | bytes 262176 | tf_op jit(solution)/shard_map/ppermute | solution.py:330
  189.0 2.8 %collective-permute-done.29 = bf16[256,256]{1,0:T(8,128)(2,1)} collective-permute-done((bf16[256,256]{1,0:T(8,128)(2,1)}, bf16[256,256]{1,0:T(8,128)(2,1)}, u32[]{:S(2)}, u32[]{:S(2)}) %collective-permute-start.29) | collective-permute-done | bytes 131104 | tf_op jit(solution)/shard_map/ppermute | solution.py:243
  191.8 2.8 %collective-permute-done.30 = bf16[256,256]{1,0:T(8,128)(2,1)} collective-permute-done((bf16[256,256]{1,0:T(8,128)(2,1)}, bf16[256,256]{1,0:T(8,128)(2,1)}, u32[]{:S(2)}, u32[]{:S(2)}) %collective-permute-start.30) | collective-permute-done | bytes 131104 | tf_op jit(solution)/shard_map/ppermute | solution.py:243
  194.7 2.7 %collective-permute-done.31 = bf16[256,256]{1,0:T(8,128)(2,1)} collective-permute-done((bf16[256,256]{1,0:T(8,128)(2,1)S(1)}, bf16[256,256]{1,0:T(8,128)(2,1)}, u32[]{:S(2)}, u32[]{:S(2)}) %collective-permute-start.31) | collective-permute-done | bytes 131104 | tf_op jit(solution)/shard_map/ppermute | solution.py:243
  197.4 3.1 %add_bitcast_fusion = (f32[1,1,256,256]{3,2,1,0:T(8,128)}, bf16[256,256]{1,0:T(8,128)(2,1)}) fusion(f32[256]{0:T(256)S(1)} %bitcast.42, f32[256]{0:T(256)S(1)} %broadcast_multiply_fusion.2, f32[256]{0:T(256)S(1)} %bitcast.45, bf16[256,256]{1,0:T(8,128)(2,1)} %collective-permute-done.31, bf16[256,256]{1,0:T(8,128)(2,1)} %collective-permute-done.30, ...), kind=kLoop, calls=%fused_computation.90 | loop fusion | flops 4587520 | bytes 2362371 | tf_op jit(solution)/shard_map/broadcast_in_dim | solution.py:334
  (84 shorter events, 10.8 us)
Async XLA Ops:
  0.6 31.9 %copy-start.21 = (f32[1,1,256]{2,1,0:T(1,128)S(1)}, f32[1,1,256]{2,1,0:T(1,128)}, u32[]{:S(2)}) copy-start(f32[1,1,256]{2,1,0:T(1,128)} %sigma.1) | copy-start | bytes 3076
  0.6 31.9 %copy-start.19 = (f32[1,1,256]{2,1,0:T(1,128)S(1)}, f32[1,1,256]{2,1,0:T(1,128)}, u32[]{:S(2)}) copy-start(f32[1,1,256]{2,1,0:T(1,128)} %coef_b.1) | copy-start | bytes 3076
  0.7 31.8 %copy-start.20 = (f32[1,1,256]{2,1,0:T(1,128)S(1)}, f32[1,1,256]{2,1,0:T(1,128)}, u32[]{:S(2)}) copy-start(f32[1,1,256]{2,1,0:T(1,128)} %coef_a.1) | copy-start | bytes 3076
  0.7 33.2 %copy-start.18 = (s32[1,1,3]{2,1,0:T(1,128)S(1)}, s32[1,1,3]{2,1,0:T(1,128)}, u32[]{:S(2)}) copy-start(s32[1,1,3]{2,1,0:T(1,128)} %picks.11) | copy-start | bytes 40
  0.7 15.1 %collective-permute-start = (bf16[1024,256]{1,0:T(8,128)(2,1)}, bf16[1024,256]{1,0:T(8,128)(2,1)S(1)}, u32[]{:S(2)}, u32[]{:S(2)}) collective-permute-start(bf16[1024,256]{1,0:T(8,128)(2,1)} %bitcast.30), channel_id=1, source_target_pairs={{0,8},{8,16},{16,24},{1,9},{9,17},{17,25},{2,10},{10,18},{18,26},{... | collective-permute-start | bytes 1572872 | tf_op jit(solution)/shard_map/ppermute | solution.py:287
  4.3 13.6 %collective-permute-start.9 = (bf16[1024,256]{1,0:T(8,128)(2,1)}, bf16[1024,256]{1,0:T(8,128)(2,1)S(1)}, u32[]{:S(2)}, u32[]{:S(2)}) collective-permute-start(bf16[1024,256]{1,0:T(8,128)(2,1)} %bitcast.31), channel_id=1, source_target_pairs={{1,0},{2,1},{3,2},{4,3},{5,4},{6,5},{7,6},{9,8},{10,9},{11,10},{12... | collective-permute-start | bytes 1572872 | tf_op jit(solution)/shard_map/ppermute | solution.py:27
  6.3 11.6 %collective-permute-start.8 = (bf16[1024,256]{1,0:T(8,128)(2,1)}, bf16[1024,256]{1,0:T(8,128)(2,1)S(1)}, u32[]{:S(2)}, u32[]{:S(2)}) collective-permute-start(bf16[1024,256]{1,0:T(8,128)(2,1)} %bitcast.32), channel_id=1, source_target_pairs={{0,1},{1,2},{2,3},{3,4},{4,5},{5,6},{6,7},{8,9},{9,10},{10,11},{11... | collective-permute-start | bytes 1572872 | tf_op jit(solution)/shard_map/ppermute | solution.py:27
  15.8 16.8 %collective-permute-start.6 = (bf16[1024,256]{1,0:T(8,128)(2,1)S(1)}, bf16[1024,256]{1,0:T(8,128)(2,1)S(1)}, u32[]{:S(2)}, u32[]{:S(2)}) collective-permute-start(bf16[1024,256]{1,0:T(8,128)(2,1)S(1)} %collective-permute-done.own), channel_id=1, source_target_pairs={{9,8},{10,9},{11,10},{12,11},{13,12},{14,13},{15,14},{17,16},{18,1... | collective-permute-start | bytes 1572872 | tf_op jit(solution)/shard_map/ppermute | solution.py:27
  16.5 17.4 %collective-permute-start.5 = (bf16[1024,256]{1,0:T(8,128)(2,1)S(1)}, bf16[1024,256]{1,0:T(8,128)(2,1)S(1)}, u32[]{:S(2)}, u32[]{:S(2)}) collective-permute-start(bf16[1024,256]{1,0:T(8,128)(2,1)S(1)} %collective-permute-done.own), channel_id=1, source_target_pairs={{8,9},{9,10},{10,11},{11,12},{12,13},{13,14},{14,15},{16,17},{17,1... | collective-permute-start | bytes 1572872 | tf_op jit(solution)/shard_map/ppermute | solution.py:27
  17.9 1.9 copy-start
  19.8 1.0 copy-start.3
  20.8 0.7 copy-start.17
  21.5 11.0 %copy-start.7 = (f32[1,1,256,256]{3,2,1,0:T(8,128)S(1)}, f32[1,1,256,256]{3,2,1,0:T(8,128)}, u32[]{:S(2)}) copy-start(f32[1,1,256,256]{3,2,1,0:T(8,128)} %state.1) | copy-start | bytes 786436
  21.5 12.4 %copy-start.1 = (bf16[1,1024,1536]{2,1,0:T(8,128)(2,1)S(1)}, bf16[1,1024,1536]{2,1,0:T(8,128)(2,1)}, u32[]{:S(2)}) copy-start(bf16[1,1024,1536]{2,1,0:T(8,128)(2,1)} %tile.11) | copy-start | bytes 9437188
  21.5 12.4 %copy-start.2 = (f32[1,1,256,256]{3,2,1,0:T(8,128)S(1)}, f32[1,1,256,256]{3,2,1,0:T(8,128)}, u32[]{:S(2)}) copy-start(f32[1,1,256,256]{3,2,1,0:T(8,128)} %stress.7) | copy-start | bytes 786436
  23.2 12.6 %collective-permute-start.10 = (bf16[256,256]{1,0:T(8,128)(2,1)S(1)}, bf16[256,256]{1,0:T(8,128)(2,1)S(1)}, u32[]{:S(2)}, u32[]{:S(2)}) collective-permute-start(bf16[256,256]{1,0:T(8,128)(2,1)S(1)} %get-tuple-element.55), channel_id=1, source_target_pairs={{0,8},{8,16},{16,24},{24,0},{1,9},{9,17},{17,25},{25,1},{2,10},{10... | collective-permute-start | bytes 393224 | tf_op jit(solution)/shard_map/ppermute | solution.py:243
  28.6 12.4 %collective-permute-start.11 = (bf16[256,256]{1,0:T(8,128)(2,1)S(1)}, bf16[256,256]{1,0:T(8,128)(2,1)S(1)}, u32[]{:S(2)}, u32[]{:S(2)}) collective-permute-start(bf16[256,256]{1,0:T(8,128)(2,1)S(1)} %get-tuple-element.56), channel_id=1, source_target_pairs={{0,16},{8,24},{16,0},{24,8},{1,17},{9,25},{17,1},{25,9},{2,18},{10... | collective-permute-start | bytes 393224 | tf_op jit(solution)/shard_map/ppermute | solution.py:243
  31.1 9.8 %collective-permute-start.12 = (bf16[256,256]{1,0:T(8,128)(2,1)S(1)}, bf16[256,256]{1,0:T(8,128)(2,1)S(1)}, u32[]{:S(2)}, u32[]{:S(2)}) collective-permute-start(bf16[256,256]{1,0:T(8,128)(2,1)S(1)} %get-tuple-element.57), channel_id=1, source_target_pairs={{0,24},{8,0},{16,8},{24,16},{1,25},{9,1},{17,9},{25,17},{2,26},{10... | collective-permute-start | bytes 393224 | tf_op jit(solution)/shard_map/ppermute | solution.py:243
  32.5 33.8 %copy-start.5 = (f32[264,256]{1,0:T(8,128)}, f32[264,256]{1,0:T(8,128)S(1)}, u32[]{:S(2)}) copy-start(f32[264,256]{1,0:T(8,128)S(1)} %pack.1.refs_0_) | copy-start | bytes 811012
  32.6 35.9 %collective-permute-start.21 = (f32[264,256]{1,0:T(8,128)S(1)}, f32[264,256]{1,0:T(8,128)S(1)}, u32[]{:S(2)}, u32[]{:S(2)}) collective-permute-start(f32[264,256]{1,0:T(8,128)S(1)} %pack.1.refs_0_), channel_id=1, source_target_pairs={{24,0},{25,1},{26,2},{27,3},{28,4},{29,5},{30,6},{31,7}} | collective-permute-start | bytes 811016 | tf_op jit(solution)/shard_map/ppermute | solution.py:286
  34.5 36.0 %collective-permute-start.7 = (bf16[1024,256]{1,0:T(8,128)(2,1)S(1)}, bf16[1024,256]{1,0:T(8,128)(2,1)S(1)}, u32[]{:S(2)}, u32[]{:S(2)}) collective-permute-start(bf16[1024,256]{1,0:T(8,128)(2,1)S(1)} %block_product.5), channel_id=1, source_target_pairs={{8,0},{24,16},{9,1},{25,17},{10,2},{26,18},{11,3},{27,19},{12,4},{... | collective-permute-start | bytes 1572872 | tf_op jit(solution)/shard_map/ppermute | solution.py:256
  42.0 21.6 %collective-permute-start.15 = (bf16[256,256]{1,0:T(8,128)(2,1)S(1)}, bf16[256,256]{1,0:T(8,128)(2,1)S(1)}, u32[]{:S(2)}, u32[]{:S(2)}) collective-permute-start(bf16[256,256]{1,0:T(8,128)(2,1)S(1)} %fusion.61.refs_0_), channel_id=1, source_target_pairs={{0,24},{8,0},{16,8},{24,16},{1,25},{9,1},{17,9},{25,17},{2,26},{10... | collective-permute-start | bytes 393224 | tf_op jit(solution)/shard_map/ppermute | solution.py:293
  46.2 18.8 %collective-permute-start.14 = (bf16[256,256]{1,0:T(8,128)(2,1)S(1)}, bf16[256,256]{1,0:T(8,128)(2,1)S(1)}, u32[]{:S(2)}, u32[]{:S(2)}) collective-permute-start(bf16[256,256]{1,0:T(8,128)(2,1)S(1)} %fusion.61.refs_0_), channel_id=1, source_target_pairs={{0,16},{8,24},{16,0},{24,8},{1,17},{9,25},{17,1},{25,9},{2,18},{10... | collective-permute-start | bytes 393224 | tf_op jit(solution)/shard_map/ppermute | solution.py:293
  52.3 14.1 %collective-permute-start.13 = (bf16[256,256]{1,0:T(8,128)(2,1)S(1)}, bf16[256,256]{1,0:T(8,128)(2,1)S(1)}, u32[]{:S(2)}, u32[]{:S(2)}) collective-permute-start(bf16[256,256]{1,0:T(8,128)(2,1)S(1)} %fusion.61.refs_0_), channel_id=1, source_target_pairs={{0,8},{8,16},{16,24},{24,0},{1,9},{9,17},{17,25},{25,1},{2,10},{10... | collective-permute-start | bytes 393224 | tf_op jit(solution)/shard_map/ppermute | solution.py:293
  63.6 14.7 %collective-permute-start.1 = (bf16[1024,256]{1,0:T(8,128)(2,1)S(1)}, bf16[1024,256]{1,0:T(8,128)(2,1)}, u32[]{:S(2)}, u32[]{:S(2)}) collective-permute-start(bf16[1024,256]{1,0:T(8,128)(2,1)S(1)} %collective-permute-done.own), channel_id=1, source_target_pairs={{8,16},{16,24},{9,17},{17,25},{10,18},{18,26},{11,19},{19,27},{12,... | collective-permute-start | bytes 1572872 | tf_op jit(solution)/shard_map/ppermute | solution.py:298
  65.0 11.3 %collective-permute-start.20 = (f32[264,256]{1,0:T(8,128)S(1)}, f32[264,256]{1,0:T(8,128)S(1)}, u32[]{:S(2)}, u32[]{:S(2)}) collective-permute-start(f32[264,256]{1,0:T(8,128)S(1)} %pack.1.refs_0_), channel_id=1, source_target_pairs={{16,0},{17,1},{18,2},{19,3},{20,4},{21,5},{22,6},{23,7}} | collective-permute-start | bytes 811016 | tf_op jit(solution)/shard_map/ppermute | solution.py:286
  66.3 15.6 %collective-permute-start.19 = (f32[264,256]{1,0:T(8,128)S(1)}, f32[264,256]{1,0:T(8,128)S(1)}, u32[]{:S(2)}, u32[]{:S(2)}) collective-permute-start(f32[264,256]{1,0:T(8,128)S(1)} %pack.1.refs_0_), channel_id=1, source_target_pairs={{8,0},{9,1},{10,2},{11,3},{12,4},{13,5},{14,6},{15,7}} | collective-permute-start | bytes 811016 | tf_op jit(solution)/shard_map/ppermute | solution.py:286
  68.5 13.5 %copy-start.10 = (f32[264,256]{1,0:T(8,128)}, f32[264,256]{1,0:T(8,128)S(1)}, u32[]{:S(2)}) copy-start(f32[264,256]{1,0:T(8,128)S(1)} %collective-permute-done.21.refs_3_) | copy-start | bytes 811012
  68.5 20.8 %collective-permute-start.17 = (bf16[1024,256]{1,0:T(8,128)(2,1)}, bf16[1024,256]{1,0:T(8,128)(2,1)}, u32[]{:S(2)}, u32[]{:S(2)}) collective-permute-start(bf16[1024,256]{1,0:T(8,128)(2,1)} %assemble.1.own), channel_id=1, source_target_pairs={{1,0},{2,1},{3,2},{4,3},{5,4},{6,5},{7,6},{9,8},{10,9},{11,10},{12... | collective-permute-start | bytes 1572872 | tf_op jit(solution)/shard_map/ppermute | solution.py:27
  70.5 13.6 %copy-start.23 = (bf16[1024,256]{1,0:T(8,128)(2,1)}, bf16[1024,256]{1,0:T(8,128)(2,1)S(1)}, u32[]{:S(2)}) copy-start(bf16[1024,256]{1,0:T(8,128)(2,1)S(1)} %collective-permute-done.7) | copy-start | bytes 1572868
  70.5 18.8 %collective-permute-start.16 = (bf16[1024,256]{1,0:T(8,128)(2,1)}, bf16[1024,256]{1,0:T(8,128)(2,1)}, u32[]{:S(2)}, u32[]{:S(2)}) collective-permute-start(bf16[1024,256]{1,0:T(8,128)(2,1)} %assemble.1.own), channel_id=1, source_target_pairs={{0,1},{1,2},{2,3},{3,4},{4,5},{5,6},{6,7},{8,9},{9,10},{10,11},{11... | collective-permute-start | bytes 1572872 | tf_op jit(solution)/shard_map/ppermute | solution.py:27
  76.3 0.7 copy-start.12
  77.0 17.0 %collective-permute-start.18 = (bf16[1024,256]{1,0:T(8,128)(2,1)}, bf16[1024,256]{1,0:T(8,128)(2,1)}, u32[]{:S(2)}, u32[]{:S(2)}) collective-permute-start(bf16[1024,256]{1,0:T(8,128)(2,1)} %add_convert_fusion), channel_id=1, source_target_pairs={{16,0},{17,1},{18,2},{19,3},{20,4},{21,5},{22,6},{23,7}} | collective-permute-start | bytes 1572872 | tf_op jit(solution)/shard_map/ppermute | solution.py:256
  78.3 39.2 %collective-permute-start.3 = (bf16[1024,256]{1,0:T(8,128)(2,1)}, bf16[1024,256]{1,0:T(8,128)(2,1)}, u32[]{:S(2)}, u32[]{:S(2)}) collective-permute-start(bf16[1024,256]{1,0:T(8,128)(2,1)} %collective-permute-done.1.own), channel_id=1, source_target_pairs={{17,16},{18,17},{19,18},{20,19},{21,20},{22,21},{23,22},{25,24},{2... | collective-permute-start | bytes 1572872 | tf_op jit(solution)/shard_map/ppermute | solution.py:27
  82.0 0.7 copy-start.14
  82.7 34.8 %collective-permute-start.2 = (bf16[1024,256]{1,0:T(8,128)(2,1)}, bf16[1024,256]{1,0:T(8,128)(2,1)}, u32[]{:S(2)}, u32[]{:S(2)}) collective-permute-start(bf16[1024,256]{1,0:T(8,128)(2,1)} %collective-permute-done.1.own), channel_id=1, source_target_pairs={{16,17},{17,18},{18,19},{19,20},{20,21},{21,22},{22,23},{24,25},{2... | collective-permute-start | bytes 1572872 | tf_op jit(solution)/shard_map/ppermute | solution.py:27
  84.2 1.0 copy-start.6
  85.1 1.0 copy-start.11
  86.1 1.0 copy-start.13
  87.0 1.0 copy-start.15
  93.2 0.8 copy-start.22
  102.9 22.5 %collective-permute-start.23 = (bf16[1024,256]{1,0:T(8,128)(2,1)}, bf16[1024,256]{1,0:T(8,128)(2,1)S(1)}, u32[]{:S(2)}, u32[]{:S(2)}) collective-permute-start(bf16[1024,256]{1,0:T(8,128)(2,1)} %get-tuple-element.61.own), channel_id=1, source_target_pairs={{1,0},{2,1},{3,2},{4,3},{5,4},{6,5},{7,6}} | collective-permute-start | bytes 1572872 | tf_op jit(solution)/shard_map/ppermute | solution.py:27
  116.2 27.6 %collective-permute-start.25 = (bf16[1024,256]{1,0:T(8,128)(2,1)}, bf16[1024,256]{1,0:T(8,128)(2,1)}, u32[]{:S(2)}, u32[]{:S(2)}) collective-permute-start(bf16[1024,256]{1,0:T(8,128)(2,1)} %copy-done.22), channel_id=1, source_target_pairs={{8,0},{9,1},{10,2},{11,3},{12,4},{13,5},{14,6},{15,7}} | collective-permute-start | bytes 1572872 | tf_op jit(solution)/shard_map/ppermute | solution.py:306
  118.9 24.9 %collective-permute-start.24 = (bf16[1024,256]{1,0:T(8,128)(2,1)}, bf16[1024,256]{1,0:T(8,128)(2,1)}, u32[]{:S(2)}, u32[]{:S(2)}) collective-permute-start(bf16[1024,256]{1,0:T(8,128)(2,1)} %block_product.4), channel_id=1, source_target_pairs={{24,0},{25,1},{26,2},{27,3},{28,4},{29,5},{30,6},{31,7}} | collective-permute-start | bytes 1572872 | tf_op jit(solution)/shard_map/ppermute | solution.py:302
  120.2 23.6 %collective-permute-start.4 = (bf16[1024,256]{1,0:T(8,128)(2,1)}, bf16[1024,256]{1,0:T(8,128)(2,1)}, u32[]{:S(2)}, u32[]{:S(2)}) collective-permute-start(bf16[1024,256]{1,0:T(8,128)(2,1)} %block_product.4), channel_id=1, source_target_pairs={{16,0},{17,1},{18,2},{19,3},{20,4},{21,5},{22,6},{23,7}} | collective-permute-start | bytes 1572872 | tf_op jit(solution)/shard_map/ppermute | solution.py:302
  121.5 10.8 %collective-permute-start.22 = (bf16[1024,256]{1,0:T(8,128)(2,1)}, bf16[1024,256]{1,0:T(8,128)(2,1)}, u32[]{:S(2)}, u32[]{:S(2)}) collective-permute-start(bf16[1024,256]{1,0:T(8,128)(2,1)} %get-tuple-element.61.own), channel_id=1, source_target_pairs={{0,1},{1,2},{2,3},{3,4},{4,5},{5,6},{6,7}} | collective-permute-start | bytes 1572872 | tf_op jit(solution)/shard_map/ppermute | solution.py:27
  125.4 0.8 copy-start.8
  126.2 26.1 %collective-permute-start.26 = (bf16[1024,256]{1,0:T(8,128)(2,1)}, bf16[1024,256]{1,0:T(8,128)(2,1)}, u32[]{:S(2)}, u32[]{:S(2)}) collective-permute-start(bf16[1024,256]{1,0:T(8,128)(2,1)} %broadcast_select_fusion), channel_id=1, source_target_pairs={{0,8},{16,24},{1,9},{17,25},{2,10},{18,26},{3,11},{19,27},{4,12},{... | collective-permute-start | bytes 1572872 | tf_op jit(solution)/shard_map/ppermute | solution.py:325
  132.4 1.0 copy-start.9
  153.6 22.5 %collective-permute-start.28 = (bf16[1024,256]{1,0:T(8,128)(2,1)S(1)}, bf16[1024,256]{1,0:T(8,128)(2,1)S(1)}, u32[]{:S(2)}, u32[]{:S(2)}) collective-permute-start(bf16[1024,256]{1,0:T(8,128)(2,1)S(1)} %select_select_fusion.own), channel_id=1, source_target_pairs={{1,0},{2,1},{3,2},{4,3},{5,4},{6,5},{7,6},{9,8},{10,9},{11,10},{12... | collective-permute-start | bytes 1572872 | tf_op jit(solution)/shard_map/ppermute | solution.py:27
  166.7 10.5 %collective-permute-start.27 = (bf16[1024,256]{1,0:T(8,128)(2,1)S(1)}, bf16[1024,256]{1,0:T(8,128)(2,1)S(1)}, u32[]{:S(2)}, u32[]{:S(2)}) collective-permute-start(bf16[1024,256]{1,0:T(8,128)(2,1)S(1)} %select_select_fusion.own), channel_id=1, source_target_pairs={{0,1},{1,2},{2,3},{3,4},{4,5},{5,6},{6,7},{8,9},{9,10},{10,11},{11... | collective-permute-start | bytes 1572872 | tf_op jit(solution)/shard_map/ppermute | solution.py:27
  168.7 15.5 %copy-start.4 = (bf16[1,1024,256]{2,1,0:T(8,128)(2,1)S(1)}, bf16[1,1024,256]{2,1,0:T(8,128)(2,1)}, u32[]{:S(2)}) copy-start(bf16[1,1024,256]{2,1,0:T(8,128)(2,1)} %param.16) | copy-start | bytes 1572868
  170.7 9.6 %collective-permute-start.34 = (f32[256,256]{1,0:T(8,128)S(1)}, f32[256,256]{1,0:T(8,128)S(1)}, u32[]{:S(2)}, u32[]{:S(2)}) collective-permute-start(f32[256,256]{1,0:T(8,128)S(1)} %get-tuple-element.92), channel_id=1, source_target_pairs={{0,8},{1,9},{2,10},{3,11},{4,12},{5,13},{6,14},{7,15}} | collective-permute-start | bytes 786440 | tf_op jit(solution)/shard_map/ppermute | solution.py:330
  172.0 12.8 %collective-permute-start.33 = (f32[256,256]{1,0:T(8,128)}, f32[256,256]{1,0:T(8,128)}, u32[]{:S(2)}, u32[]{:S(2)}) collective-permute-start(f32[256,256]{1,0:T(8,128)} %get-tuple-element.93), channel_id=1, source_target_pairs={{0,16},{1,17},{2,18},{3,19},{4,20},{5,21},{6,22},{7,23}} | collective-permute-start | bytes 786440 | tf_op jit(solution)/shard_map/ppermute | solution.py:330
  174.0 15.1 %collective-permute-start.32 = (f32[256,256]{1,0:T(8,128)}, f32[256,256]{1,0:T(8,128)}, u32[]{:S(2)}, u32[]{:S(2)}) collective-permute-start(f32[256,256]{1,0:T(8,128)} %get-tuple-element.94), channel_id=1, source_target_pairs={{0,24},{1,25},{2,26},{3,27},{4,28},{5,29},{6,30},{7,31}} | collective-permute-start | bytes 786440 | tf_op jit(solution)/shard_map/ppermute | solution.py:330
  179.6 0.7 copy-start.16
  180.3 11.6 %collective-permute-start.29 = (bf16[256,256]{1,0:T(8,128)(2,1)}, bf16[256,256]{1,0:T(8,128)(2,1)}, u32[]{:S(2)}, u32[]{:S(2)}) collective-permute-start(bf16[256,256]{1,0:T(8,128)(2,1)} %get-tuple-element.66), channel_id=1, source_target_pairs={{0,8},{8,16},{16,24},{24,0},{1,9},{9,17},{17,25},{25,1},{2,10},{10... | collective-permute-start | bytes 393224 | tf_op jit(solution)/shard_map/ppermute | solution.py:243
  180.3 14.4 %collective-permute-start.30 = (bf16[256,256]{1,0:T(8,128)(2,1)}, bf16[256,256]{1,0:T(8,128)(2,1)}, u32[]{:S(2)}, u32[]{:S(2)}) collective-permute-start(bf16[256,256]{1,0:T(8,128)(2,1)} %get-tuple-element.67), channel_id=1, source_target_pairs={{0,16},{8,24},{16,0},{24,8},{1,17},{9,25},{17,1},{25,9},{2,18},{10... | collective-permute-start | bytes 393224 | tf_op jit(solution)/shard_map/ppermute | solution.py:243
  180.3 3.9 %copy-start.24 = (f32[256,256]{1,0:T(8,128)}, f32[256,256]{1,0:T(8,128)S(1)}, u32[]{:S(2)}) copy-start(f32[256,256]{1,0:T(8,128)S(1)} %collective-permute-done.34) | copy-start | bytes 786436
  180.3 17.1 %collective-permute-start.31 = (bf16[256,256]{1,0:T(8,128)(2,1)S(1)}, bf16[256,256]{1,0:T(8,128)(2,1)}, u32[]{:S(2)}, u32[]{:S(2)}) collective-permute-start(bf16[256,256]{1,0:T(8,128)(2,1)S(1)} %get-tuple-element.68), channel_id=1, source_target_pairs={{0,24},{8,0},{16,8},{24,16},{1,25},{9,1},{17,9},{25,17},{2,26},{10... | collective-permute-start | bytes 393224 | tf_op jit(solution)/shard_map/ppermute | solution.py:243

commit v12 on v11

--- a/solution.py
+++ b/solution.py
@@ -160,7 +160,7 @@
 
 
 def unpack_kernel(lags, *refs):
-    packed, state, columns = refs[:lags], refs[lags], refs[lags + 1]
+    packed, state, coefs = refs[:lags], refs[lags], refs[lags + 1]
     rows = state.shape[0] // lags
 
     @pl.when(lax.axis_index("lag") == 0)
@@ -168,20 +168,21 @@
         for d, ref in enumerate(packed):
             spot = pl.ds(d * rows, rows)
             state[spot, :] = ref[pl.ds(0, rows), :]
-            columns[spot, :] = jnp.transpose(ref[pl.ds(rows, 8), :])[:rows]
+            coefs[d] = ref[pl.ds(rows, 8), :]
 
 
 def unpack(packed):
     lags, (height, cols) = len(packed), packed[0].shape
     rows = (height - 8) * lags
-    return pl.pallas_call(
+    state, coefs = pl.pallas_call(
         functools.partial(unpack_kernel, lags),
         in_specs=[VMEM] * lags,
         out_specs=[VMEM] * 2,
-        out_shape=[jax.ShapeDtypeStruct((rows, cols), jnp.float32), jax.ShapeDtypeStruct((rows, 8), jnp.float32)],
+        out_shape=[jax.ShapeDtypeStruct((rows, cols), jnp.float32), jax.ShapeDtypeStruct((lags, 8, cols), jnp.float32)],
         compiler_params=PARAMS,
         name="unpack",
     )(*packed)
+    return state, *(coefs[:, k, : rows // lags].reshape(rows) for k in range(2))
 
 
 def assemble_kernel(*refs):
@@ -297,7 +298,7 @@
     base_1 = tree_to_first(low, lags, 1)
     twice = lax.ppermute(once, "lag", [(i, i + 1) for i in rest[:-1]])
     window_2 = window_of(twice, rest[1:])
-    state, columns = unpack(packed)
+    state, *coefs = unpack(packed)
     (low,) = block_product(*local, window_2, prestress, rest[1:], kinds[1:])
     base_2 = [lax.ppermute(low, "lag", [(d, 0)]) for d in rest[1:]]
 
@@ -305,25 +306,27 @@
     high, low = block_product(*local, window, prestress, [0, 1], kinds)
     base_2 = base_2 + [lax.ppermute(low, "lag", [(1, 0)])]
 
-    def on_first(step, *values):
-        like = (jax.ShapeDtypeStruct(field.shape, jnp.bfloat16), jax.ShapeDtypeStruct(field.shape, jnp.float32))
-        return lax.cond(me == 0, step, lambda *_: tuple(jnp.zeros(x.shape, x.dtype) for x in like), *values)
-
-    def second_step(high, start, first, columns, *received):
+    def nothing(high, start, first, *values):
+        return jnp.zeros(first.shape, first.dtype), jnp.zeros(start.shape, start.dtype)
+
+    def second_step(high, start, first, ratio, strength, *received):
         begun = evolved(start, first.astype(jnp.float32))
-        return settle_friction(block_load(high, *received), begun, columns[:, 0:1], columns[:, 1:2])
-
-    def third_step(high, start, columns, *received):
-        return settle_friction(block_load(high, *received), start, columns[:, 0:1], columns[:, 1:2])
-
-    second, state = on_first(second_step, high, state, first, columns, *base_1)
+        return settle_friction(block_load(high, *received), begun, ratio[:, None], strength[:, None])
+
+    def third_step(high, start, ratio, strength, first, moved, *received):
+        return settle_friction(block_load(high, *received), start, ratio[:, None], strength[:, None])
+
+    def last_field(high, start, ratio, strength, first, moved, *received):
+        return jnp.where(me == 2, first, moved), jnp.zeros(start.shape, start.dtype)
+
+    second, state = lax.cond(me == 0, second_step, nothing, high, state, first, *coefs, *base_1)
     window = window_of(second, [0])
     (high,) = block_product(*local, window, prestress, [0], kinds[:1])
-    third, state = on_first(third_step, high, state, columns, *base_2)
-
     source = jnp.where(me == 0, second, twice)
     moved = lax.ppermute(source, "lag", [(0, 1)] + [(i, i + 1) for i in every[2:-1]])
-    last = jnp.where(me == 0, third, jnp.where(me == 2, first, moved))
+    values = (high, state, *coefs, first, moved, *base_2)
+    last, state = lax.cond(me == 0, third_step, last_field, *values)
+
     below, own, above = window_of(last, every)
     mine = state[:rows]
     for d in rest:

time: 204 us -> 195 us (0.956)
  waiting for transfers between devices: 48.1 us -> 82.7 us
  starting transfers between devices: 93.3 us -> 65.8 us
  local copies, waits for them, and re-layouts: 16.7 us -> 7.8 us
  other arithmetic: 24 us -> 20.6 us
  Pallas kernels: 16.6 us -> 14.3 us
    ppermute x12, starting transfers between devices: 43.2 us -> 26.5 us  [exchange(): return (lax.ppermute(value, axes, up), lax.ppermute(value, axes, down))]
    ppermute x3, waiting for transfers between devices: 11.3 us -> 27.5 us  [shards(): lax.ppermute(rates, 'lag', [(i, (i + d) % lags) for i in every])]
    ppermute x1, waiting for transfers between devices: 6.52 us -> 18.7 us  [shards(): base_2 = base_2 + [lax.ppermute(low, 'lag', [(1, 0)])]]
    ppermute x12, waiting for transfers between devices: 1.37 us -> 7.8 us  [exchange(): return (lax.ppermute(value, axes, up), lax.ppermute(value, axes, down))]
    ppermute x2, waiting for transfers between devices: 0.01 us -> 5.81 us  [tree_to_first(): arrived = lax.ppermute(value, 'lag', route)]
    unnamed x50 -> x46, local copies, waits for them, and re-layouts: 12.2 us -> 6.95 us
    ppermute x1, starting transfers between devices: 6.02 us -> 1.32 us  [shards(): lax.ppermute(source, 'lag', [(0, 1)] + [(i, i + 1) for i in every[2:-1]])]
    ppermute x3, waiting for transfers between devices: 4.69 us -> 0.01 us  [shards(): packed = [packed] + [lax.ppermute(packed, 'lag', [(d, 0)]) for d in rest]]
  transfers between devices with their start and end apart: 35 -> 35, of which waited for: 13 -> 18; matrix products, arithmetic and copies ran while one was open for 12% -> 6% of each run, Pallas kernels for 8% -> 7%
where the time goes in v12:
time: 195 us; the launch traced here: 193 us
  waiting for transfers between devices  82.7 us (42%)
  starting transfers between devices  65.8 us (34%)
  other arithmetic  20.6 us (11%)
  Pallas kernels  14.3 us (7%)
  local copies, waits for them, and re-layouts  7.8 us (4%)
    ppermute x3, waiting for transfers between devices, shards(): lax.ppermute(rates, 'lag', [(i, (i + d) % lags) for i in every])  27.5 us
    ppermute x12, starting transfers between devices, exchange(): return (lax.ppermute(value, axes, up), lax.ppermute(value, axes, down))  26.5 us
    ppermute x1, waiting for transfers between devices, shards(): base_2 = base_2 + [lax.ppermute(low, 'lag', [(1, 0)])]  18.7 us
    add x2, other arithmetic, evolved(): state + time_step * (jnp.exp(-state) - jnp.sqrt(speed_of * speed_of + cre...  13.4 us
    ppermute x6, starting transfers between devices, scatter_sum(): total = total + lax.ppermute(parts[d], 'lag', route).astype(jnp.float32)  10.6 us
    ppermute x6, waiting for transfers between devices, scatter_sum(): total = total + lax.ppermute(parts[d], 'lag', route).astype(jnp.float32)  10.6 us
    ppermute x12, waiting for transfers between devices, exchange(): return (lax.ppermute(value, axes, up), lax.ppermute(value, axes, down))  7.8 us
    pallas_call x4, Pallas kernels, block_product(): pl.pallas_call(functools.partial(block_kernel, chunks, (planes[0], planes...  7.02 us
  transfers between devices with their start and end apart: 35, of which 18 were waited for; matrix products, arithmetic and copies ran while one was open for 6% of the time, Pallas kernels for 7%

profile of v12, /device:TPU:2, one launch (start us, length us, event | category | flops | bytes accessed | tf_op | source)
XLA Modules:
  0.0 193.0 jit_solution(15061416221999891482)
XLA Ops:
  0.7 4.4 %collective-permute-start.8 = (bf16[1024,256]{1,0:T(8,128)(2,1)}, bf16[1024,256]{1,0:T(8,128)(2,1)}, u32[]{:S(2)}, u32[]{:S(2)}) collective-permute-start(bf16[1024,256]{1,0:T(8,128)(2,1)} %bitcast.30), channel_id=1, source_target_pairs={{0,8},{8,16},{16,24},{1,9},{9,17},{17,25},{2,10},{10,18},{18,26},{... | collective-permute-start | bytes 1572872 | tf_op jit(solution)/shard_map/ppermute | solution.py:288
  5.1 1.9 collective-permute-start
  7.0 3.6 %collective-permute-start.1 = (bf16[1024,256]{1,0:T(8,128)(2,1)}, bf16[1024,256]{1,0:T(8,128)(2,1)S(1)}, u32[]{:S(2)}, u32[]{:S(2)}) collective-permute-start(bf16[1024,256]{1,0:T(8,128)(2,1)} %bitcast.32), channel_id=1, source_target_pairs={{1,0},{2,1},{3,2},{4,3},{5,4},{6,5},{7,6},{9,8},{10,9},{11,10},{12... | collective-permute-start | bytes 1572872 | tf_op jit(solution)/shard_map/ppermute | solution.py:27
  11.3 4.4 %collective-permute-done.8.own = bf16[1024,256]{1,0:T(8,128)(2,1)} collective-permute-done((bf16[1024,256]{1,0:T(8,128)(2,1)}, bf16[1024,256]{1,0:T(8,128)(2,1)}, u32[]{:S(2)}, u32[]{:S(2)}) %collective-permute-start.8) | collective-permute-done | bytes 524320 | tf_op jit(solution)/shard_map/ppermute | solution.py:288
  17.9 2.7 %collective-permute-done.1.above = bf16[1024,256]{1,0:T(8,128)(2,1)S(1)} collective-permute-done((bf16[1024,256]{1,0:T(8,128)(2,1)}, bf16[1024,256]{1,0:T(8,128)(2,1)S(1)}, u32[]{:S(2)}, u32[]{:S(2)}) %collective-permute-start.1) | collective-permute-done | bytes 524320 | tf_op jit(solution)/shard_map/ppermute | solution.py:27
  20.6 1.9 copy-done
  22.4 1.0 copy-done.3
  24.1 1.7 product_by_rows.2
  25.8 2.8 %collective-permute-start.2 = (bf16[256,256]{1,0:T(8,128)(2,1)S(1)}, bf16[256,256]{1,0:T(8,128)(2,1)S(1)}, u32[]{:S(2)}, u32[]{:S(2)}) collective-permute-start(bf16[256,256]{1,0:T(8,128)(2,1)S(1)} %get-tuple-element.70), channel_id=1, source_target_pairs={{0,8},{8,16},{16,24},{24,0},{1,9},{9,17},{17,25},{25,1},{2,10},{10... | collective-permute-start | bytes 393224 | tf_op jit(solution)/shard_map/ppermute | solution.py:244
  28.7 2.6 %collective-permute-start.3 = (bf16[256,256]{1,0:T(8,128)(2,1)S(1)}, bf16[256,256]{1,0:T(8,128)(2,1)S(1)}, u32[]{:S(2)}, u32[]{:S(2)}) collective-permute-start(bf16[256,256]{1,0:T(8,128)(2,1)S(1)} %get-tuple-element.71), channel_id=1, source_target_pairs={{0,16},{8,24},{16,0},{24,8},{1,17},{9,25},{17,1},{25,9},{2,18},{10... | collective-permute-start | bytes 393224 | tf_op jit(solution)/shard_map/ppermute | solution.py:244
  31.2 1.3 collective-permute-start.4
  33.4 1.3 collective-permute-start.15
  35.3 1.3 collective-permute-start.11
  36.6 4.2 %collective-permute-done.3 = bf16[256,256]{1,0:T(8,128)(2,1)S(1)} collective-permute-done((bf16[256,256]{1,0:T(8,128)(2,1)S(1)}, bf16[256,256]{1,0:T(8,128)(2,1)S(1)}, u32[]{:S(2)}, u32[]{:S(2)}) %collective-permute-start.3) | collective-permute-done | bytes 131104 | tf_op jit(solution)/shard_map/ppermute | solution.py:244
  40.8 1.0 fusion.61.refs_0_
  41.8 3.4 %collective-permute-start.5 = (bf16[256,256]{1,0:T(8,128)(2,1)S(1)}, bf16[256,256]{1,0:T(8,128)(2,1)S(1)}, u32[]{:S(2)}, u32[]{:S(2)}) collective-permute-start(bf16[256,256]{1,0:T(8,128)(2,1)S(1)} %fusion.61.refs_0_), channel_id=1, source_target_pairs={{0,8},{8,16},{16,24},{24,0},{1,9},{9,17},{17,25},{25,1},{2,10},{10... | collective-permute-start | bytes 393224 | tf_op jit(solution)/shard_map/ppermute | solution.py:294
  45.1 1.7 collective-permute-start.6
  47.6 7.6 %collective-permute-done.5.refs_1_ = bf16[256,256]{1,0:T(8,128)(2,1)S(1)} collective-permute-done((bf16[256,256]{1,0:T(8,128)(2,1)S(1)}, bf16[256,256]{1,0:T(8,128)(2,1)S(1)}, u32[]{:S(2)}, u32[]{:S(2)}) %collective-permute-start.5) | collective-permute-done | bytes 131104 | tf_op jit(solution)/shard_map/ppermute | solution.py:294
  55.2 1.3 collective-permute-start.16
  56.5 1.5 collective-permute-done.6.refs_2_
  58.0 1.3 collective-permute-start.17
  59.3 18.4 %collective-permute-done.7.refs_3_ = bf16[256,256]{1,0:T(8,128)(2,1)S(1)} collective-permute-done((bf16[256,256]{1,0:T(8,128)(2,1)S(1)}, bf16[256,256]{1,0:T(8,128)(2,1)S(1)}, u32[]{:S(2)}, u32[]{:S(2)}) %collective-permute-start.7) | collective-permute-done | bytes 131104 | tf_op jit(solution)/shard_map/ppermute | solution.py:294
  77.7 1.5 collective-permute-start.18
  79.2 0.8 assemble.1.own
  80.0 1.9 %collective-permute-start.12 = (bf16[1024,256]{1,0:T(8,128)(2,1)}, bf16[1024,256]{1,0:T(8,128)(2,1)}, u32[]{:S(2)}, u32[]{:S(2)}) collective-permute-start(bf16[1024,256]{1,0:T(8,128)(2,1)} %assemble.1.own), channel_id=1, source_target_pairs={{0,1},{1,2},{2,3},{3,4},{4,5},{5,6},{6,7},{8,9},{9,10},{10,11},{11... | collective-permute-start | bytes 1572872 | tf_op jit(solution)/shard_map/ppermute | solution.py:27
  82.0 3.6 %collective-permute-start.13 = (bf16[1024,256]{1,0:T(8,128)(2,1)}, bf16[1024,256]{1,0:T(8,128)(2,1)}, u32[]{:S(2)}, u32[]{:S(2)}) collective-permute-start(bf16[1024,256]{1,0:T(8,128)(2,1)} %assemble.1.own), channel_id=1, source_target_pairs={{1,0},{2,1},{3,2},{4,3},{5,4},{6,5},{7,6},{9,8},{10,9},{11,10},{12... | collective-permute-start | bytes 1572872 | tf_op jit(solution)/shard_map/ppermute | solution.py:27
  85.6 1.0 add_convert_fusion
  87.3 1.3 collective-permute-start.14
  88.6 0.9 copy-done.7
  89.5 1.0 copy-done.9
  90.5 1.2 unpack.1
  91.7 1.5 collective-permute-start.20
  93.1 1.5 collective-permute-start.21
  94.6 0.8 collective-permute-done.13.above
  95.4 2.8 %block_product.5 = (f32[1024,256]{1,0:T(8,128)S(1)}, bf16[1024,256]{1,0:T(8,128)(2,1)S(1)}) custom-call(s32[1,1,3]{2,1,0:T(1,128)S(1)} %copy-done.12, s32[1]{0:T(128)S(6)} %copy.19.live, bf16[1,1024,1536]{2,1,0:T(8,128)(2,1)S(1)} %copy-done.1, bf16[1024,256]{1,0:T(8,128)(2,1)} %collective-permute-done.12.below, bf16[1024,256]{1,0:T(8,128)(2,1)} %assemble.1.own, ...), custom_call_target="tpu_custom_call" | custom-call | flops 805306368 | bytes 5242880 | tf_op jit(solution)/shard_map/block_product/pallas_call | solution.py:122
  98.3 5.8 %collective-permute-done.14 = bf16[1024,256]{1,0:T(8,128)(2,1)} collective-permute-done((bf16[1024,256]{1,0:T(8,128)(2,1)}, bf16[1024,256]{1,0:T(8,128)(2,1)}, u32[]{:S(2)}, u32[]{:S(2)}) %collective-permute-start.14) | collective-permute-done | bytes 524320 | tf_op jit(solution)/shard_map/ppermute | solution.py:257
  104.1 7.2 %conditional.2 = (bf16[1024,256]{1,0:T(8,128)(2,1)}, f32[1024,256]{1,0:T(8,128)S(1)}) conditional(s32[]{:T(128)} %convert_element_type.61, () %tuple.24, (bf16[1024,256]{1,0:T(8,128)(2,1)S(1)}, f32[1024,256]{1,0:T(8,128)S(1)}, bf16[1024,256]{1,0:T(8,128)(2,1)}, f32[4,1,256]{2,1,0:T(1,128)S(1)}, f32[1024,256]{1,0:T(8,128)S(1)}, ...), branch_computations={%region_0.1_spmd, %region_1.2_spmd} | conditional | flops 18613248 | bytes 5263376 | solution.py:322
  104.1 7.2 %multiply_add_fusion = (f32[1024,256]{1,0:T(8,128)S(1)}, bf16[1024,256]{1,0:T(8,128)(2,1)}) fusion(f32[1024,256]{1,0:T(8,128)S(1)} %get-tuple-element.38, bf16[1024,256]{1,0:T(8,128)(2,1)} %get-tuple-element.39, f32[1024]{0:T(1024)S(1)} %bitcast.37, f32[1024]{0:T(1024)S(1)} %broadcast_multiply_fusion, f32[1024]{0:T(1024)S(1)} %bitcast.43, ...), kind=kLoop, calls=%fused_computation.18 | loop fusion | flops 18612224 | bytes 5255168 | tf_op jit(solution)/shard_map/cond/branch_1_fun/add | solution.py:236
  111.3 1.5 broadcast_select_fusion.1
  112.7 1.3 collective-permute-start.19
  114.1 1.3 collective-permute-start.26
  115.4 1.9 collective-permute-start.23
  117.3 3.6 %collective-permute-start.24 = (bf16[1024,256]{1,0:T(8,128)(2,1)}, bf16[1024,256]{1,0:T(8,128)(2,1)S(1)}, u32[]{:S(2)}, u32[]{:S(2)}) collective-permute-start(bf16[1024,256]{1,0:T(8,128)(2,1)} %get-tuple-element.76.own), channel_id=1, source_target_pairs={{1,0},{2,1},{3,2},{4,3},{5,4},{6,5},{7,6}} | collective-permute-start | bytes 1572872 | tf_op jit(solution)/shard_map/ppermute | solution.py:27
  121.6 1.3 collective-permute-start.22
  122.9 1.8 collective-permute-done.19
  124.7 1.3 collective-permute-start.25
  126.1 3.7 %collective-permute-done.24.above = bf16[1024,256]{1,0:T(8,128)(2,1)S(1)} collective-permute-done((bf16[1024,256]{1,0:T(8,128)(2,1)}, bf16[1024,256]{1,0:T(8,128)(2,1)S(1)}, u32[]{:S(2)}, u32[]{:S(2)}) %collective-permute-start.24) | collective-permute-done | bytes 524320 | tf_op jit(solution)/shard_map/ppermute | solution.py:27
  129.7 3.0 %block_product.7 = f32[1024,256]{1,0:T(8,128)} custom-call(s32[1,1,3]{2,1,0:T(1,128)S(1)} %copy-done.12, s32[1]{0:T(128)S(6)} %copy.19.live, bf16[1,1024,1536]{2,1,0:T(8,128)(2,1)S(1)} %copy-done.1, bf16[1024,256]{1,0:T(8,128)(2,1)S(1)} %collective-permute-done.23.below, bf16[1024,256]{1,0:T(8,128)(2,1)} %get-tuple-element.76.own, ...), custom_call_target="tpu_custom_call" | custom-call | flops 805306368 | bytes 5242880 | tf_op jit(solution)/shard_map/block_product/pallas_call | solution.py:122
  132.8 18.7 %collective-permute-done.26 = bf16[1024,256]{1,0:T(8,128)(2,1)S(1)} collective-permute-done((bf16[1024,256]{1,0:T(8,128)(2,1)}, bf16[1024,256]{1,0:T(8,128)(2,1)S(1)}, u32[]{:S(2)}, u32[]{:S(2)}) %collective-permute-start.26) | collective-permute-done | bytes 524320 | tf_op jit(solution)/shard_map/ppermute | solution.py:307
  151.5 6.2 %conditional.3 = (bf16[1024,256]{1,0:T(8,128)(2,1)S(1)}, f32[1024,256]{1,0:T(8,128)S(1)}) conditional(s32[]{:T(128)} %convert_element_type.61, (s32[]{:T(128)}, bf16[1024,256]{1,0:T(8,128)(2,1)}, bf16[1024,256]{1,0:T(8,128)(2,1)S(1)}) %tuple.26, (bf16[1024,256]{1,0:T(8,128)(2,1)S(1)}, f32[1024,256]{1,0:T(8,128)}, bf16[1024,256]{1,0:T(8,128)(2,1)S(1)}, ...), branch_computations={%region_2.3_spmd, %region_3.4_spmd} | conditional | flops 17302528 | bytes 5263376 | solution.py:328
  151.5 6.2 %multiply_add_fusion.2 = (f32[1024,256]{1,0:T(8,128)S(1)}, bf16[1024,256]{1,0:T(8,128)(2,1)S(1)}) fusion(f32[1024,256]{1,0:T(8,128)} %get-tuple-element.49, f32[1024]{0:T(1024)S(1)} %bitcast.39, f32[1024]{0:T(1024)S(1)} %broadcast_multiply_fusion.1, f32[1024]{0:T(1024)S(1)} %bitcast.44, bf16[1024,256]{1,0:T(8,128)(2,1)S(1)} %get-tuple-element.47, ...), kind=kLoop, calls=%fused_computation.43 | loop fusion | flops 17301504 | bytes 5255168 | tf_op jit(solution)/shard_map/cond/branch_1_fun/add | solution.py:236
  157.7 1.9 collective-permute-start.27
  159.7 3.6 %collective-permute-start.28 = (bf16[1024,256]{1,0:T(8,128)(2,1)S(1)}, bf16[1024,256]{1,0:T(8,128)(2,1)S(1)}, u32[]{:S(2)}, u32[]{:S(2)}) collective-permute-start(bf16[1024,256]{1,0:T(8,128)(2,1)S(1)} %get-tuple-element.79.own), channel_id=1, source_target_pairs={{1,0},{2,1},{3,2},{4,3},{5,4},{6,5},{7,6},{9,8},{10,9},{11,10},{12... | collective-permute-start | bytes 1572872 | tf_op jit(solution)/shard_map/ppermute | solution.py:27
  163.3 0.8 fusion.65
  164.2 1.3 collective-permute-start.32
  165.5 2.0 %collective-permute-start.33 = (f32[256,256]{1,0:T(8,128)}, f32[256,256]{1,0:T(8,128)}, u32[]{:S(2)}, u32[]{:S(2)}) collective-permute-start(f32[256,256]{1,0:T(8,128)} %get-tuple-element.92), channel_id=1, source_target_pairs={{0,16},{1,17},{2,18},{3,19},{4,20},{5,21},{6,22},{7,23}} | collective-permute-start | bytes 786440 | tf_op jit(solution)/shard_map/ppermute | solution.py:333
  167.5 2.0 %collective-permute-start.34 = (f32[256,256]{1,0:T(8,128)}, f32[256,256]{1,0:T(8,128)}, u32[]{:S(2)}, u32[]{:S(2)}) collective-permute-start(f32[256,256]{1,0:T(8,128)} %get-tuple-element.91), channel_id=1, source_target_pairs={{0,8},{1,9},{2,10},{3,11},{4,12},{5,13},{6,14},{7,15}} | collective-permute-start | bytes 786440 | tf_op jit(solution)/shard_map/ppermute | solution.py:333
  170.0 2.3 %product_by_rows.3 = (f32[256,256]{1,0:T(8,128)S(1)}, bf16[256,256]{1,0:T(8,128)(2,1)}, bf16[256,256]{1,0:T(8,128)(2,1)}, bf16[256,256]{1,0:T(8,128)(2,1)S(1)}) custom-call(s32[1,1,3]{2,1,0:T(1,128)S(1)} %copy-done.12, s32[1]{0:T(128)S(6)} %copy.19.live, bf16[1,1024,1536]{2,1,0:T(8,128)(2,1)S(1)} %copy-done.1, ...), custom_call_target="tpu_custom_call" | custom-call | flops 805306368 | bytes 5242880 | tf_op jit(solution)/shard_map/product_by_rows/pallas_call | solution.py:70
  173.0 3.9 %collective-permute-start.31 = (bf16[256,256]{1,0:T(8,128)(2,1)S(1)}, bf16[256,256]{1,0:T(8,128)(2,1)}, u32[]{:S(2)}, u32[]{:S(2)}) collective-permute-start(bf16[256,256]{1,0:T(8,128)(2,1)S(1)} %get-tuple-element.83), channel_id=1, source_target_pairs={{0,24},{8,0},{16,8},{24,16},{1,25},{9,1},{17,9},{25,17},{2,26},{10... | collective-permute-start | bytes 393224 | tf_op jit(solution)/shard_map/ppermute | solution.py:244
  177.9 5.6 %collective-permute-done.34 = f32[256,256]{1,0:T(8,128)} collective-permute-done((f32[256,256]{1,0:T(8,128)}, f32[256,256]{1,0:T(8,128)}, u32[]{:S(2)}, u32[]{:S(2)}) %collective-permute-start.34) | collective-permute-done | bytes 262176 | tf_op jit(solution)/shard_map/ppermute | solution.py:333
  183.6 2.8 %collective-permute-done.29 = bf16[256,256]{1,0:T(8,128)(2,1)} collective-permute-done((bf16[256,256]{1,0:T(8,128)(2,1)}, bf16[256,256]{1,0:T(8,128)(2,1)}, u32[]{:S(2)}, u32[]{:S(2)}) %collective-permute-start.29) | collective-permute-done | bytes 131104 | tf_op jit(solution)/shard_map/ppermute | solution.py:244
  186.4 2.3 %collective-permute-done.30 = bf16[256,256]{1,0:T(8,128)(2,1)} collective-permute-done((bf16[256,256]{1,0:T(8,128)(2,1)}, bf16[256,256]{1,0:T(8,128)(2,1)}, u32[]{:S(2)}, u32[]{:S(2)}) %collective-permute-start.30) | collective-permute-done | bytes 131104 | tf_op jit(solution)/shard_map/ppermute | solution.py:244
  188.7 1.3 collective-permute-done.31
  190.0 3.1 %add_bitcast_fusion = (f32[1,1,256,256]{3,2,1,0:T(8,128)}, bf16[256,256]{1,0:T(8,128)(2,1)}) fusion(f32[256]{0:T(256)S(1)} %bitcast.42, f32[256]{0:T(256)S(1)} %broadcast_multiply_fusion.2, f32[256]{0:T(256)S(1)} %bitcast.46, bf16[256,256]{1,0:T(8,128)(2,1)} %collective-permute-done.31, bf16[256,256]{1,0:T(8,128)(2,1)} %collective-permute-done.30, ...), kind=kLoop, calls=%fused_computation.90 | loop fusion | flops 4587520 | bytes 2362371 | tf_op jit(solution)/shard_map/broadcast_in_dim | solution.py:337
  (76 shorter events, 8.6 us)
Async XLA Ops:
  0.6 32.0 %copy-start.14 = (f32[1,1,256]{2,1,0:T(1,128)S(1)}, f32[1,1,256]{2,1,0:T(1,128)}, u32[]{:S(2)}) copy-start(f32[1,1,256]{2,1,0:T(1,128)} %coef_a.1) | copy-start | bytes 3076
  0.6 32.0 %copy-start.13 = (f32[1,1,256]{2,1,0:T(1,128)S(1)}, f32[1,1,256]{2,1,0:T(1,128)}, u32[]{:S(2)}) copy-start(f32[1,1,256]{2,1,0:T(1,128)} %coef_b.1) | copy-start | bytes 3076
  0.7 32.0 %copy-start.15 = (f32[1,1,256]{2,1,0:T(1,128)S(1)}, f32[1,1,256]{2,1,0:T(1,128)}, u32[]{:S(2)}) copy-start(f32[1,1,256]{2,1,0:T(1,128)} %sigma.1) | copy-start | bytes 3076
  0.7 34.0 %copy-start.12 = (s32[1,1,3]{2,1,0:T(1,128)S(1)}, s32[1,1,3]{2,1,0:T(1,128)}, u32[]{:S(2)}) copy-start(s32[1,1,3]{2,1,0:T(1,128)} %picks.11) | copy-start | bytes 40
  0.7 15.1 %collective-permute-start.8 = (bf16[1024,256]{1,0:T(8,128)(2,1)}, bf16[1024,256]{1,0:T(8,128)(2,1)}, u32[]{:S(2)}, u32[]{:S(2)}) collective-permute-start(bf16[1024,256]{1,0:T(8,128)(2,1)} %bitcast.30), channel_id=1, source_target_pairs={{0,8},{8,16},{16,24},{1,9},{9,17},{17,25},{2,10},{10,18},{18,26},{... | collective-permute-start | bytes 1572872 | tf_op jit(solution)/shard_map/ppermute | solution.py:288
  5.1 12.8 %collective-permute-start = (bf16[1024,256]{1,0:T(8,128)(2,1)}, bf16[1024,256]{1,0:T(8,128)(2,1)S(1)}, u32[]{:S(2)}, u32[]{:S(2)}) collective-permute-start(bf16[1024,256]{1,0:T(8,128)(2,1)} %bitcast.31), channel_id=1, source_target_pairs={{0,1},{1,2},{2,3},{3,4},{4,5},{5,6},{6,7},{8,9},{9,10},{10,11},{11... | collective-permute-start | bytes 1572872 | tf_op jit(solution)/shard_map/ppermute | solution.py:27
  7.0 13.5 %collective-permute-start.1 = (bf16[1024,256]{1,0:T(8,128)(2,1)}, bf16[1024,256]{1,0:T(8,128)(2,1)S(1)}, u32[]{:S(2)}, u32[]{:S(2)}) collective-permute-start(bf16[1024,256]{1,0:T(8,128)(2,1)} %bitcast.32), channel_id=1, source_target_pairs={{1,0},{2,1},{3,2},{4,3},{5,4},{6,5},{7,6},{9,8},{10,9},{11,10},{12... | collective-permute-start | bytes 1572872 | tf_op jit(solution)/shard_map/ppermute | solution.py:27
  15.8 17.6 %collective-permute-start.10 = (bf16[1024,256]{1,0:T(8,128)(2,1)}, bf16[1024,256]{1,0:T(8,128)(2,1)S(1)}, u32[]{:S(2)}, u32[]{:S(2)}) collective-permute-start(bf16[1024,256]{1,0:T(8,128)(2,1)} %collective-permute-done.8.own), channel_id=1, source_target_pairs={{9,8},{10,9},{11,10},{12,11},{13,12},{14,13},{15,14},{17,16},{18,1... | collective-permute-start | bytes 1572872 | tf_op jit(solution)/shard_map/ppermute | solution.py:27
  16.5 18.2 %collective-permute-start.9 = (bf16[1024,256]{1,0:T(8,128)(2,1)}, bf16[1024,256]{1,0:T(8,128)(2,1)S(1)}, u32[]{:S(2)}, u32[]{:S(2)}) collective-permute-start(bf16[1024,256]{1,0:T(8,128)(2,1)} %collective-permute-done.8.own), channel_id=1, source_target_pairs={{8,9},{9,10},{10,11},{11,12},{12,13},{13,14},{14,15},{16,17},{17,1... | collective-permute-start | bytes 1572872 | tf_op jit(solution)/shard_map/ppermute | solution.py:27
  20.6 1.9 copy-start
  22.4 1.0 copy-start.3
  23.5 0.7 copy-start.11
  24.1 8.5 %copy-start.5 = (f32[1,1,256,256]{3,2,1,0:T(8,128)S(1)}, f32[1,1,256,256]{3,2,1,0:T(8,128)}, u32[]{:S(2)}) copy-start(f32[1,1,256,256]{3,2,1,0:T(8,128)} %state.1) | copy-start | bytes 786436
  24.1 10.5 %copy-start.1 = (bf16[1,1024,1536]{2,1,0:T(8,128)(2,1)S(1)}, bf16[1,1024,1536]{2,1,0:T(8,128)(2,1)}, u32[]{:S(2)}) copy-start(bf16[1,1024,1536]{2,1,0:T(8,128)(2,1)} %tile.11) | copy-start | bytes 9437188
  24.1 10.5 %copy-start.2 = (f32[1,1,256,256]{3,2,1,0:T(8,128)S(1)}, f32[1,1,256,256]{3,2,1,0:T(8,128)}, u32[]{:S(2)}) copy-start(f32[1,1,256,256]{3,2,1,0:T(8,128)} %stress.7) | copy-start | bytes 786436
  25.8 10.8 %collective-permute-start.2 = (bf16[256,256]{1,0:T(8,128)(2,1)S(1)}, bf16[256,256]{1,0:T(8,128)(2,1)S(1)}, u32[]{:S(2)}, u32[]{:S(2)}) collective-permute-start(bf16[256,256]{1,0:T(8,128)(2,1)S(1)} %get-tuple-element.70), channel_id=1, source_target_pairs={{0,8},{8,16},{16,24},{24,0},{1,9},{9,17},{17,25},{25,1},{2,10},{10... | collective-permute-start | bytes 393224 | tf_op jit(solution)/shard_map/ppermute | solution.py:244
  28.7 12.1 %collective-permute-start.3 = (bf16[256,256]{1,0:T(8,128)(2,1)S(1)}, bf16[256,256]{1,0:T(8,128)(2,1)S(1)}, u32[]{:S(2)}, u32[]{:S(2)}) collective-permute-start(bf16[256,256]{1,0:T(8,128)(2,1)S(1)} %get-tuple-element.71), channel_id=1, source_target_pairs={{0,16},{8,24},{16,0},{24,8},{1,17},{9,25},{17,1},{25,9},{2,18},{10... | collective-permute-start | bytes 393224 | tf_op jit(solution)/shard_map/ppermute | solution.py:244
  31.2 9.5 %collective-permute-start.4 = (bf16[256,256]{1,0:T(8,128)(2,1)S(1)}, bf16[256,256]{1,0:T(8,128)(2,1)S(1)}, u32[]{:S(2)}, u32[]{:S(2)}) collective-permute-start(bf16[256,256]{1,0:T(8,128)(2,1)S(1)} %get-tuple-element.72), channel_id=1, source_target_pairs={{0,24},{8,0},{16,8},{24,16},{1,25},{9,1},{17,9},{25,17},{2,26},{10... | collective-permute-start | bytes 393224 | tf_op jit(solution)/shard_map/ppermute | solution.py:244
  33.4 46.6 %collective-permute-start.15 = (f32[264,256]{1,0:T(8,128)}, f32[264,256]{1,0:T(8,128)S(1)}, u32[]{:S(2)}, u32[]{:S(2)}) collective-permute-start(f32[264,256]{1,0:T(8,128)} %pack.1.refs_0_), channel_id=1, source_target_pairs={{8,0},{9,1},{10,2},{11,3},{12,4},{13,5},{14,6},{15,7}} | collective-permute-start | bytes 811016 | tf_op jit(solution)/shard_map/ppermute | solution.py:287
  35.3 46.7 %collective-permute-start.11 = (bf16[1024,256]{1,0:T(8,128)(2,1)S(1)}, bf16[1024,256]{1,0:T(8,128)(2,1)S(1)}, u32[]{:S(2)}, u32[]{:S(2)}) collective-permute-start(bf16[1024,256]{1,0:T(8,128)(2,1)S(1)} %block_product.4), channel_id=1, source_target_pairs={{8,0},{24,16},{9,1},{25,17},{10,2},{26,18},{11,3},{27,19},{12,4},{... | collective-permute-start | bytes 1572872 | tf_op jit(solution)/shard_map/ppermute | solution.py:257
  41.8 13.4 %collective-permute-start.5 = (bf16[256,256]{1,0:T(8,128)(2,1)S(1)}, bf16[256,256]{1,0:T(8,128)(2,1)S(1)}, u32[]{:S(2)}, u32[]{:S(2)}) collective-permute-start(bf16[256,256]{1,0:T(8,128)(2,1)S(1)} %fusion.61.refs_0_), channel_id=1, source_target_pairs={{0,8},{8,16},{16,24},{24,0},{1,9},{9,17},{17,25},{25,1},{2,10},{10... | collective-permute-start | bytes 393224 | tf_op jit(solution)/shard_map/ppermute | solution.py:294
  45.1 12.9 %collective-permute-start.6 = (bf16[256,256]{1,0:T(8,128)(2,1)S(1)}, bf16[256,256]{1,0:T(8,128)(2,1)S(1)}, u32[]{:S(2)}, u32[]{:S(2)}) collective-permute-start(bf16[256,256]{1,0:T(8,128)(2,1)S(1)} %fusion.61.refs_0_), channel_id=1, source_target_pairs={{0,16},{8,24},{16,0},{24,8},{1,17},{9,25},{17,1},{25,9},{2,18},{10... | collective-permute-start | bytes 393224 | tf_op jit(solution)/shard_map/ppermute | solution.py:294
  46.9 30.8 %collective-permute-start.7 = (bf16[256,256]{1,0:T(8,128)(2,1)S(1)}, bf16[256,256]{1,0:T(8,128)(2,1)S(1)}, u32[]{:S(2)}, u32[]{:S(2)}) collective-permute-start(bf16[256,256]{1,0:T(8,128)(2,1)S(1)} %fusion.61.refs_0_), channel_id=1, source_target_pairs={{0,24},{8,0},{16,8},{24,16},{1,25},{9,1},{17,9},{25,17},{2,26},{10... | collective-permute-start | bytes 393224 | tf_op jit(solution)/shard_map/ppermute | solution.py:294
  55.2 31.4 %collective-permute-start.16 = (f32[264,256]{1,0:T(8,128)}, f32[264,256]{1,0:T(8,128)S(1)}, u32[]{:S(2)}, u32[]{:S(2)}) collective-permute-start(f32[264,256]{1,0:T(8,128)} %pack.1.refs_0_), channel_id=1, source_target_pairs={{16,0},{17,1},{18,2},{19,3},{20,4},{21,5},{22,6},{23,7}} | collective-permute-start | bytes 811016 | tf_op jit(solution)/shard_map/ppermute | solution.py:287
  58.0 30.6 %collective-permute-start.17 = (f32[264,256]{1,0:T(8,128)}, f32[264,256]{1,0:T(8,128)}, u32[]{:S(2)}, u32[]{:S(2)}) collective-permute-start(f32[264,256]{1,0:T(8,128)} %pack.1.refs_0_), channel_id=1, source_target_pairs={{24,0},{25,1},{26,2},{27,3},{28,4},{29,5},{30,6},{31,7}} | collective-permute-start | bytes 811016 | tf_op jit(solution)/shard_map/ppermute | solution.py:287
  77.7 14.0 %collective-permute-start.18 = (bf16[1024,256]{1,0:T(8,128)(2,1)}, bf16[1024,256]{1,0:T(8,128)(2,1)}, u32[]{:S(2)}, u32[]{:S(2)}) collective-permute-start(bf16[1024,256]{1,0:T(8,128)(2,1)} %collective-permute-done.8.own), channel_id=1, source_target_pairs={{8,16},{16,24},{9,17},{17,25},{10,18},{18,26},{11,19},{19,27},{12,... | collective-permute-start | bytes 1572872 | tf_op jit(solution)/shard_map/ppermute | solution.py:299
  80.0 6.6 %copy-start.6 = (f32[264,256]{1,0:T(8,128)}, f32[264,256]{1,0:T(8,128)S(1)}, u32[]{:S(2)}) copy-start(f32[264,256]{1,0:T(8,128)S(1)} %collective-permute-done.15.refs_1_) | copy-start | bytes 811012
  80.0 14.6 %collective-permute-start.12 = (bf16[1024,256]{1,0:T(8,128)(2,1)}, bf16[1024,256]{1,0:T(8,128)(2,1)}, u32[]{:S(2)}, u32[]{:S(2)}) collective-permute-start(bf16[1024,256]{1,0:T(8,128)(2,1)} %assemble.1.own), channel_id=1, source_target_pairs={{0,1},{1,2},{2,3},{3,4},{4,5},{5,6},{6,7},{8,9},{9,10},{10,11},{11... | collective-permute-start | bytes 1572872 | tf_op jit(solution)/shard_map/ppermute | solution.py:27
  82.0 4.6 %copy-start.20 = (bf16[1024,256]{1,0:T(8,128)(2,1)}, bf16[1024,256]{1,0:T(8,128)(2,1)S(1)}, u32[]{:S(2)}) copy-start(bf16[1024,256]{1,0:T(8,128)(2,1)S(1)} %collective-permute-done.11) | copy-start | bytes 1572868
  82.0 13.5 %collective-permute-start.13 = (bf16[1024,256]{1,0:T(8,128)(2,1)}, bf16[1024,256]{1,0:T(8,128)(2,1)}, u32[]{:S(2)}, u32[]{:S(2)}) collective-permute-start(bf16[1024,256]{1,0:T(8,128)(2,1)} %assemble.1.own), channel_id=1, source_target_pairs={{1,0},{2,1},{3,2},{4,3},{5,4},{6,5},{7,6},{9,8},{10,9},{11,10},{12... | collective-permute-start | bytes 1572872 | tf_op jit(solution)/shard_map/ppermute | solution.py:27
  86.6 0.7 copy-start.8
  87.3 16.8 %collective-permute-start.14 = (bf16[1024,256]{1,0:T(8,128)(2,1)}, bf16[1024,256]{1,0:T(8,128)(2,1)}, u32[]{:S(2)}, u32[]{:S(2)}) collective-permute-start(bf16[1024,256]{1,0:T(8,128)(2,1)} %add_convert_fusion), channel_id=1, source_target_pairs={{16,0},{17,1},{18,2},{19,3},{20,4},{21,5},{22,6},{23,7}} | collective-permute-start | bytes 1572872 | tf_op jit(solution)/shard_map/ppermute | solution.py:257
  88.6 1.0 copy-start.7
  89.5 1.0 copy-start.9
  90.5 13.6 %copy-start.21 = (bf16[1024,256]{1,0:T(8,128)(2,1)S(1)}, bf16[1024,256]{1,0:T(8,128)(2,1)}, u32[]{:S(2)}) copy-start(bf16[1024,256]{1,0:T(8,128)(2,1)} %copy-done.20) | copy-start | bytes 1572868
  91.7 25.6 %collective-permute-start.20 = (bf16[1024,256]{1,0:T(8,128)(2,1)}, bf16[1024,256]{1,0:T(8,128)(2,1)}, u32[]{:S(2)}, u32[]{:S(2)}) collective-permute-start(bf16[1024,256]{1,0:T(8,128)(2,1)} %collective-permute-done.18.own), channel_id=1, source_target_pairs={{16,17},{17,18},{18,19},{19,20},{20,21},{21,22},{22,23},{24,25},{2... | collective-permute-start | bytes 1572872 | tf_op jit(solution)/shard_map/ppermute | solution.py:27
  93.1 27.8 %collective-permute-start.21 = (bf16[1024,256]{1,0:T(8,128)(2,1)}, bf16[1024,256]{1,0:T(8,128)(2,1)}, u32[]{:S(2)}, u32[]{:S(2)}) collective-permute-start(bf16[1024,256]{1,0:T(8,128)(2,1)} %collective-permute-done.18.own), channel_id=1, source_target_pairs={{17,16},{18,17},{19,18},{20,19},{21,20},{22,21},{23,22},{25,24},{2... | collective-permute-start | bytes 1572872 | tf_op jit(solution)/shard_map/ppermute | solution.py:27
  98.3 5.8 %copy-start.16 = (bf16[1024,256]{1,0:T(8,128)(2,1)}, bf16[1024,256]{1,0:T(8,128)(2,1)S(1)}, u32[]{:S(2)}) copy-start(bf16[1024,256]{1,0:T(8,128)(2,1)S(1)} %get-tuple-element.77) | copy-start | bytes 1572868
  111.3 9.7 %copy-start.18 = (f32[1024,256]{1,0:T(8,128)}, f32[1024,256]{1,0:T(8,128)S(1)}, u32[]{:S(2)}) copy-start(f32[1024,256]{1,0:T(8,128)S(1)} %get-tuple-element.78) | copy-start | bytes 3145732
  112.7 11.9 %collective-permute-start.19 = (bf16[1024,256]{1,0:T(8,128)(2,1)S(1)}, bf16[1024,256]{1,0:T(8,128)(2,1)S(1)}, u32[]{:S(2)}, u32[]{:S(2)}) collective-permute-start(bf16[1024,256]{1,0:T(8,128)(2,1)S(1)} %broadcast_select_fusion.1), channel_id=1, source_target_pairs={{0,8},{16,24},{1,9},{17,25},{2,10},{18,26},{3,11},{19,27},{4,12},{... | collective-permute-start | bytes 1572872 | tf_op jit(solution)/shard_map/ppermute | solution.py:326
  114.1 37.4 %collective-permute-start.26 = (bf16[1024,256]{1,0:T(8,128)(2,1)}, bf16[1024,256]{1,0:T(8,128)(2,1)S(1)}, u32[]{:S(2)}, u32[]{:S(2)}) collective-permute-start(bf16[1024,256]{1,0:T(8,128)(2,1)} %copy-done.16), channel_id=1, source_target_pairs={{8,0},{9,1},{10,2},{11,3},{12,4},{13,5},{14,6},{15,7}} | collective-permute-start | bytes 1572872 | tf_op jit(solution)/shard_map/ppermute | solution.py:307
  115.4 10.7 %collective-permute-start.23 = (bf16[1024,256]{1,0:T(8,128)(2,1)}, bf16[1024,256]{1,0:T(8,128)(2,1)S(1)}, u32[]{:S(2)}, u32[]{:S(2)}) collective-permute-start(bf16[1024,256]{1,0:T(8,128)(2,1)} %get-tuple-element.76.own), channel_id=1, source_target_pairs={{0,1},{1,2},{2,3},{3,4},{4,5},{5,6},{6,7}} | collective-permute-start | bytes 1572872 | tf_op jit(solution)/shard_map/ppermute | solution.py:27
  117.3 12.4 %collective-permute-start.24 = (bf16[1024,256]{1,0:T(8,128)(2,1)}, bf16[1024,256]{1,0:T(8,128)(2,1)S(1)}, u32[]{:S(2)}, u32[]{:S(2)}) collective-permute-start(bf16[1024,256]{1,0:T(8,128)(2,1)} %get-tuple-element.76.own), channel_id=1, source_target_pairs={{1,0},{2,1},{3,2},{4,3},{5,4},{6,5},{7,6}} | collective-permute-start | bytes 1572872 | tf_op jit(solution)/shard_map/ppermute | solution.py:27
  121.6 29.9 %collective-permute-start.22 = (bf16[1024,256]{1,0:T(8,128)(2,1)S(1)}, bf16[1024,256]{1,0:T(8,128)(2,1)S(1)}, u32[]{:S(2)}, u32[]{:S(2)}) collective-permute-start(bf16[1024,256]{1,0:T(8,128)(2,1)S(1)} %block_product.6), channel_id=1, source_target_pairs={{16,0},{17,1},{18,2},{19,3},{20,4},{21,5},{22,6},{23,7}} | collective-permute-start | bytes 1572872 | tf_op jit(solution)/shard_map/ppermute | solution.py:303
  124.7 26.8 %collective-permute-start.25 = (bf16[1024,256]{1,0:T(8,128)(2,1)S(1)}, bf16[1024,256]{1,0:T(8,128)(2,1)S(1)}, u32[]{:S(2)}, u32[]{:S(2)}) collective-permute-start(bf16[1024,256]{1,0:T(8,128)(2,1)S(1)} %block_product.6), channel_id=1, source_target_pairs={{24,0},{25,1},{26,2},{27,3},{28,4},{29,5},{30,6},{31,7}} | collective-permute-start | bytes 1572872 | tf_op jit(solution)/shard_map/ppermute | solution.py:303
  157.7 11.8 %copy-start.17 = (f32[1024,256]{1,0:T(8,128)}, f32[1024,256]{1,0:T(8,128)S(1)}, u32[]{:S(2)}) copy-start(f32[1024,256]{1,0:T(8,128)S(1)} %get-tuple-element.84) | copy-start | bytes 3145732
  157.7 11.8 %copy-start.19 = (bf16[1024,256]{1,0:T(8,128)(2,1)}, bf16[1024,256]{1,0:T(8,128)(2,1)S(1)}, u32[]{:S(2)}) copy-start(bf16[1024,256]{1,0:T(8,128)(2,1)S(1)} %get-tuple-element.79.own) | copy-start | bytes 1572868
  157.7 11.8 %collective-permute-start.27 = (bf16[1024,256]{1,0:T(8,128)(2,1)S(1)}, bf16[1024,256]{1,0:T(8,128)(2,1)S(1)}, u32[]{:S(2)}, u32[]{:S(2)}) collective-permute-start(bf16[1024,256]{1,0:T(8,128)(2,1)S(1)} %get-tuple-element.79.own), channel_id=1, source_target_pairs={{0,1},{1,2},{2,3},{3,4},{4,5},{5,6},{6,7},{8,9},{9,10},{10,11},{11... | collective-permute-start | bytes 1572872 | tf_op jit(solution)/shard_map/ppermute | solution.py:27
  159.7 10.3 %collective-permute-start.28 = (bf16[1024,256]{1,0:T(8,128)(2,1)S(1)}, bf16[1024,256]{1,0:T(8,128)(2,1)S(1)}, u32[]{:S(2)}, u32[]{:S(2)}) collective-permute-start(bf16[1024,256]{1,0:T(8,128)(2,1)S(1)} %get-tuple-element.79.own), channel_id=1, source_target_pairs={{1,0},{2,1},{3,2},{4,3},{5,4},{6,5},{7,6},{9,8},{10,9},{11,10},{12... | collective-permute-start | bytes 1572872 | tf_op jit(solution)/shard_map/ppermute | solution.py:27
  163.3 13.6 %copy-start.4 = (bf16[1,1024,256]{2,1,0:T(8,128)(2,1)S(1)}, bf16[1,1024,256]{2,1,0:T(8,128)(2,1)}, u32[]{:S(2)}) copy-start(bf16[1,1024,256]{2,1,0:T(8,128)(2,1)} %param.16) | copy-start | bytes 1572868
  164.2 8.8 %collective-permute-start.32 = (f32[256,256]{1,0:T(8,128)S(1)}, f32[256,256]{1,0:T(8,128)S(1)}, u32[]{:S(2)}, u32[]{:S(2)}) collective-permute-start(f32[256,256]{1,0:T(8,128)S(1)} %get-tuple-element.93), channel_id=1, source_target_pairs={{0,24},{1,25},{2,26},{3,27},{4,28},{5,29},{6,30},{7,31}} | collective-permute-start | bytes 786440 | tf_op jit(solution)/shard_map/ppermute | solution.py:333
  165.5 12.5 %collective-permute-start.33 = (f32[256,256]{1,0:T(8,128)}, f32[256,256]{1,0:T(8,128)}, u32[]{:S(2)}, u32[]{:S(2)}) collective-permute-start(f32[256,256]{1,0:T(8,128)} %get-tuple-element.92), channel_id=1, source_target_pairs={{0,16},{1,17},{2,18},{3,19},{4,20},{5,21},{6,22},{7,23}} | collective-permute-start | bytes 786440 | tf_op jit(solution)/shard_map/ppermute | solution.py:333
  167.5 16.1 %collective-permute-start.34 = (f32[256,256]{1,0:T(8,128)}, f32[256,256]{1,0:T(8,128)}, u32[]{:S(2)}, u32[]{:S(2)}) collective-permute-start(f32[256,256]{1,0:T(8,128)} %get-tuple-element.91), channel_id=1, source_target_pairs={{0,8},{1,9},{2,10},{3,11},{4,12},{5,13},{6,14},{7,15}} | collective-permute-start | bytes 786440 | tf_op jit(solution)/shard_map/ppermute | solution.py:333
  172.3 0.7 copy-start.10
  173.0 13.3 %collective-permute-start.29 = (bf16[256,256]{1,0:T(8,128)(2,1)}, bf16[256,256]{1,0:T(8,128)(2,1)}, u32[]{:S(2)}, u32[]{:S(2)}) collective-permute-start(bf16[256,256]{1,0:T(8,128)(2,1)} %get-tuple-element.81), channel_id=1, source_target_pairs={{0,8},{8,16},{16,24},{24,0},{1,9},{9,17},{17,25},{25,1},{2,10},{10... | collective-permute-start | bytes 393224 | tf_op jit(solution)/shard_map/ppermute | solution.py:244
  173.0 15.6 %collective-permute-start.30 = (bf16[256,256]{1,0:T(8,128)(2,1)}, bf16[256,256]{1,0:T(8,128)(2,1)}, u32[]{:S(2)}, u32[]{:S(2)}) collective-permute-start(bf16[256,256]{1,0:T(8,128)(2,1)} %get-tuple-element.82), channel_id=1, source_target_pairs={{0,16},{8,24},{16,0},{24,8},{1,17},{9,25},{17,1},{25,9},{2,18},{10... | collective-permute-start | bytes 393224 | tf_op jit(solution)/shard_map/ppermute | solution.py:244
  173.0 3.9 %copy-start.23 = (f32[256,256]{1,0:T(8,128)}, f32[256,256]{1,0:T(8,128)S(1)}, u32[]{:S(2)}) copy-start(f32[256,256]{1,0:T(8,128)S(1)} %collective-permute-done.32) | copy-start | bytes 786436
  173.0 16.9 %collective-permute-start.31 = (bf16[256,256]{1,0:T(8,128)(2,1)S(1)}, bf16[256,256]{1,0:T(8,128)(2,1)}, u32[]{:S(2)}, u32[]{:S(2)}) collective-permute-start(bf16[256,256]{1,0:T(8,128)(2,1)S(1)} %get-tuple-element.83), channel_id=1, source_target_pairs={{0,24},{8,0},{16,8},{24,16},{1,25},{9,1},{17,9},{25,17},{2,26},{10... | collective-permute-start | bytes 393224 | tf_op jit(solution)/shard_map/ppermute | solution.py:244

commit v13 on v12

--- a/solution.py
+++ b/solution.py
@@ -290,7 +290,7 @@
     traction = scatter_sum(product_by_rows(*local, below, own, above, lags))
     coef_a, coef_b, sigma = (c[0, 0][:, None] for c in (fric_a, fric_b, normal_stress))
     row_pair = (coef_b / coef_a, sigma * coef_a)
-    rates, _ = settle_friction(prestress[0, 0] + traction, log_state[0, 0], *row_pair)
+    rates, row_state = settle_friction(prestress[0, 0] + traction, log_state[0, 0], *row_pair)
     arrived = [lax.ppermute(rates, "lag", [(i, (i + d) % lags) for i in every]) for d in rest]
     first = assemble([rates] + arrived)
     kinds = [jnp.float32, jnp.bfloat16]
@@ -300,7 +300,7 @@
     window_2 = window_of(twice, rest[1:])
     state, *coefs = unpack(packed)
     (low,) = block_product(*local, window_2, prestress, rest[1:], kinds[1:])
-    base_2 = [lax.ppermute(low, "lag", [(d, 0)]) for d in rest[1:]]
+    base_2 = tree_to_first(low, lags, 2)
 
     window = window_of(first, [0, 1])
     high, low = block_product(*local, window, prestress, [0, 1], kinds)
@@ -310,8 +310,7 @@
         return jnp.zeros(first.shape, first.dtype), jnp.zeros(start.shape, start.dtype)
 
     def second_step(high, start, first, ratio, strength, *received):
-        begun = evolved(start, first.astype(jnp.float32))
-        return settle_friction(block_load(high, *received), begun, ratio[:, None], strength[:, None])
+        return settle_friction(block_load(high, *received), start, ratio[:, None], strength[:, None])
 
     def third_step(high, start, ratio, strength, first, moved, *received):
         return settle_friction(block_load(high, *received), start, ratio[:, None], strength[:, None])
@@ -319,7 +318,8 @@
     def last_field(high, start, ratio, strength, first, moved, *received):
         return jnp.where(me == 2, first, moved), jnp.zeros(start.shape, start.dtype)
 
-    second, state = lax.cond(me == 0, second_step, nothing, high, state, first, *coefs, *base_1)
+    begun = lax.optimization_barrier(evolved(state, first.astype(jnp.float32)))
+    second, state = lax.cond(me == 0, second_step, nothing, high, begun, first, *coefs, *base_1)
     window = window_of(second, [0])
     (high,) = block_product(*local, window, prestress, [0], kinds[:1])
     source = jnp.where(me == 0, second, twice)
@@ -328,10 +328,12 @@
     last, state = lax.cond(me == 0, third_step, last_field, *values)
 
     below, own, above = window_of(last, every)
-    mine = state[:rows]
+    change = (state - begun).astype(jnp.bfloat16)
+    mine = change[:rows]
     for d in rest:
-        piece = lax.ppermute(state[d * rows : (d + 1) * rows], "lag", [(0, d)])
+        piece = lax.ppermute(change[d * rows : (d + 1) * rows], "lag", [(0, d)])
         mine = jnp.where(me == d, piece, mine)
+    mine = row_state + mine.astype(jnp.float32)
     traction = scatter_sum(product_by_rows(*local, below, own, above, lags))
     rates, state = settle_friction(prestress[0, 0] + traction, mine, *row_pair)
     return rates[None, None], state[None, None]

time: 195 us -> 178 us (0.913)
  waiting for transfers between devices: 82.7 us -> 57.2 us
  local copies, waits for them, and re-layouts: 7.8 us -> 14.3 us
  other arithmetic: 20.6 us -> 23.7 us
    ppermute x3, waiting for transfers between devices: 27.5 us -> 6.27 us  [shards(): lax.ppermute(rates, 'lag', [(i, (i + d) % lags) for i in every])]
    ppermute x1, waiting for transfers between devices: 18.7 us -> 0.01 us  [shards(): base_2 = base_2 + [lax.ppermute(low, 'lag', [(1, 0)])]]
    ppermute x3, waiting for transfers between devices: 0.01 us -> 12.9 us  [shards(): packed = [packed] + [lax.ppermute(packed, 'lag', [(d, 0)]) for d in rest]]
    unnamed x46 -> x60, local copies, waits for them, and re-layouts: 6.95 us -> 13.6 us
    ppermute x5 -> x3, waiting for transfers between devices: 6.06 us -> 0.01 us  [shards(): piece = lax.ppermute(change[d * rows:(d + 1) * rows], 'lag', [(0, d)])]
    ppermute x1, waiting for transfers between devices: 1.79 us -> 7.68 us  [shards(): lax.ppermute(source, 'lag', [(0, 1)] + [(i, i + 1) for i in every[2:-1]])]
    ppermute x2 -> x4, starting transfers between devices: 2.57 us -> 5.35 us  [tree_to_first(): arrived = lax.ppermute(value, 'lag', route)]
    ppermute x5 -> x3, starting transfers between devices: 7.87 us -> 5.19 us  [shards(): piece = lax.ppermute(change[d * rows:(d + 1) * rows], 'lag', [(0, d)])]
  transfers between devices with their start and end apart: 35 -> 35, of which waited for: 18 -> 13; matrix products, arithmetic and copies ran while one was open for 6% -> 8% of each run, Pallas kernels for 7% -> 8%
where the time goes in v13:
time: 178 us; the launch traced here: 175 us
  starting transfers between devices  64 us (36%)
  waiting for transfers between devices  57.2 us (32%)
  other arithmetic  23.7 us (13%)
  local copies, waits for them, and re-layouts  14.3 us (8%)
  Pallas kernels  14.1 us (8%)
  between operations  1.8 us (1%)
    ppermute x12, starting transfers between devices, exchange(): return (lax.ppermute(value, axes, up), lax.ppermute(value, axes, down))  26.6 us
    unnamed x60, local copies, waits for them, and re-layouts  13.6 us
    add x3, other arithmetic, evolved(): state + time_step * (jnp.exp(-state) - jnp.sqrt(speed_of * speed_of + cre...  13.5 us
    ppermute x3, waiting for transfers between devices, shards(): packed = [packed] + [lax.ppermute(packed, 'lag', [(d, 0)]) for d in rest]  12.9 us
    ppermute x6, waiting for transfers between devices, scatter_sum(): total = total + lax.ppermute(parts[d], 'lag', route).astype(jnp.float32)  11.5 us
    ppermute x6, starting transfers between devices, scatter_sum(): total = total + lax.ppermute(parts[d], 'lag', route).astype(jnp.float32)  11.3 us
    pallas_call x4, Pallas kernels, block_product(): pl.pallas_call(functools.partial(block_kernel, chunks, (planes[0], planes...  8.41 us
    ppermute x1, waiting for transfers between devices, shards(): lax.ppermute(source, 'lag', [(0, 1)] + [(i, i + 1) for i in every[2:-1]])  7.68 us
  transfers between devices with their start and end apart: 35, of which 13 were waited for; matrix products, arithmetic and copies ran while one was open for 8% of the time, Pallas kernels for 8%

profile of v13, /device:TPU:2, one launch (start us, length us, event | category | flops | bytes accessed | tf_op | source)
XLA Modules:
  0.0 175.1 jit_solution(14405826712007823180)
XLA Ops:
  0.7 3.6 %collective-permute-start.8 = (bf16[1024,256]{1,0:T(8,128)(2,1)}, bf16[1024,256]{1,0:T(8,128)(2,1)S(1)}, u32[]{:S(2)}, u32[]{:S(2)}) collective-permute-start(bf16[1024,256]{1,0:T(8,128)(2,1)} %bitcast.42), channel_id=1, source_target_pairs={{0,8},{8,16},{16,24},{1,9},{9,17},{17,25},{2,10},{10,18},{18,26},{... | collective-permute-start | bytes 1572872 | tf_op jit(solution)/shard_map/ppermute | solution.py:288
  4.3 1.9 %collective-permute-start = (bf16[1024,256]{1,0:T(8,128)(2,1)}, bf16[1024,256]{1,0:T(8,128)(2,1)S(1)}, u32[]{:S(2)}, u32[]{:S(2)}) collective-permute-start(bf16[1024,256]{1,0:T(8,128)(2,1)} %bitcast.43), channel_id=1, source_target_pairs={{0,1},{1,2},{2,3},{3,4},{4,5},{5,6},{6,7},{8,9},{9,10},{10,11},{11... | collective-permute-start | bytes 1572872 | tf_op jit(solution)/shard_map/ppermute | solution.py:27
  6.3 3.6 %collective-permute-start.1 = (bf16[1024,256]{1,0:T(8,128)(2,1)}, bf16[1024,256]{1,0:T(8,128)(2,1)S(1)}, u32[]{:S(2)}, u32[]{:S(2)}) collective-permute-start(bf16[1024,256]{1,0:T(8,128)(2,1)} %bitcast.44), channel_id=1, source_target_pairs={{1,0},{2,1},{3,2},{4,3},{5,4},{6,5},{7,6},{9,8},{10,9},{11,10},{12... | collective-permute-start | bytes 1572872 | tf_op jit(solution)/shard_map/ppermute | solution.py:27
  10.6 5.2 %collective-permute-done.8.own = bf16[1024,256]{1,0:T(8,128)(2,1)S(1)} collective-permute-done((bf16[1024,256]{1,0:T(8,128)(2,1)}, bf16[1024,256]{1,0:T(8,128)(2,1)S(1)}, u32[]{:S(2)}, u32[]{:S(2)}) %collective-permute-start.8) | collective-permute-done | bytes 524320 | tf_op jit(solution)/shard_map/ppermute | solution.py:288
  17.9 1.9 %collective-permute-done.1.above = bf16[1024,256]{1,0:T(8,128)(2,1)S(1)} collective-permute-done((bf16[1024,256]{1,0:T(8,128)(2,1)}, bf16[1024,256]{1,0:T(8,128)(2,1)S(1)}, u32[]{:S(2)}, u32[]{:S(2)}) %collective-permute-start.1) | collective-permute-done | bytes 524320 | tf_op jit(solution)/shard_map/ppermute | solution.py:27
  19.8 1.9 %copy-done = bf16[1,1024,1536]{2,1,0:T(8,128)(2,1)S(1)} copy-done((bf16[1,1024,1536]{2,1,0:T(8,128)(2,1)S(1)}, bf16[1,1024,1536]{2,1,0:T(8,128)(2,1)}, u32[]{:S(2)}) %copy-start) | copy-done | bytes 3145752
  21.7 1.0 copy-done.4
  23.4 1.7 product_by_rows.2
  25.1 3.5 %collective-permute-start.2 = (bf16[256,256]{1,0:T(8,128)(2,1)S(1)}, bf16[256,256]{1,0:T(8,128)(2,1)S(1)}, u32[]{:S(2)}, u32[]{:S(2)}) collective-permute-start(bf16[256,256]{1,0:T(8,128)(2,1)S(1)} %get-tuple-element.64), channel_id=1, source_target_pairs={{0,8},{8,16},{16,24},{24,0},{1,9},{9,17},{17,25},{25,1},{2,10},{10... | collective-permute-start | bytes 393224 | tf_op jit(solution)/shard_map/ppermute | solution.py:244
  28.6 2.6 %collective-permute-start.3 = (bf16[256,256]{1,0:T(8,128)(2,1)S(1)}, bf16[256,256]{1,0:T(8,128)(2,1)S(1)}, u32[]{:S(2)}, u32[]{:S(2)}) collective-permute-start(bf16[256,256]{1,0:T(8,128)(2,1)S(1)} %get-tuple-element.65), channel_id=1, source_target_pairs={{0,16},{8,24},{16,0},{24,8},{1,17},{9,25},{17,1},{25,9},{2,18},{10... | collective-permute-start | bytes 393224 | tf_op jit(solution)/shard_map/ppermute | solution.py:244
  31.1 1.3 collective-permute-start.4
  32.6 1.3 collective-permute-start.15
  33.9 1.3 collective-permute-start.16
  35.2 1.4 block_product.4
  36.6 1.3 collective-permute-start.17
  37.9 2.7 %collective-permute-done.3 = bf16[256,256]{1,0:T(8,128)(2,1)S(1)} collective-permute-done((bf16[256,256]{1,0:T(8,128)(2,1)S(1)}, bf16[256,256]{1,0:T(8,128)(2,1)S(1)}, u32[]{:S(2)}, u32[]{:S(2)}) %collective-permute-start.3) | collective-permute-done | bytes 131104 | tf_op jit(solution)/shard_map/ppermute | solution.py:244
  40.6 1.5 collective-permute-start.18
  42.1 1.3 collective-permute-start.11
  43.4 1.7 fusion.70
  45.1 12.9 %collective-permute-done.15.refs_1_ = f32[264,256]{1,0:T(8,128)S(1)} collective-permute-done((f32[264,256]{1,0:T(8,128)S(1)}, f32[264,256]{1,0:T(8,128)S(1)}, u32[]{:S(2)}, u32[]{:S(2)}) %collective-permute-start.15) | collective-permute-done | bytes 270368 | tf_op jit(solution)/shard_map/ppermute | solution.py:287
  60.1 3.8 %collective-permute-start.7 = (bf16[256,256]{1,0:T(8,128)(2,1)S(1)}, bf16[256,256]{1,0:T(8,128)(2,1)}, u32[]{:S(2)}, u32[]{:S(2)}) collective-permute-start(bf16[256,256]{1,0:T(8,128)(2,1)S(1)} %get-tuple-element.85.refs_0_), channel_id=1, source_target_pairs={{0,24},{8,0},{16,8},{24,16},{1,25},{9,1},{17,9},{25,17},{2,26},{10... | collective-permute-start | bytes 393224 | tf_op jit(solution)/shard_map/ppermute | solution.py:294
  63.9 1.5 collective-permute-start.20
  65.4 1.6 collective-permute-done.5.refs_1_
  67.7 1.5 collective-permute-start.21
  69.1 1.0 copy-done.7
  70.1 1.0 copy-done.9
  72.0 1.0 copy-done.13
  73.0 4.7 %collective-permute-done.7.refs_3_ = bf16[256,256]{1,0:T(8,128)(2,1)} collective-permute-done((bf16[256,256]{1,0:T(8,128)(2,1)S(1)}, bf16[256,256]{1,0:T(8,128)(2,1)}, u32[]{:S(2)}, u32[]{:S(2)}) %collective-permute-start.7) | collective-permute-done | bytes 131104 | tf_op jit(solution)/shard_map/ppermute | solution.py:294
  78.6 1.0 assemble.1.own
  79.6 2.0 %collective-permute-start.12 = (bf16[1024,256]{1,0:T(8,128)(2,1)S(1)}, bf16[1024,256]{1,0:T(8,128)(2,1)S(1)}, u32[]{:S(2)}, u32[]{:S(2)}) collective-permute-start(bf16[1024,256]{1,0:T(8,128)(2,1)S(1)} %assemble.1.own), channel_id=1, source_target_pairs={{0,1},{1,2},{2,3},{3,4},{4,5},{5,6},{6,7},{8,9},{9,10},{10,11},{11... | collective-permute-start | bytes 1572872 | tf_op jit(solution)/shard_map/ppermute | solution.py:27
  81.6 3.6 %collective-permute-start.13 = (bf16[1024,256]{1,0:T(8,128)(2,1)S(1)}, bf16[1024,256]{1,0:T(8,128)(2,1)S(1)}, u32[]{:S(2)}, u32[]{:S(2)}) collective-permute-start(bf16[1024,256]{1,0:T(8,128)(2,1)S(1)} %assemble.1.own), channel_id=1, source_target_pairs={{1,0},{2,1},{3,2},{4,3},{5,4},{6,5},{7,6},{9,8},{10,9},{11,10},{12... | collective-permute-start | bytes 1572872 | tf_op jit(solution)/shard_map/ppermute | solution.py:27
  85.2 1.3 add_convert_fusion.1
  86.5 1.3 collective-permute-start.14
  87.9 1.4 block_product.6
  89.3 1.5 collective-permute-start.22
  91.3 3.4 %collective-permute-done.13.above = bf16[1024,256]{1,0:T(8,128)(2,1)S(1)} collective-permute-done((bf16[1024,256]{1,0:T(8,128)(2,1)S(1)}, bf16[1024,256]{1,0:T(8,128)(2,1)S(1)}, u32[]{:S(2)}, u32[]{:S(2)}) %collective-permute-start.13) | collective-permute-done | bytes 524320 | tf_op jit(solution)/shard_map/ppermute | solution.py:27
  94.8 2.7 %block_product.5 = (f32[1024,256]{1,0:T(8,128)S(1)}, bf16[1024,256]{1,0:T(8,128)(2,1)}) custom-call(s32[1,1,3]{2,1,0:T(1,128)S(1)} %copy-done.18, s32[1]{0:T(128)S(6)} %copy.19.live, bf16[1,1024,1536]{2,1,0:T(8,128)(2,1)S(1)} %copy-done.1, bf16[1024,256]{1,0:T(8,128)(2,1)S(1)} %collective-permute-done.12.below, bf16[1024,256]{1,0:T(8,128)(2,1)S(1)} %assemble.1.own, ...), custom_call_target="tpu_custom_call" | custom-call | flops 805306368 | bytes 5242880 | tf_op jit(solution)/shard_map/block_product/pallas_call | solution.py:122
  97.5 1.3 collective-permute-start.26
  98.8 4.3 %collective-permute-done.14 = bf16[1024,256]{1,0:T(8,128)(2,1)S(1)} collective-permute-done((bf16[1024,256]{1,0:T(8,128)(2,1)S(1)}, bf16[1024,256]{1,0:T(8,128)(2,1)S(1)}, u32[]{:S(2)}, u32[]{:S(2)}) %collective-permute-start.14) | collective-permute-done | bytes 524320 | tf_op jit(solution)/shard_map/ppermute | solution.py:257
  103.0 6.1 %conditional.2 = (bf16[1024,256]{1,0:T(8,128)(2,1)S(1)}, f32[1024,256]{1,0:T(8,128)S(1)}) conditional(s32[]{:T(128)} %convert_element_type.73, () %tuple.24, (bf16[1024,256]{1,0:T(8,128)(2,1)}, f32[1024,256]{1,0:T(8,128)S(1)}, bf16[1024,256]{1,0:T(8,128)(2,1)S(1)}, f32[4,1,256]{2,1,0:T(1,128)S(1)}, f32[1024,256]{1,0:T(8,128)S(1)}, ...), branch_computations={%region_0.1_spmd, %region_1.2_spmd} | conditional | flops 16778240 | bytes 4739088 | solution.py:322
  103.1 6.1 %multiply_add_fusion = (f32[1024,256]{1,0:T(8,128)S(1)}, bf16[1024,256]{1,0:T(8,128)(2,1)S(1)}) fusion(f32[1024,256]{1,0:T(8,128)S(1)} %get-tuple-element.34, f32[1024]{0:T(1024)S(1)} %bitcast.49, f32[1024]{0:T(1024)S(1)} %broadcast_multiply_fusion, f32[1024]{0:T(1024)S(1)} %bitcast.52, bf16[1024,256]{1,0:T(8,128)(2,1)S(1)} %get-tuple-element.32, ...), kind=kLoop, calls=%fused_computation.18 | loop fusion | flops 16777216 | bytes 4730880 | tf_op jit(solution)/shard_map/cond/branch_1_fun/add | solution.py:236
  109.2 1.9 %collective-permute-start.24 = (bf16[1024,256]{1,0:T(8,128)(2,1)S(1)}, bf16[1024,256]{1,0:T(8,128)(2,1)S(1)}, u32[]{:S(2)}, u32[]{:S(2)}) collective-permute-start(bf16[1024,256]{1,0:T(8,128)(2,1)S(1)} %get-tuple-element.70.own), channel_id=1, source_target_pairs={{0,1},{1,2},{2,3},{3,4},{4,5},{5,6},{6,7}} | collective-permute-start | bytes 1572872 | tf_op jit(solution)/shard_map/ppermute | solution.py:27
  111.1 3.6 %collective-permute-start.25 = (bf16[1024,256]{1,0:T(8,128)(2,1)S(1)}, bf16[1024,256]{1,0:T(8,128)(2,1)S(1)}, u32[]{:S(2)}, u32[]{:S(2)}) collective-permute-start(bf16[1024,256]{1,0:T(8,128)(2,1)S(1)} %get-tuple-element.70.own), channel_id=1, source_target_pairs={{1,0},{2,1},{3,2},{4,3},{5,4},{6,5},{7,6}} | collective-permute-start | bytes 1572872 | tf_op jit(solution)/shard_map/ppermute | solution.py:27
  114.8 1.5 collective-permute-start.19
  116.3 1.3 add_convert_fusion
  117.7 1.3 collective-permute-start.23
  119.0 7.7 %collective-permute-done.19 = bf16[1024,256]{1,0:T(8,128)(2,1)S(1)} collective-permute-done((bf16[1024,256]{1,0:T(8,128)(2,1)S(1)}, bf16[1024,256]{1,0:T(8,128)(2,1)S(1)}, u32[]{:S(2)}, u32[]{:S(2)}) %collective-permute-start.19) | collective-permute-done | bytes 524320 | tf_op jit(solution)/shard_map/ppermute | solution.py:326
  127.5 2.9 %block_product.7 = f32[1024,256]{1,0:T(8,128)} custom-call(s32[1,1,3]{2,1,0:T(1,128)S(1)} %copy-done.18, s32[1]{0:T(128)S(6)} %copy.19.live, bf16[1,1024,1536]{2,1,0:T(8,128)(2,1)S(1)} %copy-done.1, bf16[1024,256]{1,0:T(8,128)(2,1)S(1)} %collective-permute-done.24.below, bf16[1024,256]{1,0:T(8,128)(2,1)} %copy-done.24, ...), custom_call_target="tpu_custom_call" | custom-call | flops 805306368 | bytes 5242880 | tf_op jit(solution)/shard_map/block_product/pallas_call | solution.py:122
  130.4 2.8 %collective-permute-done.23 = bf16[1024,256]{1,0:T(8,128)(2,1)S(1)} collective-permute-done((bf16[1024,256]{1,0:T(8,128)(2,1)S(1)}, bf16[1024,256]{1,0:T(8,128)(2,1)S(1)}, u32[]{:S(2)}, u32[]{:S(2)}) %collective-permute-start.23) | collective-permute-done | bytes 524320 | tf_op jit(solution)/shard_map/ppermute | solution.py:257
  133.2 6.9 %conditional.3 = (bf16[1024,256]{1,0:T(8,128)(2,1)}, f32[1024,256]{1,0:T(8,128)S(1)}) conditional(s32[]{:T(128)} %convert_element_type.73, (s32[]{:T(128)}, bf16[1024,256]{1,0:T(8,128)(2,1)}, bf16[1024,256]{1,0:T(8,128)(2,1)}) %tuple.46, (bf16[1024,256]{1,0:T(8,128)(2,1)S(1)}, f32[1024,256]{1,0:T(8,128)}, bf16[1024,256]{1,0:T(8,128)(2,1)}, ...), branch_computations={%region_2.3_spmd, %region_3.4_spmd} | conditional | flops 16778240 | bytes 4739088 | solution.py:328
  133.2 6.9 %multiply_add_fusion.1 = (f32[1024,256]{1,0:T(8,128)S(1)}, bf16[1024,256]{1,0:T(8,128)(2,1)}) fusion(f32[1024,256]{1,0:T(8,128)} %get-tuple-element.43, f32[1024]{0:T(1024)S(1)} %bitcast.51, f32[1024]{0:T(1024)S(1)} %broadcast_multiply_fusion.1, f32[1024]{0:T(1024)S(1)} %bitcast.53, bf16[1024,256]{1,0:T(8,128)(2,1)} %get-tuple-element.41, ...), kind=kLoop, calls=%fused_computation.42 | loop fusion | flops 16777216 | bytes 4730880 | tf_op jit(solution)/shard_map/cond/branch_1_fun/add | solution.py:236
  140.2 1.0 copy-done.25
  141.1 1.9 %collective-permute-start.27 = (bf16[1024,256]{1,0:T(8,128)(2,1)}, bf16[1024,256]{1,0:T(8,128)(2,1)S(1)}, u32[]{:S(2)}, u32[]{:S(2)}) collective-permute-start(bf16[1024,256]{1,0:T(8,128)(2,1)} %get-tuple-element.73.own), channel_id=1, source_target_pairs={{0,1},{1,2},{2,3},{3,4},{4,5},{5,6},{6,7},{8,9},{9,10},{10,11},{11... | collective-permute-start | bytes 1572872 | tf_op jit(solution)/shard_map/ppermute | solution.py:27
  143.0 3.6 %collective-permute-start.28 = (bf16[1024,256]{1,0:T(8,128)(2,1)}, bf16[1024,256]{1,0:T(8,128)(2,1)S(1)}, u32[]{:S(2)}, u32[]{:S(2)}) collective-permute-start(bf16[1024,256]{1,0:T(8,128)(2,1)} %get-tuple-element.73.own), channel_id=1, source_target_pairs={{1,0},{2,1},{3,2},{4,3},{5,4},{6,5},{7,6},{9,8},{10,9},{11,10},{12... | collective-permute-start | bytes 1572872 | tf_op jit(solution)/shard_map/ppermute | solution.py:27
  146.7 1.7 subtract_convert_fusion
  149.1 1.3 collective-permute-start.32
  150.4 2.0 %collective-permute-start.33 = (bf16[256,256]{1,0:T(8,128)(2,1)}, bf16[256,256]{1,0:T(8,128)(2,1)}, u32[]{:S(2)}, u32[]{:S(2)}) collective-permute-start(bf16[256,256]{1,0:T(8,128)(2,1)} %get-tuple-element.88), channel_id=1, source_target_pairs={{0,16},{1,17},{2,18},{3,19},{4,20},{5,21},{6,22},{7,23}} | collective-permute-start | bytes 393224 | tf_op jit(solution)/shard_map/ppermute | solution.py:334
  152.4 1.9 %collective-permute-start.34 = (bf16[256,256]{1,0:T(8,128)(2,1)}, bf16[256,256]{1,0:T(8,128)(2,1)}, u32[]{:S(2)}, u32[]{:S(2)}) collective-permute-start(bf16[256,256]{1,0:T(8,128)(2,1)} %get-tuple-element.87), channel_id=1, source_target_pairs={{0,8},{1,9},{2,10},{3,11},{4,12},{5,13},{6,14},{7,15}} | collective-permute-start | bytes 393224 | tf_op jit(solution)/shard_map/ppermute | solution.py:334
  154.3 1.2 collective-permute-done.28.above
  155.5 2.3 %product_by_rows.3 = (f32[256,256]{1,0:T(8,128)S(1)}, bf16[256,256]{1,0:T(8,128)(2,1)}, bf16[256,256]{1,0:T(8,128)(2,1)}, bf16[256,256]{1,0:T(8,128)(2,1)S(1)}) custom-call(s32[1,1,3]{2,1,0:T(1,128)S(1)} %copy-done.18, s32[1]{0:T(128)S(6)} %copy.19.live, bf16[1,1024,1536]{2,1,0:T(8,128)(2,1)S(1)} %copy-done.1, ...), custom_call_target="tpu_custom_call" | custom-call | flops 805306368 | bytes 5242880 | tf_op jit(solution)/shard_map/product_by_rows/pallas_call | solution.py:70
  158.5 3.9 %collective-permute-start.31 = (bf16[256,256]{1,0:T(8,128)(2,1)S(1)}, bf16[256,256]{1,0:T(8,128)(2,1)}, u32[]{:S(2)}, u32[]{:S(2)}) collective-permute-start(bf16[256,256]{1,0:T(8,128)(2,1)S(1)} %get-tuple-element.77), channel_id=1, source_target_pairs={{0,24},{8,0},{16,8},{24,16},{1,25},{9,1},{17,9},{25,17},{2,26},{10... | collective-permute-start | bytes 393224 | tf_op jit(solution)/shard_map/ppermute | solution.py:244
  163.0 4.2 %collective-permute-done.29 = bf16[256,256]{1,0:T(8,128)(2,1)} collective-permute-done((bf16[256,256]{1,0:T(8,128)(2,1)}, bf16[256,256]{1,0:T(8,128)(2,1)}, u32[]{:S(2)}, u32[]{:S(2)}) %collective-permute-start.29) | collective-permute-done | bytes 131104 | tf_op jit(solution)/shard_map/ppermute | solution.py:244
  167.1 4.6 %collective-permute-done.30 = bf16[256,256]{1,0:T(8,128)(2,1)} collective-permute-done((bf16[256,256]{1,0:T(8,128)(2,1)}, bf16[256,256]{1,0:T(8,128)(2,1)}, u32[]{:S(2)}, u32[]{:S(2)}) %collective-permute-start.30) | collective-permute-done | bytes 131104 | tf_op jit(solution)/shard_map/ppermute | solution.py:244
  171.7 3.4 %add_bitcast_fusion = (f32[1,1,256,256]{3,2,1,0:T(8,128)}, bf16[256,256]{1,0:T(8,128)(2,1)}) fusion(f32[256]{0:T(256)S(1)} %bitcast.56, f32[256]{0:T(256)S(1)} %broadcast_multiply_fusion.2, f32[256]{0:T(256)S(1)} %bitcast.58, bf16[256,256]{1,0:T(8,128)(2,1)} %collective-permute-done.31, bf16[256,256]{1,0:T(8,128)(2,1)} %collective-permute-done.30, ...), kind=kLoop, calls=%fused_computation.98 | loop fusion | flops 5111808 | bytes 2362371 | tf_op jit(solution)/shard_map/broadcast_in_dim | solution.py:339
  (93 shorter events, 11.0 us)
Async XLA Ops:
  0.6 31.9 %copy-start.20 = (f32[1,1,256]{2,1,0:T(1,128)S(1)}, f32[1,1,256]{2,1,0:T(1,128)}, u32[]{:S(2)}) copy-start(f32[1,1,256]{2,1,0:T(1,128)} %coef_a.1) | copy-start | bytes 3076
  0.6 31.9 %copy-start.19 = (f32[1,1,256]{2,1,0:T(1,128)S(1)}, f32[1,1,256]{2,1,0:T(1,128)}, u32[]{:S(2)}) copy-start(f32[1,1,256]{2,1,0:T(1,128)} %coef_b.1) | copy-start | bytes 3076
  0.7 31.8 %copy-start.21 = (f32[1,1,256]{2,1,0:T(1,128)S(1)}, f32[1,1,256]{2,1,0:T(1,128)}, u32[]{:S(2)}) copy-start(f32[1,1,256]{2,1,0:T(1,128)} %sigma.1) | copy-start | bytes 3076
  0.7 34.5 %copy-start.18 = (s32[1,1,3]{2,1,0:T(1,128)S(1)}, s32[1,1,3]{2,1,0:T(1,128)}, u32[]{:S(2)}) copy-start(s32[1,1,3]{2,1,0:T(1,128)} %picks.11) | copy-start | bytes 40
  0.7 15.1 %collective-permute-start.8 = (bf16[1024,256]{1,0:T(8,128)(2,1)}, bf16[1024,256]{1,0:T(8,128)(2,1)S(1)}, u32[]{:S(2)}, u32[]{:S(2)}) collective-permute-start(bf16[1024,256]{1,0:T(8,128)(2,1)} %bitcast.42), channel_id=1, source_target_pairs={{0,8},{8,16},{16,24},{1,9},{9,17},{17,25},{2,10},{10,18},{18,26},{... | collective-permute-start | bytes 1572872 | tf_op jit(solution)/shard_map/ppermute | solution.py:288
  4.3 13.6 %collective-permute-start = (bf16[1024,256]{1,0:T(8,128)(2,1)}, bf16[1024,256]{1,0:T(8,128)(2,1)S(1)}, u32[]{:S(2)}, u32[]{:S(2)}) collective-permute-start(bf16[1024,256]{1,0:T(8,128)(2,1)} %bitcast.43), channel_id=1, source_target_pairs={{0,1},{1,2},{2,3},{3,4},{4,5},{5,6},{6,7},{8,9},{9,10},{10,11},{11... | collective-permute-start | bytes 1572872 | tf_op jit(solution)/shard_map/ppermute | solution.py:27
  6.3 13.5 %collective-permute-start.1 = (bf16[1024,256]{1,0:T(8,128)(2,1)}, bf16[1024,256]{1,0:T(8,128)(2,1)S(1)}, u32[]{:S(2)}, u32[]{:S(2)}) collective-permute-start(bf16[1024,256]{1,0:T(8,128)(2,1)} %bitcast.44), channel_id=1, source_target_pairs={{1,0},{2,1},{3,2},{4,3},{5,4},{6,5},{7,6},{9,8},{10,9},{11,10},{12... | collective-permute-start | bytes 1572872 | tf_op jit(solution)/shard_map/ppermute | solution.py:27
  15.8 16.8 %collective-permute-start.10 = (bf16[1024,256]{1,0:T(8,128)(2,1)S(1)}, bf16[1024,256]{1,0:T(8,128)(2,1)S(1)}, u32[]{:S(2)}, u32[]{:S(2)}) collective-permute-start(bf16[1024,256]{1,0:T(8,128)(2,1)S(1)} %collective-permute-done.8.own), channel_id=1, source_target_pairs={{9,8},{10,9},{11,10},{12,11},{13,12},{14,13},{15,14},{17,16},{18,1... | collective-permute-start | bytes 1572872 | tf_op jit(solution)/shard_map/ppermute | solution.py:27
  16.5 17.4 %collective-permute-start.9 = (bf16[1024,256]{1,0:T(8,128)(2,1)S(1)}, bf16[1024,256]{1,0:T(8,128)(2,1)S(1)}, u32[]{:S(2)}, u32[]{:S(2)}) collective-permute-start(bf16[1024,256]{1,0:T(8,128)(2,1)S(1)} %collective-permute-done.8.own), channel_id=1, source_target_pairs={{8,9},{9,10},{10,11},{11,12},{12,13},{13,14},{14,15},{16,17},{17,1... | collective-permute-start | bytes 1572872 | tf_op jit(solution)/shard_map/ppermute | solution.py:27
  19.8 1.9 %copy-start = (bf16[1,1024,1536]{2,1,0:T(8,128)(2,1)S(1)}, bf16[1,1024,1536]{2,1,0:T(8,128)(2,1)}, u32[]{:S(2)}) copy-start(bf16[1,1024,1536]{2,1,0:T(8,128)(2,1)} %tile.11) | copy-start | bytes 9437188
  21.7 1.0 copy-start.4
  22.7 0.7 copy-start.17
  23.4 9.1 %copy-start.3 = (f32[1,1,256,256]{3,2,1,0:T(8,128)S(1)}, f32[1,1,256,256]{3,2,1,0:T(8,128)}, u32[]{:S(2)}) copy-start(f32[1,1,256,256]{3,2,1,0:T(8,128)} %state.1) | copy-start | bytes 786436
  23.4 11.8 %copy-start.1 = (bf16[1,1024,1536]{2,1,0:T(8,128)(2,1)S(1)}, bf16[1,1024,1536]{2,1,0:T(8,128)(2,1)}, u32[]{:S(2)}) copy-start(bf16[1,1024,1536]{2,1,0:T(8,128)(2,1)} %tile.11) | copy-start | bytes 9437188
  23.4 11.8 %copy-start.2 = (f32[1,1,256,256]{3,2,1,0:T(8,128)S(1)}, f32[1,1,256,256]{3,2,1,0:T(8,128)}, u32[]{:S(2)}) copy-start(f32[1,1,256,256]{3,2,1,0:T(8,128)} %stress.7) | copy-start | bytes 786436
  25.1 11.6 %collective-permute-start.2 = (bf16[256,256]{1,0:T(8,128)(2,1)S(1)}, bf16[256,256]{1,0:T(8,128)(2,1)S(1)}, u32[]{:S(2)}, u32[]{:S(2)}) collective-permute-start(bf16[256,256]{1,0:T(8,128)(2,1)S(1)} %get-tuple-element.64), channel_id=1, source_target_pairs={{0,8},{8,16},{16,24},{24,0},{1,9},{9,17},{17,25},{25,1},{2,10},{10... | collective-permute-start | bytes 393224 | tf_op jit(solution)/shard_map/ppermute | solution.py:244
  28.6 12.1 %collective-permute-start.3 = (bf16[256,256]{1,0:T(8,128)(2,1)S(1)}, bf16[256,256]{1,0:T(8,128)(2,1)S(1)}, u32[]{:S(2)}, u32[]{:S(2)}) collective-permute-start(bf16[256,256]{1,0:T(8,128)(2,1)S(1)} %get-tuple-element.65), channel_id=1, source_target_pairs={{0,16},{8,24},{16,0},{24,8},{1,17},{9,25},{17,1},{25,9},{2,18},{10... | collective-permute-start | bytes 393224 | tf_op jit(solution)/shard_map/ppermute | solution.py:244
  31.1 11.0 %collective-permute-start.4 = (bf16[256,256]{1,0:T(8,128)(2,1)S(1)}, bf16[256,256]{1,0:T(8,128)(2,1)S(1)}, u32[]{:S(2)}, u32[]{:S(2)}) collective-permute-start(bf16[256,256]{1,0:T(8,128)(2,1)S(1)} %get-tuple-element.66), channel_id=1, source_target_pairs={{0,24},{8,0},{16,8},{24,16},{1,25},{9,1},{17,9},{25,17},{2,26},{10... | collective-permute-start | bytes 393224 | tf_op jit(solution)/shard_map/ppermute | solution.py:244
  32.5 12.6 %copy-start.6 = (f32[264,256]{1,0:T(8,128)}, f32[264,256]{1,0:T(8,128)S(1)}, u32[]{:S(2)}) copy-start(f32[264,256]{1,0:T(8,128)S(1)} %pack.1.refs_0_) | copy-start | bytes 811012
  32.6 25.4 %collective-permute-start.15 = (f32[264,256]{1,0:T(8,128)S(1)}, f32[264,256]{1,0:T(8,128)S(1)}, u32[]{:S(2)}, u32[]{:S(2)}) collective-permute-start(f32[264,256]{1,0:T(8,128)S(1)} %pack.1.refs_0_), channel_id=1, source_target_pairs={{8,0},{9,1},{10,2},{11,3},{12,4},{13,5},{14,6},{15,7}} | collective-permute-start | bytes 811016 | tf_op jit(solution)/shard_map/ppermute | solution.py:287
  33.9 24.8 %collective-permute-start.16 = (f32[264,256]{1,0:T(8,128)S(1)}, f32[264,256]{1,0:T(8,128)S(1)}, u32[]{:S(2)}, u32[]{:S(2)}) collective-permute-start(f32[264,256]{1,0:T(8,128)S(1)} %pack.1.refs_0_), channel_id=1, source_target_pairs={{16,0},{17,1},{18,2},{19,3},{20,4},{21,5},{22,6},{23,7}} | collective-permute-start | bytes 811016 | tf_op jit(solution)/shard_map/ppermute | solution.py:287
  36.6 22.8 %collective-permute-start.17 = (f32[264,256]{1,0:T(8,128)S(1)}, f32[264,256]{1,0:T(8,128)S(1)}, u32[]{:S(2)}, u32[]{:S(2)}) collective-permute-start(f32[264,256]{1,0:T(8,128)S(1)} %pack.1.refs_0_), channel_id=1, source_target_pairs={{24,0},{25,1},{26,2},{27,3},{28,4},{29,5},{30,6},{31,7}} | collective-permute-start | bytes 811016 | tf_op jit(solution)/shard_map/ppermute | solution.py:287
  40.6 23.3 %collective-permute-start.18 = (bf16[1024,256]{1,0:T(8,128)(2,1)S(1)}, bf16[1024,256]{1,0:T(8,128)(2,1)}, u32[]{:S(2)}, u32[]{:S(2)}) collective-permute-start(bf16[1024,256]{1,0:T(8,128)(2,1)S(1)} %collective-permute-done.8.own), channel_id=1, source_target_pairs={{8,16},{16,24},{9,17},{17,25},{10,18},{18,26},{11,19},{19,27},{12,... | collective-permute-start | bytes 1572872 | tf_op jit(solution)/shard_map/ppermute | solution.py:299
  42.1 43.1 %collective-permute-start.11 = (bf16[1024,256]{1,0:T(8,128)(2,1)}, bf16[1024,256]{1,0:T(8,128)(2,1)}, u32[]{:S(2)}, u32[]{:S(2)}) collective-permute-start(bf16[1024,256]{1,0:T(8,128)(2,1)} %block_product.4), channel_id=1, source_target_pairs={{8,0},{24,16},{9,1},{25,17},{10,2},{26,18},{11,3},{27,19},{12,4},{... | collective-permute-start | bytes 1572872 | tf_op jit(solution)/shard_map/ppermute | solution.py:257
  58.0 0.7 copy-start.8
  58.7 8.3 %collective-permute-start.5 = (bf16[256,256]{1,0:T(8,128)(2,1)S(1)}, bf16[256,256]{1,0:T(8,128)(2,1)S(1)}, u32[]{:S(2)}, u32[]{:S(2)}) collective-permute-start(bf16[256,256]{1,0:T(8,128)(2,1)S(1)} %get-tuple-element.85.refs_0_), channel_id=1, source_target_pairs={{0,8},{8,16},{16,24},{24,0},{1,9},{9,17},{17,25},{25,1},{2,10},{10... | collective-permute-start | bytes 393224 | tf_op jit(solution)/shard_map/ppermute | solution.py:294
  58.7 0.7 copy-start.10
  59.4 13.6 %collective-permute-start.6 = (bf16[256,256]{1,0:T(8,128)(2,1)S(1)}, bf16[256,256]{1,0:T(8,128)(2,1)}, u32[]{:S(2)}, u32[]{:S(2)}) collective-permute-start(bf16[256,256]{1,0:T(8,128)(2,1)S(1)} %get-tuple-element.85.refs_0_), channel_id=1, source_target_pairs={{0,16},{8,24},{16,0},{24,8},{1,17},{9,25},{17,1},{25,9},{2,18},{10... | collective-permute-start | bytes 393224 | tf_op jit(solution)/shard_map/ppermute | solution.py:294
  59.4 0.7 copy-start.12
  60.1 17.6 %collective-permute-start.7 = (bf16[256,256]{1,0:T(8,128)(2,1)S(1)}, bf16[256,256]{1,0:T(8,128)(2,1)}, u32[]{:S(2)}, u32[]{:S(2)}) collective-permute-start(bf16[256,256]{1,0:T(8,128)(2,1)S(1)} %get-tuple-element.85.refs_0_), channel_id=1, source_target_pairs={{0,24},{8,0},{16,8},{24,16},{1,25},{9,1},{17,9},{25,17},{2,26},{10... | collective-permute-start | bytes 393224 | tf_op jit(solution)/shard_map/ppermute | solution.py:294
  63.9 23.9 %collective-permute-start.20 = (bf16[1024,256]{1,0:T(8,128)(2,1)}, bf16[1024,256]{1,0:T(8,128)(2,1)}, u32[]{:S(2)}, u32[]{:S(2)}) collective-permute-start(bf16[1024,256]{1,0:T(8,128)(2,1)} %collective-permute-done.18.own), channel_id=1, source_target_pairs={{16,17},{17,18},{18,19},{19,20},{20,21},{21,22},{22,23},{24,25},{2... | collective-permute-start | bytes 1572872 | tf_op jit(solution)/shard_map/ppermute | solution.py:27
  67.7 20.2 %collective-permute-start.21 = (bf16[1024,256]{1,0:T(8,128)(2,1)}, bf16[1024,256]{1,0:T(8,128)(2,1)}, u32[]{:S(2)}, u32[]{:S(2)}) collective-permute-start(bf16[1024,256]{1,0:T(8,128)(2,1)} %collective-permute-done.18.own), channel_id=1, source_target_pairs={{17,16},{18,17},{19,18},{20,19},{21,20},{22,21},{23,22},{25,24},{2... | collective-permute-start | bytes 1572872 | tf_op jit(solution)/shard_map/ppermute | solution.py:27
  69.1 1.0 copy-start.7
  70.1 1.0 copy-start.9
  71.0 1.0 copy-start.11
  72.0 1.0 copy-start.13
  77.7 0.9 copy-start.16
  79.6 15.1 %copy-start.23 = (bf16[1024,256]{1,0:T(8,128)(2,1)}, bf16[1024,256]{1,0:T(8,128)(2,1)S(1)}, u32[]{:S(2)}) copy-start(bf16[1024,256]{1,0:T(8,128)(2,1)S(1)} %assemble.1.own) | copy-start | bytes 1572868
  79.6 11.7 %collective-permute-start.12 = (bf16[1024,256]{1,0:T(8,128)(2,1)S(1)}, bf16[1024,256]{1,0:T(8,128)(2,1)S(1)}, u32[]{:S(2)}, u32[]{:S(2)}) collective-permute-start(bf16[1024,256]{1,0:T(8,128)(2,1)S(1)} %assemble.1.own), channel_id=1, source_target_pairs={{0,1},{1,2},{2,3},{3,4},{4,5},{5,6},{6,7},{8,9},{9,10},{10,11},{11... | collective-permute-start | bytes 1572872 | tf_op jit(solution)/shard_map/ppermute | solution.py:27
  81.6 13.2 %collective-permute-start.13 = (bf16[1024,256]{1,0:T(8,128)(2,1)S(1)}, bf16[1024,256]{1,0:T(8,128)(2,1)S(1)}, u32[]{:S(2)}, u32[]{:S(2)}) collective-permute-start(bf16[1024,256]{1,0:T(8,128)(2,1)S(1)} %assemble.1.own), channel_id=1, source_target_pairs={{1,0},{2,1},{3,2},{4,3},{5,4},{6,5},{7,6},{9,8},{10,9},{11,10},{12... | collective-permute-start | bytes 1572872 | tf_op jit(solution)/shard_map/ppermute | solution.py:27
  86.5 16.5 %collective-permute-start.14 = (bf16[1024,256]{1,0:T(8,128)(2,1)S(1)}, bf16[1024,256]{1,0:T(8,128)(2,1)S(1)}, u32[]{:S(2)}, u32[]{:S(2)}) collective-permute-start(bf16[1024,256]{1,0:T(8,128)(2,1)S(1)} %add_convert_fusion.1), channel_id=1, source_target_pairs={{16,0},{17,1},{18,2},{19,3},{20,4},{21,5},{22,6},{23,7}} | collective-permute-start | bytes 1572872 | tf_op jit(solution)/shard_map/ppermute | solution.py:257
  89.3 27.0 %collective-permute-start.22 = (bf16[1024,256]{1,0:T(8,128)(2,1)}, bf16[1024,256]{1,0:T(8,128)(2,1)}, u32[]{:S(2)}, u32[]{:S(2)}) collective-permute-start(bf16[1024,256]{1,0:T(8,128)(2,1)} %block_product.6), channel_id=1, source_target_pairs={{24,16},{25,17},{26,18},{27,19},{28,20},{29,21},{30,22},{31,23}} | collective-permute-start | bytes 1572872 | tf_op jit(solution)/shard_map/ppermute | solution.py:257
  91.3 11.7 %copy-start.22 = (f32[1024,256]{1,0:T(8,128)}, f32[1024,256]{1,0:T(8,128)S(1)}, u32[]{:S(2)}) copy-start(f32[1024,256]{1,0:T(8,128)S(1)} %multiply_add_fusion.2) | copy-start | bytes 3145732
  97.5 32.9 %collective-permute-start.26 = (bf16[1024,256]{1,0:T(8,128)(2,1)}, bf16[1024,256]{1,0:T(8,128)(2,1)}, u32[]{:S(2)}, u32[]{:S(2)}) collective-permute-start(bf16[1024,256]{1,0:T(8,128)(2,1)} %get-tuple-element.71), channel_id=1, source_target_pairs={{8,0},{9,1},{10,2},{11,3},{12,4},{13,5},{14,6},{15,7}} | collective-permute-start | bytes 1572872 | tf_op jit(solution)/shard_map/ppermute | solution.py:307
  109.2 17.5 %copy-start.24 = (bf16[1024,256]{1,0:T(8,128)(2,1)}, bf16[1024,256]{1,0:T(8,128)(2,1)S(1)}, u32[]{:S(2)}) copy-start(bf16[1024,256]{1,0:T(8,128)(2,1)S(1)} %get-tuple-element.70.own) | copy-start | bytes 1572868
  109.2 17.5 %copy-start.26 = (f32[1024,256]{1,0:T(8,128)}, f32[1024,256]{1,0:T(8,128)S(1)}, u32[]{:S(2)}) copy-start(f32[1024,256]{1,0:T(8,128)S(1)} %get-tuple-element.72) | copy-start | bytes 3145732
  109.2 17.5 %collective-permute-start.24 = (bf16[1024,256]{1,0:T(8,128)(2,1)S(1)}, bf16[1024,256]{1,0:T(8,128)(2,1)S(1)}, u32[]{:S(2)}, u32[]{:S(2)}) collective-permute-start(bf16[1024,256]{1,0:T(8,128)(2,1)S(1)} %get-tuple-element.70.own), channel_id=1, source_target_pairs={{0,1},{1,2},{2,3},{3,4},{4,5},{5,6},{6,7}} | collective-permute-start | bytes 1572872 | tf_op jit(solution)/shard_map/ppermute | solution.py:27
  111.1 16.4 %collective-permute-start.25 = (bf16[1024,256]{1,0:T(8,128)(2,1)S(1)}, bf16[1024,256]{1,0:T(8,128)(2,1)S(1)}, u32[]{:S(2)}, u32[]{:S(2)}) collective-permute-start(bf16[1024,256]{1,0:T(8,128)(2,1)S(1)} %get-tuple-element.70.own), channel_id=1, source_target_pairs={{1,0},{2,1},{3,2},{4,3},{5,4},{6,5},{7,6}} | collective-permute-start | bytes 1572872 | tf_op jit(solution)/shard_map/ppermute | solution.py:27
  114.8 11.8 %collective-permute-start.19 = (bf16[1024,256]{1,0:T(8,128)(2,1)S(1)}, bf16[1024,256]{1,0:T(8,128)(2,1)S(1)}, u32[]{:S(2)}, u32[]{:S(2)}) collective-permute-start(bf16[1024,256]{1,0:T(8,128)(2,1)S(1)} %broadcast_select_fusion.1), channel_id=1, source_target_pairs={{0,8},{16,24},{1,9},{17,25},{2,10},{18,26},{3,11},{19,27},{4,12},{... | collective-permute-start | bytes 1572872 | tf_op jit(solution)/shard_map/ppermute | solution.py:326
  117.7 15.6 %collective-permute-start.23 = (bf16[1024,256]{1,0:T(8,128)(2,1)S(1)}, bf16[1024,256]{1,0:T(8,128)(2,1)S(1)}, u32[]{:S(2)}, u32[]{:S(2)}) collective-permute-start(bf16[1024,256]{1,0:T(8,128)(2,1)S(1)} %add_convert_fusion), channel_id=1, source_target_pairs={{16,0},{17,1},{18,2},{19,3},{20,4},{21,5},{22,6},{23,7}} | collective-permute-start | bytes 1572872 | tf_op jit(solution)/shard_map/ppermute | solution.py:257
  126.7 0.8 copy-start.28
  140.2 1.0 copy-start.25
  141.1 13.2 %collective-permute-start.27 = (bf16[1024,256]{1,0:T(8,128)(2,1)}, bf16[1024,256]{1,0:T(8,128)(2,1)S(1)}, u32[]{:S(2)}, u32[]{:S(2)}) collective-permute-start(bf16[1024,256]{1,0:T(8,128)(2,1)} %get-tuple-element.73.own), channel_id=1, source_target_pairs={{0,1},{1,2},{2,3},{3,4},{4,5},{5,6},{6,7},{8,9},{9,10},{10,11},{11... | collective-permute-start | bytes 1572872 | tf_op jit(solution)/shard_map/ppermute | solution.py:27
  143.0 12.4 %collective-permute-start.28 = (bf16[1024,256]{1,0:T(8,128)(2,1)}, bf16[1024,256]{1,0:T(8,128)(2,1)S(1)}, u32[]{:S(2)}, u32[]{:S(2)}) collective-permute-start(bf16[1024,256]{1,0:T(8,128)(2,1)} %get-tuple-element.73.own), channel_id=1, source_target_pairs={{1,0},{2,1},{3,2},{4,3},{5,4},{6,5},{7,6},{9,8},{10,9},{11,10},{12... | collective-permute-start | bytes 1572872 | tf_op jit(solution)/shard_map/ppermute | solution.py:27
  148.4 5.9 %copy-start.27 = (bf16[1024,256]{1,0:T(8,128)(2,1)}, bf16[1024,256]{1,0:T(8,128)(2,1)S(1)}, u32[]{:S(2)}) copy-start(bf16[1024,256]{1,0:T(8,128)(2,1)S(1)} %subtract_convert_fusion) | copy-start | bytes 1572868
  148.4 14.0 %copy-start.5 = (bf16[1,1024,256]{2,1,0:T(8,128)(2,1)S(1)}, bf16[1,1024,256]{2,1,0:T(8,128)(2,1)}, u32[]{:S(2)}) copy-start(bf16[1,1024,256]{2,1,0:T(8,128)(2,1)} %param.16) | copy-start | bytes 1572868
  149.1 9.4 %collective-permute-start.32 = (bf16[256,256]{1,0:T(8,128)(2,1)S(1)}, bf16[256,256]{1,0:T(8,128)(2,1)S(1)}, u32[]{:S(2)}, u32[]{:S(2)}) collective-permute-start(bf16[256,256]{1,0:T(8,128)(2,1)S(1)} %get-tuple-element.89), channel_id=1, source_target_pairs={{0,24},{1,25},{2,26},{3,27},{4,28},{5,29},{6,30},{7,31}} | collective-permute-start | bytes 393224 | tf_op jit(solution)/shard_map/ppermute | solution.py:334
  150.4 12.6 %collective-permute-start.33 = (bf16[256,256]{1,0:T(8,128)(2,1)}, bf16[256,256]{1,0:T(8,128)(2,1)}, u32[]{:S(2)}, u32[]{:S(2)}) collective-permute-start(bf16[256,256]{1,0:T(8,128)(2,1)} %get-tuple-element.88), channel_id=1, source_target_pairs={{0,16},{1,17},{2,18},{3,19},{4,20},{5,21},{6,22},{7,23}} | collective-permute-start | bytes 393224 | tf_op jit(solution)/shard_map/ppermute | solution.py:334
  152.4 10.6 %collective-permute-start.34 = (bf16[256,256]{1,0:T(8,128)(2,1)}, bf16[256,256]{1,0:T(8,128)(2,1)}, u32[]{:S(2)}, u32[]{:S(2)}) collective-permute-start(bf16[256,256]{1,0:T(8,128)(2,1)} %get-tuple-element.87), channel_id=1, source_target_pairs={{0,8},{1,9},{2,10},{3,11},{4,12},{5,13},{6,14},{7,15}} | collective-permute-start | bytes 393224 | tf_op jit(solution)/shard_map/ppermute | solution.py:334
  157.8 0.7 copy-start.14
  158.5 8.6 %collective-permute-start.29 = (bf16[256,256]{1,0:T(8,128)(2,1)}, bf16[256,256]{1,0:T(8,128)(2,1)}, u32[]{:S(2)}, u32[]{:S(2)}) collective-permute-start(bf16[256,256]{1,0:T(8,128)(2,1)} %get-tuple-element.75), channel_id=1, source_target_pairs={{0,8},{8,16},{16,24},{24,0},{1,9},{9,17},{17,25},{25,1},{2,10},{10... | collective-permute-start | bytes 393224 | tf_op jit(solution)/shard_map/ppermute | solution.py:244
  158.5 13.2 %collective-permute-start.30 = (bf16[256,256]{1,0:T(8,128)(2,1)}, bf16[256,256]{1,0:T(8,128)(2,1)}, u32[]{:S(2)}, u32[]{:S(2)}) collective-permute-start(bf16[256,256]{1,0:T(8,128)(2,1)} %get-tuple-element.76), channel_id=1, source_target_pairs={{0,16},{8,24},{16,0},{24,8},{1,17},{9,25},{17,1},{25,9},{2,18},{10... | collective-permute-start | bytes 393224 | tf_op jit(solution)/shard_map/ppermute | solution.py:244
  158.5 3.9 %copy-start.29 = (bf16[256,256]{1,0:T(8,128)(2,1)}, bf16[256,256]{1,0:T(8,128)(2,1)S(1)}, u32[]{:S(2)}) copy-start(bf16[256,256]{1,0:T(8,128)(2,1)S(1)} %collective-permute-done.32) | copy-start | bytes 393220
  158.5 13.2 %collective-permute-start.31 = (bf16[256,256]{1,0:T(8,128)(2,1)S(1)}, bf16[256,256]{1,0:T(8,128)(2,1)}, u32[]{:S(2)}, u32[]{:S(2)}) collective-permute-start(bf16[256,256]{1,0:T(8,128)(2,1)S(1)} %get-tuple-element.77), channel_id=1, source_target_pairs={{0,24},{8,0},{16,8},{24,16},{1,25},{9,1},{17,9},{25,17},{2,26},{10... | collective-permute-start | bytes 393224 | tf_op jit(solution)/shard_map/ppermute | solution.py:244
  (1 other events, 0.7 us)
